TPU v7x, 32 devices: a whole 2x2x4 slice. The times are simulated.
32 devices in a mesh: exp: 8 (over y, x, core), tp: 4 (over z).
Axes of the slice: x: 2, y: 2, z: 4, core: 2. Of those that a mesh axis runs over, the one named last changes fastest.
Arguments:
- attn_part: bfloat16 [4, 256, 7168], P('tp', 'exp'), may hold values from -2.5 to 2.5
- resid: bfloat16 [256, 7168], P('exp', 'tp'), may hold values from -50 to 50
- refusal: float32 [7168], replicated, may hold values from -4 to 4
- norm_gain: float32 [7168], P('tp'), may hold values from 0.5 to 1.5
- route_ids: int32 [256, 8], P('exp'), may hold values from 0 to 31, all different within a row; in each aligned block of 32 rows (0 to 31, 32 to 63, ...) at most 16 rows name the same one
- gate_q: int32 [256, 8], P('exp'), may hold values from 16 to 255
- w_gate: bfloat16 [32, 7168, 2048], P('exp', None, 'tp'), may hold values from -0.0625 to 0.0625
- w_up: bfloat16 [32, 7168, 2048], P('exp', None, 'tp'), may hold values from -0.0625 to 0.0625
- w_down: bfloat16 [32, 2048, 7168], P('exp', 'tp'), may hold values from -0.125 to 0.125
Outputs:
- layer_out: bfloat16 [256, 7168], P('exp', 'tp')
Inputs may be any that keep to these rules, and one draw needn't show every extreme that they name: `route_ids`: each row names 8 different experts; in each aligned block of 32 rows (the tokens of one index of exp) no expert is named by more than 16 rows, a bound that some block reaches.
All inputs are finite; a program needn't handle non-finite values.
Results may differ from a plain program's by a relative error of at most 0.015.
Values may be sent and summed in bfloat16 or wider, within the bound.
No kernel may reach another device: no remote copies, remote signals or barrier semaphores. Data moves between devices by JAX's collectives and lax.ppermute only.
A program may use at most 256 MiB of HBM per device.

v0:
```python
import jax
import jax.numpy as jnp
from jax import lax
from jax.sharding import PartitionSpec as P

CAP = 16


EPSILON = 1e-06
GATE_UNIT = 128.0


def route_tables(route_ids, gate_q, experts, slot_count):
    row_count = route_ids.shape[0]
    matches = route_ids[:, :, None] == jnp.arange(experts, dtype=jnp.int32)[None, None, :]
    named_count = jnp.sum(matches.astype(jnp.int32), axis=1, dtype=jnp.int32)
    weight = jnp.sum(jnp.where(matches, gate_q[:, :, None], 0), axis=1, dtype=jnp.int32)
    before = jnp.cumsum(named_count, axis=0, dtype=jnp.int32) - named_count
    placed = (named_count[:, :, None] == 1) & (
        before[:, :, None] == jnp.arange(slot_count, dtype=jnp.int32)[None, None, :]
    )
    select = placed.reshape(row_count, experts * slot_count)
    scaled = jnp.where(placed, weight[:, :, None].astype(jnp.float32) / GATE_UNIT, 0.0)
    scaled = scaled.reshape(row_count, experts * slot_count)
    return (select.astype(jnp.bfloat16).T, scaled.astype(jnp.bfloat16))


def apply_experts(inputs, gate_weight, up_weight, down_weight):
    gate_act = jnp.einsum("sicd,idh->sich", inputs, gate_weight, preferred_element_type=jnp.float32)
    up_act = jnp.einsum("sicd,idh->sich", inputs, up_weight, preferred_element_type=jnp.float32)
    activation = (jax.nn.silu(gate_act) * up_act).astype(jnp.bfloat16)
    term = jnp.einsum("sich,ihd->sicd", activation, down_weight, preferred_element_type=jnp.float32)
    return term.astype(jnp.bfloat16)


def local(attn_part, resid, refusal, norm_gain, route_ids, gate_q, w_gate, w_up, w_down):
    highest = lax.Precision.HIGHEST
    tp_count = lax.axis_size("tp")
    exp_count = lax.axis_size("exp")
    full_width = refusal.shape[0]
    col_count = full_width // tp_count
    local_experts = w_gate.shape[0]
    experts = local_experts * exp_count
    attn_summed = lax.psum_scatter(
        attn_part[0].astype(jnp.float32).astype(jnp.bfloat16), "tp", scatter_dimension=1, tiled=True
    ).astype(jnp.float32)
    summed_heads = resid.astype(jnp.float32) + attn_summed
    unit = refusal * lax.rsqrt(jnp.sum(refusal * refusal) + EPSILON)
    unit_cols = lax.dynamic_slice_in_dim(unit, lax.axis_index("tp") * col_count, col_count, 0)
    along_part = jnp.dot(summed_heads, unit_cols, precision=highest)
    along, energy = lax.psum((along_part, jnp.sum(summed_heads * summed_heads, axis=1)), "tp")
    projected = summed_heads - along[:, None] * unit_cols[None, :]
    squares = energy - along * along * (2.0 - jnp.sum(unit * unit))
    inverse = lax.rsqrt(squares / full_width + EPSILON)
    normed = (projected * inverse[:, None] * norm_gain[None, :]).astype(jnp.bfloat16)
    select, scaled = route_tables(route_ids, gate_q, experts, CAP)
    full_rows = lax.all_gather(normed, "tp", axis=1, tiled=True)
    outgoing = jnp.dot(select, full_rows, preferred_element_type=jnp.float32).astype(jnp.bfloat16)
    outgoing = outgoing.reshape(exp_count, local_experts, CAP, full_width)
    expert_terms = apply_experts(
        lax.all_to_all(outgoing, "exp", split_axis=0, concat_axis=0, tiled=True),
        w_gate,
        w_up,
        w_down,
    )
    returned = lax.all_to_all(expert_terms, "exp", split_axis=0, concat_axis=0, tiled=True)
    partial_sum = jnp.dot(
        scaled, returned.reshape(experts * CAP, full_width), preferred_element_type=jnp.float32
    )
    mixed_cols = lax.psum_scatter(
        partial_sum.astype(jnp.bfloat16), "tp", scatter_dimension=1, tiled=True
    ).astype(jnp.float32)
    return (projected + mixed_cols).astype(jnp.bfloat16)


def solution(mesh):
    return jax.shard_map(
        local,
        mesh=mesh,
        in_specs=(
            P("tp", "exp", None),
            P("exp", "tp"),
            P(),
            P("tp"),
            P("exp", None),
            P("exp", None),
            P("exp", None, "tp"),
            P("exp", None, "tp"),
            P("exp", "tp", None),
        ),
        out_specs=P("exp", "tp"),
        check_vma=False,
    )
```

profile of v0, /device:TPU:0, one launch (start us, length us, event | category | flops | bytes accessed | tf_op | source)
XLA Modules:
  0.0 321.4 jit_solution(12197363555979041016)
XLA Ops:
  6.5 0.7 reduce-scatter.3.cloned.1.call-update
  7.3 1.4 multiply_reduce_fusion.2
  9.3 1.4 multiply_reduce_fusion.1
  10.7 0.1 dynamic_slice.3
  10.8 0.8 copy.26
  11.5 0.8 copy.29
  12.3 0.2 convert_reduce_fusion
  12.4 0.1 reduce_window_sum.11
  12.5 0.1 copy.28
  12.6 0.1 copy.27
  12.7 0.1 eq.66
  13.4 0.1 fusion.35
  13.6 19.8 %reduce-scatter.3.cloned.1.call-done = bf16[32,1792]{1,0:T(8,128)(2,1)} async-done(((bf16[32,7168]{1,0:T(8,128)(2,1)}), bf16[32,1792]{1,0:T(8,128)(2,1)}) %reduce-scatter.3.cloned.1.call-update) | async-done | bytes 114704 | tf_op jit(solution)/shard_map/reduce_scatter | solution.py:44
  33.4 1.1 multiply_reduce_fusion
  34.5 1.2 convolution_bitcast_fusion
  35.7 8.7 %all-reduce = (f32[32]{0:T(128)S(1)}, f32[32]{0:T(128)S(1)}) all-reduce(f32[32]{0:T(128)S(1)} %multiply_reduce_fusion, f32[32]{0:T(128)S(1)} %convolution_bitcast_fusion), channel_id=1, replica_groups=mesh['exp'=8,'tp'=4] {'tp'}, use_global_device_ids=true, to_apply=%region_7.8 | all-reduce | flops 64 | bytes 512 | tf_op jit(solution)/shard_map/psum | solution.py:51
  44.4 1.1 multiply_convert_fusion
  45.5 14.5 %all_gather.3 = bf16[32,7168]{1,0:T(8,128)(2,1)S(1)} all-gather(bf16[32,1792]{1,0:T(8,128)(2,1)S(1)} %multiply_convert_fusion), channel_id=1, replica_groups=mesh['exp'=8,'tp'=4] {'tp'}, dimensions={1}, use_global_device_ids=true | all-gather | bytes 573440 | tf_op jit(solution)/shard_map/all_gather | solution.py:57
  59.9 2.0 convolution_convert_fusion
  62.0 86.6 %all_to_all.10 = bf16[8,4,16,7168]{3,2,1,0:T(8,128)(2,1)} all-to-all(bf16[8,4,16,7168]{3,2,1,0:T(8,128)(2,1)S(1)} %bitcast.55), channel_id=1, replica_groups=mesh['exp'=8,'tp'=4] {'exp'}, dimensions={0} | all-to-all | bytes 14680064 | tf_op jit(solution)/shard_map/all_to_all | solution.py:61
  148.6 13.5 %fusion.14 = f32[8,4,16,512]{3,2,0,1:T(8,128)S(1)} fusion(bf16[4,7168,512]{2,1,0:T(8,128)(2,1)} %param.15, bf16[8,4,16,7168]{3,2,1,0:T(8,128)(2,1)} %all_to_all.10), kind=kOutput, calls=%fused_computation.12 | convolution fusion | flops 3758096384 | bytes 37748736 | tf_op jit(solution)/shard_map/sicd,idh->sich/dot_general | solution.py:29
  162.1 15.5 %fusion.29 = bf16[8,4,16,512]{3,2,0,1:T(8,128)(2,1)S(1)} fusion(bf16[4,7168,512]{2,1,0:T(8,128)(2,1)} %param.16, bf16[8,4,16,7168]{3,2,1,0:T(8,128)(2,1)} %all_to_all.10, f32[8,4,16,512]{3,2,0,1:T(8,128)S(1)} %fusion.14), kind=kOutput, calls=%fused_computation.15 | convolution fusion | flops 3759669248 | bytes 38273024 | tf_op jit(solution)/shard_map/sicd,idh->sich/dot_general | solution.py:30
  177.6 16.3 %fusion.9 = bf16[8,4,16,7168]{3,2,0,1:T(8,128)(2,1)} fusion(bf16[8,4,16,512]{3,2,0,1:T(8,128)(2,1)S(1)} %fusion.29, bf16[4,512,7168]{2,1,0:T(8,128)(2,1)} %param.17), kind=kOutput, calls=%fused_computation.8 | convolution fusion | flops 3761766400 | bytes 37224448 | tf_op jit(solution)/shard_map/sich,ihd->sicd/dot_general | solution.py:32
  194.0 6.9 %copy.33 = bf16[8,4,16,7168]{3,2,1,0:T(8,128)(2,1)} copy(bf16[8,4,16,7168]{3,2,0,1:T(8,128)(2,1)} %fusion.9) | data formatting | bytes 14680064 | tf_op jit(solution)/shard_map/convert_element_type | solution.py:33
  200.8 4.8 %all-to-all-start.1 = ((bf16[8,4,16,7168]{3,2,1,0:T(8,128)(2,1)}), bf16[8,4,16,7168]{3,2,1,0:T(8,128)(2,1)}, u32[]{:S(2)}, u32[]{:S(2)}) async-start(bf16[8,4,16,7168]{3,2,1,0:T(8,128)(2,1)} %copy.33), calls=%async_computation.2 | async-start | bytes 14680064 | tf_op jit(solution)/shard_map/all_to_all | solution.py:66
  205.7 0.0 reduce-scatter.5.cloned.1.call-start
  205.8 0.1 copy.30
  205.8 0.1 select_convert_fusion
  205.9 82.6 %all-to-all-done.1 = bf16[8,4,16,7168]{3,2,1,0:T(8,128)(2,1)} async-done(((bf16[8,4,16,7168]{3,2,1,0:T(8,128)(2,1)}), bf16[8,4,16,7168]{3,2,1,0:T(8,128)(2,1)}, u32[]{:S(2)}, u32[]{:S(2)}) %all-to-all-start.1) | async-done | bytes 7340064 | tf_op jit(solution)/shard_map/all_to_all | solution.py:66
  288.5 5.3 %convolution_convert_fusion.1 = bf16[32,7168]{1,0:T(8,128)(2,1)} fusion(bf16[32,512]{0,1:T(8,128)(2,1)S(1)} %bitcast.56, bf16[512,7168]{1,0:T(8,128)(2,1)} %bitcast.15), kind=kOutput, calls=%fused_computation.9 | convolution fusion | flops 235110400 | bytes 7831552 | tf_op jit(solution)/shard_map/dot_general | solution.py:67
  293.8 19.1 %reduce-scatter.5.cloned.1.call-done = bf16[32,1792]{1,0:T(8,128)(2,1)} async-done(((bf16[32,7168]{1,0:T(8,128)(2,1)}), bf16[32,1792]{1,0:T(8,128)(2,1)}) %reduce-scatter.5.cloned.1.call-update) | async-done | bytes 114704 | tf_op jit(solution)/shard_map/reduce_scatter | solution.py:70
  312.9 1.6 add_convert_fusion
  (12 shorter events, 0.1 us)
Async XLA Ops:
  6.5 26.8 %reduce-scatter.3.cloned.1.call-start = ((), (), s32[]{:S(2)}) async-start(), calls=%async_computation.4 | async-start | bytes 573440 | tf_op jit(solution)/shard_map/reduce_scatter | solution.py:44
  200.8 87.7 %all-to-all-start.1 = ((bf16[8,4,16,7168]{3,2,1,0:T(8,128)(2,1)}), bf16[8,4,16,7168]{3,2,1,0:T(8,128)(2,1)}, u32[]{:S(2)}, u32[]{:S(2)}) async-start(bf16[8,4,16,7168]{3,2,1,0:T(8,128)(2,1)} %copy.33), calls=%async_computation.2 | async-start | bytes 14680064 | tf_op jit(solution)/shard_map/all_to_all | solution.py:66
  205.7 107.3 %copy-start = (bf16[32,1792]{1,0:T(8,128)(2,1)S(1)}, bf16[32,1792]{1,0:T(8,128)(2,1)}, u32[]{:S(2)}) copy-start(bf16[32,1792]{1,0:T(8,128)(2,1)} %param.10) | copy-start | bytes 344068
  205.7 107.2 %copy-start.1 = (bf16[32,1792]{1,0:T(8,128)(2,1)S(1)}, bf16[32,1792]{1,0:T(8,128)(2,1)}, u32[]{:S(2)}) copy-start(bf16[32,1792]{1,0:T(8,128)(2,1)} %reduce-scatter.3.cloned.1.call-done) | copy-start | bytes 344068
  205.7 107.2 %reduce-scatter.5.cloned.1.call-start = ((), (), s32[]{:S(2)}) async-start(), calls=%async_computation.5 | async-start | bytes 573440 | tf_op jit(solution)/shard_map/reduce_scatter | solution.py:70
Sparse Core Ops, SparseCore 0:
  9.6 23.6 reduce-scatter.2
  293.9 18.9 reduce-scatter.4
where the time goes:
time: 322 us; the launch traced here: 321 us
  waiting for transfers between devices  122 us (38%)
  blocking collectives  110 us (34%)
  matrix products  53.8 us (17%)
  between operations  14.9 us (5%)
  local copies, waits for them, and re-layouts  8.82 us (3%)
  other arithmetic  6.99 us (2%)
  starting transfers between devices  4.89 us (2%)
    all_to_all x1, blocking collectives, local(): lax.all_to_all(outgoing, 'exp', split_axis=0, concat_axis=0, tiled=True)  86.6 us
    all_to_all x1, waiting for transfers between devices, local(): lax.all_to_all(expert_terms, 'exp', split_axis=0, concat_axis=0, tiled=True)  82.6 us
    reduce_scatter x1, waiting for transfers between devices, local(): lax.psum_scatter(attn_part[0].astype(jnp.float32).astype(jnp.bfloat16), '...  19.8 us
    reduce_scatter x1, waiting for transfers between devices, local(): lax.psum_scatter(partial_sum.astype(jnp.bfloat16), 'tp', scatter_dimensio...  19.1 us
    dot_general x1, matrix products, apply_experts(): jnp.einsum('sich,ihd->sicd', activation, down_weight, preferred_element_t...  16.3 us
    dot_general x1, matrix products, apply_experts(): jnp.einsum('sicd,idh->sich', inputs, up_weight, preferred_element_type=jn...  15.5 us
    all_gather x1, blocking collectives, local(): full_rows = lax.all_gather(normed, 'tp', axis=1, tiled=True)  14.5 us
    dot_general x1, matrix products, apply_experts(): jnp.einsum('sicd,idh->sich', inputs, gate_weight, preferred_element_type=...  13.5 us
  transfers between devices with their start and end apart: 3, of which 3 were waited for; matrix products, arithmetic and copies ran while one was open for 2% of the time, Pallas kernels for 0%

commit v1 on v0

v1 whole, which is shorter than its diff:
```python
import functools
import jax
import jax.numpy as jnp
from jax import lax
from jax.experimental import pallas as pl
from jax.experimental.pallas import tpu as pltpu
from jax.sharding import PartitionSpec as P

EPSILON = 1e-06
GATE_UNIT = 128.0
LANES = 128
VMEM_LIMIT = 56 << 20
F32 = jnp.float32
BF16 = jnp.bfloat16


def vmem():
    return pl.BlockSpec(memory_space=pltpu.VMEM)


def smem():
    return pl.BlockSpec(memory_space=pltpu.SMEM)


def params():
    return pltpu.CompilerParams(vmem_limit_bytes=VMEM_LIMIT)


def swap(value, axis, bit):
    count = lax.axis_size(axis)
    return lax.ppermute(value, axis, [(i, i ^ bit) for i in range(count)])


def exp_bits(exp_count):
    plane = [1 << i for i in range(1, exp_count.bit_length() - 1)]
    x_bits, y_bits = plane[: len(plane) // 2], plane[len(plane) // 2 :]
    return [1] if exp_count > 1 else [], (x_bits + y_bits, y_bits + x_bits)


def relative_order(bits):
    order = [0]
    for bit in reversed(bits):
        order = order + [pattern ^ bit for pattern in order]
    return order


def three_parts(value):
    first = value.astype(BF16)
    rest = value - first.astype(F32)
    second = rest.astype(BF16)
    third = (rest - second.astype(F32)).astype(BF16)
    return first.astype(F32), second.astype(F32), third.astype(F32)


def sum_kernel(*refs):
    parts, (resid, unit, message, summed) = refs[:-4], refs[-4:]
    total = parts[0][...].astype(F32)
    for part in parts[1:]:
        total = total + part[...].astype(F32)
    rows = resid[...].astype(F32) + total
    summed[...] = rows
    u = unit[...]
    inner = jnp.sum(rows * u, axis=1, keepdims=True)
    own = inner / (jnp.sum(u * u) + EPSILON)
    width = rows.shape[1]
    message[:, :width] = (rows - own * u).astype(BF16)
    first, second, third = three_parts(inner)
    lane = lax.broadcasted_iota(jnp.int32, (rows.shape[0], LANES), 1)
    packed = jnp.where(lane == 0, first, jnp.where(lane == 1, second, jnp.where(lane == 2, third, 0.0)))
    message[:, width:] = packed.astype(BF16)


def norm_kernel(tp_count, me, unit, ids, gates, *refs):
    messages, gains = refs[:tp_count], refs[tp_count : 2 * tp_count]
    outs, along_out = refs[2 * tp_count : -1], refs[-1]
    width = gains[0].shape[1]
    rows = messages[0].shape[0]
    inner, units = [], []
    for k in range(tp_count):
        tail = messages[k][:, width:].astype(F32)
        inner.append(jnp.sum(tail, axis=1, keepdims=True))
        units.append(unit[:, pl.ds(pl.multiple_of((me[0] ^ k) * width, LANES), width)])
    along = functools.reduce(lambda a, b: a + b, inner)
    along_out[...] = jnp.broadcast_to(along, along_out.shape)
    projected, square = [], 0.0
    for k in range(tp_count):
        u = units[k]
        own = inner[k] / (jnp.sum(u * u) + EPSILON)
        value = messages[k][:, :width].astype(F32) + (own - along) * u
        square = square + jnp.sum(value * value, axis=1, keepdims=True)
        projected.append(value)
    inverse = lax.rsqrt(square / (width * tp_count) + EPSILON)
    half = rows // len(outs)
    for k in range(tp_count):
        normed = (projected[k] * inverse * gains[k][...]).astype(BF16)
        for i, out in enumerate(outs):
            out[:, k * width : (k + 1) * width] = normed[i * half : (i + 1) * half]
    lane = lax.broadcasted_iota(jnp.int32, (rows, LANES), 1)
    table = jnp.zeros((rows, LANES), F32)
    for i in range(ids.shape[1]):
        table = table + jnp.where(ids[:, i : i + 1] == lane, gates[:, i : i + 1].astype(F32), 0.0)
    table = (table / GATE_UNIT).astype(BF16)
    for i, out in enumerate(outs):
        out[:, tp_count * width :] = table[i * half : (i + 1) * half]


def up_kernel(piece_count, me, first, w_gate, w_up, *refs):
    pieces, (out, rows, table, gate_acc, up_acc) = refs[:piece_count], refs[piece_count:]
    expert, k = pl.program_id(0), pl.program_id(1)
    depth = w_gate.shape[1]
    full = rows.shape[1]

    @pl.when((expert == 0) & (k == 0))
    def _():
        height = pieces[0].shape[0]
        for i, piece in enumerate(pieces):
            rows[i * height : (i + 1) * height, :] = piece[:, :full]
            table[i * height : (i + 1) * height, :] = piece[:, full:]

    x = rows[:, pl.ds(pl.multiple_of(k * depth, LANES), depth)]
    gate = jnp.dot(x, w_gate[0], preferred_element_type=F32)
    up = jnp.dot(x, w_up[0], preferred_element_type=F32)

    @pl.when(k == 0)
    def _():
        gate_acc[...] = gate
        up_acc[...] = up

    @pl.when(k > 0)
    def _():
        gate_acc[...] += gate
        up_acc[...] += up

    @pl.when(k == pl.num_programs(1) - 1)
    def _():
        lane = lax.broadcasted_iota(jnp.int32, table.shape, 1)
        weight = jnp.sum(jnp.where(lane == first[0] + expert, table[...].astype(F32), 0.0), axis=1, keepdims=True)
        out[...] = (jax.nn.silu(gate_acc[...]) * up_acc[...] * weight).astype(BF16)


def down_kernel(me, activation, w_down, keep, send):
    weights = w_down[...].reshape(-1, w_down.shape[2])
    total = jnp.dot(activation[...], weights, preferred_element_type=F32).astype(BF16)
    half = keep.shape[0]
    keep[...] = total[:half]
    send[...] = total[half:]


def gather_rows(halves, core, orders):
    gathered = []
    for half, order in zip(halves, orders):
        pieces = {0: half}
        for bit in list(order) + core:
            pieces.update({pattern ^ bit: swap(piece, "exp", bit) for pattern, piece in list(pieces.items())})
        gathered.append(pieces)
    return gathered


def add(a, b):
    return (a.astype(F32) + b.astype(F32)).astype(BF16)


def scatter_rows(keep, send, core, orders):
    got = swap(send, "exp", core[0])
    results = []
    height = keep.shape[0] // len(orders)
    for i, order in enumerate(orders):
        mine, theirs = keep[i * height : (i + 1) * height], got[i * height : (i + 1) * height]
        for bit in order:
            middle = mine.shape[0] // 2
            away = add(mine[middle:], theirs[middle:])
            mine = add(mine[:middle], theirs[:middle])
            theirs = swap(away, "exp", bit)
        results.append((mine, theirs))
    return results


def local(attn_part, resid, refusal, norm_gain, route_ids, gate_q, w_gate, w_up, w_down):
    tp_count = lax.axis_size("tp")
    exp_count = lax.axis_size("exp")
    rows, cols = resid.shape
    full = refusal.shape[0]
    local_experts, _, hidden = w_gate.shape
    t = lax.axis_index("tp")
    me = t.astype(jnp.int32).reshape(1)
    first = (lax.axis_index("exp") * local_experts).astype(jnp.int32).reshape(1)
    core, orders = exp_bits(exp_count)
    half = rows // 2

    own = [lax.dynamic_slice_in_dim(attn_part[0], (t ^ k) * cols, cols, 1) for k in range(tp_count)]
    heads = [own[0]] + [swap(own[k], "tp", k) for k in range(1, tp_count)]
    gain = norm_gain.reshape(1, cols)
    gains = [gain] + [swap(gain, "tp", k) for k in range(1, tp_count)]
    unit = (refusal * lax.rsqrt(jnp.sum(refusal * refusal) + EPSILON)).reshape(1, full)
    unit_cols = lax.dynamic_slice_in_dim(unit, t * cols, cols, 1)

    message, summed = pl.pallas_call(
        sum_kernel,
        out_shape=(
            jax.ShapeDtypeStruct((rows, cols + LANES), BF16),
            jax.ShapeDtypeStruct((rows, cols), F32),
        ),
        in_specs=[vmem()] * (tp_count + 2),
        out_specs=(vmem(), vmem()),
        compiler_params=params(),
        name="sum_heads",
    )(*heads, resid, unit_cols)
    messages = [message] + [swap(message, "tp", k) for k in range(1, tp_count)]

    *halves, along = pl.pallas_call(
        functools.partial(norm_kernel, tp_count),
        out_shape=(
            jax.ShapeDtypeStruct((half, full + LANES), BF16),
            jax.ShapeDtypeStruct((half, full + LANES), BF16),
            jax.ShapeDtypeStruct((rows, LANES), F32),
        ),
        in_specs=[smem()] + [vmem()] * (3 + 2 * tp_count),
        out_specs=(vmem(), vmem(), vmem()),
        compiler_params=params(),
        name="norm_rows",
    )(me, unit, route_ids, gate_q, *messages, *gains)

    gathered = gather_rows(halves, core, orders)
    pieces = []
    for bit in [0] + core:
        for found, order in zip(gathered, orders):
            pieces += [found[bit ^ pattern] for pattern in relative_order(order)]
    total_rows = rows * exp_count

    activation = pl.pallas_call(
        functools.partial(up_kernel, len(pieces)),
        out_shape=jax.ShapeDtypeStruct((total_rows, local_experts * hidden), BF16),
        grid_spec=pltpu.PrefetchScalarGridSpec(
            num_scalar_prefetch=2,
            grid=(local_experts, tp_count),
            in_specs=[
                pl.BlockSpec((1, cols, hidden), lambda e, k, me, first: (e, me[0] ^ k, 0)),
                pl.BlockSpec((1, cols, hidden), lambda e, k, me, first: (e, me[0] ^ k, 0)),
            ]
            + [vmem()] * len(pieces),
            out_specs=pl.BlockSpec((total_rows, hidden), lambda e, k, me, first: (0, e)),
            scratch_shapes=[
                pltpu.VMEM((total_rows, full), BF16),
                pltpu.VMEM((total_rows, LANES), BF16),
                pltpu.VMEM((total_rows, hidden), F32),
                pltpu.VMEM((total_rows, hidden), F32),
            ],
        ),
        compiler_params=params(),
        name="gate_up",
    )(me, first, w_gate, w_up, *pieces)

    chunks = 2 if cols % (2 * LANES) == 0 else 1
    width = cols // chunks
    outs = []
    for chunk in range(chunks):
        keep, send = pl.pallas_call(
            down_kernel,
            out_shape=[jax.ShapeDtypeStruct((total_rows // 2, tp_count * width), BF16)] * 2,
            grid_spec=pltpu.PrefetchScalarGridSpec(
                num_scalar_prefetch=1,
                grid=(tp_count,),
                in_specs=[
                    vmem(),
                    pl.BlockSpec(
                        (local_experts, hidden, width),
                        lambda k, me, chunk=chunk: (0, 0, (me[0] ^ k) * chunks + chunk),
                    ),
                ],
                out_specs=[pl.BlockSpec((total_rows // 2, width), lambda k, me: (0, k))] * 2,
            ),
            compiler_params=params(),
            name="down",
        )(me, activation, w_down)
        results = scatter_rows(keep, send, core, orders)
        columns = []
        for k in range(tp_count):
            part = [
                add(mine[:, k * width : (k + 1) * width], theirs[:, k * width : (k + 1) * width])
                for mine, theirs in results
            ]
            part = jnp.concatenate(part, axis=0)
            columns.append(part if k == 0 else swap(part, "tp", k))
        mixed = functools.reduce(lambda a, b: a + b, [c.astype(F32) for c in columns])
        here = slice(chunk * width, (chunk + 1) * width)
        projected = summed[:, here] - along[:, :1] * unit_cols[:, here]
        outs.append((projected + mixed).astype(BF16))
    return jnp.concatenate(outs, axis=1)


def solution(mesh):
    return jax.shard_map(
        local,
        mesh=mesh,
        in_specs=(
            P("tp", "exp", None),
            P("exp", "tp"),
            P(),
            P("tp"),
            P("exp", None),
            P("exp", None),
            P("exp", None, "tp"),
            P("exp", None, "tp"),
            P("exp", "tp", None),
        ),
        out_specs=P("exp", "tp"),
        check_vma=False,
    )
```

time: 322 us -> 146 us (0.45)
  blocking collectives: 110 us -> 0 us
  waiting for transfers between devices: 122 us -> 40.1 us
  Pallas kernels: 0 us -> 54.4 us
  matrix products: 53.8 us -> 0 us
  starting transfers between devices: 4.89 us -> 36.7 us
  between operations: 14.9 us -> 1.07 us
    all_to_all x1 -> x0, blocking collectives: 86.6 us -> none  [local(): lax.all_to_all(outgoing, 'exp', split_axis=0, concat_axis=0, tiled=True)]
    all_to_all x1 -> x0, waiting for transfers between devices: 82.6 us -> none  [local(): lax.all_to_all(expert_terms, 'exp', split_axis=0, concat_axis=0, tiled=True)]
    pallas_call x0 -> x5, Pallas kernels: none -> 54.4 us  [the longest x1 31.1 us: local(): pl.pallas_call(functools.partial(up_kernel, len(pieces)), out_shape=jax.S...]
    dot_general x6 -> x0, matrix products: 53.8 us -> none  [the longest x1 16.3 us: apply_experts(): jnp.einsum('sich,ihd->sicd', activation, down_weight, preferred_element_t...]
    ppermute x0 -> x39, waiting for transfers between devices: none -> 40.1 us  [swap(): return lax.ppermute(value, axis, [(i, i ^ bit) for i in range(count)])]
    reduce_scatter x2 -> x0, waiting for transfers between devices: 38.9 us -> none  [the longest x1 19.8 us: local(): lax.psum_scatter(attn_part[0].astype(jnp.float32).astype(jnp.bfloat16), '...]
    ppermute x0 -> x39, starting transfers between devices: none -> 36.7 us  [swap(): return lax.ppermute(value, axis, [(i, i ^ bit) for i in range(count)])]
    all_gather x1 -> x0, blocking collectives: 14.5 us -> none  [local(): full_rows = lax.all_gather(normed, 'tp', axis=1, tiled=True)]
  transfers between devices with their start and end apart: 3 -> 39, of which waited for: 3 -> 17; matrix products, arithmetic and copies ran while one was open for 2% -> 6% of each run, Pallas kernels for 0% -> 6%
where the time goes in v1:
time: 146 us; the launch traced here: 145 us
  Pallas kernels  54.4 us (37%)
  waiting for transfers between devices  40.1 us (27%)
  starting transfers between devices  36.7 us (25%)
  local copies, waits for them, and re-layouts  7.97 us (5%)
  other arithmetic  4.99 us (3%)
    ppermute x39, waiting for transfers between devices, swap(): return lax.ppermute(value, axis, [(i, i ^ bit) for i in range(count)])  40.1 us
    ppermute x39, starting transfers between devices, swap(): return lax.ppermute(value, axis, [(i, i ^ bit) for i in range(count)])  36.7 us
    pallas_call x1, Pallas kernels, local(): pl.pallas_call(functools.partial(up_kernel, len(pieces)), out_shape=jax.S...  31.1 us
    pallas_call x2, Pallas kernels, local(): pl.pallas_call(down_kernel, out_shape=[jax.ShapeDtypeStruct((total_rows /...  18.8 us
    unnamed x60, local copies, waits for them, and re-layouts  4.72 us
  transfers between devices with their start and end apart: 39, of which 17 were waited for; matrix products, arithmetic and copies ran while one was open for 6% of the time, Pallas kernels for 6%

profile of v1, /device:TPU:0, one launch (start us, length us, event | category | flops | bytes accessed | tf_op | source)
XLA Modules:
  0.0 145.2 jit_solution(12585975727059690937)
XLA Ops:
  0.0 1.7 %dynamic-slice_bitcast_fusion = (bf16[32,1792]{1,0:T(8,128)(2,1)S(1)}, bf16[32,1792]{1,0:T(8,128)(2,1)S(1)}, bf16[32,1792]{1,0:T(8,128)(2,1)}, bf16[32,1792]{1,0:T(8,128)(2,1)S(1)}) fusion(bf16[1,32,7168]{2,1,0:T(8,128)(2,1)} %param.9, s32[]{:T(128)S(6)} %select_n.16, s32[]{:T(128)S(6)} %select_n.14, s32[]{:T(128)S(6)} %select_n.13, s32[]{:T(128)S(6)} %select_n.15), kind=kLoop, calls=%fused_computation.19 | loop fusion | bytes 917520 | tf_op jit(solution)/shard_map/dynamic_slice | solution.py:190
  1.7 5.0 %collective-permute-start.2 = (bf16[32,1792]{1,0:T(8,128)(2,1)S(1)}, bf16[32,1792]{1,0:T(8,128)(2,1)S(1)}, u32[]{:S(2)}, u32[]{:S(2)}) collective-permute-start(bf16[32,1792]{1,0:T(8,128)(2,1)S(1)} %get-tuple-element.41), channel_id=1, source_target_pairs={{0,3},{1,2},{2,1},{3,0},{4,7},{5,6},{6,5},{7,4},{8,11},{9,10},{10,... | collective-permute-start | bytes 344072 | tf_op jit(solution)/shard_map/ppermute | solution.py:31
  10.8 2.7 %collective-permute-done.refs_1_ = bf16[32,1792]{1,0:T(8,128)(2,1)S(1)} collective-permute-done((bf16[32,1792]{1,0:T(8,128)(2,1)S(1)}, bf16[32,1792]{1,0:T(8,128)(2,1)S(1)}, u32[]{:S(2)}, u32[]{:S(2)}) %collective-permute-start) | collective-permute-done | bytes 114720 | tf_op jit(solution)/shard_map/ppermute | solution.py:31
  13.5 3.0 %collective-permute-done.1.refs_2_ = bf16[32,1792]{1,0:T(8,128)(2,1)S(1)} collective-permute-done((bf16[32,1792]{1,0:T(8,128)(2,1)S(1)}, bf16[32,1792]{1,0:T(8,128)(2,1)S(1)}, u32[]{:S(2)}, u32[]{:S(2)}) %collective-permute-start.1) | collective-permute-done | bytes 114720 | tf_op jit(solution)/shard_map/ppermute | solution.py:31
  17.1 2.0 %sum_heads.1 = (bf16[32,1920]{1,0:T(8,128)(2,1)}, f32[32,1792]{1,0:T(8,128)}) custom-call(bf16[32,1792]{1,0:T(8,128)(2,1)} %get-tuple-element.43.refs_0_, bf16[32,1792]{1,0:T(8,128)(2,1)} %copy-done.21, bf16[32,1792]{1,0:T(8,128)(2,1)} %copy-done.22, bf16[32,1792]{1,0:T(8,128)(2,1)} %copy-done.20, bf16[32,1792]{1,0:T(8,128)(2,1)} %refs_4_.1, ...), custom_call_target="tpu_custom_call" | custom-call | tf_op jit(solution)/shard_map/sum_heads/pallas_call | solution.py:197
  19.1 2.5 %collective-permute-start.5 = (bf16[32,1920]{1,0:T(8,128)(2,1)}, bf16[32,1920]{1,0:T(8,128)(2,1)S(1)}, u32[]{:S(2)}, u32[]{:S(2)}) collective-permute-start(bf16[32,1920]{1,0:T(8,128)(2,1)} %get-tuple-element.15.refs_0_), channel_id=1, source_target_pairs={{0,3},{1,2},{2,1},{3,0},{4,7},{5,6},{6,5},{7,4},{8,11},{9,10},{10,... | collective-permute-start | bytes 368648 | tf_op jit(solution)/shard_map/ppermute | solution.py:31
  21.6 1.9 %collective-permute-start.3 = (bf16[32,1920]{1,0:T(8,128)(2,1)}, bf16[32,1920]{1,0:T(8,128)(2,1)S(1)}, u32[]{:S(2)}, u32[]{:S(2)}) collective-permute-start(bf16[32,1920]{1,0:T(8,128)(2,1)} %get-tuple-element.15.refs_0_), channel_id=1, source_target_pairs={{0,1},{1,0},{2,3},{3,2},{4,5},{5,4},{6,7},{7,6},{8,9},{9,8},{10,11... | collective-permute-start | bytes 368648 | tf_op jit(solution)/shard_map/ppermute | solution.py:31
  24.2 2.5 %collective-permute-start.8 = (f32[1,1792]{1,0:T(1,128)S(1)}, f32[1,1792]{1,0:T(1,128)S(1)}, u32[]{:S(2)}, u32[]{:S(2)}) collective-permute-start(f32[1,1792]{1,0:T(1,128)S(1)} %reshape.19.refs_4_), channel_id=1, source_target_pairs={{0,3},{1,2},{2,1},{3,0},{4,7},{5,6},{6,5},{7,4},{8,11},{9,10},{10,... | collective-permute-start | bytes 21512 | tf_op jit(solution)/shard_map/ppermute | solution.py:31
  26.7 4.5 %collective-permute-done.8.refs_7_ = f32[1,1792]{1,0:T(1,128)S(1)} collective-permute-done((f32[1,1792]{1,0:T(1,128)S(1)}, f32[1,1792]{1,0:T(1,128)S(1)}, u32[]{:S(2)}, u32[]{:S(2)}) %collective-permute-start.8) | collective-permute-done | bytes 7200 | tf_op jit(solution)/shard_map/ppermute | solution.py:31
  35.8 2.5 %norm_rows.1 = (bf16[16,7296]{1,0:T(8,128)(2,1)}, bf16[16,7296]{1,0:T(8,128)(2,1)}, f32[32,128]{1,0:T(8,128)}) custom-call(s32[1]{0:T(128)} %bitcast.4.me, f32[1,7168]{1,0:T(1,128)} %bitcast.11, s32[32,8]{1,0:T(8,128)} %copy.12.ids, s32[32,8]{1,0:T(8,128)} %copy.13.gates, bf16[32,1920]{1,0:T(8,128)(2,1)} %get-tuple-element.15.refs_0_, ...), custom_call_target="tpu_custom_call" | custom-call | tf_op jit(solution)/shard_map/norm_rows/pallas_call | solution.py:210
  38.3 1.5 %collective-permute-start.10 = (bf16[16,7296]{1,0:T(8,128)(2,1)}, bf16[16,7296]{1,0:T(8,128)(2,1)S(1)}, u32[]{:S(2)}, u32[]{:S(2)}) collective-permute-start(bf16[16,7296]{1,0:T(8,128)(2,1)} %get-tuple-element.17.refs_0_), channel_id=1, source_target_pairs={{0,8},{4,12},{8,0},{12,4},{16,24},{20,28},{24,16},{28,20},{1,9},{5... | collective-permute-start | bytes 700424 | tf_op jit(solution)/shard_map/ppermute | solution.py:31
  39.8 1.5 %collective-permute-start.9 = (bf16[16,7296]{1,0:T(8,128)(2,1)}, bf16[16,7296]{1,0:T(8,128)(2,1)S(1)}, u32[]{:S(2)}, u32[]{:S(2)}) collective-permute-start(bf16[16,7296]{1,0:T(8,128)(2,1)} %get-tuple-element.17.refs_0_), channel_id=1, source_target_pairs={{0,16},{4,20},{8,24},{12,28},{16,0},{20,4},{24,8},{28,12},{1,17},{... | collective-permute-start | bytes 700424 | tf_op jit(solution)/shard_map/ppermute | solution.py:31
  42.5 4.6 %collective-permute-done.10.refs_2_ = bf16[16,7296]{1,0:T(8,128)(2,1)S(1)} collective-permute-done((bf16[16,7296]{1,0:T(8,128)(2,1)}, bf16[16,7296]{1,0:T(8,128)(2,1)S(1)}, u32[]{:S(2)}, u32[]{:S(2)}) %collective-permute-start.10) | collective-permute-done | bytes 233504 | tf_op jit(solution)/shard_map/ppermute | solution.py:31
  47.0 1.5 %collective-permute-done.9.refs_1_ = bf16[16,7296]{1,0:T(8,128)(2,1)S(1)} collective-permute-done((bf16[16,7296]{1,0:T(8,128)(2,1)}, bf16[16,7296]{1,0:T(8,128)(2,1)S(1)}, u32[]{:S(2)}, u32[]{:S(2)}) %collective-permute-start.9) | collective-permute-done | bytes 233504 | tf_op jit(solution)/shard_map/ppermute | solution.py:31
  48.6 1.5 %collective-permute-start.11 = (bf16[16,7296]{1,0:T(8,128)(2,1)S(1)}, bf16[16,7296]{1,0:T(8,128)(2,1)S(1)}, u32[]{:S(2)}, u32[]{:S(2)}) collective-permute-start(bf16[16,7296]{1,0:T(8,128)(2,1)S(1)} %collective-permute-done.10.refs_2_), channel_id=1, source_target_pairs={{0,16},{4,20},{8,24},{12,28},{16,0},{20,4},{24,8},{28,12},{1,17},{... | collective-permute-start | bytes 700424 | tf_op jit(solution)/shard_map/ppermute | solution.py:31
  50.1 3.5 %collective-permute-done.13.refs_6_ = bf16[16,7296]{1,0:T(8,128)(2,1)S(1)} collective-permute-done((bf16[16,7296]{1,0:T(8,128)(2,1)}, bf16[16,7296]{1,0:T(8,128)(2,1)S(1)}, u32[]{:S(2)}, u32[]{:S(2)}) %collective-permute-start.13) | collective-permute-done | bytes 233504 | tf_op jit(solution)/shard_map/ppermute | solution.py:31
  54.7 3.1 %collective-permute-done.11.refs_3_ = bf16[16,7296]{1,0:T(8,128)(2,1)S(1)} collective-permute-done((bf16[16,7296]{1,0:T(8,128)(2,1)S(1)}, bf16[16,7296]{1,0:T(8,128)(2,1)S(1)}, u32[]{:S(2)}, u32[]{:S(2)}) %collective-permute-start.11) | collective-permute-done | bytes 233504 | tf_op jit(solution)/shard_map/ppermute | solution.py:31
  57.9 2.0 %collective-permute-done.14.refs_7_ = bf16[16,7296]{1,0:T(8,128)(2,1)S(1)} collective-permute-done((bf16[16,7296]{1,0:T(8,128)(2,1)S(1)}, bf16[16,7296]{1,0:T(8,128)(2,1)S(1)}, u32[]{:S(2)}, u32[]{:S(2)}) %collective-permute-start.14) | collective-permute-done | bytes 233504 | tf_op jit(solution)/shard_map/ppermute | solution.py:31
  59.9 1.4 collective-permute-done.22.refs_15_
  62.0 31.1 %gate_up.1.activation = bf16[256,2048]{1,0:T(8,128)(2,1)} custom-call(s32[1]{0:T(128)} %bitcast.4.me, s32[1]{0:T(128)} %bitcast.6.first, bf16[4,7168,512]{2,1,0:T(8,128)(2,1)} %w_gate.1, bf16[4,7168,512]{2,1,0:T(8,128)(2,1)} %w_up.1, bf16[16,7296]{1,0:T(8,128)(2,1)} %get-tuple-element.17.refs_0_, bf16[16,7296]{1,0:T(8,128)(2,1)} %copy-done.3, ...), custom_call_target="tpu_custom_call" | custom-call | tf_op jit(solution)/shard_map/gate_up/pallas_call | solution.py:230
  93.2 9.4 %down.2 = (bf16[128,3584]{1,0:T(8,128)(2,1)}, bf16[128,3584]{1,0:T(8,128)(2,1)}) custom-call(s32[1]{0:T(128)} %bitcast.4.me, bf16[256,2048]{1,0:T(8,128)(2,1)} %gate_up.1.activation, bf16[4,512,7168]{2,1,0:T(8,128)(2,1)} %w_down.3), custom_call_target="tpu_custom_call" | custom-call | tf_op jit(solution)/shard_map/down/pallas_call | solution.py:257
  102.8 9.4 %down.3 = (bf16[128,3584]{1,0:T(8,128)(2,1)}, bf16[128,3584]{1,0:T(8,128)(2,1)}) custom-call(s32[1]{0:T(128)} %bitcast.4.me, bf16[256,2048]{1,0:T(8,128)(2,1)} %gate_up.1.activation, bf16[4,512,7168]{2,1,0:T(8,128)(2,1)} %w_down.3), custom_call_target="tpu_custom_call" | custom-call | tf_op jit(solution)/shard_map/down/pallas_call | solution.py:257
  112.7 1.6 %collective-permute-start.26 = (bf16[32,3584]{1,0:T(8,128)(2,1)S(1)}, bf16[32,3584]{1,0:T(8,128)(2,1)S(1)}, u32[]{:S(2)}, u32[]{:S(2)}) collective-permute-start(bf16[32,3584]{1,0:T(8,128)(2,1)S(1)} %get-tuple-element.26), channel_id=1, source_target_pairs={{0,16},{4,20},{8,24},{12,28},{16,0},{20,4},{24,8},{28,12},{1,17},{... | collective-permute-start | bytes 688136 | tf_op jit(solution)/shard_map/ppermute | solution.py:31
  114.9 1.5 %add_convert_fusion.3 = (bf16[32,3584]{1,0:T(8,128)(2,1)S(1)}, bf16[32,3584]{1,0:T(8,128)(2,1)S(1)}, bf16[32,3584]{1,0:T(8,128)(2,1)S(1)}, bf16[32,3584]{1,0:T(8,128)(2,1)S(1)}) fusion(bf16[128,3584]{1,0:T(8,128)(2,1)S(1)} %collective-permute-done.31, bf16[128,3584]{1,0:T(8,128)(2,1)} %get-tuple-element.21), kind=kLoop, calls=%fused_computation.3 | loop fusion | flops 1835008 | bytes 2752512 | tf_op jit(solution)/shard_map/convert_element_type | solution.py:160
  116.4 1.6 %collective-permute-start.34 = (bf16[32,3584]{1,0:T(8,128)(2,1)S(1)}, bf16[32,3584]{1,0:T(8,128)(2,1)S(1)}, u32[]{:S(2)}, u32[]{:S(2)}) collective-permute-start(bf16[32,3584]{1,0:T(8,128)(2,1)S(1)} %get-tuple-element.30), channel_id=1, source_target_pairs={{0,16},{4,20},{8,24},{12,28},{16,0},{20,4},{24,8},{28,12},{1,17},{... | collective-permute-start | bytes 688136 | tf_op jit(solution)/shard_map/ppermute | solution.py:31
  118.5 2.7 %collective-permute-done.26 = bf16[32,3584]{1,0:T(8,128)(2,1)S(1)} collective-permute-done((bf16[32,3584]{1,0:T(8,128)(2,1)S(1)}, bf16[32,3584]{1,0:T(8,128)(2,1)S(1)}, u32[]{:S(2)}, u32[]{:S(2)}) %collective-permute-start.26) | collective-permute-done | bytes 229408 | tf_op jit(solution)/shard_map/ppermute | solution.py:31
  123.5 2.6 %collective-permute-done.34 = bf16[32,3584]{1,0:T(8,128)(2,1)S(1)} collective-permute-done((bf16[32,3584]{1,0:T(8,128)(2,1)S(1)}, bf16[32,3584]{1,0:T(8,128)(2,1)S(1)}, u32[]{:S(2)}, u32[]{:S(2)}) %collective-permute-start.34) | collective-permute-done | bytes 229408 | tf_op jit(solution)/shard_map/ppermute | solution.py:31
  128.5 1.7 %collective-permute-done.27 = bf16[16,3584]{1,0:T(8,128)(2,1)S(1)} collective-permute-done((bf16[16,3584]{1,0:T(8,128)(2,1)S(1)}, bf16[16,3584]{1,0:T(8,128)(2,1)S(1)}, u32[]{:S(2)}, u32[]{:S(2)}) %collective-permute-start.27) | collective-permute-done | bytes 114720 | tf_op jit(solution)/shard_map/ppermute | solution.py:31
  131.2 2.6 %collective-permute-start.29 = (bf16[32,896]{1,0:T(8,128)(2,1)S(1)}, bf16[32,896]{1,0:T(8,128)(2,1)S(1)}, u32[]{:S(2)}, u32[]{:S(2)}) collective-permute-start(bf16[32,896]{1,0:T(8,128)(2,1)S(1)} %pad_maximum_fusion.2), channel_id=1, source_target_pairs={{0,2},{1,3},{2,0},{3,1},{4,6},{5,7},{6,4},{7,5},{8,10},{9,11},{10,... | collective-permute-start | bytes 172040 | tf_op jit(solution)/shard_map/ppermute | solution.py:31
  134.9 3.5 %collective-permute-start.37 = (bf16[32,896]{1,0:T(8,128)(2,1)S(1)}, bf16[32,896]{1,0:T(8,128)(2,1)S(1)}, u32[]{:S(2)}, u32[]{:S(2)}) collective-permute-start(bf16[32,896]{1,0:T(8,128)(2,1)S(1)} %pad_maximum_fusion.5), channel_id=1, source_target_pairs={{0,2},{1,3},{2,0},{3,1},{4,6},{5,7},{6,4},{7,5},{8,10},{9,11},{10,... | collective-permute-start | bytes 172040 | tf_op jit(solution)/shard_map/ppermute | solution.py:31
  140.2 2.3 %collective-permute-done.37 = bf16[32,896]{1,0:T(8,128)(2,1)S(1)} collective-permute-done((bf16[32,896]{1,0:T(8,128)(2,1)S(1)}, bf16[32,896]{1,0:T(8,128)(2,1)S(1)}, u32[]{:S(2)}, u32[]{:S(2)}) %collective-permute-start.37) | collective-permute-done | bytes 57376 | tf_op jit(solution)/shard_map/ppermute | solution.py:31
  142.4 2.0 %collective-permute-done.38 = bf16[32,896]{1,0:T(8,128)(2,1)S(1)} collective-permute-done((bf16[32,896]{1,0:T(8,128)(2,1)S(1)}, bf16[32,896]{1,0:T(8,128)(2,1)S(1)}, u32[]{:S(2)}, u32[]{:S(2)}) %collective-permute-start.38) | collective-permute-done | bytes 57376 | tf_op jit(solution)/shard_map/ppermute | solution.py:31
  (137 shorter events, 23.3 us)
Async XLA Ops:
  1.7 9.1 %collective-permute-start.2 = (bf16[32,1792]{1,0:T(8,128)(2,1)S(1)}, bf16[32,1792]{1,0:T(8,128)(2,1)S(1)}, u32[]{:S(2)}, u32[]{:S(2)}) collective-permute-start(bf16[32,1792]{1,0:T(8,128)(2,1)S(1)} %get-tuple-element.41), channel_id=1, source_target_pairs={{0,3},{1,2},{2,1},{3,0},{4,7},{5,6},{6,5},{7,4},{8,11},{9,10},{10,... | collective-permute-start | bytes 344072 | tf_op jit(solution)/shard_map/ppermute | solution.py:31
  6.8 6.7 %collective-permute-start = (bf16[32,1792]{1,0:T(8,128)(2,1)S(1)}, bf16[32,1792]{1,0:T(8,128)(2,1)S(1)}, u32[]{:S(2)}, u32[]{:S(2)}) collective-permute-start(bf16[32,1792]{1,0:T(8,128)(2,1)S(1)} %get-tuple-element.42), channel_id=1, source_target_pairs={{0,1},{1,0},{2,3},{3,2},{4,5},{5,4},{6,7},{7,6},{8,9},{9,8},{10,11... | collective-permute-start | bytes 344072 | tf_op jit(solution)/shard_map/ppermute | solution.py:31
  6.8 9.7 %collective-permute-start.1 = (bf16[32,1792]{1,0:T(8,128)(2,1)S(1)}, bf16[32,1792]{1,0:T(8,128)(2,1)S(1)}, u32[]{:S(2)}, u32[]{:S(2)}) collective-permute-start(bf16[32,1792]{1,0:T(8,128)(2,1)S(1)} %get-tuple-element.44), channel_id=1, source_target_pairs={{0,2},{1,3},{2,0},{3,1},{4,6},{5,7},{6,4},{7,5},{8,10},{9,11},{10,... | collective-permute-start | bytes 344072 | tf_op jit(solution)/shard_map/ppermute | solution.py:31
  19.1 16.0 %collective-permute-start.5 = (bf16[32,1920]{1,0:T(8,128)(2,1)}, bf16[32,1920]{1,0:T(8,128)(2,1)S(1)}, u32[]{:S(2)}, u32[]{:S(2)}) collective-permute-start(bf16[32,1920]{1,0:T(8,128)(2,1)} %get-tuple-element.15.refs_0_), channel_id=1, source_target_pairs={{0,3},{1,2},{2,1},{3,0},{4,7},{5,6},{6,5},{7,4},{8,11},{9,10},{10,... | collective-permute-start | bytes 368648 | tf_op jit(solution)/shard_map/ppermute | solution.py:31
  21.6 13.5 %collective-permute-start.4 = (bf16[32,1920]{1,0:T(8,128)(2,1)}, bf16[32,1920]{1,0:T(8,128)(2,1)S(1)}, u32[]{:S(2)}, u32[]{:S(2)}) collective-permute-start(bf16[32,1920]{1,0:T(8,128)(2,1)} %get-tuple-element.15.refs_0_), channel_id=1, source_target_pairs={{0,2},{1,3},{2,0},{3,1},{4,6},{5,7},{6,4},{7,5},{8,10},{9,11},{10,... | collective-permute-start | bytes 368648 | tf_op jit(solution)/shard_map/ppermute | solution.py:31
  21.6 13.5 %collective-permute-start.3 = (bf16[32,1920]{1,0:T(8,128)(2,1)}, bf16[32,1920]{1,0:T(8,128)(2,1)S(1)}, u32[]{:S(2)}, u32[]{:S(2)}) collective-permute-start(bf16[32,1920]{1,0:T(8,128)(2,1)} %get-tuple-element.15.refs_0_), channel_id=1, source_target_pairs={{0,1},{1,0},{2,3},{3,2},{4,5},{5,4},{6,7},{7,6},{8,9},{9,8},{10,11... | collective-permute-start | bytes 368648 | tf_op jit(solution)/shard_map/ppermute | solution.py:31
  24.2 6.9 %collective-permute-start.8 = (f32[1,1792]{1,0:T(1,128)S(1)}, f32[1,1792]{1,0:T(1,128)S(1)}, u32[]{:S(2)}, u32[]{:S(2)}) collective-permute-start(f32[1,1792]{1,0:T(1,128)S(1)} %reshape.19.refs_4_), channel_id=1, source_target_pairs={{0,3},{1,2},{2,1},{3,0},{4,7},{5,6},{6,5},{7,4},{8,11},{9,10},{10,... | collective-permute-start | bytes 21512 | tf_op jit(solution)/shard_map/ppermute | solution.py:31
  26.6 8.4 %collective-permute-start.7 = (f32[1,1792]{1,0:T(1,128)S(1)}, f32[1,1792]{1,0:T(1,128)S(1)}, u32[]{:S(2)}, u32[]{:S(2)}) collective-permute-start(f32[1,1792]{1,0:T(1,128)S(1)} %reshape.19.refs_4_), channel_id=1, source_target_pairs={{0,2},{1,3},{2,0},{3,1},{4,6},{5,7},{6,4},{7,5},{8,10},{9,11},{10,... | collective-permute-start | bytes 21512 | tf_op jit(solution)/shard_map/ppermute | solution.py:31
  38.3 8.7 %collective-permute-start.10 = (bf16[16,7296]{1,0:T(8,128)(2,1)}, bf16[16,7296]{1,0:T(8,128)(2,1)S(1)}, u32[]{:S(2)}, u32[]{:S(2)}) collective-permute-start(bf16[16,7296]{1,0:T(8,128)(2,1)} %get-tuple-element.17.refs_0_), channel_id=1, source_target_pairs={{0,8},{4,12},{8,0},{12,4},{16,24},{20,28},{24,16},{28,20},{1,9},{5... | collective-permute-start | bytes 700424 | tf_op jit(solution)/shard_map/ppermute | solution.py:31
  39.8 8.7 %collective-permute-start.9 = (bf16[16,7296]{1,0:T(8,128)(2,1)}, bf16[16,7296]{1,0:T(8,128)(2,1)S(1)}, u32[]{:S(2)}, u32[]{:S(2)}) collective-permute-start(bf16[16,7296]{1,0:T(8,128)(2,1)} %get-tuple-element.17.refs_0_), channel_id=1, source_target_pairs={{0,16},{4,20},{8,24},{12,28},{16,0},{20,4},{24,8},{28,12},{1,17},{... | collective-permute-start | bytes 700424 | tf_op jit(solution)/shard_map/ppermute | solution.py:31
  41.3 12.2 %collective-permute-start.13 = (bf16[16,7296]{1,0:T(8,128)(2,1)}, bf16[16,7296]{1,0:T(8,128)(2,1)S(1)}, u32[]{:S(2)}, u32[]{:S(2)}) collective-permute-start(bf16[16,7296]{1,0:T(8,128)(2,1)} %get-tuple-element.18.refs_4_), channel_id=1, source_target_pairs={{0,16},{4,20},{8,24},{12,28},{16,0},{20,4},{24,8},{28,12},{1,17},{... | collective-permute-start | bytes 700424 | tf_op jit(solution)/shard_map/ppermute | solution.py:31
  41.8 12.3 %collective-permute-start.19 = (bf16[16,7296]{1,0:T(8,128)(2,1)}, bf16[16,7296]{1,0:T(8,128)(2,1)S(1)}, u32[]{:S(2)}, u32[]{:S(2)}) collective-permute-start(bf16[16,7296]{1,0:T(8,128)(2,1)} %get-tuple-element.18.refs_4_), channel_id=1, source_target_pairs={{0,4},{4,0},{8,12},{12,8},{16,20},{20,16},{24,28},{28,24},{1,5},{5... | collective-permute-start | bytes 700424 | tf_op jit(solution)/shard_map/ppermute | solution.py:31
  41.9 12.3 %collective-permute-start.12 = (bf16[16,7296]{1,0:T(8,128)(2,1)}, bf16[16,7296]{1,0:T(8,128)(2,1)S(1)}, u32[]{:S(2)}, u32[]{:S(2)}) collective-permute-start(bf16[16,7296]{1,0:T(8,128)(2,1)} %get-tuple-element.18.refs_4_), channel_id=1, source_target_pairs={{0,8},{4,12},{8,0},{12,4},{16,24},{20,28},{24,16},{28,20},{1,9},{5... | collective-permute-start | bytes 700424 | tf_op jit(solution)/shard_map/ppermute | solution.py:31
  47.0 7.6 %collective-permute-start.17 = (bf16[16,7296]{1,0:T(8,128)(2,1)S(1)}, bf16[16,7296]{1,0:T(8,128)(2,1)S(1)}, u32[]{:S(2)}, u32[]{:S(2)}) collective-permute-start(bf16[16,7296]{1,0:T(8,128)(2,1)S(1)} %collective-permute-done.10.refs_2_), channel_id=1, source_target_pairs={{0,4},{4,0},{8,12},{12,8},{16,20},{20,16},{24,28},{28,24},{1,5},{5... | collective-permute-start | bytes 700424 | tf_op jit(solution)/shard_map/ppermute | solution.py:31
  48.6 9.3 %collective-permute-start.11 = (bf16[16,7296]{1,0:T(8,128)(2,1)S(1)}, bf16[16,7296]{1,0:T(8,128)(2,1)S(1)}, u32[]{:S(2)}, u32[]{:S(2)}) collective-permute-start(bf16[16,7296]{1,0:T(8,128)(2,1)S(1)} %collective-permute-done.10.refs_2_), channel_id=1, source_target_pairs={{0,16},{4,20},{8,24},{12,28},{16,0},{20,4},{24,8},{28,12},{1,17},{... | collective-permute-start | bytes 700424 | tf_op jit(solution)/shard_map/ppermute | solution.py:31
  53.6 6.3 %collective-permute-start.14 = (bf16[16,7296]{1,0:T(8,128)(2,1)S(1)}, bf16[16,7296]{1,0:T(8,128)(2,1)S(1)}, u32[]{:S(2)}, u32[]{:S(2)}) collective-permute-start(bf16[16,7296]{1,0:T(8,128)(2,1)S(1)} %collective-permute-done.13.refs_6_), channel_id=1, source_target_pairs={{0,8},{4,12},{8,0},{12,4},{16,24},{20,28},{24,16},{28,20},{1,9},{5... | collective-permute-start | bytes 700424 | tf_op jit(solution)/shard_map/ppermute | solution.py:31
  54.1 5.8 %collective-permute-start.21 = (bf16[16,7296]{1,0:T(8,128)(2,1)S(1)}, bf16[16,7296]{1,0:T(8,128)(2,1)S(1)}, u32[]{:S(2)}, u32[]{:S(2)}) collective-permute-start(bf16[16,7296]{1,0:T(8,128)(2,1)S(1)} %collective-permute-done.13.refs_6_), channel_id=1, source_target_pairs={{0,4},{4,0},{8,12},{12,8},{16,20},{20,16},{24,28},{28,24},{1,5},{5... | collective-permute-start | bytes 700424 | tf_op jit(solution)/shard_map/ppermute | solution.py:31
  54.1 5.7 %collective-permute-start.16 = (bf16[16,7296]{1,0:T(8,128)(2,1)S(1)}, bf16[16,7296]{1,0:T(8,128)(2,1)S(1)}, u32[]{:S(2)}, u32[]{:S(2)}) collective-permute-start(bf16[16,7296]{1,0:T(8,128)(2,1)S(1)} %collective-permute-done.9.refs_1_), channel_id=1, source_target_pairs={{0,4},{4,0},{8,12},{12,8},{16,20},{20,16},{24,28},{28,24},{1,5},{5... | collective-permute-start | bytes 700424 | tf_op jit(solution)/shard_map/ppermute | solution.py:31
  102.6 9.9 %collective-permute-start.23 = (bf16[128,3584]{1,0:T(8,128)(2,1)}, bf16[128,3584]{1,0:T(8,128)(2,1)S(1)}, u32[]{:S(2)}, u32[]{:S(2)}) collective-permute-start(bf16[128,3584]{1,0:T(8,128)(2,1)} %get-tuple-element.20), channel_id=1, source_target_pairs={{0,4},{4,0},{8,12},{12,8},{16,20},{20,16},{24,28},{28,24},{1,5},{5... | collective-permute-start | bytes 2752520 | tf_op jit(solution)/shard_map/ppermute | solution.py:31
  112.7 8.5 %collective-permute-start.26 = (bf16[32,3584]{1,0:T(8,128)(2,1)S(1)}, bf16[32,3584]{1,0:T(8,128)(2,1)S(1)}, u32[]{:S(2)}, u32[]{:S(2)}) collective-permute-start(bf16[32,3584]{1,0:T(8,128)(2,1)S(1)} %get-tuple-element.26), channel_id=1, source_target_pairs={{0,16},{4,20},{8,24},{12,28},{16,0},{20,4},{24,8},{28,12},{1,17},{... | collective-permute-start | bytes 688136 | tf_op jit(solution)/shard_map/ppermute | solution.py:31
  114.3 8.5 %collective-permute-start.24 = (bf16[32,3584]{1,0:T(8,128)(2,1)S(1)}, bf16[32,3584]{1,0:T(8,128)(2,1)S(1)}, u32[]{:S(2)}, u32[]{:S(2)}) collective-permute-start(bf16[32,3584]{1,0:T(8,128)(2,1)S(1)} %get-tuple-element.28), channel_id=1, source_target_pairs={{0,8},{4,12},{8,0},{12,4},{16,24},{20,28},{24,16},{28,20},{1,9},{5... | collective-permute-start | bytes 688136 | tf_op jit(solution)/shard_map/ppermute | solution.py:31
  116.4 9.8 %collective-permute-start.34 = (bf16[32,3584]{1,0:T(8,128)(2,1)S(1)}, bf16[32,3584]{1,0:T(8,128)(2,1)S(1)}, u32[]{:S(2)}, u32[]{:S(2)}) collective-permute-start(bf16[32,3584]{1,0:T(8,128)(2,1)S(1)} %get-tuple-element.30), channel_id=1, source_target_pairs={{0,16},{4,20},{8,24},{12,28},{16,0},{20,4},{24,8},{28,12},{1,17},{... | collective-permute-start | bytes 688136 | tf_op jit(solution)/shard_map/ppermute | solution.py:31
  118.0 9.7 %collective-permute-start.32 = (bf16[32,3584]{1,0:T(8,128)(2,1)S(1)}, bf16[32,3584]{1,0:T(8,128)(2,1)S(1)}, u32[]{:S(2)}, u32[]{:S(2)}) collective-permute-start(bf16[32,3584]{1,0:T(8,128)(2,1)S(1)} %get-tuple-element.32), channel_id=1, source_target_pairs={{0,8},{4,12},{8,0},{12,4},{16,24},{20,28},{24,16},{28,20},{1,9},{5... | collective-permute-start | bytes 688136 | tf_op jit(solution)/shard_map/ppermute | solution.py:31
  121.3 8.9 %collective-permute-start.27 = (bf16[16,3584]{1,0:T(8,128)(2,1)S(1)}, bf16[16,3584]{1,0:T(8,128)(2,1)S(1)}, u32[]{:S(2)}, u32[]{:S(2)}) collective-permute-start(bf16[16,3584]{1,0:T(8,128)(2,1)S(1)} %get-tuple-element.36), channel_id=1, source_target_pairs={{0,8},{4,12},{8,0},{12,4},{16,24},{20,28},{24,16},{28,20},{1,9},{5... | collective-permute-start | bytes 344072 | tf_op jit(solution)/shard_map/ppermute | solution.py:31
  122.8 7.4 %collective-permute-start.25 = (bf16[16,3584]{1,0:T(8,128)(2,1)S(1)}, bf16[16,3584]{1,0:T(8,128)(2,1)S(1)}, u32[]{:S(2)}, u32[]{:S(2)}) collective-permute-start(bf16[16,3584]{1,0:T(8,128)(2,1)S(1)} %get-tuple-element.34), channel_id=1, source_target_pairs={{0,16},{4,20},{8,24},{12,28},{16,0},{20,4},{24,8},{28,12},{1,17},{... | collective-permute-start | bytes 344072 | tf_op jit(solution)/shard_map/ppermute | solution.py:31
  126.2 8.5 %collective-permute-start.35 = (bf16[16,3584]{1,0:T(8,128)(2,1)S(1)}, bf16[16,3584]{1,0:T(8,128)(2,1)S(1)}, u32[]{:S(2)}, u32[]{:S(2)}) collective-permute-start(bf16[16,3584]{1,0:T(8,128)(2,1)S(1)} %get-tuple-element.40), channel_id=1, source_target_pairs={{0,8},{4,12},{8,0},{12,4},{16,24},{20,28},{24,16},{28,20},{1,9},{5... | collective-permute-start | bytes 344072 | tf_op jit(solution)/shard_map/ppermute | solution.py:31
  127.8 7.0 %collective-permute-start.33 = (bf16[16,3584]{1,0:T(8,128)(2,1)S(1)}, bf16[16,3584]{1,0:T(8,128)(2,1)S(1)}, u32[]{:S(2)}, u32[]{:S(2)}) collective-permute-start(bf16[16,3584]{1,0:T(8,128)(2,1)S(1)} %get-tuple-element.38), channel_id=1, source_target_pairs={{0,16},{4,20},{8,24},{12,28},{16,0},{20,4},{24,8},{28,12},{1,17},{... | collective-permute-start | bytes 344072 | tf_op jit(solution)/shard_map/ppermute | solution.py:31
  130.3 8.2 %collective-permute-start.28 = (bf16[32,896]{1,0:T(8,128)(2,1)S(1)}, bf16[32,896]{1,0:T(8,128)(2,1)S(1)}, u32[]{:S(2)}, u32[]{:S(2)}) collective-permute-start(bf16[32,896]{1,0:T(8,128)(2,1)S(1)} %pad_maximum_fusion.1), channel_id=1, source_target_pairs={{0,1},{1,0},{2,3},{3,2},{4,5},{5,4},{6,7},{7,6},{8,9},{9,8},{10,11... | collective-permute-start | bytes 172040 | tf_op jit(solution)/shard_map/ppermute | solution.py:31
  131.2 8.3 %collective-permute-start.29 = (bf16[32,896]{1,0:T(8,128)(2,1)S(1)}, bf16[32,896]{1,0:T(8,128)(2,1)S(1)}, u32[]{:S(2)}, u32[]{:S(2)}) collective-permute-start(bf16[32,896]{1,0:T(8,128)(2,1)S(1)} %pad_maximum_fusion.2), channel_id=1, source_target_pairs={{0,2},{1,3},{2,0},{3,1},{4,6},{5,7},{6,4},{7,5},{8,10},{9,11},{10,... | collective-permute-start | bytes 172040 | tf_op jit(solution)/shard_map/ppermute | solution.py:31
  133.9 6.3 %collective-permute-start.30 = (bf16[32,896]{1,0:T(8,128)(2,1)S(1)}, bf16[32,896]{1,0:T(8,128)(2,1)S(1)}, u32[]{:S(2)}, u32[]{:S(2)}) collective-permute-start(bf16[32,896]{1,0:T(8,128)(2,1)S(1)} %pad_maximum_fusion.3), channel_id=1, source_target_pairs={{0,3},{1,2},{2,1},{3,0},{4,7},{5,6},{6,5},{7,4},{8,11},{9,10},{10,... | collective-permute-start | bytes 172040 | tf_op jit(solution)/shard_map/ppermute | solution.py:31
  134.9 7.5 %collective-permute-start.37 = (bf16[32,896]{1,0:T(8,128)(2,1)S(1)}, bf16[32,896]{1,0:T(8,128)(2,1)S(1)}, u32[]{:S(2)}, u32[]{:S(2)}) collective-permute-start(bf16[32,896]{1,0:T(8,128)(2,1)S(1)} %pad_maximum_fusion.5), channel_id=1, source_target_pairs={{0,2},{1,3},{2,0},{3,1},{4,6},{5,7},{6,4},{7,5},{8,10},{9,11},{10,... | collective-permute-start | bytes 172040 | tf_op jit(solution)/shard_map/ppermute | solution.py:31
  138.4 6.0 %collective-permute-start.38 = (bf16[32,896]{1,0:T(8,128)(2,1)S(1)}, bf16[32,896]{1,0:T(8,128)(2,1)S(1)}, u32[]{:S(2)}, u32[]{:S(2)}) collective-permute-start(bf16[32,896]{1,0:T(8,128)(2,1)S(1)} %pad_maximum_fusion.6), channel_id=1, source_target_pairs={{0,3},{1,2},{2,1},{3,0},{4,7},{5,6},{6,5},{7,4},{8,11},{9,10},{10,... | collective-permute-start | bytes 172040 | tf_op jit(solution)/shard_map/ppermute | solution.py:31
  (36 other events, 281.3 us)

commit v2 on v0

v2 whole, which is shorter than its diff:
```python
import functools
import jax
import jax.numpy as jnp
from jax import lax
from jax.experimental import pallas as pl
from jax.experimental.pallas import tpu as pltpu
from jax.sharding import PartitionSpec as P

EPSILON = 1e-06
GATE_UNIT = 128.0
LANES = 128
PARTS = 3
F32 = jnp.float32
BF16 = jnp.bfloat16


def vmem():
    return pl.BlockSpec(memory_space=pltpu.VMEM)


def smem():
    return pl.BlockSpec(memory_space=pltpu.SMEM)


def params(mib):
    return pltpu.CompilerParams(vmem_limit_bytes=mib << 20)


def shape(*dims, dtype=BF16):
    return jax.ShapeDtypeStruct(dims, dtype)


def swap(value, axis, bit):
    count = lax.axis_size(axis)
    return lax.ppermute(value, axis, [(i, i ^ bit) for i in range(count)])


def exp_bits(exp_count):
    plane = [1 << i for i in range(1, exp_count.bit_length() - 1)]
    x_bits, y_bits = plane[: len(plane) // 2], plane[len(plane) // 2 :]
    return 1, (x_bits + y_bits, y_bits + x_bits)


def relative_order(bits):
    order = [0]
    for bit in reversed(bits):
        order = order + [pattern ^ bit for pattern in order]
    return order


def three_parts(value):
    first = value.astype(BF16).astype(F32)
    second = (value - first).astype(BF16).astype(F32)
    return first, second, (value - first - second).astype(BF16).astype(F32)


def unit_of(refusal):
    return refusal * lax.rsqrt(jnp.sum(refusal * refusal) + EPSILON)


def cut_kernel(me, attn, resid, refusal, *outs):
    slices, inner = outs[:-1], outs[-1]
    width = resid.shape[1]
    for k, out in enumerate(slices):
        out[...] = attn[:, pl.ds(pl.multiple_of((me[0] ^ k) * width, LANES), width)]
    u = unit_of(refusal[...])
    scale = lax.rsqrt(jnp.sum(refusal[...] * refusal[...]) + EPSILON)
    own = refusal[:, pl.ds(pl.multiple_of(me[0] * width, LANES), width)] * scale
    total = jnp.sum(attn[...].astype(F32) * u, axis=1, keepdims=True)
    total = total + jnp.sum(resid[...].astype(F32) * own, axis=1, keepdims=True)
    inner[...] = jnp.broadcast_to(total, inner.shape)


def project_kernel(tp_count, experts, me, resid, refusal, gain, ids, gates, *refs):
    parts, inner, (message, projected) = refs[:tp_count], refs[tp_count : 2 * tp_count], refs[2 * tp_count :]
    rows, width = resid.shape
    total = parts[0][...].astype(F32)
    for part in parts[1:]:
        total = total + part[...].astype(F32)
    along = inner[0][...]
    for share in inner[1:]:
        along = along + share[...]
    scale = lax.rsqrt(jnp.sum(refusal[...] * refusal[...]) + EPSILON)
    u = refusal[:, pl.ds(pl.multiple_of(me[0] * width, LANES), width)] * scale
    value = resid[...].astype(F32) + total - along[:, :1] * u
    projected[...] = value
    message[:, :width] = (value * gain[...]).astype(BF16)
    lane = lax.broadcasted_iota(jnp.int32, (rows, message.shape[1] - width), 1)
    tail = jnp.zeros(lane.shape, F32)
    for i in range(ids.shape[1]):
        tail = tail + jnp.where(ids[:, i : i + 1] == lane, gates[:, i : i + 1].astype(F32), 0.0)
    tail = tail / GATE_UNIT
    for i, part in enumerate(three_parts(jnp.sum(value * value, axis=1, keepdims=True))):
        tail = jnp.where(lane == experts + i, part, tail)
    message[:, width:] = tail.astype(BF16)


def up_kernel(spots, start, last, full, experts, me, first, w_gate, w_up, *refs):
    count = len(spots)
    pieces, refs = refs[:count], refs[count:]
    if not start:
        refs = refs[3:] if not last else refs
    if last:
        gate_in, up_in, side_in, out, x, side = refs
    else:
        gate_acc, up_acc, side, x = refs
    expert = pl.program_id(0)
    depth = w_gate.shape[1]

    @pl.when(expert == 0)
    def _():
        for piece, spot in zip(pieces, spots):
            height = piece.shape[0] // len(spot)
            for i, place in enumerate(spot):
                here, there = slice(i * height, (i + 1) * height), slice(place * height, (place + 1) * height)
                x[there, :] = piece[here, :depth]
                tail = piece[here, depth:].astype(F32)
                lane = lax.broadcasted_iota(jnp.int32, tail.shape, 1)
                if not start:
                    before = side_in if last else side
                    tail = before[there, :] + jnp.where(lane >= experts, tail, 0.0)
                side[there, :] = tail

    gate = jnp.dot(x[...], w_gate[0], preferred_element_type=F32)
    up = jnp.dot(x[...], w_up[0], preferred_element_type=F32)
    if start:
        gate_acc[expert] = gate
        up_acc[expert] = up
    elif not last:
        gate_acc[expert] += gate
        up_acc[expert] += up
    else:
        beside = side[...]
        lane = lax.broadcasted_iota(jnp.int32, beside.shape, 1)
        weight = jnp.sum(jnp.where(lane == first[0] + expert, beside, 0.0), axis=1, keepdims=True)
        square = jnp.sum(jnp.where(lane >= experts, beside, 0.0), axis=1, keepdims=True)
        inverse = lax.rsqrt(square / full + EPSILON)
        gate = (gate_in[expert] + gate) * inverse
        up = (up_in[expert] + up) * inverse
        out[...] = (jax.nn.silu(gate) * up * weight).astype(BF16)


def down_kernel(order, me, activation, w_down, keep, send):
    weights = w_down[...].reshape(-1, w_down.shape[2])
    total = jnp.dot(activation[...], weights, preferred_element_type=F32).astype(BF16)
    height = total.shape[0] // len(order)
    middle = len(order) // 2
    for i, pattern in enumerate(order):
        out = keep if i < middle else send
        place = i % middle
        out[place * height : (place + 1) * height, :] = total[pattern * height : (pattern + 1) * height]


def gather_rows(block, order, core, merge):
    found = [([0], block)]
    for bit in list(order) + [core]:
        found += [([pattern ^ bit for pattern in patterns], swap(piece, "exp", bit)) for patterns, piece in found]
        if merge:
            found = [(sum((p for p, _ in found), []), jnp.concatenate([piece for _, piece in found], axis=0))]
    return found


def add(a, b):
    return (a.astype(F32) + b.astype(F32)).astype(BF16)


def local(attn_part, resid, refusal, norm_gain, route_ids, gate_q, w_gate, w_up, w_down):
    tp_count = lax.axis_size("tp")
    exp_count = lax.axis_size("exp")
    rows, cols = resid.shape
    full = refusal.shape[0]
    local_experts, _, hidden = w_gate.shape
    experts = local_experts * exp_count
    tail = -(-(experts + PARTS) // LANES) * LANES
    total_rows = rows * exp_count
    me = lax.axis_index("tp").astype(jnp.int32).reshape(1)
    first = (lax.axis_index("exp") * local_experts).astype(jnp.int32).reshape(1)
    core, orders = exp_bits(exp_count)
    refusal = refusal.reshape(1, full)

    *slices, inner = pl.pallas_call(
        cut_kernel,
        out_shape=[shape(rows, cols)] * tp_count + [shape(rows, LANES, dtype=F32)],
        in_specs=[smem()] + [vmem()] * 3,
        out_specs=[vmem()] * (tp_count + 1),
        compiler_params=params(8),
        name="cut_heads",
    )(me, attn_part[0], resid, refusal)
    heads = slices[:1] + [swap(slices[k], "tp", k) for k in range(1, tp_count)]
    shares = [inner] + [swap(inner, "tp", k) for k in range(1, tp_count)]

    message, projected = pl.pallas_call(
        functools.partial(project_kernel, tp_count, experts),
        out_shape=[shape(rows, cols + tail), shape(rows, cols, dtype=F32)],
        in_specs=[smem()] + [vmem()] * (5 + 2 * tp_count),
        out_specs=[vmem()] * 2,
        compiler_params=params(8),
        name="project",
    )(me, resid, refusal, norm_gain.reshape(1, cols), route_ids, gate_q, *heads, *shares)
    messages = [message] + [swap(message, "tp", k) for k in range(1, tp_count)]

    state = []
    for k in range(tp_count):
        found = gather_rows(messages[k], orders[k % 2], core, exp_count > 8)
        spots, pieces = [s for s, _ in found], [p for _, p in found]
        start, last = k == 0, k == tp_count - 1
        acc = pltpu.VMEM((local_experts, total_rows, hidden), F32)
        if last:
            out_shape = [shape(total_rows, local_experts * hidden)]
            out_specs = [pl.BlockSpec((total_rows, hidden), lambda e, *_: (0, e))]
        else:
            out_shape = [acc, acc, pltpu.VMEM((total_rows, tail), F32)]
            out_specs = [vmem()] * 3
        weights = pl.BlockSpec((1, cols, hidden), lambda e, me, first, k=k: (e, me[0] ^ k, 0))
        state = pl.pallas_call(
            functools.partial(up_kernel, spots, start, last, full, experts),
            out_shape=out_shape,
            grid_spec=pltpu.PrefetchScalarGridSpec(
                num_scalar_prefetch=2,
                grid=(local_experts,),
                in_specs=[weights, weights] + [vmem()] * (len(pieces) + len(state)),
                out_specs=out_specs,
                scratch_shapes=[pltpu.VMEM((total_rows, cols), BF16)] + ([pltpu.VMEM((total_rows, tail), F32)] if last else []),
            ),
            input_output_aliases={} if start or last else {4 + len(pieces) + i: i for i in range(3)},
            compiler_params=params(24),
            cost_estimate=pl.CostEstimate(
                flops=4 * total_rows * cols * hidden * local_experts,
                bytes_accessed=4 * cols * hidden * local_experts,
                transcendentals=0,
            ),
            name="gate_up",
        )(me, first, w_gate, w_up, *pieces, *state)
    activation = state[0]

    steps = 2 if cols % (2 * LANES) == 0 else 1
    width = cols // steps
    mixed = projected
    columns = []
    for k in reversed(range(tp_count)):
        order = orders[k % 2]
        keep, send = pl.pallas_call(
            functools.partial(down_kernel, relative_order([core] + order)),
            out_shape=[shape(total_rows // 2, cols)] * 2,
            grid_spec=pltpu.PrefetchScalarGridSpec(
                num_scalar_prefetch=1,
                grid=(steps,),
                in_specs=[
                    vmem(),
                    pl.BlockSpec((local_experts, hidden, width), lambda i, me, k=k: (0, 0, (me[0] ^ k) * steps + i)),
                ],
                out_specs=[pl.BlockSpec((total_rows // 2, width), lambda i, me: (0, i))] * 2,
            ),
            compiler_params=params(24),
            cost_estimate=pl.CostEstimate(
                flops=2 * total_rows * cols * hidden * local_experts,
                bytes_accessed=2 * cols * hidden * local_experts,
                transcendentals=0,
            ),
            name="down",
        )(me, activation, w_down)
        mine, theirs = keep, swap(send, "exp", core)
        for bit in order:
            middle = mine.shape[0] // 2
            away = add(mine[middle:], theirs[middle:])
            mine, theirs = add(mine[:middle], theirs[:middle]), swap(away, "exp", bit)
        if k:
            columns.append(swap(add(mine, theirs), "tp", k))
        else:
            columns += [mine, theirs]
    for column in columns:
        mixed = mixed + column.astype(F32)
    return mixed.astype(BF16)


def solution(mesh):
    return jax.shard_map(
        local,
        mesh=mesh,
        in_specs=(
            P("tp", "exp", None),
            P("exp", "tp"),
            P(),
            P("tp"),
            P("exp", None),
            P("exp", None),
            P("exp", None, "tp"),
            P("exp", None, "tp"),
            P("exp", "tp", None),
        ),
        out_specs=P("exp", "tp"),
        check_vma=False,
    )
```

time: 322 us -> 141 us (0.44)
  blocking collectives: 110 us -> 0 us
  waiting for transfers between devices: 122 us -> 33.3 us
  matrix products: 53.8 us -> 0 us
  Pallas kernels: 0 us -> 45.5 us
  starting transfers between devices: 4.89 us -> 43.9 us
  between operations: 14.9 us -> 0.28 us
  local copies, waits for them, and re-layouts: 8.82 us -> 15.9 us
  other arithmetic: 6.99 us -> 1.43 us
    all_to_all x1 -> x0, blocking collectives: 86.6 us -> none  [local(): lax.all_to_all(outgoing, 'exp', split_axis=0, concat_axis=0, tiled=True)]
    all_to_all x1 -> x0, waiting for transfers between devices: 82.6 us -> none  [local(): lax.all_to_all(expert_terms, 'exp', split_axis=0, concat_axis=0, tiled=True)]
    dot_general x6 -> x0, matrix products: 53.8 us -> none  [the longest x1 16.3 us: apply_experts(): jnp.einsum('sich,ihd->sicd', activation, down_weight, preferred_element_t...]
    pallas_call x0 -> x10, Pallas kernels: none -> 45.5 us  [the longest x4 31.4 us: local(): pl.pallas_call(functools.partial(up_kernel, spots, start, last, full, exp...]
    ppermute x0 -> x52, starting transfers between devices: none -> 43.9 us  [swap(): return lax.ppermute(value, axis, [(i, i ^ bit) for i in range(count)])]
    reduce_scatter x2 -> x0, waiting for transfers between devices: 38.9 us -> none  [the longest x1 19.8 us: local(): lax.psum_scatter(attn_part[0].astype(jnp.float32).astype(jnp.bfloat16), '...]
    ppermute x0 -> x52, waiting for transfers between devices: none -> 33.3 us  [swap(): return lax.ppermute(value, axis, [(i, i ^ bit) for i in range(count)])]
    all_gather x1 -> x0, blocking collectives: 14.5 us -> none  [local(): full_rows = lax.all_gather(normed, 'tp', axis=1, tiled=True)]
  transfers between devices with their start and end apart: 3 -> 52, of which waited for: 3 -> 15; matrix products, arithmetic and copies ran while one was open for 2% -> 2% of each run, Pallas kernels for 0% -> 24%
where the time goes in v2:
time: 141 us; the launch traced here: 140 us
  Pallas kernels  45.5 us (32%)
  starting transfers between devices  43.9 us (31%)
  waiting for transfers between devices  33.3 us (24%)
  local copies, waits for them, and re-layouts  15.9 us (11%)
  other arithmetic  1.43 us (1%)
    ppermute x52, starting transfers between devices, swap(): return lax.ppermute(value, axis, [(i, i ^ bit) for i in range(count)])  43.9 us
    ppermute x52, waiting for transfers between devices, swap(): return lax.ppermute(value, axis, [(i, i ^ bit) for i in range(count)])  33.3 us
    pallas_call x4, Pallas kernels, local(): pl.pallas_call(functools.partial(up_kernel, spots, start, last, full, exp...  31.4 us
    unnamed x14, local copies, waits for them, and re-layouts  15.2 us
    pallas_call x4, Pallas kernels, local(): pl.pallas_call(functools.partial(down_kernel, relative_order([core] + ord...  13.3 us
  transfers between devices with their start and end apart: 52, of which 15 were waited for; matrix products, arithmetic and copies ran while one was open for 2% of the time, Pallas kernels for 24%

profile of v2, /device:TPU:0, one launch (start us, length us, event | category | flops | bytes accessed | tf_op | source)
XLA Modules:
  0.0 140.3 jit_solution(4026116706103580480)
XLA Ops:
  3.1 3.0 %collective-permute-start = (bf16[32,1792]{1,0:T(8,128)(2,1)S(1)}, bf16[32,1792]{1,0:T(8,128)(2,1)S(1)}, u32[]{:S(2)}, u32[]{:S(2)}) collective-permute-start(bf16[32,1792]{1,0:T(8,128)(2,1)S(1)} %get-tuple-element.30), channel_id=1, source_target_pairs={{0,1},{1,0},{2,3},{3,2},{4,5},{5,4},{6,7},{7,6},{8,9},{9,8},{10,11... | collective-permute-start | bytes 344072 | tf_op jit(solution)/shard_map/ppermute | solution.py:35
  6.1 2.6 %collective-permute-start.1 = (bf16[32,1792]{1,0:T(8,128)(2,1)S(1)}, bf16[32,1792]{1,0:T(8,128)(2,1)S(1)}, u32[]{:S(2)}, u32[]{:S(2)}) collective-permute-start(bf16[32,1792]{1,0:T(8,128)(2,1)S(1)} %get-tuple-element.31), channel_id=1, source_target_pairs={{0,2},{1,3},{2,0},{3,1},{4,6},{5,7},{6,4},{7,5},{8,10},{9,11},{10,... | collective-permute-start | bytes 344072 | tf_op jit(solution)/shard_map/ppermute | solution.py:35
  9.6 3.5 %collective-permute-start.4 = (f32[32,128]{1,0:T(8,128)S(1)}, f32[32,128]{1,0:T(8,128)S(1)}, u32[]{:S(2)}, u32[]{:S(2)}) collective-permute-start(f32[32,128]{1,0:T(8,128)S(1)} %get-tuple-element.33.refs_4_), channel_id=1, source_target_pairs={{0,2},{1,3},{2,0},{3,1},{4,6},{5,7},{6,4},{7,5},{8,10},{9,11},{10,... | collective-permute-start | bytes 49160 | tf_op jit(solution)/shard_map/ppermute | solution.py:35
  14.0 2.5 %collective-permute-start.5 = (f32[32,128]{1,0:T(8,128)S(1)}, f32[32,128]{1,0:T(8,128)S(1)}, u32[]{:S(2)}, u32[]{:S(2)}) collective-permute-start(f32[32,128]{1,0:T(8,128)S(1)} %get-tuple-element.33.refs_4_), channel_id=1, source_target_pairs={{0,3},{1,2},{2,1},{3,0},{4,7},{5,6},{6,5},{7,4},{8,11},{9,10},{10,... | collective-permute-start | bytes 49160 | tf_op jit(solution)/shard_map/ppermute | solution.py:35
  18.7 1.6 %collective-permute-done.4.refs_6_ = f32[32,128]{1,0:T(8,128)S(1)} collective-permute-done((f32[32,128]{1,0:T(8,128)S(1)}, f32[32,128]{1,0:T(8,128)S(1)}, u32[]{:S(2)}, u32[]{:S(2)}) %collective-permute-start.4) | collective-permute-done | bytes 16416 | tf_op jit(solution)/shard_map/ppermute | solution.py:35
  22.3 1.6 %collective-permute-start.30 = (bf16[32,1920]{1,0:T(8,128)(2,1)S(1)}, bf16[32,1920]{1,0:T(8,128)(2,1)S(1)}, u32[]{:S(2)}, u32[]{:S(2)}) collective-permute-start(bf16[32,1920]{1,0:T(8,128)(2,1)S(1)} %get-tuple-element.35.refs_0_), channel_id=1, source_target_pairs={{0,8},{4,12},{8,0},{12,4},{16,24},{20,28},{24,16},{28,20},{1,9},{5... | collective-permute-start | bytes 368648 | tf_op jit(solution)/shard_map/ppermute | solution.py:35
  26.1 2.3 %collective-permute-start.14 = (bf16[32,1920]{1,0:T(8,128)(2,1)S(1)}, bf16[32,1920]{1,0:T(8,128)(2,1)S(1)}, u32[]{:S(2)}, u32[]{:S(2)}) collective-permute-start(bf16[32,1920]{1,0:T(8,128)(2,1)S(1)} %get-tuple-element.35.refs_0_), channel_id=1, source_target_pairs={{0,2},{1,3},{2,0},{3,1},{4,6},{5,7},{6,4},{7,5},{8,10},{9,11},{10,... | collective-permute-start | bytes 368648 | tf_op jit(solution)/shard_map/ppermute | solution.py:35
  31.3 2.1 %collective-permute-done.22.refs_0_ = bf16[32,1920]{1,0:T(8,128)(2,1)S(1)} collective-permute-done((bf16[32,1920]{1,0:T(8,128)(2,1)S(1)}, bf16[32,1920]{1,0:T(8,128)(2,1)S(1)}, u32[]{:S(2)}, u32[]{:S(2)}) %collective-permute-start.22) | collective-permute-done | bytes 122912 | tf_op jit(solution)/shard_map/ppermute | solution.py:35
  33.4 5.1 %collective-permute-done.14.refs_0_ = bf16[32,1920]{1,0:T(8,128)(2,1)S(1)} collective-permute-done((bf16[32,1920]{1,0:T(8,128)(2,1)S(1)}, bf16[32,1920]{1,0:T(8,128)(2,1)S(1)}, u32[]{:S(2)}, u32[]{:S(2)}) %collective-permute-start.14) | collective-permute-done | bytes 122912 | tf_op jit(solution)/shard_map/ppermute | solution.py:35
  39.5 1.6 %collective-permute-start.15 = (bf16[32,1920]{1,0:T(8,128)(2,1)S(1)}, bf16[32,1920]{1,0:T(8,128)(2,1)S(1)}, u32[]{:S(2)}, u32[]{:S(2)}) collective-permute-start(bf16[32,1920]{1,0:T(8,128)(2,1)S(1)} %collective-permute-done.14.refs_0_), channel_id=1, source_target_pairs={{0,8},{4,12},{8,0},{12,4},{16,24},{20,28},{24,16},{28,20},{1,9},{5... | collective-permute-start | bytes 368648 | tf_op jit(solution)/shard_map/ppermute | solution.py:35
  41.1 1.5 %collective-permute-start.16 = (bf16[32,1920]{1,0:T(8,128)(2,1)S(1)}, bf16[32,1920]{1,0:T(8,128)(2,1)S(1)}, u32[]{:S(2)}, u32[]{:S(2)}) collective-permute-start(bf16[32,1920]{1,0:T(8,128)(2,1)S(1)} %collective-permute-done.14.refs_0_), channel_id=1, source_target_pairs={{0,16},{4,20},{8,24},{12,28},{16,0},{20,4},{24,8},{28,12},{1,17},{... | collective-permute-start | bytes 368648 | tf_op jit(solution)/shard_map/ppermute | solution.py:35
  43.4 1.7 %collective-permute-done.24.refs_2_ = bf16[32,1920]{1,0:T(8,128)(2,1)S(1)} collective-permute-done((bf16[32,1920]{1,0:T(8,128)(2,1)S(1)}, bf16[32,1920]{1,0:T(8,128)(2,1)S(1)}, u32[]{:S(2)}, u32[]{:S(2)}) %collective-permute-start.24) | collective-permute-done | bytes 122912 | tf_op jit(solution)/shard_map/ppermute | solution.py:35
  49.1 1.8 %collective-permute-done.25.refs_3_ = bf16[32,1920]{1,0:T(8,128)(2,1)S(1)} collective-permute-done((bf16[32,1920]{1,0:T(8,128)(2,1)S(1)}, bf16[32,1920]{1,0:T(8,128)(2,1)S(1)}, u32[]{:S(2)}, u32[]{:S(2)}) %collective-permute-start.25) | collective-permute-done | bytes 122912 | tf_op jit(solution)/shard_map/ppermute | solution.py:35
  50.9 7.8 %gate_up.4 = (f32[4,256,512]{2,1,0:T(8,128)S(1)}, f32[4,256,512]{2,1,0:T(8,128)S(1)}, f32[256,128]{1,0:T(8,128)S(1)}) custom-call(s32[1]{0:T(128)} %bitcast.me, s32[1]{0:T(128)} %bitcast.3.first, bf16[4,7168,512]{2,1,0:T(8,128)(2,1)} %w_gate.7, bf16[4,7168,512]{2,1,0:T(8,128)(2,1)} %w_up.7, bf16[32,1920]{1,0:T(8,128)(2,1)S(1)} %get-tuple-element.35.refs_0_, ...), custom_call_target="tpu_custom_call" | custom-call | flops 3758096384 | bytes 14680064 | tf_op jit(solution)/shard_map/gate_up/pallas_call | solution.py:215
  59.5 1.7 %collective-permute-start.9 = (bf16[32,1920]{1,0:T(8,128)(2,1)S(1)}, bf16[32,1920]{1,0:T(8,128)(2,1)S(1)}, u32[]{:S(2)}, u32[]{:S(2)}) collective-permute-start(bf16[32,1920]{1,0:T(8,128)(2,1)S(1)} %collective-permute-done.7.refs_1_), channel_id=1, source_target_pairs={{0,8},{4,12},{8,0},{12,4},{16,24},{20,28},{24,16},{28,20},{1,9},{5... | collective-permute-start | bytes 368648 | tf_op jit(solution)/shard_map/ppermute | solution.py:35
  61.3 7.8 %gate_up.5 = (f32[4,256,512]{2,1,0:T(8,128)S(1)}, f32[4,256,512]{2,1,0:T(8,128)S(1)}, f32[256,128]{1,0:T(8,128)S(1)}) custom-call(s32[1]{0:T(128)} %bitcast.me, s32[1]{0:T(128)} %bitcast.3.first, bf16[4,7168,512]{2,1,0:T(8,128)(2,1)} %w_gate.7, bf16[4,7168,512]{2,1,0:T(8,128)(2,1)} %w_up.7, ...), custom_call_target="tpu_custom_call", output_to_operand_aliasing={{0}: (12, {}), {1}: (13, {}), {2}: (14, {})} | custom-call | flops 3758096384 | bytes 14680064 | tf_op jit(solution)/shard_map/gate_up/pallas_call | solution.py:215
  70.3 7.8 %gate_up.6 = (f32[4,256,512]{2,1,0:T(8,128)S(1)}, f32[4,256,512]{2,1,0:T(8,128)S(1)}, f32[256,128]{1,0:T(8,128)S(1)}) custom-call(s32[1]{0:T(128)} %bitcast.me, s32[1]{0:T(128)} %bitcast.3.first, bf16[4,7168,512]{2,1,0:T(8,128)(2,1)} %w_gate.7, bf16[4,7168,512]{2,1,0:T(8,128)(2,1)} %w_up.7, ...), custom_call_target="tpu_custom_call", output_to_operand_aliasing={{0}: (12, {}), {1}: (13, {}), {2}: (14, {})} | custom-call | flops 3758096384 | bytes 14680064 | tf_op jit(solution)/shard_map/gate_up/pallas_call | solution.py:215
  78.2 8.0 %gate_up.7.activation = bf16[256,2048]{1,0:T(8,128)(2,1)S(1)} custom-call(s32[1]{0:T(128)} %bitcast.me, s32[1]{0:T(128)} %bitcast.3.first, bf16[4,7168,512]{2,1,0:T(8,128)(2,1)} %w_gate.7, bf16[4,7168,512]{2,1,0:T(8,128)(2,1)} %w_up.7, bf16[32,1920]{1,0:T(8,128)(2,1)S(1)} %collective-permute-done.6.refs_0_, ...), custom_call_target="tpu_custom_call" | custom-call | flops 3758096384 | bytes 14680064 | tf_op jit(solution)/shard_map/gate_up/pallas_call | solution.py:215
  86.2 9.3 %copy-done = bf16[4,512,7168]{2,1,0:T(8,128)(2,1)S(1)} copy-done((bf16[4,512,7168]{2,1,0:T(8,128)(2,1)S(1)}, bf16[4,512,7168]{2,1,0:T(8,128)(2,1)}, u32[]{:S(2)}) %copy-start) | copy-done | bytes 29360152
  95.5 3.3 %down.4 = (bf16[128,1792]{1,0:T(8,128)(2,1)S(1)}, bf16[128,1792]{1,0:T(8,128)(2,1)S(1)}) custom-call(s32[1]{0:T(128)} %bitcast.me, bf16[256,2048]{1,0:T(8,128)(2,1)S(1)} %gate_up.7.activation, bf16[4,512,7168]{2,1,0:T(8,128)(2,1)S(1)} %copy-done), custom_call_target="tpu_custom_call" | custom-call | flops 1879048192 | bytes 7340032 | tf_op jit(solution)/shard_map/down/pallas_call | solution.py:242
  99.4 3.3 %down.5 = (bf16[128,1792]{1,0:T(8,128)(2,1)S(1)}, bf16[128,1792]{1,0:T(8,128)(2,1)S(1)}) custom-call(s32[1]{0:T(128)} %bitcast.me, bf16[256,2048]{1,0:T(8,128)(2,1)S(1)} %gate_up.7.activation, bf16[4,512,7168]{2,1,0:T(8,128)(2,1)S(1)} %copy-done), custom_call_target="tpu_custom_call" | custom-call | flops 1879048192 | bytes 7340032 | tf_op jit(solution)/shard_map/down/pallas_call | solution.py:242
  102.8 3.3 %down.6 = (bf16[128,1792]{1,0:T(8,128)(2,1)S(1)}, bf16[128,1792]{1,0:T(8,128)(2,1)S(1)}) custom-call(s32[1]{0:T(128)} %bitcast.me, bf16[256,2048]{1,0:T(8,128)(2,1)S(1)} %gate_up.7.activation, bf16[4,512,7168]{2,1,0:T(8,128)(2,1)S(1)} %copy-done), custom_call_target="tpu_custom_call" | custom-call | flops 1879048192 | bytes 7340032 | tf_op jit(solution)/shard_map/down/pallas_call | solution.py:242
  106.7 3.3 %down.7 = (bf16[128,1792]{1,0:T(8,128)(2,1)S(1)}, bf16[128,1792]{1,0:T(8,128)(2,1)S(1)}) custom-call(s32[1]{0:T(128)} %bitcast.me, bf16[256,2048]{1,0:T(8,128)(2,1)S(1)} %gate_up.7.activation, bf16[4,512,7168]{2,1,0:T(8,128)(2,1)S(1)} %copy-done), custom_call_target="tpu_custom_call" | custom-call | flops 1879048192 | bytes 7340032 | tf_op jit(solution)/shard_map/down/pallas_call | solution.py:242
  110.3 1.6 %collective-permute-start.38 = (bf16[64,1792]{1,0:T(8,128)(2,1)S(1)}, bf16[64,1792]{1,0:T(8,128)(2,1)S(1)}, u32[]{:S(2)}, u32[]{:S(2)}) collective-permute-start(bf16[64,1792]{1,0:T(8,128)(2,1)S(1)} %get-tuple-element.54), channel_id=1, source_target_pairs={{0,16},{4,20},{8,24},{12,28},{16,0},{20,4},{24,8},{28,12},{1,17},{... | collective-permute-start | bytes 688136 | tf_op jit(solution)/shard_map/ppermute | solution.py:35
  113.1 1.8 %collective-permute-start.50 = (bf16[64,1792]{1,0:T(8,128)(2,1)S(1)}, bf16[64,1792]{1,0:T(8,128)(2,1)S(1)}, u32[]{:S(2)}, u32[]{:S(2)}) collective-permute-start(bf16[64,1792]{1,0:T(8,128)(2,1)S(1)} %get-tuple-element.60), channel_id=1, source_target_pairs={{0,8},{4,12},{8,0},{12,4},{16,24},{20,28},{24,16},{28,20},{1,9},{5... | collective-permute-start | bytes 688136 | tf_op jit(solution)/shard_map/ppermute | solution.py:35
  114.9 3.8 %collective-permute-done.38 = bf16[64,1792]{1,0:T(8,128)(2,1)S(1)} collective-permute-done((bf16[64,1792]{1,0:T(8,128)(2,1)S(1)}, bf16[64,1792]{1,0:T(8,128)(2,1)S(1)}, u32[]{:S(2)}, u32[]{:S(2)}) %collective-permute-start.38) | collective-permute-done | bytes 229408 | tf_op jit(solution)/shard_map/ppermute | solution.py:35
  121.1 2.6 %collective-permute-done.46 = bf16[64,1792]{1,0:T(8,128)(2,1)S(1)} collective-permute-done((bf16[64,1792]{1,0:T(8,128)(2,1)S(1)}, bf16[64,1792]{1,0:T(8,128)(2,1)S(1)}, u32[]{:S(2)}, u32[]{:S(2)}) %collective-permute-start.46) | collective-permute-done | bytes 229408 | tf_op jit(solution)/shard_map/ppermute | solution.py:35
  126.0 1.9 %collective-permute-done.39 = bf16[32,1792]{1,0:T(8,128)(2,1)S(1)} collective-permute-done((bf16[32,1792]{1,0:T(8,128)(2,1)S(1)}, bf16[32,1792]{1,0:T(8,128)(2,1)S(1)}, u32[]{:S(2)}, u32[]{:S(2)}) %collective-permute-start.39) | collective-permute-done | bytes 114720 | tf_op jit(solution)/shard_map/ppermute | solution.py:35
  127.9 2.5 %collective-permute-start.40 = (bf16[32,1792]{1,0:T(8,128)(2,1)S(1)}, bf16[32,1792]{1,0:T(8,128)(2,1)S(1)}, u32[]{:S(2)}, u32[]{:S(2)}) collective-permute-start(bf16[32,1792]{1,0:T(8,128)(2,1)S(1)} %add_convert_fusion.17), channel_id=1, source_target_pairs={{0,3},{1,2},{2,1},{3,0},{4,7},{5,6},{6,5},{7,4},{8,11},{9,10},{10,... | collective-permute-start | bytes 344072 | tf_op jit(solution)/shard_map/ppermute | solution.py:35
  130.6 2.0 %collective-permute-start.48 = (bf16[32,1792]{1,0:T(8,128)(2,1)S(1)}, bf16[32,1792]{1,0:T(8,128)(2,1)S(1)}, u32[]{:S(2)}, u32[]{:S(2)}) collective-permute-start(bf16[32,1792]{1,0:T(8,128)(2,1)S(1)} %add_convert_fusion.11), channel_id=1, source_target_pairs={{0,1},{1,0},{2,3},{3,2},{4,5},{5,4},{6,7},{7,6},{8,9},{9,8},{10,11... | collective-permute-start | bytes 344072 | tf_op jit(solution)/shard_map/ppermute | solution.py:35
  132.6 3.1 %collective-permute-done.40 = bf16[32,1792]{1,0:T(8,128)(2,1)S(1)} collective-permute-done((bf16[32,1792]{1,0:T(8,128)(2,1)S(1)}, bf16[32,1792]{1,0:T(8,128)(2,1)S(1)}, u32[]{:S(2)}, u32[]{:S(2)}) %collective-permute-start.40) | collective-permute-done | bytes 114720 | tf_op jit(solution)/shard_map/ppermute | solution.py:35
  135.7 3.8 %collective-permute-done.44 = bf16[32,1792]{1,0:T(8,128)(2,1)S(1)} collective-permute-done((bf16[32,1792]{1,0:T(8,128)(2,1)S(1)}, bf16[32,1792]{1,0:T(8,128)(2,1)S(1)}, u32[]{:S(2)}, u32[]{:S(2)}) %collective-permute-start.44) | collective-permute-done | bytes 114720 | tf_op jit(solution)/shard_map/ppermute | solution.py:35
  (109 shorter events, 30.3 us)
Async XLA Ops:
  3.1 17.2 %collective-permute-start = (bf16[32,1792]{1,0:T(8,128)(2,1)S(1)}, bf16[32,1792]{1,0:T(8,128)(2,1)S(1)}, u32[]{:S(2)}, u32[]{:S(2)}) collective-permute-start(bf16[32,1792]{1,0:T(8,128)(2,1)S(1)} %get-tuple-element.30), channel_id=1, source_target_pairs={{0,1},{1,0},{2,3},{3,2},{4,5},{5,4},{6,7},{7,6},{8,9},{9,8},{10,11... | collective-permute-start | bytes 344072 | tf_op jit(solution)/shard_map/ppermute | solution.py:35
  6.1 14.2 %collective-permute-start.1 = (bf16[32,1792]{1,0:T(8,128)(2,1)S(1)}, bf16[32,1792]{1,0:T(8,128)(2,1)S(1)}, u32[]{:S(2)}, u32[]{:S(2)}) collective-permute-start(bf16[32,1792]{1,0:T(8,128)(2,1)S(1)} %get-tuple-element.31), channel_id=1, source_target_pairs={{0,2},{1,3},{2,0},{3,1},{4,6},{5,7},{6,4},{7,5},{8,10},{9,11},{10,... | collective-permute-start | bytes 344072 | tf_op jit(solution)/shard_map/ppermute | solution.py:35
  8.7 11.6 %collective-permute-start.2 = (bf16[32,1792]{1,0:T(8,128)(2,1)S(1)}, bf16[32,1792]{1,0:T(8,128)(2,1)S(1)}, u32[]{:S(2)}, u32[]{:S(2)}) collective-permute-start(bf16[32,1792]{1,0:T(8,128)(2,1)S(1)} %get-tuple-element.32), channel_id=1, source_target_pairs={{0,3},{1,2},{2,1},{3,0},{4,7},{5,6},{6,5},{7,4},{8,11},{9,10},{10,... | collective-permute-start | bytes 344072 | tf_op jit(solution)/shard_map/ppermute | solution.py:35
  9.6 10.7 %collective-permute-start.4 = (f32[32,128]{1,0:T(8,128)S(1)}, f32[32,128]{1,0:T(8,128)S(1)}, u32[]{:S(2)}, u32[]{:S(2)}) collective-permute-start(f32[32,128]{1,0:T(8,128)S(1)} %get-tuple-element.33.refs_4_), channel_id=1, source_target_pairs={{0,2},{1,3},{2,0},{3,1},{4,6},{5,7},{6,4},{7,5},{8,10},{9,11},{10,... | collective-permute-start | bytes 49160 | tf_op jit(solution)/shard_map/ppermute | solution.py:35
  25.4 8.0 %collective-permute-start.22 = (bf16[32,1920]{1,0:T(8,128)(2,1)S(1)}, bf16[32,1920]{1,0:T(8,128)(2,1)S(1)}, u32[]{:S(2)}, u32[]{:S(2)}) collective-permute-start(bf16[32,1920]{1,0:T(8,128)(2,1)S(1)} %get-tuple-element.35.refs_0_), channel_id=1, source_target_pairs={{0,1},{1,0},{2,3},{3,2},{4,5},{5,4},{6,7},{7,6},{8,9},{9,8},{10,11... | collective-permute-start | bytes 368648 | tf_op jit(solution)/shard_map/ppermute | solution.py:35
  26.1 12.4 %collective-permute-start.14 = (bf16[32,1920]{1,0:T(8,128)(2,1)S(1)}, bf16[32,1920]{1,0:T(8,128)(2,1)S(1)}, u32[]{:S(2)}, u32[]{:S(2)}) collective-permute-start(bf16[32,1920]{1,0:T(8,128)(2,1)S(1)} %get-tuple-element.35.refs_0_), channel_id=1, source_target_pairs={{0,2},{1,3},{2,0},{3,1},{4,6},{5,7},{6,4},{7,5},{8,10},{9,11},{10,... | collective-permute-start | bytes 368648 | tf_op jit(solution)/shard_map/ppermute | solution.py:35
  28.4 10.6 %collective-permute-start.6 = (bf16[32,1920]{1,0:T(8,128)(2,1)S(1)}, bf16[32,1920]{1,0:T(8,128)(2,1)S(1)}, u32[]{:S(2)}, u32[]{:S(2)}) collective-permute-start(bf16[32,1920]{1,0:T(8,128)(2,1)S(1)} %get-tuple-element.35.refs_0_), channel_id=1, source_target_pairs={{0,3},{1,2},{2,1},{3,0},{4,7},{5,6},{6,5},{7,4},{8,11},{9,10},{10,... | collective-permute-start | bytes 368648 | tf_op jit(solution)/shard_map/ppermute | solution.py:35
  29.8 9.7 %collective-permute-start.32 = (bf16[32,1920]{1,0:T(8,128)(2,1)S(1)}, bf16[32,1920]{1,0:T(8,128)(2,1)S(1)}, u32[]{:S(2)}, u32[]{:S(2)}) collective-permute-start(bf16[32,1920]{1,0:T(8,128)(2,1)S(1)} %collective-permute-done.30.refs_1_), channel_id=1, source_target_pairs={{0,16},{4,20},{8,24},{12,28},{16,0},{20,4},{24,8},{28,12},{1,17},{... | collective-permute-start | bytes 368648 | tf_op jit(solution)/shard_map/ppermute | solution.py:35
  31.3 8.3 %collective-permute-start.34 = (bf16[32,1920]{1,0:T(8,128)(2,1)S(1)}, bf16[32,1920]{1,0:T(8,128)(2,1)S(1)}, u32[]{:S(2)}, u32[]{:S(2)}) collective-permute-start(bf16[32,1920]{1,0:T(8,128)(2,1)S(1)} %collective-permute-done.30.refs_1_), channel_id=1, source_target_pairs={{0,4},{4,0},{8,12},{12,8},{16,20},{20,16},{24,28},{28,24},{1,5},{5... | collective-permute-start | bytes 368648 | tf_op jit(solution)/shard_map/ppermute | solution.py:35
  46.5 12.1 %collective-permute-start.7 = (bf16[32,1920]{1,0:T(8,128)(2,1)S(1)}, bf16[32,1920]{1,0:T(8,128)(2,1)S(1)}, u32[]{:S(2)}, u32[]{:S(2)}) collective-permute-start(bf16[32,1920]{1,0:T(8,128)(2,1)S(1)} %collective-permute-done.6.refs_0_), channel_id=1, source_target_pairs={{0,16},{4,20},{8,24},{12,28},{16,0},{20,4},{24,8},{28,12},{1,17},{... | collective-permute-start | bytes 368648 | tf_op jit(solution)/shard_map/ppermute | solution.py:35
  48.0 11.0 %collective-permute-start.27 = (bf16[32,1920]{1,0:T(8,128)(2,1)S(1)}, bf16[32,1920]{1,0:T(8,128)(2,1)S(1)}, u32[]{:S(2)}, u32[]{:S(2)}) collective-permute-start(bf16[32,1920]{1,0:T(8,128)(2,1)S(1)} %collective-permute-done.23.refs_1_), channel_id=1, source_target_pairs={{0,4},{4,0},{8,12},{12,8},{16,20},{20,16},{24,28},{28,24},{1,5},{5... | collective-permute-start | bytes 368648 | tf_op jit(solution)/shard_map/ppermute | solution.py:35
  48.0 11.3 %collective-permute-start.28 = (bf16[32,1920]{1,0:T(8,128)(2,1)S(1)}, bf16[32,1920]{1,0:T(8,128)(2,1)S(1)}, u32[]{:S(2)}, u32[]{:S(2)}) collective-permute-start(bf16[32,1920]{1,0:T(8,128)(2,1)S(1)} %collective-permute-done.24.refs_2_), channel_id=1, source_target_pairs={{0,4},{4,0},{8,12},{12,8},{16,20},{20,16},{24,28},{28,24},{1,5},{5... | collective-permute-start | bytes 368648 | tf_op jit(solution)/shard_map/ppermute | solution.py:35
  48.6 11.0 %collective-permute-start.17 = (bf16[32,1920]{1,0:T(8,128)(2,1)S(1)}, bf16[32,1920]{1,0:T(8,128)(2,1)S(1)}, u32[]{:S(2)}, u32[]{:S(2)}) collective-permute-start(bf16[32,1920]{1,0:T(8,128)(2,1)S(1)} %collective-permute-done.15.refs_1_), channel_id=1, source_target_pairs={{0,16},{4,20},{8,24},{12,28},{16,0},{20,4},{24,8},{28,12},{1,17},{... | collective-permute-start | bytes 368648 | tf_op jit(solution)/shard_map/ppermute | solution.py:35
  50.9 10.4 %collective-permute-start.29 = (bf16[32,1920]{1,0:T(8,128)(2,1)S(1)}, bf16[32,1920]{1,0:T(8,128)(2,1)S(1)}, u32[]{:S(2)}, u32[]{:S(2)}) collective-permute-start(bf16[32,1920]{1,0:T(8,128)(2,1)S(1)} %collective-permute-done.25.refs_3_), channel_id=1, source_target_pairs={{0,4},{4,0},{8,12},{12,8},{16,20},{20,16},{24,28},{28,24},{1,5},{5... | collective-permute-start | bytes 368648 | tf_op jit(solution)/shard_map/ppermute | solution.py:35
  58.7 10.5 %collective-permute-start.8 = (bf16[32,1920]{1,0:T(8,128)(2,1)S(1)}, bf16[32,1920]{1,0:T(8,128)(2,1)S(1)}, u32[]{:S(2)}, u32[]{:S(2)}) collective-permute-start(bf16[32,1920]{1,0:T(8,128)(2,1)S(1)} %collective-permute-done.6.refs_0_), channel_id=1, source_target_pairs={{0,8},{4,12},{8,0},{12,4},{16,24},{20,28},{24,16},{28,20},{1,9},{5... | collective-permute-start | bytes 368648 | tf_op jit(solution)/shard_map/ppermute | solution.py:35
  59.0 10.7 %collective-permute-start.19 = (bf16[32,1920]{1,0:T(8,128)(2,1)S(1)}, bf16[32,1920]{1,0:T(8,128)(2,1)S(1)}, u32[]{:S(2)}, u32[]{:S(2)}) collective-permute-start(bf16[32,1920]{1,0:T(8,128)(2,1)S(1)} %collective-permute-done.15.refs_1_), channel_id=1, source_target_pairs={{0,4},{4,0},{8,12},{12,8},{16,20},{20,16},{24,28},{28,24},{1,5},{5... | collective-permute-start | bytes 368648 | tf_op jit(solution)/shard_map/ppermute | solution.py:35
  59.3 10.5 %collective-permute-start.20 = (bf16[32,1920]{1,0:T(8,128)(2,1)S(1)}, bf16[32,1920]{1,0:T(8,128)(2,1)S(1)}, u32[]{:S(2)}, u32[]{:S(2)}) collective-permute-start(bf16[32,1920]{1,0:T(8,128)(2,1)S(1)} %collective-permute-done.16.refs_2_), channel_id=1, source_target_pairs={{0,4},{4,0},{8,12},{12,8},{16,20},{20,16},{24,28},{28,24},{1,5},{5... | collective-permute-start | bytes 368648 | tf_op jit(solution)/shard_map/ppermute | solution.py:35
  59.5 10.7 %collective-permute-start.9 = (bf16[32,1920]{1,0:T(8,128)(2,1)S(1)}, bf16[32,1920]{1,0:T(8,128)(2,1)S(1)}, u32[]{:S(2)}, u32[]{:S(2)}) collective-permute-start(bf16[32,1920]{1,0:T(8,128)(2,1)S(1)} %collective-permute-done.7.refs_1_), channel_id=1, source_target_pairs={{0,8},{4,12},{8,0},{12,4},{16,24},{20,28},{24,16},{28,20},{1,9},{5... | collective-permute-start | bytes 368648 | tf_op jit(solution)/shard_map/ppermute | solution.py:35
  61.3 9.0 %collective-permute-start.21 = (bf16[32,1920]{1,0:T(8,128)(2,1)S(1)}, bf16[32,1920]{1,0:T(8,128)(2,1)S(1)}, u32[]{:S(2)}, u32[]{:S(2)}) collective-permute-start(bf16[32,1920]{1,0:T(8,128)(2,1)S(1)} %collective-permute-done.17.refs_3_), channel_id=1, source_target_pairs={{0,4},{4,0},{8,12},{12,8},{16,20},{20,16},{24,28},{28,24},{1,5},{5... | collective-permute-start | bytes 368648 | tf_op jit(solution)/shard_map/ppermute | solution.py:35
  69.1 9.0 %collective-permute-start.10 = (bf16[32,1920]{1,0:T(8,128)(2,1)S(1)}, bf16[32,1920]{1,0:T(8,128)(2,1)S(1)}, u32[]{:S(2)}, u32[]{:S(2)}) collective-permute-start(bf16[32,1920]{1,0:T(8,128)(2,1)S(1)} %collective-permute-done.6.refs_0_), channel_id=1, source_target_pairs={{0,4},{4,0},{8,12},{12,8},{16,20},{20,16},{24,28},{28,24},{1,5},{5... | collective-permute-start | bytes 368648 | tf_op jit(solution)/shard_map/ppermute | solution.py:35
  69.7 8.5 %collective-permute-start.11 = (bf16[32,1920]{1,0:T(8,128)(2,1)S(1)}, bf16[32,1920]{1,0:T(8,128)(2,1)S(1)}, u32[]{:S(2)}, u32[]{:S(2)}) collective-permute-start(bf16[32,1920]{1,0:T(8,128)(2,1)S(1)} %collective-permute-done.7.refs_1_), channel_id=1, source_target_pairs={{0,4},{4,0},{8,12},{12,8},{16,20},{20,16},{24,28},{28,24},{1,5},{5... | collective-permute-start | bytes 368648 | tf_op jit(solution)/shard_map/ppermute | solution.py:35
  69.8 8.4 %collective-permute-start.12 = (bf16[32,1920]{1,0:T(8,128)(2,1)S(1)}, bf16[32,1920]{1,0:T(8,128)(2,1)S(1)}, u32[]{:S(2)}, u32[]{:S(2)}) collective-permute-start(bf16[32,1920]{1,0:T(8,128)(2,1)S(1)} %collective-permute-done.8.refs_2_), channel_id=1, source_target_pairs={{0,4},{4,0},{8,12},{12,8},{16,20},{20,16},{24,28},{28,24},{1,5},{5... | collective-permute-start | bytes 368648 | tf_op jit(solution)/shard_map/ppermute | solution.py:35
  98.9 11.3 %collective-permute-start.37 = (bf16[128,1792]{1,0:T(8,128)(2,1)S(1)}, bf16[128,1792]{1,0:T(8,128)(2,1)S(1)}, u32[]{:S(2)}, u32[]{:S(2)}) collective-permute-start(bf16[128,1792]{1,0:T(8,128)(2,1)S(1)} %get-tuple-element.46), channel_id=1, source_target_pairs={{0,4},{4,0},{8,12},{12,8},{16,20},{20,16},{24,28},{28,24},{1,5},{5... | collective-permute-start | bytes 1376264 | tf_op jit(solution)/shard_map/ppermute | solution.py:35
  102.7 9.2 %collective-permute-start.41 = (bf16[128,1792]{1,0:T(8,128)(2,1)S(1)}, bf16[128,1792]{1,0:T(8,128)(2,1)S(1)}, u32[]{:S(2)}, u32[]{:S(2)}) collective-permute-start(bf16[128,1792]{1,0:T(8,128)(2,1)S(1)} %get-tuple-element.48), channel_id=1, source_target_pairs={{0,4},{4,0},{8,12},{12,8},{16,20},{20,16},{24,28},{28,24},{1,5},{5... | collective-permute-start | bytes 1376264 | tf_op jit(solution)/shard_map/ppermute | solution.py:35
  110.3 8.5 %collective-permute-start.38 = (bf16[64,1792]{1,0:T(8,128)(2,1)S(1)}, bf16[64,1792]{1,0:T(8,128)(2,1)S(1)}, u32[]{:S(2)}, u32[]{:S(2)}) collective-permute-start(bf16[64,1792]{1,0:T(8,128)(2,1)S(1)} %get-tuple-element.54), channel_id=1, source_target_pairs={{0,16},{4,20},{8,24},{12,28},{16,0},{20,4},{24,8},{28,12},{1,17},{... | collective-permute-start | bytes 688136 | tf_op jit(solution)/shard_map/ppermute | solution.py:35
  111.9 8.5 %collective-permute-start.42 = (bf16[64,1792]{1,0:T(8,128)(2,1)S(1)}, bf16[64,1792]{1,0:T(8,128)(2,1)S(1)}, u32[]{:S(2)}, u32[]{:S(2)}) collective-permute-start(bf16[64,1792]{1,0:T(8,128)(2,1)S(1)} %get-tuple-element.56), channel_id=1, source_target_pairs={{0,8},{4,12},{8,0},{12,4},{16,24},{20,28},{24,16},{28,20},{1,9},{5... | collective-permute-start | bytes 688136 | tf_op jit(solution)/shard_map/ppermute | solution.py:35
  112.4 11.2 %collective-permute-start.46 = (bf16[64,1792]{1,0:T(8,128)(2,1)S(1)}, bf16[64,1792]{1,0:T(8,128)(2,1)S(1)}, u32[]{:S(2)}, u32[]{:S(2)}) collective-permute-start(bf16[64,1792]{1,0:T(8,128)(2,1)S(1)} %get-tuple-element.58), channel_id=1, source_target_pairs={{0,16},{4,20},{8,24},{12,28},{16,0},{20,4},{24,8},{28,12},{1,17},{... | collective-permute-start | bytes 688136 | tf_op jit(solution)/shard_map/ppermute | solution.py:35
  113.1 12.3 %collective-permute-start.50 = (bf16[64,1792]{1,0:T(8,128)(2,1)S(1)}, bf16[64,1792]{1,0:T(8,128)(2,1)S(1)}, u32[]{:S(2)}, u32[]{:S(2)}) collective-permute-start(bf16[64,1792]{1,0:T(8,128)(2,1)S(1)} %get-tuple-element.60), channel_id=1, source_target_pairs={{0,8},{4,12},{8,0},{12,4},{16,24},{20,28},{24,16},{28,20},{1,9},{5... | collective-permute-start | bytes 688136 | tf_op jit(solution)/shard_map/ppermute | solution.py:35
  118.8 9.1 %collective-permute-start.39 = (bf16[32,1792]{1,0:T(8,128)(2,1)S(1)}, bf16[32,1792]{1,0:T(8,128)(2,1)S(1)}, u32[]{:S(2)}, u32[]{:S(2)}) collective-permute-start(bf16[32,1792]{1,0:T(8,128)(2,1)S(1)} %add_convert_fusion.18), channel_id=1, source_target_pairs={{0,8},{4,12},{8,0},{12,4},{16,24},{20,28},{24,16},{28,20},{1,9},{5... | collective-permute-start | bytes 344072 | tf_op jit(solution)/shard_map/ppermute | solution.py:35
  120.5 9.9 %collective-permute-start.43 = (bf16[32,1792]{1,0:T(8,128)(2,1)S(1)}, bf16[32,1792]{1,0:T(8,128)(2,1)S(1)}, u32[]{:S(2)}, u32[]{:S(2)}) collective-permute-start(bf16[32,1792]{1,0:T(8,128)(2,1)S(1)} %add_convert_fusion.15), channel_id=1, source_target_pairs={{0,16},{4,20},{8,24},{12,28},{16,0},{20,4},{24,8},{28,12},{1,17},{... | collective-permute-start | bytes 344072 | tf_op jit(solution)/shard_map/ppermute | solution.py:35
  130.4 9.1 %collective-permute-start.44 = (bf16[32,1792]{1,0:T(8,128)(2,1)S(1)}, bf16[32,1792]{1,0:T(8,128)(2,1)S(1)}, u32[]{:S(2)}, u32[]{:S(2)}) collective-permute-start(bf16[32,1792]{1,0:T(8,128)(2,1)S(1)} %add_convert_fusion.14), channel_id=1, source_target_pairs={{0,2},{1,3},{2,0},{3,1},{4,6},{5,7},{6,4},{7,5},{8,10},{9,11},{10,... | collective-permute-start | bytes 344072 | tf_op jit(solution)/shard_map/ppermute | solution.py:35
  130.6 8.9 %collective-permute-start.48 = (bf16[32,1792]{1,0:T(8,128)(2,1)S(1)}, bf16[32,1792]{1,0:T(8,128)(2,1)S(1)}, u32[]{:S(2)}, u32[]{:S(2)}) collective-permute-start(bf16[32,1792]{1,0:T(8,128)(2,1)S(1)} %add_convert_fusion.11), channel_id=1, source_target_pairs={{0,1},{1,0},{2,3},{3,2},{4,5},{5,4},{6,7},{7,6},{8,9},{9,8},{10,11... | collective-permute-start | bytes 344072 | tf_op jit(solution)/shard_map/ppermute | solution.py:35
  (26 other events, 134.1 us)

commit v3 on v2

v3 whole, which is shorter than its diff:
```python
import functools
import jax
import jax.numpy as jnp
from jax import lax
from jax.experimental import pallas as pl
from jax.experimental.pallas import tpu as pltpu
from jax.sharding import PartitionSpec as P

EPSILON = 1e-06
GATE_UNIT = 128.0
LANES = 128
PARTS = 3
F32 = jnp.float32
BF16 = jnp.bfloat16


def vmem():
    return pl.BlockSpec(memory_space=pltpu.VMEM)


def smem():
    return pl.BlockSpec(memory_space=pltpu.SMEM)


def on_chip(value):
    return pltpu.with_memory_space_constraint(value, pltpu.VMEM)


def off_chip(value):
    return pltpu.with_memory_space_constraint(value, pltpu.HBM)


def params(mib):
    return pltpu.CompilerParams(vmem_limit_bytes=mib << 20)


def shape(*dims, dtype=BF16):
    return jax.ShapeDtypeStruct(dims, dtype)


def swap(value, axis, bit):
    count = lax.axis_size(axis)
    return lax.ppermute(value, axis, [(i, i ^ bit) for i in range(count)])


def exp_bits(exp_count):
    plane = [1 << i for i in range(1, exp_count.bit_length() - 1)]
    x_bits, y_bits = plane[: len(plane) // 2], plane[len(plane) // 2 :]
    return 1, (x_bits + y_bits, y_bits + x_bits)


def relative_order(bits):
    order = [0]
    for bit in reversed(bits):
        order = order + [pattern ^ bit for pattern in order]
    return order


def three_parts(value):
    first = value.astype(BF16).astype(F32)
    second = (value - first).astype(BF16).astype(F32)
    return first, second, (value - first - second).astype(BF16).astype(F32)


def cut_kernel(me, attn_hbm, resid_hbm, refusal_hbm, *refs):
    slices, (base, share, unit, attn, resid, refusal, sems) = refs[:-7], refs[-7:]
    copies = [
        pltpu.make_async_copy(source, target, sems.at[i])
        for i, (source, target) in enumerate(((attn_hbm, attn), (resid_hbm, resid), (refusal_hbm, refusal)))
    ]
    for copy in copies:
        copy.start()
    for copy in copies:
        copy.wait()
    rows, width = resid.shape
    scale = lax.rsqrt(jnp.sum(refusal[...] * refusal[...]) + EPSILON)
    own = refusal[:, pl.ds(pl.multiple_of(me[0] * width, LANES), width)] * scale
    unit[...] = own
    total = jnp.sum(attn[...].astype(F32) * (refusal[...] * scale), axis=1, keepdims=True)
    total = total + jnp.sum(resid[...].astype(F32) * own, axis=1, keepdims=True)
    share[...] = jnp.broadcast_to(total, share.shape)
    lane = lax.broadcasted_iota(jnp.int32, share.shape, 1)
    tail = jnp.zeros(share.shape, F32)
    for i, part in enumerate(three_parts(total)):
        tail = jnp.where(lane == i, part, tail)
    tail = tail.astype(BF16)
    for i, out in enumerate(slices):
        out[:, :width] = attn[:, pl.ds(pl.multiple_of((me[0] ^ (i + 1)) * width, LANES), width)]
        out[:, width:] = tail
    here = attn[:, pl.ds(pl.multiple_of(me[0] * width, LANES), width)]
    base[...] = resid[...].astype(F32) + here.astype(F32)


def project_kernel(experts, base, share, unit, gain, ids, gates, *refs):
    parts, (message, projected) = refs[:-2], refs[-2:]
    rows, width = base.shape
    total, along = base[...], share[:, :1]
    for part in parts:
        total = total + part[:, :width].astype(F32)
        along = along + jnp.sum(part[:, width:].astype(F32), axis=1, keepdims=True)
    value = total - along * unit[...]
    projected[...] = value
    message[:, :width] = (value * gain[...]).astype(BF16)
    lane = lax.broadcasted_iota(jnp.int32, (rows, message.shape[1] - width), 1)
    tail = jnp.zeros(lane.shape, F32)
    for i in range(ids.shape[1]):
        tail = tail + jnp.where(ids[:, i : i + 1] == lane, gates[:, i : i + 1].astype(F32), 0.0)
    tail = tail / GATE_UNIT
    for i, part in enumerate(three_parts(jnp.sum(value * value, axis=1, keepdims=True))):
        tail = jnp.where(lane == experts + i, part, tail)
    message[:, width:] = tail.astype(BF16)


def up_kernel(start, last, chunks, ahead, full, experts, me, first, w_gate, w_up, down_hbm, *refs):
    *refs, sem = refs
    x = refs[-1 - last]
    held_down = refs[-2 - last]
    if last:
        out, side = refs[-4], refs[-1]
        pieces, (gate_in, up_in, side_in) = refs[:-7], refs[-7:-4]
    else:
        gate_acc, up_acc, side = refs[-5:-2]
        pieces = refs[:-5] if start else refs[:-8]
    expert = pl.program_id(0)
    columns = held_down.shape[2]
    block = (me[0] ^ ahead) // (columns // (x.shape[1] // chunks))
    copy = pltpu.make_async_copy(
        down_hbm.at[:, :, pl.ds(pl.multiple_of(block * columns, LANES), columns)], held_down, sem
    )
    width = x.shape[1] // chunks

    @pl.when(expert == 0)
    def _():
        copy.start()
        height = pieces[0].shape[0] // chunks
        for i, piece in enumerate(pieces):
            there = slice(i * height, (i + 1) * height)
            for j in range(chunks):
                here = slice(j * height, (j + 1) * height)
                slot = (me[0] & (chunks - 1)) ^ j
                x[there, pl.ds(pl.multiple_of(slot * width, LANES), width)] = piece[here, :width]
                tail = piece[here, width:].astype(F32)
                lane = lax.broadcasted_iota(jnp.int32, tail.shape, 1)
                if j or not start:
                    before = side_in if last and not j else side
                    tail = before[there, :] + jnp.where(lane >= experts, tail, 0.0)
                side[there, :] = tail

    gate = jnp.dot(x[...], w_gate[0], preferred_element_type=F32)
    up = jnp.dot(x[...], w_up[0], preferred_element_type=F32)
    if start:
        gate_acc[expert] = gate
        up_acc[expert] = up
    elif not last:
        gate_acc[expert] += gate
        up_acc[expert] += up
    else:
        beside = side[...]
        lane = lax.broadcasted_iota(jnp.int32, beside.shape, 1)
        weight = jnp.sum(jnp.where(lane == first[0] + expert, beside, 0.0), axis=1, keepdims=True)
        square = jnp.sum(jnp.where(lane >= experts, beside, 0.0), axis=1, keepdims=True)
        inverse = lax.rsqrt(square / full + EPSILON)
        gate = (gate_in[expert] + gate) * inverse
        up = (up_in[expert] + up) * inverse
        out[...] = (jax.nn.silu(gate) * up * weight).astype(BF16)

    @pl.when(expert == pl.num_programs(0) - 1)
    def _():
        copy.wait()


def down_kernel(order, place, cols, me, activation, w_down, keep, send):
    width = keep.shape[1]
    slot = (me[0] ^ place) & (w_down.shape[2] // cols - 1)
    here = pl.ds(pl.multiple_of(slot * cols + pl.program_id(0) * width, LANES), width)
    weights = w_down[:, :, here].reshape(-1, width)
    total = jnp.dot(activation[...], weights, preferred_element_type=F32).astype(BF16)
    height = total.shape[0] // len(order)
    middle = len(order) // 2
    for i, pattern in enumerate(order):
        out = keep if i < middle else send
        at = i % middle
        out[at * height : (at + 1) * height, :] = total[pattern * height : (pattern + 1) * height]


def join_kernel(*refs):
    *parts, out = refs
    at = 0
    for part in parts:
        out[at : at + part.shape[0], :] = part[...]
        at += part.shape[0]


def join(*parts):
    return pl.pallas_call(
        join_kernel,
        out_shape=shape(sum(part.shape[0] for part in parts), parts[0].shape[1]),
        in_specs=[vmem()] * len(parts),
        out_specs=vmem(),
        compiler_params=params(4),
        name="join",
    )(*parts)


def gather_rows(block, exp_count):
    found = {0: block}
    found.update({pattern: swap(block, "exp", pattern) for pattern in range(2, exp_count, 2)})
    found.update({pattern ^ 1: swap(piece, "exp", 1) for pattern, piece in list(found.items())})
    return [found[pattern] for pattern in range(exp_count)]


def add(a, b):
    return (a.astype(F32) + b.astype(F32)).astype(BF16)


def sum_of(a, b):
    return a.astype(F32) + b.astype(F32)


def local(attn_part, resid, refusal, norm_gain, route_ids, gate_q, w_gate, w_up, w_down):
    tp_count = lax.axis_size("tp")
    exp_count = lax.axis_size("exp")
    rows, cols = resid.shape
    full = refusal.shape[0]
    local_experts, _, hidden = w_gate.shape
    experts = local_experts * exp_count
    tail = -(-(experts + PARTS) // LANES) * LANES
    total_rows = rows * exp_count
    me = lax.axis_index("tp").astype(jnp.int32).reshape(1)
    first = (lax.axis_index("exp") * local_experts).astype(jnp.int32).reshape(1)
    me, first = lax.optimization_barrier((me, first))
    core, orders = exp_bits(exp_count)
    refusal = refusal.reshape(1, full)

    *slices, base, share, unit = pl.pallas_call(
        cut_kernel,
        out_shape=[shape(rows, cols + LANES)] * (tp_count - 1)
        + [shape(rows, cols, dtype=F32), shape(rows, LANES, dtype=F32), shape(1, cols, dtype=F32)],
        in_specs=[smem()] + [pl.BlockSpec(memory_space=pltpu.HBM)] * 3,
        out_specs=[vmem()] * (tp_count + 2),
        scratch_shapes=[
            pltpu.VMEM((rows, full), BF16),
            pltpu.VMEM((rows, cols), BF16),
            pltpu.VMEM((1, full), F32),
            pltpu.SemaphoreType.DMA((3,)),
        ],
        compiler_params=params(4),
        name="cut_heads",
    )(me, off_chip(attn_part[0]), off_chip(resid), off_chip(refusal))
    parts = [swap(value, "tp", k + 1) for k, value in enumerate(slices)]

    message, projected = pl.pallas_call(
        functools.partial(project_kernel, experts),
        out_shape=[shape(rows, cols + tail), shape(rows, cols, dtype=F32)],
        in_specs=[vmem()] * (5 + tp_count),
        out_specs=[vmem()] * 2,
        compiler_params=params(4),
        name="project",
    )(base, share, unit, norm_gain.reshape(1, cols), route_ids, gate_q, *parts)

    groups = [join(message, swap(message, "tp", 1))]
    bit = 2
    while bit < tp_count:
        groups.append(swap(groups[0] if bit == 2 else join(*groups), "tp", bit))
        bit *= 2

    state, held_down = [], {}
    sizes = [group.shape[0] // rows for group in groups]
    starts = [0] + sizes[1:]
    for i, group in enumerate(groups):
        pieces = gather_rows(group, exp_count)
        chunks, flip = sizes[i], starts[i]
        ahead, columns = starts[-1 - i], sizes[-1 - i] * cols
        start, last = i == 0, i == len(groups) - 1
        down_shape = pltpu.VMEM((local_experts, hidden, columns), BF16)
        acc = pltpu.VMEM((local_experts, total_rows, hidden), F32)
        if last:
            out_shape = [shape(total_rows, local_experts * hidden), down_shape]
            out_specs = [pl.BlockSpec((total_rows, hidden), lambda e, *_: (0, e)), vmem()]
        else:
            out_shape = [acc, acc, pltpu.VMEM((total_rows, tail), F32), down_shape]
            out_specs = [vmem()] * 4
        weights = [off_chip(w_gate), off_chip(w_up)]
        specs = [
            pl.BlockSpec(
                (1, chunks * cols, hidden),
                lambda e, me, first, flip=flip, chunks=chunks: (e, (me[0] ^ flip) // chunks, 0),
            )
        ] * 2
        scratch = [pltpu.VMEM((total_rows, chunks * cols), BF16)]
        *state, held_down[ahead] = pl.pallas_call(
            functools.partial(up_kernel, start, last, chunks, ahead, full, experts),
            out_shape=out_shape,
            grid_spec=pltpu.PrefetchScalarGridSpec(
                num_scalar_prefetch=2,
                grid=(local_experts,),
                in_specs=specs + [pl.BlockSpec(memory_space=pltpu.HBM)] + [vmem()] * (len(pieces) + len(state)),
                out_specs=out_specs,
                scratch_shapes=scratch
                + ([pltpu.VMEM((total_rows, tail), F32)] if last else [])
                + [pltpu.SemaphoreType.DMA(())],
            ),
            input_output_aliases={} if start or last else {5 + len(pieces) + j: j for j in range(3)},
            compiler_params=params(22),
            cost_estimate=pl.CostEstimate(
                flops=4 * total_rows * chunks * cols * hidden * local_experts,
                bytes_accessed=4 * chunks * cols * hidden * local_experts,
                transcendentals=0,
            ),
            name="gate_up",
        )(me, first, *weights, off_chip(w_down), *pieces, *[on_chip(v) for v in state])
    activation = state[0]

    steps = 2 if cols % (2 * LANES) == 0 else 1
    width = cols // steps
    results, gates_open = {}, []
    for k in reversed(range(tp_count)):
        order = orders[k % 2]
        block = max(place for place in held_down if place <= k)
        source = activation
        if len(gates_open) > 1:
            source, _ = lax.optimization_barrier((activation, gates_open[-2]))
        keep, send = pl.pallas_call(
            functools.partial(down_kernel, relative_order([core] + order), k, cols),
            out_shape=[shape(total_rows // 2, cols)] * 2,
            grid_spec=pltpu.PrefetchScalarGridSpec(
                num_scalar_prefetch=1,
                grid=(steps,),
                in_specs=[vmem()] * 2,
                out_specs=[pl.BlockSpec((total_rows // 2, width), lambda i, me: (0, i))] * 2,
            ),
            compiler_params=params(8),
            cost_estimate=pl.CostEstimate(
                flops=2 * total_rows * cols * hidden * local_experts,
                bytes_accessed=2 * cols * hidden * local_experts,
                transcendentals=0,
            ),
            name="down",
        )(me, source, on_chip(held_down[block]))
        mine, theirs = keep, swap(send, "exp", core)
        for i, bit in enumerate(order):
            middle = mine.shape[0] // 2
            away = add(mine[middle:], theirs[middle:])
            if i == 0:
                gates_open.append(away)
            mine, theirs = add(mine[:middle], theirs[:middle]), swap(away, "exp", bit)
        results[k] = (mine, theirs)

    bit = tp_count // 2
    while bit:
        far = jnp.concatenate([functools.reduce(sum_of, results[k]) for k in range(bit, 2 * bit)], axis=0)
        got = swap(far.astype(BF16), "tp", bit)
        for k in range(bit):
            results[k] = results[k] + (got[k * rows : (k + 1) * rows],)
        bit //= 2
    return (projected + functools.reduce(sum_of, results[0])).astype(BF16)


def solution(mesh):
    return jax.shard_map(
        local,
        mesh=mesh,
        in_specs=(
            P("tp", "exp", None),
            P("exp", "tp"),
            P(),
            P("tp"),
            P("exp", None),
            P("exp", None),
            P("exp", None, "tp"),
            P("exp", None, "tp"),
            P("exp", "tp", None),
        ),
        out_specs=P("exp", "tp"),
        check_vma=False,
    )
```

time: 141 us -> 123 us (0.87)
  local copies, waits for them, and re-layouts: 15.9 us -> 2.22 us
  starting transfers between devices: 43.9 us -> 30.5 us
  waiting for transfers between devices: 33.3 us -> 44.1 us
    unnamed x14 -> x2, local copies, waits for them, and re-layouts: 15.2 us -> 1.52 us
    ppermute x52 -> x33, starting transfers between devices: 43.9 us -> 30.5 us  [swap(): return lax.ppermute(value, axis, [(i, i ^ bit) for i in range(count)])]
    ppermute x52 -> x33, waiting for transfers between devices: 33.3 us -> 44.1 us  [swap(): return lax.ppermute(value, axis, [(i, i ^ bit) for i in range(count)])]
    pallas_call x4, Pallas kernels: 13.3 us -> 10.5 us  [local(): pl.pallas_call(functools.partial(down_kernel, relative_order([core] + ord...]
    pallas_call x6 -> x5, Pallas kernels: 32.2 us -> 33.8 us  [the longest x2 32 us: local(): pl.pallas_call(functools.partial(up_kernel, start, last, chunks, ahead, f...]
  transfers between devices with their start and end apart: 52 -> 33, of which waited for: 15 -> 17; matrix products, arithmetic and copies ran while one was open for 2% -> 2% of each run, Pallas kernels for 24% -> 19%
where the time goes in v3:
time: 123 us
  Pallas kernels  44.3 us (36%)
  waiting for transfers between devices  44.1 us (36%)
  starting transfers between devices  30.5 us (25%)
  local copies, waits for them, and re-layouts  2.22 us (2%)
  other arithmetic  1.47 us (1%)
    ppermute x33, waiting for transfers between devices, swap(): return lax.ppermute(value, axis, [(i, i ^ bit) for i in range(count)])  44.1 us
    pallas_call x2, Pallas kernels, local(): pl.pallas_call(functools.partial(up_kernel, start, last, chunks, ahead, f...  32 us
    ppermute x33, starting transfers between devices, swap(): return lax.ppermute(value, axis, [(i, i ^ bit) for i in range(count)])  30.5 us
    pallas_call x4, Pallas kernels, local(): pl.pallas_call(functools.partial(down_kernel, relative_order([core] + ord...  10.5 us
  transfers between devices with their start and end apart: 33, of which 17 were waited for; matrix products, arithmetic and copies ran while one was open for 2% of the time, Pallas kernels for 19%

profile of v3, /device:TPU:0, one launch (start us, length us, event | category | flops | bytes accessed | tf_op | source)
XLA Modules:
  0.0 122.8 jit_solution(7506687446556447638)
XLA Ops:
  0.0 1.5 %cut_heads.1 = (bf16[32,1920]{1,0:T(8,128)(2,1)S(1)}, bf16[32,1920]{1,0:T(8,128)(2,1)S(1)}, bf16[32,1920]{1,0:T(8,128)(2,1)S(1)}, f32[32,1792]{1,0:T(8,128)S(1)}...) custom-call(s32[1]{0:T(128)} %bitcast.me, bf16[32,7168]{1,0:T(8,128)(2,1)} %bitcast.4, bf16[32,1792]{1,0:T(8,128)(2,1)} %resid_hbm.1, ...), custom_call_target="tpu_custom_call" | custom-call | tf_op jit(solution)/shard_map/cut_heads/pallas_call | solution.py:235
  1.5 3.1 %collective-permute-start = (bf16[32,1920]{1,0:T(8,128)(2,1)S(1)}, bf16[32,1920]{1,0:T(8,128)(2,1)S(1)}, u32[]{:S(2)}, u32[]{:S(2)}) collective-permute-start(bf16[32,1920]{1,0:T(8,128)(2,1)S(1)} %get-tuple-element.35), channel_id=1, source_target_pairs={{0,1},{1,0},{2,3},{3,2},{4,5},{5,4},{6,7},{7,6},{8,9},{9,8},{10,11... | collective-permute-start | bytes 368648 | tf_op jit(solution)/shard_map/ppermute | solution.py:43
  4.6 2.6 %collective-permute-start.1 = (bf16[32,1920]{1,0:T(8,128)(2,1)S(1)}, bf16[32,1920]{1,0:T(8,128)(2,1)S(1)}, u32[]{:S(2)}, u32[]{:S(2)}) collective-permute-start(bf16[32,1920]{1,0:T(8,128)(2,1)S(1)} %get-tuple-element.36), channel_id=1, source_target_pairs={{0,2},{1,3},{2,0},{3,1},{4,6},{5,7},{6,4},{7,5},{8,10},{9,11},{10,... | collective-permute-start | bytes 368648 | tf_op jit(solution)/shard_map/ppermute | solution.py:43
  9.4 7.5 %collective-permute-done.1.refs_1_ = bf16[32,1920]{1,0:T(8,128)(2,1)S(1)} collective-permute-done((bf16[32,1920]{1,0:T(8,128)(2,1)S(1)}, bf16[32,1920]{1,0:T(8,128)(2,1)S(1)}, u32[]{:S(2)}, u32[]{:S(2)}) %collective-permute-start.1) | collective-permute-done | bytes 122912 | tf_op jit(solution)/shard_map/ppermute | solution.py:43
  17.2 1.9 %collective-permute-start.3 = (bf16[32,1920]{1,0:T(8,128)(2,1)S(1)}, bf16[32,1920]{1,0:T(8,128)(2,1)S(1)}, u32[]{:S(2)}, u32[]{:S(2)}) collective-permute-start(bf16[32,1920]{1,0:T(8,128)(2,1)S(1)} %get-tuple-element.40.refs_0_), channel_id=1, source_target_pairs={{0,1},{1,0},{2,3},{3,2},{4,5},{5,4},{6,7},{7,6},{8,9},{9,8},{10,11... | collective-permute-start | bytes 368648 | tf_op jit(solution)/shard_map/ppermute | solution.py:43
  19.2 3.0 %collective-permute-done.3.refs_1_ = bf16[32,1920]{1,0:T(8,128)(2,1)S(1)} collective-permute-done((bf16[32,1920]{1,0:T(8,128)(2,1)S(1)}, bf16[32,1920]{1,0:T(8,128)(2,1)S(1)}, u32[]{:S(2)}, u32[]{:S(2)}) %collective-permute-start.3) | collective-permute-done | bytes 122912 | tf_op jit(solution)/shard_map/ppermute | solution.py:43
  22.2 2.5 %collective-permute-start.17 = (bf16[64,1920]{1,0:T(8,128)(2,1)S(1)}, bf16[64,1920]{1,0:T(8,128)(2,1)S(1)}, u32[]{:S(2)}, u32[]{:S(2)}) collective-permute-start(bf16[64,1920]{1,0:T(8,128)(2,1)S(1)} %join.1.refs_0_), channel_id=1, source_target_pairs={{0,24},{4,28},{8,16},{12,20},{16,8},{20,12},{24,0},{28,4},{1,25},{... | collective-permute-start | bytes 737288 | tf_op jit(solution)/shard_map/ppermute | solution.py:43
  25.2 2.9 %collective-permute-start.4 = (bf16[64,1920]{1,0:T(8,128)(2,1)S(1)}, bf16[64,1920]{1,0:T(8,128)(2,1)S(1)}, u32[]{:S(2)}, u32[]{:S(2)}) collective-permute-start(bf16[64,1920]{1,0:T(8,128)(2,1)S(1)} %join.1.refs_0_), channel_id=1, source_target_pairs={{0,2},{1,3},{2,0},{3,1},{4,6},{5,7},{6,4},{7,5},{8,10},{9,11},{10,... | collective-permute-start | bytes 737288 | tf_op jit(solution)/shard_map/ppermute | solution.py:43
  28.6 2.3 %collective-permute-done.17.refs_6_ = bf16[64,1920]{1,0:T(8,128)(2,1)S(1)} collective-permute-done((bf16[64,1920]{1,0:T(8,128)(2,1)S(1)}, bf16[64,1920]{1,0:T(8,128)(2,1)S(1)}, u32[]{:S(2)}, u32[]{:S(2)}) %collective-permute-start.17) | collective-permute-done | bytes 245792 | tf_op jit(solution)/shard_map/ppermute | solution.py:43
  30.9 2.8 %collective-permute-done.15.refs_4_ = bf16[64,1920]{1,0:T(8,128)(2,1)S(1)} collective-permute-done((bf16[64,1920]{1,0:T(8,128)(2,1)S(1)}, bf16[64,1920]{1,0:T(8,128)(2,1)S(1)}, u32[]{:S(2)}, u32[]{:S(2)}) %collective-permute-start.15) | collective-permute-done | bytes 245792 | tf_op jit(solution)/shard_map/ppermute | solution.py:43
  33.7 2.9 %collective-permute-done.4.refs_0_ = bf16[64,1920]{1,0:T(8,128)(2,1)S(1)} collective-permute-done((bf16[64,1920]{1,0:T(8,128)(2,1)S(1)}, bf16[64,1920]{1,0:T(8,128)(2,1)S(1)}, u32[]{:S(2)}, u32[]{:S(2)}) %collective-permute-start.4) | collective-permute-done | bytes 245792 | tf_op jit(solution)/shard_map/ppermute | solution.py:43
  36.6 1.5 %collective-permute-start.10 = (bf16[64,1920]{1,0:T(8,128)(2,1)S(1)}, bf16[64,1920]{1,0:T(8,128)(2,1)S(1)}, u32[]{:S(2)}, u32[]{:S(2)}) collective-permute-start(bf16[64,1920]{1,0:T(8,128)(2,1)S(1)} %collective-permute-done.4.refs_0_), channel_id=1, source_target_pairs={{0,24},{4,28},{8,16},{12,20},{16,8},{20,12},{24,0},{28,4},{1,25},{... | collective-permute-start | bytes 737288 | tf_op jit(solution)/shard_map/ppermute | solution.py:43
  38.6 1.5 %collective-permute-start.6 = (bf16[64,1920]{1,0:T(8,128)(2,1)S(1)}, bf16[64,1920]{1,0:T(8,128)(2,1)S(1)}, u32[]{:S(2)}, u32[]{:S(2)}) collective-permute-start(bf16[64,1920]{1,0:T(8,128)(2,1)S(1)} %collective-permute-done.4.refs_0_), channel_id=1, source_target_pairs={{0,8},{4,12},{8,0},{12,4},{16,24},{20,28},{24,16},{28,20},{1,9},{5... | collective-permute-start | bytes 737288 | tf_op jit(solution)/shard_map/ppermute | solution.py:43
  40.7 5.8 %collective-permute-done.10.refs_6_ = bf16[64,1920]{1,0:T(8,128)(2,1)S(1)} collective-permute-done((bf16[64,1920]{1,0:T(8,128)(2,1)S(1)}, bf16[64,1920]{1,0:T(8,128)(2,1)S(1)}, u32[]{:S(2)}, u32[]{:S(2)}) %collective-permute-start.10) | collective-permute-done | bytes 245792 | tf_op jit(solution)/shard_map/ppermute | solution.py:43
  46.5 3.3 %collective-permute-done.8.refs_4_ = bf16[64,1920]{1,0:T(8,128)(2,1)S(1)} collective-permute-done((bf16[64,1920]{1,0:T(8,128)(2,1)S(1)}, bf16[64,1920]{1,0:T(8,128)(2,1)S(1)}, u32[]{:S(2)}, u32[]{:S(2)}) %collective-permute-start.8) | collective-permute-done | bytes 245792 | tf_op jit(solution)/shard_map/ppermute | solution.py:43
  50.3 15.9 %gate_up.2 = (f32[4,256,512]{2,1,0:T(8,128)S(1)}, f32[4,256,512]{2,1,0:T(8,128)S(1)}, f32[256,128]{1,0:T(8,128)S(1)}, bf16[4,512,3584]{2,1,0:T(8,128)(2,1)S(1)}) custom-call(s32[1]{0:T(128)} %bitcast.me, s32[1]{0:T(128)} %bitcast.1.first, bf16[4,7168,512]{2,1,0:T(8,128)(2,1)} %w_gate.3, bf16[4,7168,512]{2,1,0:T(8,128)(2,1)} %w_up.3, ...), custom_call_target="tpu_custom_call" | custom-call | flops 7516192768 | bytes 29360128 | tf_op jit(solution)/shard_map/gate_up/pallas_call | solution.py:291
  66.3 16.1 %gate_up.3 = (bf16[256,2048]{1,0:T(8,128)(2,1)S(1)}, bf16[4,512,3584]{2,1,0:T(8,128)(2,1)S(1)}) custom-call(s32[1]{0:T(128)} %bitcast.me, s32[1]{0:T(128)} %bitcast.1.first, bf16[4,7168,512]{2,1,0:T(8,128)(2,1)} %w_gate.3, bf16[4,7168,512]{2,1,0:T(8,128)(2,1)} %w_up.3, bf16[4,512,7168]{2,1,0:T(8,128)(2,1)} %down_hbm.3, ...), custom_call_target="tpu_custom_call" | custom-call | flops 7516192768 | bytes 29360128 | tf_op jit(solution)/shard_map/gate_up/pallas_call | solution.py:291
  82.4 2.6 %down.4 = (bf16[128,1792]{1,0:T(8,128)(2,1)S(1)}, bf16[128,1792]{1,0:T(8,128)(2,1)S(1)}) custom-call(s32[1]{0:T(128)} %bitcast.me, bf16[256,2048]{1,0:T(8,128)(2,1)S(1)} %get-tuple-element.48.activation, bf16[4,512,3584]{2,1,0:T(8,128)(2,1)S(1)} %get-tuple-element.45.w_down), custom_call_target="tpu_custom_call" | custom-call | flops 1879048192 | bytes 7340032 | tf_op jit(solution)/shard_map/down/pallas_call | solution.py:323
  85.2 2.6 %down.6 = (bf16[128,1792]{1,0:T(8,128)(2,1)S(1)}, bf16[128,1792]{1,0:T(8,128)(2,1)S(1)}) custom-call(s32[1]{0:T(128)} %bitcast.me, bf16[256,2048]{1,0:T(8,128)(2,1)S(1)} %get-tuple-element.48.activation, bf16[4,512,3584]{2,1,0:T(8,128)(2,1)S(1)} %get-tuple-element.45.w_down), custom_call_target="tpu_custom_call" | custom-call | flops 1879048192 | bytes 7340032 | tf_op jit(solution)/shard_map/down/pallas_call | solution.py:323
  90.7 2.6 %down.5 = (bf16[128,1792]{1,0:T(8,128)(2,1)S(1)}, bf16[128,1792]{1,0:T(8,128)(2,1)S(1)}) custom-call(s32[1]{0:T(128)} %bitcast.me, bf16[256,2048]{1,0:T(8,128)(2,1)S(1)} %get-tuple-element.48.activation, bf16[4,512,3584]{2,1,0:T(8,128)(2,1)S(1)} %get-tuple-element.49.w_down), custom_call_target="tpu_custom_call" | custom-call | flops 1879048192 | bytes 7340032 | tf_op jit(solution)/shard_map/down/pallas_call | solution.py:323
  93.5 2.6 %down.7 = (bf16[128,1792]{1,0:T(8,128)(2,1)S(1)}, bf16[128,1792]{1,0:T(8,128)(2,1)S(1)}) custom-call(s32[1]{0:T(128)} %bitcast.me, bf16[256,2048]{1,0:T(8,128)(2,1)S(1)} %get-tuple-element.48.activation, bf16[4,512,3584]{2,1,0:T(8,128)(2,1)S(1)} %get-tuple-element.49.w_down), custom_call_target="tpu_custom_call" | custom-call | flops 1879048192 | bytes 7340032 | tf_op jit(solution)/shard_map/down/pallas_call | solution.py:323
  96.6 1.2 collective-permute-done.26
  98.5 1.6 %collective-permute-start.24 = (bf16[32,1792]{1,0:T(8,128)(2,1)S(1)}, bf16[32,1792]{1,0:T(8,128)(2,1)S(1)}, u32[]{:S(2)}, u32[]{:S(2)}) collective-permute-start(bf16[32,1792]{1,0:T(8,128)(2,1)S(1)} %add_convert_fusion.16), channel_id=1, source_target_pairs={{0,16},{4,20},{8,24},{12,28},{16,0},{20,4},{24,8},{28,12},{1,17},{... | collective-permute-start | bytes 344072 | tf_op jit(solution)/shard_map/ppermute | solution.py:43
  100.0 2.6 %collective-permute-done.27 = bf16[32,1792]{1,0:T(8,128)(2,1)S(1)} collective-permute-done((bf16[32,1792]{1,0:T(8,128)(2,1)S(1)}, bf16[32,1792]{1,0:T(8,128)(2,1)S(1)}, u32[]{:S(2)}, u32[]{:S(2)}) %collective-permute-start.27) | collective-permute-done | bytes 114720 | tf_op jit(solution)/shard_map/ppermute | solution.py:43
  103.4 2.7 %collective-permute-start.28 = (bf16[64,1792]{1,0:T(8,128)(2,1)S(1)}, bf16[64,1792]{1,0:T(8,128)(2,1)S(1)}, u32[]{:S(2)}, u32[]{:S(2)}) collective-permute-start(bf16[64,1792]{1,0:T(8,128)(2,1)S(1)} %pad_maximum_fusion), channel_id=1, source_target_pairs={{0,2},{1,3},{2,0},{3,1},{4,6},{5,7},{6,4},{7,5},{8,10},{9,11},{10,... | collective-permute-start | bytes 688136 | tf_op jit(solution)/shard_map/ppermute | solution.py:43
  107.2 1.3 %collective-permute-start.21 = (bf16[64,1792]{1,0:T(8,128)(2,1)S(1)}, bf16[64,1792]{1,0:T(8,128)(2,1)S(1)}, u32[]{:S(2)}, u32[]{:S(2)}) collective-permute-start(bf16[64,1792]{1,0:T(8,128)(2,1)S(1)} %get-tuple-element.58), channel_id=1, source_target_pairs={{0,8},{4,12},{8,0},{12,4},{16,24},{20,28},{24,16},{28,20},{1,9},{5... | collective-permute-start | bytes 688136 | tf_op jit(solution)/shard_map/ppermute | solution.py:43
  108.5 3.8 %collective-permute-done.30 = bf16[64,1792]{1,0:T(8,128)(2,1)S(1)} collective-permute-done((bf16[64,1792]{1,0:T(8,128)(2,1)S(1)}, bf16[64,1792]{1,0:T(8,128)(2,1)S(1)}, u32[]{:S(2)}, u32[]{:S(2)}) %collective-permute-start.30) | collective-permute-done | bytes 229408 | tf_op jit(solution)/shard_map/ppermute | solution.py:43
  112.9 1.6 %collective-permute-done.21 = bf16[64,1792]{1,0:T(8,128)(2,1)S(1)} collective-permute-done((bf16[64,1792]{1,0:T(8,128)(2,1)S(1)}, bf16[64,1792]{1,0:T(8,128)(2,1)S(1)}, u32[]{:S(2)}, u32[]{:S(2)}) %collective-permute-start.21) | collective-permute-done | bytes 229408 | tf_op jit(solution)/shard_map/ppermute | solution.py:43
  114.5 1.3 %collective-permute-start.22 = (bf16[32,1792]{1,0:T(8,128)(2,1)S(1)}, bf16[32,1792]{1,0:T(8,128)(2,1)S(1)}, u32[]{:S(2)}, u32[]{:S(2)}) collective-permute-start(bf16[32,1792]{1,0:T(8,128)(2,1)S(1)} %add_convert_fusion.18), channel_id=1, source_target_pairs={{0,16},{4,20},{8,24},{12,28},{16,0},{20,4},{24,8},{28,12},{1,17},{... | collective-permute-start | bytes 344072 | tf_op jit(solution)/shard_map/ppermute | solution.py:43
  115.8 1.4 %collective-permute-done.31 = bf16[32,1792]{1,0:T(8,128)(2,1)S(1)} collective-permute-done((bf16[32,1792]{1,0:T(8,128)(2,1)S(1)}, bf16[32,1792]{1,0:T(8,128)(2,1)S(1)}, u32[]{:S(2)}, u32[]{:S(2)}) %collective-permute-start.31) | collective-permute-done | bytes 114720 | tf_op jit(solution)/shard_map/ppermute | solution.py:43
  117.6 1.8 %collective-permute-done.22 = bf16[32,1792]{1,0:T(8,128)(2,1)S(1)} collective-permute-done((bf16[32,1792]{1,0:T(8,128)(2,1)S(1)}, bf16[32,1792]{1,0:T(8,128)(2,1)S(1)}, u32[]{:S(2)}, u32[]{:S(2)}) %collective-permute-start.22) | collective-permute-done | bytes 114720 | tf_op jit(solution)/shard_map/ppermute | solution.py:43
  119.4 2.7 %collective-permute-done.32 = bf16[32,1792]{1,0:T(8,128)(2,1)S(1)} collective-permute-done((bf16[32,1792]{1,0:T(8,128)(2,1)S(1)}, bf16[32,1792]{1,0:T(8,128)(2,1)S(1)}, u32[]{:S(2)}, u32[]{:S(2)}) %collective-permute-start.32) | collective-permute-done | bytes 114720 | tf_op jit(solution)/shard_map/ppermute | solution.py:43
  (59 shorter events, 13.2 us)
Async XLA Ops:
  1.5 7.9 %collective-permute-start = (bf16[32,1920]{1,0:T(8,128)(2,1)S(1)}, bf16[32,1920]{1,0:T(8,128)(2,1)S(1)}, u32[]{:S(2)}, u32[]{:S(2)}) collective-permute-start(bf16[32,1920]{1,0:T(8,128)(2,1)S(1)} %get-tuple-element.35), channel_id=1, source_target_pairs={{0,1},{1,0},{2,3},{3,2},{4,5},{5,4},{6,7},{7,6},{8,9},{9,8},{10,11... | collective-permute-start | bytes 368648 | tf_op jit(solution)/shard_map/ppermute | solution.py:43
  4.6 12.3 %collective-permute-start.1 = (bf16[32,1920]{1,0:T(8,128)(2,1)S(1)}, bf16[32,1920]{1,0:T(8,128)(2,1)S(1)}, u32[]{:S(2)}, u32[]{:S(2)}) collective-permute-start(bf16[32,1920]{1,0:T(8,128)(2,1)S(1)} %get-tuple-element.36), channel_id=1, source_target_pairs={{0,2},{1,3},{2,0},{3,1},{4,6},{5,7},{6,4},{7,5},{8,10},{9,11},{10,... | collective-permute-start | bytes 368648 | tf_op jit(solution)/shard_map/ppermute | solution.py:43
  7.2 9.7 %collective-permute-start.2 = (bf16[32,1920]{1,0:T(8,128)(2,1)S(1)}, bf16[32,1920]{1,0:T(8,128)(2,1)S(1)}, u32[]{:S(2)}, u32[]{:S(2)}) collective-permute-start(bf16[32,1920]{1,0:T(8,128)(2,1)S(1)} %get-tuple-element.37), channel_id=1, source_target_pairs={{0,3},{1,2},{2,1},{3,0},{4,7},{5,6},{6,5},{7,4},{8,11},{9,10},{10,... | collective-permute-start | bytes 368648 | tf_op jit(solution)/shard_map/ppermute | solution.py:43
  17.2 4.9 %collective-permute-start.3 = (bf16[32,1920]{1,0:T(8,128)(2,1)S(1)}, bf16[32,1920]{1,0:T(8,128)(2,1)S(1)}, u32[]{:S(2)}, u32[]{:S(2)}) collective-permute-start(bf16[32,1920]{1,0:T(8,128)(2,1)S(1)} %get-tuple-element.40.refs_0_), channel_id=1, source_target_pairs={{0,1},{1,0},{2,3},{3,2},{4,5},{5,4},{6,7},{7,6},{8,9},{9,8},{10,11... | collective-permute-start | bytes 368648 | tf_op jit(solution)/shard_map/ppermute | solution.py:43
  22.2 8.7 %collective-permute-start.17 = (bf16[64,1920]{1,0:T(8,128)(2,1)S(1)}, bf16[64,1920]{1,0:T(8,128)(2,1)S(1)}, u32[]{:S(2)}, u32[]{:S(2)}) collective-permute-start(bf16[64,1920]{1,0:T(8,128)(2,1)S(1)} %join.1.refs_0_), channel_id=1, source_target_pairs={{0,24},{4,28},{8,16},{12,20},{16,8},{20,12},{24,0},{28,4},{1,25},{... | collective-permute-start | bytes 737288 | tf_op jit(solution)/shard_map/ppermute | solution.py:43
  24.7 9.0 %collective-permute-start.15 = (bf16[64,1920]{1,0:T(8,128)(2,1)S(1)}, bf16[64,1920]{1,0:T(8,128)(2,1)S(1)}, u32[]{:S(2)}, u32[]{:S(2)}) collective-permute-start(bf16[64,1920]{1,0:T(8,128)(2,1)S(1)} %join.1.refs_0_), channel_id=1, source_target_pairs={{0,16},{4,20},{8,24},{12,28},{16,0},{20,4},{24,8},{28,12},{1,17},{... | collective-permute-start | bytes 737288 | tf_op jit(solution)/shard_map/ppermute | solution.py:43
  25.2 11.4 %collective-permute-start.4 = (bf16[64,1920]{1,0:T(8,128)(2,1)S(1)}, bf16[64,1920]{1,0:T(8,128)(2,1)S(1)}, u32[]{:S(2)}, u32[]{:S(2)}) collective-permute-start(bf16[64,1920]{1,0:T(8,128)(2,1)S(1)} %join.1.refs_0_), channel_id=1, source_target_pairs={{0,2},{1,3},{2,0},{3,1},{4,6},{5,7},{6,4},{7,5},{8,10},{9,11},{10,... | collective-permute-start | bytes 737288 | tf_op jit(solution)/shard_map/ppermute | solution.py:43
  28.1 10.0 %collective-permute-start.13 = (bf16[64,1920]{1,0:T(8,128)(2,1)S(1)}, bf16[64,1920]{1,0:T(8,128)(2,1)S(1)}, u32[]{:S(2)}, u32[]{:S(2)}) collective-permute-start(bf16[64,1920]{1,0:T(8,128)(2,1)S(1)} %join.1.refs_0_), channel_id=1, source_target_pairs={{0,8},{4,12},{8,0},{12,4},{16,24},{20,28},{24,16},{28,20},{1,9},{5... | collective-permute-start | bytes 737288 | tf_op jit(solution)/shard_map/ppermute | solution.py:43
  28.6 10.0 %collective-permute-start.12 = (bf16[64,1920]{1,0:T(8,128)(2,1)S(1)}, bf16[64,1920]{1,0:T(8,128)(2,1)S(1)}, u32[]{:S(2)}, u32[]{:S(2)}) collective-permute-start(bf16[64,1920]{1,0:T(8,128)(2,1)S(1)} %join.1.refs_0_), channel_id=1, source_target_pairs={{0,4},{4,0},{8,12},{12,8},{16,20},{20,16},{24,28},{28,24},{1,5},{5... | collective-permute-start | bytes 737288 | tf_op jit(solution)/shard_map/ppermute | solution.py:43
  30.9 9.2 %collective-permute-start.18 = (bf16[64,1920]{1,0:T(8,128)(2,1)S(1)}, bf16[64,1920]{1,0:T(8,128)(2,1)S(1)}, u32[]{:S(2)}, u32[]{:S(2)}) collective-permute-start(bf16[64,1920]{1,0:T(8,128)(2,1)S(1)} %collective-permute-done.17.refs_6_), channel_id=1, source_target_pairs={{0,4},{4,0},{8,12},{12,8},{16,20},{20,16},{24,28},{28,24},{1,5},{5... | collective-permute-start | bytes 737288 | tf_op jit(solution)/shard_map/ppermute | solution.py:43
  33.7 6.4 %collective-permute-start.16 = (bf16[64,1920]{1,0:T(8,128)(2,1)S(1)}, bf16[64,1920]{1,0:T(8,128)(2,1)S(1)}, u32[]{:S(2)}, u32[]{:S(2)}) collective-permute-start(bf16[64,1920]{1,0:T(8,128)(2,1)S(1)} %collective-permute-done.15.refs_4_), channel_id=1, source_target_pairs={{0,4},{4,0},{8,12},{12,8},{16,20},{20,16},{24,28},{28,24},{1,5},{5... | collective-permute-start | bytes 737288 | tf_op jit(solution)/shard_map/ppermute | solution.py:43
  36.6 9.8 %collective-permute-start.10 = (bf16[64,1920]{1,0:T(8,128)(2,1)S(1)}, bf16[64,1920]{1,0:T(8,128)(2,1)S(1)}, u32[]{:S(2)}, u32[]{:S(2)}) collective-permute-start(bf16[64,1920]{1,0:T(8,128)(2,1)S(1)} %collective-permute-done.4.refs_0_), channel_id=1, source_target_pairs={{0,24},{4,28},{8,16},{12,20},{16,8},{20,12},{24,0},{28,4},{1,25},{... | collective-permute-start | bytes 737288 | tf_op jit(solution)/shard_map/ppermute | solution.py:43
  38.1 11.7 %collective-permute-start.8 = (bf16[64,1920]{1,0:T(8,128)(2,1)S(1)}, bf16[64,1920]{1,0:T(8,128)(2,1)S(1)}, u32[]{:S(2)}, u32[]{:S(2)}) collective-permute-start(bf16[64,1920]{1,0:T(8,128)(2,1)S(1)} %collective-permute-done.4.refs_0_), channel_id=1, source_target_pairs={{0,16},{4,20},{8,24},{12,28},{16,0},{20,4},{24,8},{28,12},{1,17},{... | collective-permute-start | bytes 737288 | tf_op jit(solution)/shard_map/ppermute | solution.py:43
  38.6 11.2 %collective-permute-start.6 = (bf16[64,1920]{1,0:T(8,128)(2,1)S(1)}, bf16[64,1920]{1,0:T(8,128)(2,1)S(1)}, u32[]{:S(2)}, u32[]{:S(2)}) collective-permute-start(bf16[64,1920]{1,0:T(8,128)(2,1)S(1)} %collective-permute-done.4.refs_0_), channel_id=1, source_target_pairs={{0,8},{4,12},{8,0},{12,4},{16,24},{20,28},{24,16},{28,20},{1,9},{5... | collective-permute-start | bytes 737288 | tf_op jit(solution)/shard_map/ppermute | solution.py:43
  40.1 10.2 %collective-permute-start.14 = (bf16[64,1920]{1,0:T(8,128)(2,1)S(1)}, bf16[64,1920]{1,0:T(8,128)(2,1)S(1)}, u32[]{:S(2)}, u32[]{:S(2)}) collective-permute-start(bf16[64,1920]{1,0:T(8,128)(2,1)S(1)} %collective-permute-done.13.refs_2_), channel_id=1, source_target_pairs={{0,4},{4,0},{8,12},{12,8},{16,20},{20,16},{24,28},{28,24},{1,5},{5... | collective-permute-start | bytes 737288 | tf_op jit(solution)/shard_map/ppermute | solution.py:43
  40.1 26.1 %collective-permute-start.5 = (bf16[64,1920]{1,0:T(8,128)(2,1)S(1)}, bf16[64,1920]{1,0:T(8,128)(2,1)S(1)}, u32[]{:S(2)}, u32[]{:S(2)}) collective-permute-start(bf16[64,1920]{1,0:T(8,128)(2,1)S(1)} %collective-permute-done.4.refs_0_), channel_id=1, source_target_pairs={{0,4},{4,0},{8,12},{12,8},{16,20},{20,16},{24,28},{28,24},{1,5},{5... | collective-permute-start | bytes 737288 | tf_op jit(solution)/shard_map/ppermute | solution.py:43
  46.5 19.8 %collective-permute-start.11 = (bf16[64,1920]{1,0:T(8,128)(2,1)S(1)}, bf16[64,1920]{1,0:T(8,128)(2,1)S(1)}, u32[]{:S(2)}, u32[]{:S(2)}) collective-permute-start(bf16[64,1920]{1,0:T(8,128)(2,1)S(1)} %collective-permute-done.10.refs_6_), channel_id=1, source_target_pairs={{0,4},{4,0},{8,12},{12,8},{16,20},{20,16},{24,28},{28,24},{1,5},{5... | collective-permute-start | bytes 737288 | tf_op jit(solution)/shard_map/ppermute | solution.py:43
  49.8 16.5 %collective-permute-start.9 = (bf16[64,1920]{1,0:T(8,128)(2,1)S(1)}, bf16[64,1920]{1,0:T(8,128)(2,1)S(1)}, u32[]{:S(2)}, u32[]{:S(2)}) collective-permute-start(bf16[64,1920]{1,0:T(8,128)(2,1)S(1)} %collective-permute-done.8.refs_4_), channel_id=1, source_target_pairs={{0,4},{4,0},{8,12},{12,8},{16,20},{20,16},{24,28},{28,24},{1,5},{5... | collective-permute-start | bytes 737288 | tf_op jit(solution)/shard_map/ppermute | solution.py:43
  49.9 16.4 %collective-permute-start.7 = (bf16[64,1920]{1,0:T(8,128)(2,1)S(1)}, bf16[64,1920]{1,0:T(8,128)(2,1)S(1)}, u32[]{:S(2)}, u32[]{:S(2)}) collective-permute-start(bf16[64,1920]{1,0:T(8,128)(2,1)S(1)} %collective-permute-done.6.refs_2_), channel_id=1, source_target_pairs={{0,4},{4,0},{8,12},{12,8},{16,20},{20,16},{24,28},{28,24},{1,5},{5... | collective-permute-start | bytes 737288 | tf_op jit(solution)/shard_map/ppermute | solution.py:43
  85.0 3.3 %collective-permute-start.19 = (bf16[128,1792]{1,0:T(8,128)(2,1)S(1)}, bf16[128,1792]{1,0:T(8,128)(2,1)S(1)}, u32[]{:S(2)}, u32[]{:S(2)}) collective-permute-start(bf16[128,1792]{1,0:T(8,128)(2,1)S(1)} %get-tuple-element.47), channel_id=1, source_target_pairs={{0,4},{4,0},{8,12},{12,8},{16,20},{20,16},{24,28},{28,24},{1,5},{5... | collective-permute-start | bytes 1376264 | tf_op jit(solution)/shard_map/ppermute | solution.py:43
  88.4 10.0 %collective-permute-start.23 = (bf16[64,1792]{1,0:T(8,128)(2,1)S(1)}, bf16[64,1792]{1,0:T(8,128)(2,1)S(1)}, u32[]{:S(2)}, u32[]{:S(2)}) collective-permute-start(bf16[64,1792]{1,0:T(8,128)(2,1)S(1)} %get-tuple-element.60), channel_id=1, source_target_pairs={{0,8},{4,12},{8,0},{12,4},{16,24},{20,28},{24,16},{28,20},{1,9},{5... | collective-permute-start | bytes 688136 | tf_op jit(solution)/shard_map/ppermute | solution.py:43
  89.8 7.9 %collective-permute-start.26 = (bf16[64,1792]{1,0:T(8,128)(2,1)S(1)}, bf16[64,1792]{1,0:T(8,128)(2,1)S(1)}, u32[]{:S(2)}, u32[]{:S(2)}) collective-permute-start(bf16[64,1792]{1,0:T(8,128)(2,1)S(1)} %get-tuple-element.62), channel_id=1, source_target_pairs={{0,16},{4,20},{8,24},{12,28},{16,0},{20,4},{24,8},{28,12},{1,17},{... | collective-permute-start | bytes 688136 | tf_op jit(solution)/shard_map/ppermute | solution.py:43
  93.4 13.7 %collective-permute-start.20 = (bf16[128,1792]{1,0:T(8,128)(2,1)S(1)}, bf16[128,1792]{1,0:T(8,128)(2,1)S(1)}, u32[]{:S(2)}, u32[]{:S(2)}) collective-permute-start(bf16[128,1792]{1,0:T(8,128)(2,1)S(1)} %get-tuple-element.51), channel_id=1, source_target_pairs={{0,4},{4,0},{8,12},{12,8},{16,20},{20,16},{24,28},{28,24},{1,5},{5... | collective-permute-start | bytes 1376264 | tf_op jit(solution)/shard_map/ppermute | solution.py:43
  96.1 9.9 %collective-permute-start.29 = (bf16[128,1792]{1,0:T(8,128)(2,1)S(1)}, bf16[128,1792]{1,0:T(8,128)(2,1)S(1)}, u32[]{:S(2)}, u32[]{:S(2)}) collective-permute-start(bf16[128,1792]{1,0:T(8,128)(2,1)S(1)} %get-tuple-element.56), channel_id=1, source_target_pairs={{0,4},{4,0},{8,12},{12,8},{16,20},{20,16},{24,28},{28,24},{1,5},{5... | collective-permute-start | bytes 1376264 | tf_op jit(solution)/shard_map/ppermute | solution.py:43
  97.8 4.9 %collective-permute-start.27 = (bf16[32,1792]{1,0:T(8,128)(2,1)S(1)}, bf16[32,1792]{1,0:T(8,128)(2,1)S(1)}, u32[]{:S(2)}, u32[]{:S(2)}) collective-permute-start(bf16[32,1792]{1,0:T(8,128)(2,1)S(1)} %add_convert_fusion.13), channel_id=1, source_target_pairs={{0,8},{4,12},{8,0},{12,4},{16,24},{20,28},{24,16},{28,20},{1,9},{5... | collective-permute-start | bytes 344072 | tf_op jit(solution)/shard_map/ppermute | solution.py:43
  98.5 4.9 %collective-permute-start.24 = (bf16[32,1792]{1,0:T(8,128)(2,1)S(1)}, bf16[32,1792]{1,0:T(8,128)(2,1)S(1)}, u32[]{:S(2)}, u32[]{:S(2)}) collective-permute-start(bf16[32,1792]{1,0:T(8,128)(2,1)S(1)} %add_convert_fusion.16), channel_id=1, source_target_pairs={{0,16},{4,20},{8,24},{12,28},{16,0},{20,4},{24,8},{28,12},{1,17},{... | collective-permute-start | bytes 344072 | tf_op jit(solution)/shard_map/ppermute | solution.py:43
  103.4 12.4 %collective-permute-start.28 = (bf16[64,1792]{1,0:T(8,128)(2,1)S(1)}, bf16[64,1792]{1,0:T(8,128)(2,1)S(1)}, u32[]{:S(2)}, u32[]{:S(2)}) collective-permute-start(bf16[64,1792]{1,0:T(8,128)(2,1)S(1)} %pad_maximum_fusion), channel_id=1, source_target_pairs={{0,2},{1,3},{2,0},{3,1},{4,6},{5,7},{6,4},{7,5},{8,10},{9,11},{10,... | collective-permute-start | bytes 688136 | tf_op jit(solution)/shard_map/ppermute | solution.py:43
  106.2 6.1 %collective-permute-start.30 = (bf16[64,1792]{1,0:T(8,128)(2,1)S(1)}, bf16[64,1792]{1,0:T(8,128)(2,1)S(1)}, u32[]{:S(2)}, u32[]{:S(2)}) collective-permute-start(bf16[64,1792]{1,0:T(8,128)(2,1)S(1)} %get-tuple-element.64), channel_id=1, source_target_pairs={{0,16},{4,20},{8,24},{12,28},{16,0},{20,4},{24,8},{28,12},{1,17},{... | collective-permute-start | bytes 688136 | tf_op jit(solution)/shard_map/ppermute | solution.py:43
  107.2 7.3 %collective-permute-start.21 = (bf16[64,1792]{1,0:T(8,128)(2,1)S(1)}, bf16[64,1792]{1,0:T(8,128)(2,1)S(1)}, u32[]{:S(2)}, u32[]{:S(2)}) collective-permute-start(bf16[64,1792]{1,0:T(8,128)(2,1)S(1)} %get-tuple-element.58), channel_id=1, source_target_pairs={{0,8},{4,12},{8,0},{12,4},{16,24},{20,28},{24,16},{28,20},{1,9},{5... | collective-permute-start | bytes 688136 | tf_op jit(solution)/shard_map/ppermute | solution.py:43
  112.3 4.9 %collective-permute-start.31 = (bf16[32,1792]{1,0:T(8,128)(2,1)S(1)}, bf16[32,1792]{1,0:T(8,128)(2,1)S(1)}, u32[]{:S(2)}, u32[]{:S(2)}) collective-permute-start(bf16[32,1792]{1,0:T(8,128)(2,1)S(1)} %add_convert_fusion.10), channel_id=1, source_target_pairs={{0,8},{4,12},{8,0},{12,4},{16,24},{20,28},{24,16},{28,20},{1,9},{5... | collective-permute-start | bytes 344072 | tf_op jit(solution)/shard_map/ppermute | solution.py:43
  114.5 4.9 %collective-permute-start.22 = (bf16[32,1792]{1,0:T(8,128)(2,1)S(1)}, bf16[32,1792]{1,0:T(8,128)(2,1)S(1)}, u32[]{:S(2)}, u32[]{:S(2)}) collective-permute-start(bf16[32,1792]{1,0:T(8,128)(2,1)S(1)} %add_convert_fusion.18), channel_id=1, source_target_pairs={{0,16},{4,20},{8,24},{12,28},{16,0},{20,4},{24,8},{28,12},{1,17},{... | collective-permute-start | bytes 344072 | tf_op jit(solution)/shard_map/ppermute | solution.py:43
  117.2 4.9 %collective-permute-start.32 = (bf16[32,1792]{1,0:T(8,128)(2,1)S(1)}, bf16[32,1792]{1,0:T(8,128)(2,1)S(1)}, u32[]{:S(2)}, u32[]{:S(2)}) collective-permute-start(bf16[32,1792]{1,0:T(8,128)(2,1)S(1)} %add_convert_fusion.9), channel_id=1, source_target_pairs={{0,1},{1,0},{2,3},{3,2},{4,5},{5,4},{6,7},{7,6},{8,9},{9,8},{10,11... | collective-permute-start | bytes 344072 | tf_op jit(solution)/shard_map/ppermute | solution.py:43
  (1 other events, 1.9 us)

commit v4 on v3

--- a/solution.py
+++ b/solution.py
@@ -111,6 +111,19 @@
     message[:, width:] = tail.astype(BF16)
 
 
+def load_kernel(me, gate_hbm, up_hbm, gate, up, sems):
+    depth = gate.shape[1]
+    here = pl.ds(pl.multiple_of((me[0] >> 1) * depth, LANES), depth)
+    copies = [
+        pltpu.make_async_copy(source.at[:, here, :], target, sems.at[i])
+        for i, (source, target) in enumerate(((gate_hbm, gate), (up_hbm, up)))
+    ]
+    for copy in copies:
+        copy.start()
+    for copy in copies:
+        copy.wait()
+
+
 def up_kernel(start, last, chunks, ahead, full, experts, me, first, w_gate, w_up, down_hbm, *refs):
     *refs, sem = refs
     x = refs[-1 - last]
@@ -123,15 +136,18 @@
         pieces = refs[:-5] if start else refs[:-8]
     expert = pl.program_id(0)
     columns = held_down.shape[2]
-    block = (me[0] ^ ahead) // (columns // (x.shape[1] // chunks))
+    block = me[0] ^ ahead
     copy = pltpu.make_async_copy(
         down_hbm.at[:, :, pl.ds(pl.multiple_of(block * columns, LANES), columns)], held_down, sem
     )
     width = x.shape[1] // chunks
 
+    @pl.when(expert == (0 if start or down_hbm.shape[0] == 1 else 1))
+    def _():
+        copy.start()
+
     @pl.when(expert == 0)
     def _():
-        copy.start()
         height = pieces[0].shape[0] // chunks
         for i, piece in enumerate(pieces):
             there = slice(i * height, (i + 1) * height)
@@ -146,8 +162,8 @@
                     tail = before[there, :] + jnp.where(lane >= experts, tail, 0.0)
                 side[there, :] = tail
 
-    gate = jnp.dot(x[...], w_gate[0], preferred_element_type=F32)
-    up = jnp.dot(x[...], w_up[0], preferred_element_type=F32)
+    gate = jnp.dot(x[...], w_gate[expert if start else 0], preferred_element_type=F32)
+    up = jnp.dot(x[...], w_up[expert if start else 0], preferred_element_type=F32)
     if start:
         gate_acc[expert] = gate
         up_acc[expert] = up
@@ -169,10 +185,21 @@
         copy.wait()
 
 
-def down_kernel(order, place, cols, me, activation, w_down, keep, send):
+def down_kernel(order, ahead, me, activation, w_down, *refs):
+    if ahead is None:
+        keep, send = refs
+    else:
+        down_hbm, keep, send, held_down, sem = refs
+        columns = held_down.shape[2]
+        there = pl.ds(pl.multiple_of((me[0] ^ ahead) * columns, LANES), columns)
+        copy = pltpu.make_async_copy(down_hbm.at[:, :, there], held_down, sem)
+
+        @pl.when(pl.program_id(0) == 0)
+        def _():
+            copy.start()
+
     width = keep.shape[1]
-    slot = (me[0] ^ place) & (w_down.shape[2] // cols - 1)
-    here = pl.ds(pl.multiple_of(slot * cols + pl.program_id(0) * width, LANES), width)
+    here = pl.ds(pl.multiple_of(pl.program_id(0) * width, LANES), width)
     weights = w_down[:, :, here].reshape(-1, width)
     total = jnp.dot(activation[...], weights, preferred_element_type=F32).astype(BF16)
     height = total.shape[0] // len(order)
@@ -181,6 +208,11 @@
         out = keep if i < middle else send
         at = i % middle
         out[at * height : (at + 1) * height, :] = total[pattern * height : (pattern + 1) * height]
+    if ahead is not None:
+
+        @pl.when(pl.program_id(0) == pl.num_programs(0) - 1)
+        def _():
+            copy.wait()
 
 
 def join_kernel(*refs):
@@ -202,11 +234,20 @@
     )(*parts)
 
 
-def gather_rows(block, exp_count):
+def after(value, *others):
+    return lax.optimization_barrier((value, *others))[0]
+
+
+def cross_plane(block, exp_count):
     found = {0: block}
     found.update({pattern: swap(block, "exp", pattern) for pattern in range(2, exp_count, 2)})
-    found.update({pattern ^ 1: swap(piece, "exp", 1) for pattern, piece in list(found.items())})
-    return [found[pattern] for pattern in range(exp_count)]
+    return found
+
+
+def cross_core(found):
+    both = dict(found)
+    both.update({pattern ^ 1: swap(piece, "exp", 1) for pattern, piece in found.items()})
+    return [both[pattern] for pattern in sorted(both)]
 
 
 def add(a, b):
@@ -264,15 +305,32 @@
         groups.append(swap(groups[0] if bit == 2 else join(*groups), "tp", bit))
         bit *= 2
 
+    plane = cross_plane(groups[0], exp_count)
+    held_gate, held_up = pl.pallas_call(
+        load_kernel,
+        out_shape=[pltpu.VMEM((local_experts, 2 * cols, hidden), BF16)] * 2,
+        in_specs=[smem()] + [pl.BlockSpec(memory_space=pltpu.HBM)] * 2,
+        out_specs=[vmem()] * 2,
+        scratch_shapes=[pltpu.SemaphoreType.DMA((2,))],
+        compiler_params=params(8),
+        cost_estimate=pl.CostEstimate(flops=0, bytes_accessed=8 * cols * hidden * local_experts, transcendentals=0),
+        name="load_weights",
+    )(after(me, plane[exp_count - 2]), off_chip(w_gate), off_chip(w_up))
+    plane[2] = after(plane[2], held_gate)
+
     state, held_down = [], {}
+    places = list(reversed(range(tp_count)))
     sizes = [group.shape[0] // rows for group in groups]
     starts = [0] + sizes[1:]
     for i, group in enumerate(groups):
-        pieces = gather_rows(group, exp_count)
+        if i:
+            plane = cross_plane(group, exp_count)
+            plane = {pattern: after(piece, state[-1]) for pattern, piece in plane.items()}
+        pieces = cross_core(plane)
         chunks, flip = sizes[i], starts[i]
-        ahead, columns = starts[-1 - i], sizes[-1 - i] * cols
+        ahead = places[i]
         start, last = i == 0, i == len(groups) - 1
-        down_shape = pltpu.VMEM((local_experts, hidden, columns), BF16)
+        down_shape = pltpu.VMEM((local_experts, hidden, cols), BF16)
         acc = pltpu.VMEM((local_experts, total_rows, hidden), F32)
         if last:
             out_shape = [shape(total_rows, local_experts * hidden), down_shape]
@@ -280,13 +338,15 @@
         else:
             out_shape = [acc, acc, pltpu.VMEM((total_rows, tail), F32), down_shape]
             out_specs = [vmem()] * 4
-        weights = [off_chip(w_gate), off_chip(w_up)]
+        weights = [on_chip(held_gate), on_chip(held_up)] if i == 0 else [off_chip(w_gate), off_chip(w_up)]
         specs = [
             pl.BlockSpec(
                 (1, chunks * cols, hidden),
                 lambda e, me, first, flip=flip, chunks=chunks: (e, (me[0] ^ flip) // chunks, 0),
             )
         ] * 2
+        if i == 0:
+            specs = [vmem()] * 2
         scratch = [pltpu.VMEM((total_rows, chunks * cols), BF16)]
         *state, held_down[ahead] = pl.pallas_call(
             functools.partial(up_kernel, start, last, chunks, ahead, full, experts),
@@ -301,7 +361,7 @@
                 + [pltpu.SemaphoreType.DMA(())],
             ),
             input_output_aliases={} if start or last else {5 + len(pieces) + j: j for j in range(3)},
-            compiler_params=params(22),
+            compiler_params=params(6 if start else 22),
             cost_estimate=pl.CostEstimate(
                 flops=4 * total_rows * chunks * cols * hidden * local_experts,
                 bytes_accessed=4 * chunks * cols * hidden * local_experts,
@@ -313,47 +373,50 @@
 
     steps = 2 if cols % (2 * LANES) == 0 else 1
     width = cols // steps
-    results, gates_open = {}, []
-    for k in reversed(range(tp_count)):
+    stages = len(orders[0]) + 1
+    events = [(float(j), 0, j, None) for j in range(tp_count)]
+    events += [(j + 1.5 + 2 * stage, stage, j, stage) for j in range(tp_count) for stage in range(stages)]
+    mine, theirs, opened, done = {}, {}, [], []
+    for _, _, j, stage in sorted(events, key=lambda event: event[:3]):
+        k = places[j]
         order = orders[k % 2]
-        block = max(place for place in held_down if place <= k)
-        source = activation
-        if len(gates_open) > 1:
-            source, _ = lax.optimization_barrier((activation, gates_open[-2]))
-        keep, send = pl.pallas_call(
-            functools.partial(down_kernel, relative_order([core] + order), k, cols),
-            out_shape=[shape(total_rows // 2, cols)] * 2,
-            grid_spec=pltpu.PrefetchScalarGridSpec(
-                num_scalar_prefetch=1,
-                grid=(steps,),
-                in_specs=[vmem()] * 2,
-                out_specs=[pl.BlockSpec((total_rows // 2, width), lambda i, me: (0, i))] * 2,
-            ),
-            compiler_params=params(8),
-            cost_estimate=pl.CostEstimate(
-                flops=2 * total_rows * cols * hidden * local_experts,
-                bytes_accessed=2 * cols * hidden * local_experts,
-                transcendentals=0,
-            ),
-            name="down",
-        )(me, source, on_chip(held_down[block]))
-        mine, theirs = keep, swap(send, "exp", core)
-        for i, bit in enumerate(order):
-            middle = mine.shape[0] // 2
-            away = add(mine[middle:], theirs[middle:])
-            if i == 0:
-                gates_open.append(away)
-            mine, theirs = add(mine[:middle], theirs[:middle]), swap(away, "exp", bit)
-        results[k] = (mine, theirs)
-
-    bit = tp_count // 2
-    while bit:
-        far = jnp.concatenate([functools.reduce(sum_of, results[k]) for k in range(bit, 2 * bit)], axis=0)
-        got = swap(far.astype(BF16), "tp", bit)
-        for k in range(bit):
-            results[k] = results[k] + (got[k * rows : (k + 1) * rows],)
-        bit //= 2
-    return (projected + functools.reduce(sum_of, results[0])).astype(BF16)
+        if stage is None:
+            ahead = places[j + len(groups)] if j + len(groups) < tp_count else None
+            held = [] if ahead is None else [pltpu.VMEM((local_experts, hidden, cols), BF16)]
+            keep, send, *found = pl.pallas_call(
+                functools.partial(down_kernel, relative_order([core] + order), ahead),
+                out_shape=[shape(total_rows // 2, cols)] * 2 + held,
+                grid_spec=pltpu.PrefetchScalarGridSpec(
+                    num_scalar_prefetch=1,
+                    grid=(steps,),
+                    in_specs=[vmem()] * 2 + [pl.BlockSpec(memory_space=pltpu.HBM)] * len(held),
+                    out_specs=[pl.BlockSpec((total_rows // 2, width), lambda i, me: (0, i))] * 2 + [vmem()] * len(held),
+                    scratch_shapes=[pltpu.SemaphoreType.DMA(())] * len(held),
+                ),
+                compiler_params=params(8),
+                cost_estimate=pl.CostEstimate(
+                    flops=2 * total_rows * cols * hidden * local_experts,
+                    bytes_accessed=2 * cols * hidden * local_experts,
+                    transcendentals=0,
+                ),
+                name="down",
+            )(me, after(activation, *opened[-1:]), on_chip(held_down[k]), *[off_chip(w_down)] * len(held))
+            if found:
+                held_down[ahead] = found[0]
+            mine[k], theirs[k] = keep, swap(send, "exp", core)
+        elif stage < stages - 1:
+            middle = mine[k].shape[0] // 2
+            got = after(theirs[k], *opened[-1:])
+            away = add(mine[k][middle:], got[middle:])
+            opened.append(away)
+            mine[k], theirs[k] = add(mine[k][:middle], got[:middle]), swap(away, "exp", order[stage])
+        elif k:
+            away = add(mine[k], after(theirs[k], *opened[-1:]))
+            opened.append(away)
+            done.append(swap(away, "tp", k))
+        else:
+            done += [mine[k], theirs[k]]
+    return functools.reduce(sum_of, [projected] + done).astype(BF16)
 
 
 def solution(mesh):

time: 123 us -> 114 us (0.927)
  waiting for transfers between devices: 44.1 us -> 27.6 us
  Pallas kernels: 44.3 us -> 48.6 us
  starting transfers between devices: 30.5 us -> 34 us
    ppermute x33 -> x34, waiting for transfers between devices: 44.1 us -> 27.6 us  [swap(): return lax.ppermute(value, axis, [(i, i ^ bit) for i in range(count)])]
    pallas_call x0 -> x1, Pallas kernels: none -> 9.39 us  [local(): pl.pallas_call(load_kernel, out_shape=[pltpu.VMEM((local_experts, 2 * col...]
    pallas_call x2, Pallas kernels: 32 us -> 23.7 us  [local(): pl.pallas_call(functools.partial(up_kernel, start, last, chunks, ahead, f...]
    ppermute x33 -> x34, starting transfers between devices: 30.5 us -> 34 us  [swap(): return lax.ppermute(value, axis, [(i, i ^ bit) for i in range(count)])]
    pallas_call x4, Pallas kernels: 10.5 us -> 13.8 us  [local(): pl.pallas_call(functools.partial(down_kernel, relative_order([core] + ord...]
  transfers between devices with their start and end apart: 33 -> 34, of which waited for: 17 -> 12; matrix products, arithmetic and copies ran while one was open for 2% -> 3% of each run, Pallas kernels for 19% -> 24%
where the time goes in v4:
time: 114 us
  Pallas kernels  48.6 us (43%)
  starting transfers between devices  34 us (30%)
  waiting for transfers between devices  27.6 us (24%)
  local copies, waits for them, and re-layouts  2.22 us (2%)
  other arithmetic  1.44 us (1%)
    ppermute x34, starting transfers between devices, swap(): return lax.ppermute(value, axis, [(i, i ^ bit) for i in range(count)])  34 us
    ppermute x34, waiting for transfers between devices, swap(): return lax.ppermute(value, axis, [(i, i ^ bit) for i in range(count)])  27.6 us
    pallas_call x2, Pallas kernels, local(): pl.pallas_call(functools.partial(up_kernel, start, last, chunks, ahead, f...  23.7 us
    pallas_call x4, Pallas kernels, local(): pl.pallas_call(functools.partial(down_kernel, relative_order([core] + ord...  13.8 us
    pallas_call x1, Pallas kernels, local(): pl.pallas_call(load_kernel, out_shape=[pltpu.VMEM((local_experts, 2 * col...  9.39 us
  transfers between devices with their start and end apart: 34, of which 12 were waited for; matrix products, arithmetic and copies ran while one was open for 3% of the time, Pallas kernels for 24%

profile of v4, /device:TPU:0, one launch (start us, length us, event | category | flops | bytes accessed | tf_op | source)
XLA Modules:
  0.0 114.2 jit_solution(11542339582482188352)
XLA Ops:
  0.0 1.5 %cut_heads.1 = (bf16[32,1920]{1,0:T(8,128)(2,1)S(1)}, bf16[32,1920]{1,0:T(8,128)(2,1)S(1)}, bf16[32,1920]{1,0:T(8,128)(2,1)S(1)}, f32[32,1792]{1,0:T(8,128)S(1)}...) custom-call(s32[1]{0:T(128)} %bitcast.me, bf16[32,7168]{1,0:T(8,128)(2,1)} %bitcast.4, bf16[32,1792]{1,0:T(8,128)(2,1)} %resid_hbm.1, ...), custom_call_target="tpu_custom_call" | custom-call | tf_op jit(solution)/shard_map/cut_heads/pallas_call | solution.py:276
  1.5 3.1 %collective-permute-start = (bf16[32,1920]{1,0:T(8,128)(2,1)S(1)}, bf16[32,1920]{1,0:T(8,128)(2,1)S(1)}, u32[]{:S(2)}, u32[]{:S(2)}) collective-permute-start(bf16[32,1920]{1,0:T(8,128)(2,1)S(1)} %get-tuple-element.55), channel_id=1, source_target_pairs={{0,1},{1,0},{2,3},{3,2},{4,5},{5,4},{6,7},{7,6},{8,9},{9,8},{10,11... | collective-permute-start | bytes 368648 | tf_op jit(solution)/shard_map/ppermute | solution.py:43
  4.6 2.6 %collective-permute-start.1 = (bf16[32,1920]{1,0:T(8,128)(2,1)S(1)}, bf16[32,1920]{1,0:T(8,128)(2,1)S(1)}, u32[]{:S(2)}, u32[]{:S(2)}) collective-permute-start(bf16[32,1920]{1,0:T(8,128)(2,1)S(1)} %get-tuple-element.56), channel_id=1, source_target_pairs={{0,2},{1,3},{2,0},{3,1},{4,6},{5,7},{6,4},{7,5},{8,10},{9,11},{10,... | collective-permute-start | bytes 368648 | tf_op jit(solution)/shard_map/ppermute | solution.py:43
  7.2 0.8 copy.10.ids
  7.9 0.8 copy.11.gates
  9.4 7.5 %collective-permute-done.1.refs_1_ = bf16[32,1920]{1,0:T(8,128)(2,1)S(1)} collective-permute-done((bf16[32,1920]{1,0:T(8,128)(2,1)S(1)}, bf16[32,1920]{1,0:T(8,128)(2,1)S(1)}, u32[]{:S(2)}, u32[]{:S(2)}) %collective-permute-start.1) | collective-permute-done | bytes 122912 | tf_op jit(solution)/shard_map/ppermute | solution.py:43
  17.2 1.9 %collective-permute-start.3 = (bf16[32,1920]{1,0:T(8,128)(2,1)S(1)}, bf16[32,1920]{1,0:T(8,128)(2,1)S(1)}, u32[]{:S(2)}, u32[]{:S(2)}) collective-permute-start(bf16[32,1920]{1,0:T(8,128)(2,1)S(1)} %get-tuple-element.60.refs_0_), channel_id=1, source_target_pairs={{0,1},{1,0},{2,3},{3,2},{4,5},{5,4},{6,7},{7,6},{8,9},{9,8},{10,11... | collective-permute-start | bytes 368648 | tf_op jit(solution)/shard_map/ppermute | solution.py:43
  19.2 3.0 %collective-permute-done.3.refs_1_ = bf16[32,1920]{1,0:T(8,128)(2,1)S(1)} collective-permute-done((bf16[32,1920]{1,0:T(8,128)(2,1)S(1)}, bf16[32,1920]{1,0:T(8,128)(2,1)S(1)}, u32[]{:S(2)}, u32[]{:S(2)}) %collective-permute-start.3) | collective-permute-done | bytes 122912 | tf_op jit(solution)/shard_map/ppermute | solution.py:43
  22.2 2.5 %collective-permute-start.5 = (bf16[64,1920]{1,0:T(8,128)(2,1)S(1)}, bf16[64,1920]{1,0:T(8,128)(2,1)S(1)}, u32[]{:S(2)}, u32[]{:S(2)}) collective-permute-start(bf16[64,1920]{1,0:T(8,128)(2,1)S(1)} %join.1.refs_0_), channel_id=1, source_target_pairs={{0,24},{4,28},{8,16},{12,20},{16,8},{20,12},{24,0},{28,4},{1,25},{... | collective-permute-start | bytes 737288 | tf_op jit(solution)/shard_map/ppermute | solution.py:43
  25.7 2.9 %collective-permute-start.4 = (bf16[64,1920]{1,0:T(8,128)(2,1)S(1)}, bf16[64,1920]{1,0:T(8,128)(2,1)S(1)}, u32[]{:S(2)}, u32[]{:S(2)}) collective-permute-start(bf16[64,1920]{1,0:T(8,128)(2,1)S(1)} %join.1.refs_0_), channel_id=1, source_target_pairs={{0,2},{1,3},{2,0},{3,1},{4,6},{5,7},{6,4},{7,5},{8,10},{9,11},{10,... | collective-permute-start | bytes 737288 | tf_op jit(solution)/shard_map/ppermute | solution.py:43
  28.6 2.5 %collective-permute-done.5.refs_6_ = bf16[64,1920]{1,0:T(8,128)(2,1)S(1)} collective-permute-done((bf16[64,1920]{1,0:T(8,128)(2,1)S(1)}, bf16[64,1920]{1,0:T(8,128)(2,1)S(1)}, u32[]{:S(2)}, u32[]{:S(2)}) %collective-permute-start.5) | collective-permute-done | bytes 245792 | tf_op jit(solution)/shard_map/ppermute | solution.py:43
  31.2 9.4 %load_weights.1 = (bf16[4,3584,512]{2,1,0:T(8,128)(2,1)S(1)}, bf16[4,3584,512]{2,1,0:T(8,128)(2,1)S(1)}) custom-call(s32[1]{0:T(128)} %bitcast.me, bf16[4,7168,512]{2,1,0:T(8,128)(2,1)} %w_gate.1, bf16[4,7168,512]{2,1,0:T(8,128)(2,1)} %w_up.1), custom_call_target="tpu_custom_call" | custom-call | bytes 29360128 | tf_op jit(solution)/shard_map/load_weights/pallas_call | solution.py:309
  41.2 2.5 %collective-permute-start.17 = (bf16[64,1920]{1,0:T(8,128)(2,1)S(1)}, bf16[64,1920]{1,0:T(8,128)(2,1)S(1)}, u32[]{:S(2)}, u32[]{:S(2)}) collective-permute-start(bf16[64,1920]{1,0:T(8,128)(2,1)S(1)} %collective-permute-done.4.refs_0_), channel_id=1, source_target_pairs={{0,24},{4,28},{8,16},{12,20},{16,8},{20,12},{24,0},{28,4},{1,25},{... | collective-permute-start | bytes 737288 | tf_op jit(solution)/shard_map/ppermute | solution.py:43
  44.7 8.5 %gate_up.2 = (f32[4,256,512]{2,1,0:T(8,128)S(1)}, f32[4,256,512]{2,1,0:T(8,128)S(1)}, f32[256,128]{1,0:T(8,128)S(1)}, bf16[4,512,1792]{2,1,0:T(8,128)(2,1)S(1)}) custom-call(s32[1]{0:T(128)} %bitcast.me, s32[1]{0:T(128)} %bitcast.1.first, bf16[4,3584,512]{2,1,0:T(8,128)(2,1)S(1)} %get-tuple-element.62.w_gate, ...), custom_call_target="tpu_custom_call" | custom-call | flops 7516192768 | bytes 29360128 | tf_op jit(solution)/shard_map/gate_up/pallas_call | solution.py:351
  53.3 2.4 %collective-permute-done.15.refs_4_ = bf16[64,1920]{1,0:T(8,128)(2,1)S(1)} collective-permute-done((bf16[64,1920]{1,0:T(8,128)(2,1)S(1)}, bf16[64,1920]{1,0:T(8,128)(2,1)S(1)}, u32[]{:S(2)}, u32[]{:S(2)}) %collective-permute-start.15) | collective-permute-done | bytes 245792 | tf_op jit(solution)/shard_map/ppermute | solution.py:43
  56.4 0.9 collective-permute-done.16.refs_5_
  57.9 15.2 %gate_up.3 = (bf16[256,2048]{1,0:T(8,128)(2,1)S(1)}, bf16[4,512,1792]{2,1,0:T(8,128)(2,1)S(1)}) custom-call(s32[1]{0:T(128)} %bitcast.me, s32[1]{0:T(128)} %bitcast.1.first, bf16[4,7168,512]{2,1,0:T(8,128)(2,1)} %w_gate.1, bf16[4,7168,512]{2,1,0:T(8,128)(2,1)} %w_up.1, bf16[4,512,7168]{2,1,0:T(8,128)(2,1)} %refs_0_.3, ...), custom_call_target="tpu_custom_call" | custom-call | flops 7516192768 | bytes 29360128 | tf_op jit(solution)/shard_map/gate_up/pallas_call | solution.py:351
  73.1 4.3 %down.4 = (bf16[128,1792]{1,0:T(8,128)(2,1)S(1)}, bf16[128,1792]{1,0:T(8,128)(2,1)S(1)}, bf16[4,512,1792]{2,1,0:T(8,128)(2,1)S(1)}) custom-call(s32[1]{0:T(128)} %bitcast.me, bf16[256,2048]{1,0:T(8,128)(2,1)S(1)} %get-tuple-element.76.activation, bf16[4,512,1792]{2,1,0:T(8,128)(2,1)S(1)} %get-tuple-element.73.w_down, bf16[4,512,7168]{2,1,0:T(8,128)(2,1)} %refs_0_.3), custom_call_target="tpu_custom_call" | custom-call | flops 1879048192 | bytes 7340032 | tf_op jit(solution)/shard_map/down/pallas_call | solution.py:386
  77.7 4.2 %down.6 = (bf16[128,1792]{1,0:T(8,128)(2,1)S(1)}, bf16[128,1792]{1,0:T(8,128)(2,1)S(1)}, bf16[4,512,1792]{2,1,0:T(8,128)(2,1)S(1)}) custom-call(s32[1]{0:T(128)} %bitcast.me, bf16[256,2048]{1,0:T(8,128)(2,1)S(1)} %get-tuple-element.76.activation, bf16[4,512,1792]{2,1,0:T(8,128)(2,1)S(1)} %get-tuple-element.80.w_down, bf16[4,512,7168]{2,1,0:T(8,128)(2,1)} %refs_0_.3), custom_call_target="tpu_custom_call" | custom-call | flops 1879048192 | bytes 7340032 | tf_op jit(solution)/shard_map/down/pallas_call | solution.py:386
  82.4 1.6 %collective-permute-start.20 = (bf16[64,1792]{1,0:T(8,128)(2,1)S(1)}, bf16[64,1792]{1,0:T(8,128)(2,1)S(1)}, u32[]{:S(2)}, u32[]{:S(2)}) collective-permute-start(bf16[64,1792]{1,0:T(8,128)(2,1)S(1)} %get-tuple-element.104), channel_id=1, source_target_pairs={{0,16},{4,20},{8,24},{12,28},{16,0},{20,4},{24,8},{28,12},{1,17},{... | collective-permute-start | bytes 688136 | tf_op jit(solution)/shard_map/ppermute | solution.py:43
  84.0 2.6 %down.5 = (bf16[128,1792]{1,0:T(8,128)(2,1)S(1)}, bf16[128,1792]{1,0:T(8,128)(2,1)S(1)}) custom-call(s32[1]{0:T(128)} %bitcast.me, bf16[256,2048]{1,0:T(8,128)(2,1)S(1)} %get-tuple-element.76.activation, bf16[4,512,1792]{2,1,0:T(8,128)(2,1)S(1)} %get-tuple-element.77.w_down), custom_call_target="tpu_custom_call" | custom-call | flops 1879048192 | bytes 7340032 | tf_op jit(solution)/shard_map/down/pallas_call | solution.py:386
  86.9 0.8 collective-permute-start.25
  87.7 2.6 %down.7 = (bf16[128,1792]{1,0:T(8,128)(2,1)S(1)}, bf16[128,1792]{1,0:T(8,128)(2,1)S(1)}) custom-call(s32[1]{0:T(128)} %bitcast.me, bf16[256,2048]{1,0:T(8,128)(2,1)S(1)} %get-tuple-element.76.activation, bf16[4,512,1792]{2,1,0:T(8,128)(2,1)S(1)} %get-tuple-element.87.w_down), custom_call_target="tpu_custom_call" | custom-call | flops 1879048192 | bytes 7340032 | tf_op jit(solution)/shard_map/down/pallas_call | solution.py:386
  90.7 1.3 %collective-permute-start.24 = (bf16[64,1792]{1,0:T(8,128)(2,1)S(1)}, bf16[64,1792]{1,0:T(8,128)(2,1)S(1)}, u32[]{:S(2)}, u32[]{:S(2)}) collective-permute-start(bf16[64,1792]{1,0:T(8,128)(2,1)S(1)} %get-tuple-element.100), channel_id=1, source_target_pairs={{0,16},{4,20},{8,24},{12,28},{16,0},{20,4},{24,8},{28,12},{1,17},{... | collective-permute-start | bytes 688136 | tf_op jit(solution)/shard_map/ppermute | solution.py:43
  92.7 1.6 %collective-permute-start.29 = (bf16[64,1792]{1,0:T(8,128)(2,1)S(1)}, bf16[64,1792]{1,0:T(8,128)(2,1)S(1)}, u32[]{:S(2)}, u32[]{:S(2)}) collective-permute-start(bf16[64,1792]{1,0:T(8,128)(2,1)S(1)} %get-tuple-element.101), channel_id=1, source_target_pairs={{0,8},{4,12},{8,0},{12,4},{16,24},{20,28},{24,16},{28,20},{1,9},{5... | collective-permute-start | bytes 688136 | tf_op jit(solution)/shard_map/ppermute | solution.py:43
  94.3 0.8 collective-permute-done.25
  95.5 3.7 %collective-permute-done.24 = bf16[64,1792]{1,0:T(8,128)(2,1)S(1)} collective-permute-done((bf16[64,1792]{1,0:T(8,128)(2,1)S(1)}, bf16[64,1792]{1,0:T(8,128)(2,1)S(1)}, u32[]{:S(2)}, u32[]{:S(2)}) %collective-permute-start.24) | collective-permute-done | bytes 229408 | tf_op jit(solution)/shard_map/ppermute | solution.py:43
  99.2 1.3 %collective-permute-start.31 = (bf16[32,1792]{1,0:T(8,128)(2,1)S(1)}, bf16[32,1792]{1,0:T(8,128)(2,1)S(1)}, u32[]{:S(2)}, u32[]{:S(2)}) collective-permute-start(bf16[32,1792]{1,0:T(8,128)(2,1)S(1)} %add_convert_fusion.16), channel_id=1, source_target_pairs={{0,8},{4,12},{8,0},{12,4},{16,24},{20,28},{24,16},{28,20},{1,9},{5... | collective-permute-start | bytes 344072 | tf_op jit(solution)/shard_map/ppermute | solution.py:43
  100.6 2.8 %collective-permute-start.27 = (bf16[32,1792]{1,0:T(8,128)(2,1)S(1)}, bf16[32,1792]{1,0:T(8,128)(2,1)S(1)}, u32[]{:S(2)}, u32[]{:S(2)}) collective-permute-start(bf16[32,1792]{1,0:T(8,128)(2,1)S(1)} %add_convert_fusion.15), channel_id=1, source_target_pairs={{0,3},{1,2},{2,1},{3,0},{4,7},{5,6},{6,5},{7,4},{8,11},{9,10},{10,... | collective-permute-start | bytes 344072 | tf_op jit(solution)/shard_map/ppermute | solution.py:43
  104.0 2.9 %collective-permute-start.30 = (bf16[32,1792]{1,0:T(8,128)(2,1)S(1)}, bf16[32,1792]{1,0:T(8,128)(2,1)S(1)}, u32[]{:S(2)}, u32[]{:S(2)}) collective-permute-start(bf16[32,1792]{1,0:T(8,128)(2,1)S(1)} %add_convert_fusion.12), channel_id=1, source_target_pairs={{0,2},{1,3},{2,0},{3,1},{4,6},{5,7},{6,4},{7,5},{8,10},{9,11},{10,... | collective-permute-start | bytes 344072 | tf_op jit(solution)/shard_map/ppermute | solution.py:43
  107.4 5.6 %collective-permute-done.30 = bf16[32,1792]{1,0:T(8,128)(2,1)S(1)} collective-permute-done((bf16[32,1792]{1,0:T(8,128)(2,1)S(1)}, bf16[32,1792]{1,0:T(8,128)(2,1)S(1)}, u32[]{:S(2)}, u32[]{:S(2)}) %collective-permute-start.30) | collective-permute-done | bytes 114720 | tf_op jit(solution)/shard_map/ppermute | solution.py:43
  113.4 0.7 add_convert_fusion.8
  (61 shorter events, 9.1 us)
Async XLA Ops:
  1.5 7.9 %collective-permute-start = (bf16[32,1920]{1,0:T(8,128)(2,1)S(1)}, bf16[32,1920]{1,0:T(8,128)(2,1)S(1)}, u32[]{:S(2)}, u32[]{:S(2)}) collective-permute-start(bf16[32,1920]{1,0:T(8,128)(2,1)S(1)} %get-tuple-element.55), channel_id=1, source_target_pairs={{0,1},{1,0},{2,3},{3,2},{4,5},{5,4},{6,7},{7,6},{8,9},{9,8},{10,11... | collective-permute-start | bytes 368648 | tf_op jit(solution)/shard_map/ppermute | solution.py:43
  4.6 12.3 %collective-permute-start.1 = (bf16[32,1920]{1,0:T(8,128)(2,1)S(1)}, bf16[32,1920]{1,0:T(8,128)(2,1)S(1)}, u32[]{:S(2)}, u32[]{:S(2)}) collective-permute-start(bf16[32,1920]{1,0:T(8,128)(2,1)S(1)} %get-tuple-element.56), channel_id=1, source_target_pairs={{0,2},{1,3},{2,0},{3,1},{4,6},{5,7},{6,4},{7,5},{8,10},{9,11},{10,... | collective-permute-start | bytes 368648 | tf_op jit(solution)/shard_map/ppermute | solution.py:43
  7.2 9.7 %collective-permute-start.2 = (bf16[32,1920]{1,0:T(8,128)(2,1)S(1)}, bf16[32,1920]{1,0:T(8,128)(2,1)S(1)}, u32[]{:S(2)}, u32[]{:S(2)}) collective-permute-start(bf16[32,1920]{1,0:T(8,128)(2,1)S(1)} %get-tuple-element.57), channel_id=1, source_target_pairs={{0,3},{1,2},{2,1},{3,0},{4,7},{5,6},{6,5},{7,4},{8,11},{9,10},{10,... | collective-permute-start | bytes 368648 | tf_op jit(solution)/shard_map/ppermute | solution.py:43
  17.2 4.9 %collective-permute-start.3 = (bf16[32,1920]{1,0:T(8,128)(2,1)S(1)}, bf16[32,1920]{1,0:T(8,128)(2,1)S(1)}, u32[]{:S(2)}, u32[]{:S(2)}) collective-permute-start(bf16[32,1920]{1,0:T(8,128)(2,1)S(1)} %get-tuple-element.60.refs_0_), channel_id=1, source_target_pairs={{0,1},{1,0},{2,3},{3,2},{4,5},{5,4},{6,7},{7,6},{8,9},{9,8},{10,11... | collective-permute-start | bytes 368648 | tf_op jit(solution)/shard_map/ppermute | solution.py:43
  22.2 9.0 %collective-permute-start.5 = (bf16[64,1920]{1,0:T(8,128)(2,1)S(1)}, bf16[64,1920]{1,0:T(8,128)(2,1)S(1)}, u32[]{:S(2)}, u32[]{:S(2)}) collective-permute-start(bf16[64,1920]{1,0:T(8,128)(2,1)S(1)} %join.1.refs_0_), channel_id=1, source_target_pairs={{0,24},{4,28},{8,16},{12,20},{16,8},{20,12},{24,0},{28,4},{1,25},{... | collective-permute-start | bytes 737288 | tf_op jit(solution)/shard_map/ppermute | solution.py:43
  24.7 15.9 %collective-permute-start.7 = (bf16[64,1920]{1,0:T(8,128)(2,1)S(1)}, bf16[64,1920]{1,0:T(8,128)(2,1)S(1)}, u32[]{:S(2)}, u32[]{:S(2)}) collective-permute-start(bf16[64,1920]{1,0:T(8,128)(2,1)S(1)} %join.1.refs_0_), channel_id=1, source_target_pairs={{0,8},{4,12},{8,0},{12,4},{16,24},{20,28},{24,16},{28,20},{1,9},{5... | collective-permute-start | bytes 737288 | tf_op jit(solution)/shard_map/ppermute | solution.py:43
  25.2 15.9 %collective-permute-start.9 = (bf16[64,1920]{1,0:T(8,128)(2,1)S(1)}, bf16[64,1920]{1,0:T(8,128)(2,1)S(1)}, u32[]{:S(2)}, u32[]{:S(2)}) collective-permute-start(bf16[64,1920]{1,0:T(8,128)(2,1)S(1)} %join.1.refs_0_), channel_id=1, source_target_pairs={{0,16},{4,20},{8,24},{12,28},{16,0},{20,4},{24,8},{28,12},{1,17},{... | collective-permute-start | bytes 737288 | tf_op jit(solution)/shard_map/ppermute | solution.py:43
  25.7 18.0 %collective-permute-start.6 = (bf16[64,1920]{1,0:T(8,128)(2,1)S(1)}, bf16[64,1920]{1,0:T(8,128)(2,1)S(1)}, u32[]{:S(2)}, u32[]{:S(2)}) collective-permute-start(bf16[64,1920]{1,0:T(8,128)(2,1)S(1)} %join.1.refs_0_), channel_id=1, source_target_pairs={{0,4},{4,0},{8,12},{12,8},{16,20},{20,16},{24,28},{28,24},{1,5},{5... | collective-permute-start | bytes 737288 | tf_op jit(solution)/shard_map/ppermute | solution.py:43
  25.7 15.5 %collective-permute-start.4 = (bf16[64,1920]{1,0:T(8,128)(2,1)S(1)}, bf16[64,1920]{1,0:T(8,128)(2,1)S(1)}, u32[]{:S(2)}, u32[]{:S(2)}) collective-permute-start(bf16[64,1920]{1,0:T(8,128)(2,1)S(1)} %join.1.refs_0_), channel_id=1, source_target_pairs={{0,2},{1,3},{2,0},{3,1},{4,6},{5,7},{6,4},{7,5},{8,10},{9,11},{10,... | collective-permute-start | bytes 737288 | tf_op jit(solution)/shard_map/ppermute | solution.py:43
  40.6 3.6 %collective-permute-start.8 = (bf16[64,1920]{1,0:T(8,128)(2,1)S(1)}, bf16[64,1920]{1,0:T(8,128)(2,1)S(1)}, u32[]{:S(2)}, u32[]{:S(2)}) collective-permute-start(bf16[64,1920]{1,0:T(8,128)(2,1)S(1)} %collective-permute-done.7.refs_2_), channel_id=1, source_target_pairs={{0,4},{4,0},{8,12},{12,8},{16,20},{20,16},{24,28},{28,24},{1,5},{5... | collective-permute-start | bytes 737288 | tf_op jit(solution)/shard_map/ppermute | solution.py:43
  40.7 4.1 %collective-permute-start.11 = (bf16[64,1920]{1,0:T(8,128)(2,1)S(1)}, bf16[64,1920]{1,0:T(8,128)(2,1)S(1)}, u32[]{:S(2)}, u32[]{:S(2)}) collective-permute-start(bf16[64,1920]{1,0:T(8,128)(2,1)S(1)} %collective-permute-done.5.refs_6_), channel_id=1, source_target_pairs={{0,4},{4,0},{8,12},{12,8},{16,20},{20,16},{24,28},{28,24},{1,5},{5... | collective-permute-start | bytes 737288 | tf_op jit(solution)/shard_map/ppermute | solution.py:43
  41.2 3.6 %collective-permute-start.10 = (bf16[64,1920]{1,0:T(8,128)(2,1)S(1)}, bf16[64,1920]{1,0:T(8,128)(2,1)S(1)}, u32[]{:S(2)}, u32[]{:S(2)}) collective-permute-start(bf16[64,1920]{1,0:T(8,128)(2,1)S(1)} %collective-permute-done.9.refs_4_), channel_id=1, source_target_pairs={{0,4},{4,0},{8,12},{12,8},{16,20},{20,16},{24,28},{28,24},{1,5},{5... | collective-permute-start | bytes 737288 | tf_op jit(solution)/shard_map/ppermute | solution.py:43
  41.2 12.0 %collective-permute-start.17 = (bf16[64,1920]{1,0:T(8,128)(2,1)S(1)}, bf16[64,1920]{1,0:T(8,128)(2,1)S(1)}, u32[]{:S(2)}, u32[]{:S(2)}) collective-permute-start(bf16[64,1920]{1,0:T(8,128)(2,1)S(1)} %collective-permute-done.4.refs_0_), channel_id=1, source_target_pairs={{0,24},{4,28},{8,16},{12,20},{16,8},{20,12},{24,0},{28,4},{1,25},{... | collective-permute-start | bytes 737288 | tf_op jit(solution)/shard_map/ppermute | solution.py:43
  43.7 12.0 %collective-permute-start.15 = (bf16[64,1920]{1,0:T(8,128)(2,1)S(1)}, bf16[64,1920]{1,0:T(8,128)(2,1)S(1)}, u32[]{:S(2)}, u32[]{:S(2)}) collective-permute-start(bf16[64,1920]{1,0:T(8,128)(2,1)S(1)} %collective-permute-done.4.refs_0_), channel_id=1, source_target_pairs={{0,16},{4,20},{8,24},{12,28},{16,0},{20,4},{24,8},{28,12},{1,17},{... | collective-permute-start | bytes 737288 | tf_op jit(solution)/shard_map/ppermute | solution.py:43
  44.2 11.7 %collective-permute-start.13 = (bf16[64,1920]{1,0:T(8,128)(2,1)S(1)}, bf16[64,1920]{1,0:T(8,128)(2,1)S(1)}, u32[]{:S(2)}, u32[]{:S(2)}) collective-permute-start(bf16[64,1920]{1,0:T(8,128)(2,1)S(1)} %collective-permute-done.4.refs_0_), channel_id=1, source_target_pairs={{0,8},{4,12},{8,0},{12,4},{16,24},{20,28},{24,16},{28,20},{1,9},{5... | collective-permute-start | bytes 737288 | tf_op jit(solution)/shard_map/ppermute | solution.py:43
  53.2 3.1 %collective-permute-start.18 = (bf16[64,1920]{1,0:T(8,128)(2,1)S(1)}, bf16[64,1920]{1,0:T(8,128)(2,1)S(1)}, u32[]{:S(2)}, u32[]{:S(2)}) collective-permute-start(bf16[64,1920]{1,0:T(8,128)(2,1)S(1)} %collective-permute-done.17.refs_6_), channel_id=1, source_target_pairs={{0,4},{4,0},{8,12},{12,8},{16,20},{20,16},{24,28},{28,24},{1,5},{5... | collective-permute-start | bytes 737288 | tf_op jit(solution)/shard_map/ppermute | solution.py:43
  55.9 1.7 %collective-permute-start.14 = (bf16[64,1920]{1,0:T(8,128)(2,1)S(1)}, bf16[64,1920]{1,0:T(8,128)(2,1)S(1)}, u32[]{:S(2)}, u32[]{:S(2)}) collective-permute-start(bf16[64,1920]{1,0:T(8,128)(2,1)S(1)} %collective-permute-done.13.refs_2_), channel_id=1, source_target_pairs={{0,4},{4,0},{8,12},{12,8},{16,20},{20,16},{24,28},{28,24},{1,5},{5... | collective-permute-start | bytes 737288 | tf_op jit(solution)/shard_map/ppermute | solution.py:43
  77.5 4.8 %collective-permute-start.19 = (bf16[128,1792]{1,0:T(8,128)(2,1)S(1)}, bf16[128,1792]{1,0:T(8,128)(2,1)S(1)}, u32[]{:S(2)}, u32[]{:S(2)}) collective-permute-start(bf16[128,1792]{1,0:T(8,128)(2,1)S(1)} %get-tuple-element.75), channel_id=1, source_target_pairs={{0,4},{4,0},{8,12},{12,8},{16,20},{20,16},{24,28},{28,24},{1,5},{5... | collective-permute-start | bytes 1376264 | tf_op jit(solution)/shard_map/ppermute | solution.py:43
  81.9 4.8 %collective-permute-start.22 = (bf16[128,1792]{1,0:T(8,128)(2,1)S(1)}, bf16[128,1792]{1,0:T(8,128)(2,1)S(1)}, u32[]{:S(2)}, u32[]{:S(2)}) collective-permute-start(bf16[128,1792]{1,0:T(8,128)(2,1)S(1)} %get-tuple-element.82), channel_id=1, source_target_pairs={{0,4},{4,0},{8,12},{12,8},{16,20},{20,16},{24,28},{28,24},{1,5},{5... | collective-permute-start | bytes 1376264 | tf_op jit(solution)/shard_map/ppermute | solution.py:43
  82.4 9.5 %collective-permute-start.20 = (bf16[64,1792]{1,0:T(8,128)(2,1)S(1)}, bf16[64,1792]{1,0:T(8,128)(2,1)S(1)}, u32[]{:S(2)}, u32[]{:S(2)}) collective-permute-start(bf16[64,1792]{1,0:T(8,128)(2,1)S(1)} %get-tuple-element.104), channel_id=1, source_target_pairs={{0,16},{4,20},{8,24},{12,28},{16,0},{20,4},{24,8},{28,12},{1,17},{... | collective-permute-start | bytes 688136 | tf_op jit(solution)/shard_map/ppermute | solution.py:43
  86.7 3.9 %collective-permute-start.21 = (bf16[128,1792]{1,0:T(8,128)(2,1)S(1)}, bf16[128,1792]{1,0:T(8,128)(2,1)S(1)}, u32[]{:S(2)}, u32[]{:S(2)}) collective-permute-start(bf16[128,1792]{1,0:T(8,128)(2,1)S(1)} %get-tuple-element.79), channel_id=1, source_target_pairs={{0,4},{4,0},{8,12},{12,8},{16,20},{20,16},{24,28},{28,24},{1,5},{5... | collective-permute-start | bytes 1376264 | tf_op jit(solution)/shard_map/ppermute | solution.py:43
  86.9 8.2 %collective-permute-start.25 = (bf16[64,1792]{1,0:T(8,128)(2,1)S(1)}, bf16[64,1792]{1,0:T(8,128)(2,1)S(1)}, u32[]{:S(2)}, u32[]{:S(2)}) collective-permute-start(bf16[64,1792]{1,0:T(8,128)(2,1)S(1)} %get-tuple-element.98), channel_id=1, source_target_pairs={{0,8},{4,12},{8,0},{12,4},{16,24},{20,28},{24,16},{28,20},{1,9},{5... | collective-permute-start | bytes 688136 | tf_op jit(solution)/shard_map/ppermute | solution.py:43
  90.3 2.3 %collective-permute-start.26 = (bf16[128,1792]{1,0:T(8,128)(2,1)S(1)}, bf16[128,1792]{1,0:T(8,128)(2,1)S(1)}, u32[]{:S(2)}, u32[]{:S(2)}) collective-permute-start(bf16[128,1792]{1,0:T(8,128)(2,1)S(1)} %get-tuple-element.89), channel_id=1, source_target_pairs={{0,4},{4,0},{8,12},{12,8},{16,20},{20,16},{24,28},{28,24},{1,5},{5... | collective-permute-start | bytes 1376264 | tf_op jit(solution)/shard_map/ppermute | solution.py:43
  90.7 8.5 %collective-permute-start.24 = (bf16[64,1792]{1,0:T(8,128)(2,1)S(1)}, bf16[64,1792]{1,0:T(8,128)(2,1)S(1)}, u32[]{:S(2)}, u32[]{:S(2)}) collective-permute-start(bf16[64,1792]{1,0:T(8,128)(2,1)S(1)} %get-tuple-element.100), channel_id=1, source_target_pairs={{0,16},{4,20},{8,24},{12,28},{16,0},{20,4},{24,8},{28,12},{1,17},{... | collective-permute-start | bytes 688136 | tf_op jit(solution)/shard_map/ppermute | solution.py:43
  92.0 8.6 %collective-permute-start.23 = (bf16[32,1792]{1,0:T(8,128)(2,1)S(1)}, bf16[32,1792]{1,0:T(8,128)(2,1)S(1)}, u32[]{:S(2)}, u32[]{:S(2)}) collective-permute-start(bf16[32,1792]{1,0:T(8,128)(2,1)S(1)} %add_convert_fusion.18), channel_id=1, source_target_pairs={{0,8},{4,12},{8,0},{12,4},{16,24},{20,28},{24,16},{28,20},{1,9},{5... | collective-permute-start | bytes 344072 | tf_op jit(solution)/shard_map/ppermute | solution.py:43
  92.7 10.7 %collective-permute-start.29 = (bf16[64,1792]{1,0:T(8,128)(2,1)S(1)}, bf16[64,1792]{1,0:T(8,128)(2,1)S(1)}, u32[]{:S(2)}, u32[]{:S(2)}) collective-permute-start(bf16[64,1792]{1,0:T(8,128)(2,1)S(1)} %get-tuple-element.101), channel_id=1, source_target_pairs={{0,8},{4,12},{8,0},{12,4},{16,24},{20,28},{24,16},{28,20},{1,9},{5... | collective-permute-start | bytes 688136 | tf_op jit(solution)/shard_map/ppermute | solution.py:43
  95.1 8.8 %collective-permute-start.28 = (bf16[32,1792]{1,0:T(8,128)(2,1)S(1)}, bf16[32,1792]{1,0:T(8,128)(2,1)S(1)}, u32[]{:S(2)}, u32[]{:S(2)}) collective-permute-start(bf16[32,1792]{1,0:T(8,128)(2,1)S(1)} %add_convert_fusion.17), channel_id=1, source_target_pairs={{0,16},{4,20},{8,24},{12,28},{16,0},{20,4},{24,8},{28,12},{1,17},{... | collective-permute-start | bytes 344072 | tf_op jit(solution)/shard_map/ppermute | solution.py:43
  99.2 7.7 %collective-permute-start.31 = (bf16[32,1792]{1,0:T(8,128)(2,1)S(1)}, bf16[32,1792]{1,0:T(8,128)(2,1)S(1)}, u32[]{:S(2)}, u32[]{:S(2)}) collective-permute-start(bf16[32,1792]{1,0:T(8,128)(2,1)S(1)} %add_convert_fusion.16), channel_id=1, source_target_pairs={{0,8},{4,12},{8,0},{12,4},{16,24},{20,28},{24,16},{28,20},{1,9},{5... | collective-permute-start | bytes 344072 | tf_op jit(solution)/shard_map/ppermute | solution.py:43
  100.6 12.5 %collective-permute-start.27 = (bf16[32,1792]{1,0:T(8,128)(2,1)S(1)}, bf16[32,1792]{1,0:T(8,128)(2,1)S(1)}, u32[]{:S(2)}, u32[]{:S(2)}) collective-permute-start(bf16[32,1792]{1,0:T(8,128)(2,1)S(1)} %add_convert_fusion.15), channel_id=1, source_target_pairs={{0,3},{1,2},{2,1},{3,0},{4,7},{5,6},{6,5},{7,4},{8,11},{9,10},{10,... | collective-permute-start | bytes 344072 | tf_op jit(solution)/shard_map/ppermute | solution.py:43
  103.4 9.6 %collective-permute-start.33 = (bf16[32,1792]{1,0:T(8,128)(2,1)S(1)}, bf16[32,1792]{1,0:T(8,128)(2,1)S(1)}, u32[]{:S(2)}, u32[]{:S(2)}) collective-permute-start(bf16[32,1792]{1,0:T(8,128)(2,1)S(1)} %add_convert_fusion.13), channel_id=1, source_target_pairs={{0,16},{4,20},{8,24},{12,28},{16,0},{20,4},{24,8},{28,12},{1,17},{... | collective-permute-start | bytes 344072 | tf_op jit(solution)/shard_map/ppermute | solution.py:43
  104.0 9.0 %collective-permute-start.30 = (bf16[32,1792]{1,0:T(8,128)(2,1)S(1)}, bf16[32,1792]{1,0:T(8,128)(2,1)S(1)}, u32[]{:S(2)}, u32[]{:S(2)}) collective-permute-start(bf16[32,1792]{1,0:T(8,128)(2,1)S(1)} %add_convert_fusion.12), channel_id=1, source_target_pairs={{0,2},{1,3},{2,0},{3,1},{4,6},{5,7},{6,4},{7,5},{8,10},{9,11},{10,... | collective-permute-start | bytes 344072 | tf_op jit(solution)/shard_map/ppermute | solution.py:43
  107.0 6.4 %collective-permute-start.32 = (bf16[32,1792]{1,0:T(8,128)(2,1)S(1)}, bf16[32,1792]{1,0:T(8,128)(2,1)S(1)}, u32[]{:S(2)}, u32[]{:S(2)}) collective-permute-start(bf16[32,1792]{1,0:T(8,128)(2,1)S(1)} %add_convert_fusion.10), channel_id=1, source_target_pairs={{0,1},{1,0},{2,3},{3,2},{4,5},{5,4},{6,7},{7,6},{8,9},{9,8},{10,11... | collective-permute-start | bytes 344072 | tf_op jit(solution)/shard_map/ppermute | solution.py:43
  (2 other events, 3.2 us)

commit v5 on v4

--- a/solution.py
+++ b/solution.py
@@ -111,43 +111,56 @@
     message[:, width:] = tail.astype(BF16)
 
 
-def load_kernel(me, gate_hbm, up_hbm, gate, up, sems):
-    depth = gate.shape[1]
-    here = pl.ds(pl.multiple_of((me[0] >> 1) * depth, LANES), depth)
-    copies = [
-        pltpu.make_async_copy(source.at[:, here, :], target, sems.at[i])
-        for i, (source, target) in enumerate(((gate_hbm, gate), (up_hbm, up)))
-    ]
+def copies_of(source, target, sems, block, axis, experts):
+    size = target.shape[1 + axis]
+    there = pl.ds(pl.multiple_of(block * size, LANES), size)
+    place = (there, slice(None)) if axis == 0 else (slice(None), there)
+    return [pltpu.make_async_copy(source.at[(e, *place)], target.at[e], sems.at[e]) for e in experts]
+
+
+def load_kernel(me, hbm, held, sems):
+    copies = copies_of(hbm, held, sems, me[0] >> 1, 0, range(held.shape[0]))
     for copy in copies:
         copy.start()
     for copy in copies:
         copy.wait()
 
 
-def up_kernel(start, last, chunks, ahead, full, experts, me, first, w_gate, w_up, down_hbm, *refs):
-    *refs, sem = refs
-    x = refs[-1 - last]
-    held_down = refs[-2 - last]
+def up_kernel(start, last, held, late, refill, chunks, ahead, full, experts, me, first, gate_hbm, up_hbm, down_hbm, *refs):
+    refs = list(refs)
+    sems = refs.pop()
+    side_scratch = refs.pop() if last else None
+    x = refs.pop()
+    held_down = refs.pop()
+    if held:
+        w_up, w_gate = refs.pop(), refs.pop()
     if last:
-        out, side = refs[-4], refs[-1]
-        pieces, (gate_in, up_in, side_in) = refs[:-7], refs[-7:-4]
+        out, side = refs.pop(), side_scratch
     else:
-        gate_acc, up_acc, side = refs[-5:-2]
-        pieces = refs[:-5] if start else refs[:-8]
+        side, up_acc, gate_acc = refs.pop(), refs.pop(), refs.pop()
+    if not start:
+        side_in, up_in, gate_in = refs.pop(), refs.pop(), refs.pop()
+    if held:
+        refs = refs[2:]
+    else:
+        w_gate, w_up, *refs = refs
+    pieces = refs
     expert = pl.program_id(0)
-    columns = held_down.shape[2]
-    block = me[0] ^ ahead
-    copy = pltpu.make_async_copy(
-        down_hbm.at[:, :, pl.ds(pl.multiple_of(block * columns, LANES), columns)], held_down, sem
-    )
+    count = down_hbm.shape[0]
     width = x.shape[1] // chunks
-
-    @pl.when(expert == (0 if start or down_hbm.shape[0] == 1 else 1))
-    def _():
-        copy.start()
+    down = copies_of(down_hbm, held_down, sems.at[0], me[0] ^ ahead, 1, range(count))
+
+    def rows_of(flip, some):
+        block = (me[0] ^ flip) // chunks
+        return copies_of(gate_hbm, w_gate, sems.at[1], block, 0, some) + copies_of(up_hbm, w_up, sems.at[2], block, 0, some)
 
     @pl.when(expert == 0)
     def _():
+        if late:
+            for copy in rows_of(chunks, [count - 1]):
+                copy.start()
+        for copy in down:
+            copy.start()
         height = pieces[0].shape[0] // chunks
         for i, piece in enumerate(pieces):
             there = slice(i * height, (i + 1) * height)
@@ -162,8 +175,24 @@
                     tail = before[there, :] + jnp.where(lane >= experts, tail, 0.0)
                 side[there, :] = tail
 
-    gate = jnp.dot(x[...], w_gate[expert if start else 0], preferred_element_type=F32)
-    up = jnp.dot(x[...], w_up[expert if start else 0], preferred_element_type=F32)
+    if late:
+
+        @pl.when(expert == count - 1)
+        def _():
+            for copy in rows_of(chunks, [count - 1]):
+                copy.wait()
+
+    if refill:
+        for e in range(count - 1):
+
+            @pl.when(expert == e + 1)
+            def _():
+                for copy in rows_of(chunks, [e]):
+                    copy.start()
+
+    here = expert if held else 0
+    gate = jnp.dot(x[...], w_gate[here], preferred_element_type=F32)
+    up = jnp.dot(x[...], w_up[here], preferred_element_type=F32)
     if start:
         gate_acc[expert] = gate
         up_acc[expert] = up
@@ -180,23 +209,23 @@
         up = (up_in[expert] + up) * inverse
         out[...] = (jax.nn.silu(gate) * up * weight).astype(BF16)
 
-    @pl.when(expert == pl.num_programs(0) - 1)
+    @pl.when(expert == count - 1)
     def _():
-        copy.wait()
+        for copy in down + (rows_of(chunks, range(count - 1)) if refill else []):
+            copy.wait()
 
 
 def down_kernel(order, ahead, me, activation, w_down, *refs):
     if ahead is None:
         keep, send = refs
     else:
-        down_hbm, keep, send, held_down, sem = refs
-        columns = held_down.shape[2]
-        there = pl.ds(pl.multiple_of((me[0] ^ ahead) * columns, LANES), columns)
-        copy = pltpu.make_async_copy(down_hbm.at[:, :, there], held_down, sem)
+        down_hbm, keep, send, held_down, sems = refs
+        copies = copies_of(down_hbm, held_down, sems, me[0] ^ ahead, 1, range(held_down.shape[0]))
 
         @pl.when(pl.program_id(0) == 0)
         def _():
-            copy.start()
+            for copy in copies:
+                copy.start()
 
     width = keep.shape[1]
     here = pl.ds(pl.multiple_of(pl.program_id(0) * width, LANES), width)
@@ -212,7 +241,8 @@
 
         @pl.when(pl.program_id(0) == pl.num_programs(0) - 1)
         def _():
-            copy.wait()
+            for copy in copies:
+                copy.wait()
 
 
 def join_kernel(*refs):
@@ -290,6 +320,21 @@
     )(me, off_chip(attn_part[0]), off_chip(resid), off_chip(refusal))
     parts = [swap(value, "tp", k + 1) for k, value in enumerate(slices)]
 
+    def load(source, at):
+        return pl.pallas_call(
+            load_kernel,
+            out_shape=pltpu.VMEM((local_experts, 2 * cols, hidden), BF16),
+            in_specs=[smem(), pl.BlockSpec(memory_space=pltpu.HBM)],
+            out_specs=vmem(),
+            scratch_shapes=[pltpu.SemaphoreType.DMA((local_experts,))],
+            compiler_params=params(8),
+            cost_estimate=pl.CostEstimate(flops=0, bytes_accessed=4 * cols * hidden * local_experts, transcendentals=0),
+            name="load_rows",
+        )(at, off_chip(source))
+
+    held_gate = load(w_gate, after(me, share))
+    base = after(base, held_gate)
+
     message, projected = pl.pallas_call(
         functools.partial(project_kernel, experts),
         out_shape=[shape(rows, cols + tail), shape(rows, cols, dtype=F32)],
@@ -304,24 +349,16 @@
     while bit < tp_count:
         groups.append(swap(groups[0] if bit == 2 else join(*groups), "tp", bit))
         bit *= 2
+    sizes = [group.shape[0] // rows for group in groups]
+    starts = [0] + sizes[1:]
 
     plane = cross_plane(groups[0], exp_count)
-    held_gate, held_up = pl.pallas_call(
-        load_kernel,
-        out_shape=[pltpu.VMEM((local_experts, 2 * cols, hidden), BF16)] * 2,
-        in_specs=[smem()] + [pl.BlockSpec(memory_space=pltpu.HBM)] * 2,
-        out_specs=[vmem()] * 2,
-        scratch_shapes=[pltpu.SemaphoreType.DMA((2,))],
-        compiler_params=params(8),
-        cost_estimate=pl.CostEstimate(flops=0, bytes_accessed=8 * cols * hidden * local_experts, transcendentals=0),
-        name="load_weights",
-    )(after(me, plane[exp_count - 2]), off_chip(w_gate), off_chip(w_up))
-    plane[2] = after(plane[2], held_gate)
+    held_up = load(w_up, after(me, groups[0]))
+    groups[1:] = [after(group, held_up) for group in groups[1:]]
+    plane = {pattern: after(piece, groups[-1]) if pattern else piece for pattern, piece in plane.items()}
 
     state, held_down = [], {}
     places = list(reversed(range(tp_count)))
-    sizes = [group.shape[0] // rows for group in groups]
-    starts = [0] + sizes[1:]
     for i, group in enumerate(groups):
         if i:
             plane = cross_plane(group, exp_count)
@@ -332,52 +369,68 @@
         start, last = i == 0, i == len(groups) - 1
         down_shape = pltpu.VMEM((local_experts, hidden, cols), BF16)
         acc = pltpu.VMEM((local_experts, total_rows, hidden), F32)
+        held = i == 0 or chunks == sizes[i - 1]
+        late = held and i > 0
+        refill = held and not late and not last and sizes[i + 1] == chunks
         if last:
-            out_shape = [shape(total_rows, local_experts * hidden), down_shape]
-            out_specs = [pl.BlockSpec((total_rows, hidden), lambda e, *_: (0, e)), vmem()]
+            out_shape = [shape(total_rows, local_experts * hidden)]
+            out_specs = [pl.BlockSpec((total_rows, hidden), lambda e, *_: (0, e))]
         else:
-            out_shape = [acc, acc, pltpu.VMEM((total_rows, tail), F32), down_shape]
-            out_specs = [vmem()] * 4
-        weights = [on_chip(held_gate), on_chip(held_up)] if i == 0 else [off_chip(w_gate), off_chip(w_up)]
-        specs = [
-            pl.BlockSpec(
-                (1, chunks * cols, hidden),
-                lambda e, me, first, flip=flip, chunks=chunks: (e, (me[0] ^ flip) // chunks, 0),
-            )
-        ] * 2
-        if i == 0:
-            specs = [vmem()] * 2
-        scratch = [pltpu.VMEM((total_rows, chunks * cols), BF16)]
-        *state, held_down[ahead] = pl.pallas_call(
-            functools.partial(up_kernel, start, last, chunks, ahead, full, experts),
-            out_shape=out_shape,
+            out_shape = [acc, acc, pltpu.VMEM((total_rows, tail), F32)]
+            out_specs = [vmem()] * 3
+        weights = [on_chip(held_gate), on_chip(held_up)] if held else [w_gate, w_up]
+        specs = [vmem()] * 2
+        if not held:
+            specs = [
+                pl.BlockSpec(
+                    (1, chunks * cols, hidden),
+                    lambda e, me, first, flip=flip, chunks=chunks: (e, (me[0] ^ flip) // chunks, 0),
+                )
+            ] * 2
+        aliases = {} if start or last else {7 + len(pieces) + j: j for j in range(3)}
+        if held:
+            aliases.update({5: len(out_shape), 6: len(out_shape) + 1})
+            out_shape += [pltpu.VMEM((local_experts, chunks * cols, hidden), BF16)] * 2
+            out_specs += [vmem()] * 2
+        found = pl.pallas_call(
+            functools.partial(up_kernel, start, last, held, late, refill, chunks, ahead, full, experts),
+            out_shape=out_shape + [down_shape],
             grid_spec=pltpu.PrefetchScalarGridSpec(
                 num_scalar_prefetch=2,
                 grid=(local_experts,),
-                in_specs=specs + [pl.BlockSpec(memory_space=pltpu.HBM)] + [vmem()] * (len(pieces) + len(state)),
-                out_specs=out_specs,
-                scratch_shapes=scratch
+                in_specs=[pl.BlockSpec(memory_space=pltpu.HBM)] * 3 + specs + [vmem()] * (len(pieces) + len(state)),
+                out_specs=out_specs + [vmem()],
+                scratch_shapes=[pltpu.VMEM((total_rows, chunks * cols), BF16)]
                 + ([pltpu.VMEM((total_rows, tail), F32)] if last else [])
-                + [pltpu.SemaphoreType.DMA(())],
+                + [pltpu.SemaphoreType.DMA((3, local_experts))],
             ),
-            input_output_aliases={} if start or last else {5 + len(pieces) + j: j for j in range(3)},
-            compiler_params=params(6 if start else 22),
+            input_output_aliases=aliases,
+            compiler_params=params(6 if held else 22),
             cost_estimate=pl.CostEstimate(
                 flops=4 * total_rows * chunks * cols * hidden * local_experts,
                 bytes_accessed=4 * chunks * cols * hidden * local_experts,
                 transcendentals=0,
             ),
             name="gate_up",
-        )(me, first, *weights, off_chip(w_down), *pieces, *[on_chip(v) for v in state])
+        )(
+            *(me, first, off_chip(w_gate), off_chip(w_up), off_chip(w_down)),
+            *weights,
+            *pieces,
+            *[on_chip(v) for v in state],
+        )
+        held_down[ahead] = found[-1]
+        if held:
+            held_gate, held_up = found[-3:-1]
+        state = found[: 1 if last else 3]
     activation = state[0]
 
     steps = 2 if cols % (2 * LANES) == 0 else 1
     width = cols // steps
     stages = len(orders[0]) + 1
-    events = [(float(j), 0, j, None) for j in range(tp_count)]
-    events += [(j + 1.5 + 2 * stage, stage, j, stage) for j in range(tp_count) for stage in range(stages)]
+    events = [(float(j), j, None) for j in range(tp_count)]
+    events += [(j + 1.5 + 2 * stage, j, stage) for j in range(tp_count) for stage in range(stages)]
     mine, theirs, opened, done = {}, {}, [], []
-    for _, _, j, stage in sorted(events, key=lambda event: event[:3]):
+    for _, j, stage in sorted(events, key=lambda event: event[:2]):
         k = places[j]
         order = orders[k % 2]
         if stage is None:
@@ -391,7 +444,7 @@
                     grid=(steps,),
                     in_specs=[vmem()] * 2 + [pl.BlockSpec(memory_space=pltpu.HBM)] * len(held),
                     out_specs=[pl.BlockSpec((total_rows // 2, width), lambda i, me: (0, i))] * 2 + [vmem()] * len(held),
-                    scratch_shapes=[pltpu.SemaphoreType.DMA(())] * len(held),
+                    scratch_shapes=[pltpu.SemaphoreType.DMA((local_experts,))] * len(held),
                 ),
                 compiler_params=params(8),
                 cost_estimate=pl.CostEstimate(

time: 114 us -> 102 us (0.89)
  waiting for transfers between devices: 27.6 us -> 20.7 us
  Pallas kernels: 48.6 us -> 45.1 us
  starting transfers between devices: 34 us -> 31.9 us
    ppermute x34, waiting for transfers between devices: 27.6 us -> 20.7 us  [swap(): return lax.ppermute(value, axis, [(i, i ^ bit) for i in range(count)])]
    pallas_call x3 -> x4, Pallas kernels: 33.1 us -> 29.4 us  [the longest x2 18.8 us: local(): pl.pallas_call(functools.partial(up_kernel, start, last, held, late, refi...]
    ppermute x34, starting transfers between devices: 34 us -> 31.9 us  [swap(): return lax.ppermute(value, axis, [(i, i ^ bit) for i in range(count)])]
  transfers between devices with their start and end apart: 34 -> 34, of which waited for: 12 -> 16; matrix products, arithmetic and copies ran while one was open for 3% -> 3% of each run, Pallas kernels for 24% -> 30%
where the time goes in v5:
time: 102 us
  Pallas kernels  45.1 us (44%)
  starting transfers between devices  31.9 us (31%)
  waiting for transfers between devices  20.7 us (20%)
  local copies, waits for them, and re-layouts  2.22 us (2%)
  other arithmetic  1.47 us (1%)
    ppermute x34, starting transfers between devices, swap(): return lax.ppermute(value, axis, [(i, i ^ bit) for i in range(count)])  31.9 us
    ppermute x34, waiting for transfers between devices, swap(): return lax.ppermute(value, axis, [(i, i ^ bit) for i in range(count)])  20.7 us
    pallas_call x2, Pallas kernels, local(): pl.pallas_call(functools.partial(up_kernel, start, last, held, late, refi...  18.8 us
    pallas_call x4, Pallas kernels, local(): pl.pallas_call(functools.partial(down_kernel, relative_order([core] + ord...  13.9 us
    pallas_call x2, Pallas kernels, load(): pl.pallas_call(load_kernel, out_shape=pltpu.VMEM((local_experts, 2 * cols...  10.6 us
  transfers between devices with their start and end apart: 34, of which 16 were waited for; matrix products, arithmetic and copies ran while one was open for 3% of the time, Pallas kernels for 30%

profile of v5, /device:TPU:0, one launch (start us, length us, event | category | flops | bytes accessed | tf_op | source)
XLA Modules:
  0.0 101.6 jit_solution(4405408763762337283)
XLA Ops:
  0.0 1.5 %cut_heads.1 = (bf16[32,1920]{1,0:T(8,128)(2,1)S(1)}, bf16[32,1920]{1,0:T(8,128)(2,1)S(1)}, bf16[32,1920]{1,0:T(8,128)(2,1)S(1)}, f32[32,1792]{1,0:T(8,128)S(1)}...) custom-call(s32[1]{0:T(128)} %bitcast.me, bf16[32,7168]{1,0:T(8,128)(2,1)} %bitcast.4, bf16[32,1792]{1,0:T(8,128)(2,1)} %resid_hbm.1, ...), custom_call_target="tpu_custom_call" | custom-call | tf_op jit(solution)/shard_map/cut_heads/pallas_call | solution.py:306
  1.5 3.1 %collective-permute-start = (bf16[32,1920]{1,0:T(8,128)(2,1)S(1)}, bf16[32,1920]{1,0:T(8,128)(2,1)S(1)}, u32[]{:S(2)}, u32[]{:S(2)}) collective-permute-start(bf16[32,1920]{1,0:T(8,128)(2,1)S(1)} %get-tuple-element.62), channel_id=1, source_target_pairs={{0,1},{1,0},{2,3},{3,2},{4,5},{5,4},{6,7},{7,6},{8,9},{9,8},{10,11... | collective-permute-start | bytes 368648 | tf_op jit(solution)/shard_map/ppermute | solution.py:43
  4.6 2.6 %collective-permute-start.1 = (bf16[32,1920]{1,0:T(8,128)(2,1)S(1)}, bf16[32,1920]{1,0:T(8,128)(2,1)S(1)}, u32[]{:S(2)}, u32[]{:S(2)}) collective-permute-start(bf16[32,1920]{1,0:T(8,128)(2,1)S(1)} %get-tuple-element.63), channel_id=1, source_target_pairs={{0,2},{1,3},{2,0},{3,1},{4,6},{5,7},{6,4},{7,5},{8,10},{9,11},{10,... | collective-permute-start | bytes 368648 | tf_op jit(solution)/shard_map/ppermute | solution.py:43
  9.4 5.3 %load_rows.2.refs_0_ = bf16[4,3584,512]{2,1,0:T(8,128)(2,1)S(1)} custom-call(s32[1]{0:T(128)} %bitcast.me, bf16[4,7168,512]{2,1,0:T(8,128)(2,1)} %gate_hbm.3), custom_call_target="tpu_custom_call" | custom-call | bytes 14680064 | tf_op jit(solution)/shard_map/load_rows/pallas_call | solution.py:324
  14.7 2.2 %collective-permute-done.1.refs_1_ = bf16[32,1920]{1,0:T(8,128)(2,1)S(1)} collective-permute-done((bf16[32,1920]{1,0:T(8,128)(2,1)S(1)}, bf16[32,1920]{1,0:T(8,128)(2,1)S(1)}, u32[]{:S(2)}, u32[]{:S(2)}) %collective-permute-start.1) | collective-permute-done | bytes 122912 | tf_op jit(solution)/shard_map/ppermute | solution.py:43
  17.2 1.9 %collective-permute-start.3 = (bf16[32,1920]{1,0:T(8,128)(2,1)S(1)}, bf16[32,1920]{1,0:T(8,128)(2,1)S(1)}, u32[]{:S(2)}, u32[]{:S(2)}) collective-permute-start(bf16[32,1920]{1,0:T(8,128)(2,1)S(1)} %get-tuple-element.67.refs_0_), channel_id=1, source_target_pairs={{0,1},{1,0},{2,3},{3,2},{4,5},{5,4},{6,7},{7,6},{8,9},{9,8},{10,11... | collective-permute-start | bytes 368648 | tf_op jit(solution)/shard_map/ppermute | solution.py:43
  19.1 3.0 %collective-permute-done.3.refs_1_ = bf16[32,1920]{1,0:T(8,128)(2,1)S(1)} collective-permute-done((bf16[32,1920]{1,0:T(8,128)(2,1)S(1)}, bf16[32,1920]{1,0:T(8,128)(2,1)S(1)}, u32[]{:S(2)}, u32[]{:S(2)}) %collective-permute-start.3) | collective-permute-done | bytes 122912 | tf_op jit(solution)/shard_map/ppermute | solution.py:43
  22.2 3.1 %collective-permute-start.6 = (bf16[64,1920]{1,0:T(8,128)(2,1)S(1)}, bf16[64,1920]{1,0:T(8,128)(2,1)S(1)}, u32[]{:S(2)}, u32[]{:S(2)}) collective-permute-start(bf16[64,1920]{1,0:T(8,128)(2,1)S(1)} %join.1.refs_2_), channel_id=1, source_target_pairs={{0,2},{1,3},{2,0},{3,1},{4,6},{5,7},{6,4},{7,5},{8,10},{9,11},{10,... | collective-permute-start | bytes 737288 | tf_op jit(solution)/shard_map/ppermute | solution.py:43
  25.2 2.4 %collective-permute-start.10 = (bf16[64,1920]{1,0:T(8,128)(2,1)S(1)}, bf16[64,1920]{1,0:T(8,128)(2,1)S(1)}, u32[]{:S(2)}, u32[]{:S(2)}) collective-permute-start(bf16[64,1920]{1,0:T(8,128)(2,1)S(1)} %join.1.refs_2_), channel_id=1, source_target_pairs={{0,24},{4,28},{8,16},{12,20},{16,8},{20,12},{24,0},{28,4},{1,25},{... | collective-permute-start | bytes 737288 | tf_op jit(solution)/shard_map/ppermute | solution.py:43
  28.7 5.3 %load_rows.3.refs_1_ = bf16[4,3584,512]{2,1,0:T(8,128)(2,1)S(1)} custom-call(s32[1]{0:T(128)} %bitcast.me, bf16[4,7168,512]{2,1,0:T(8,128)(2,1)} %up_hbm.3), custom_call_target="tpu_custom_call" | custom-call | bytes 14680064 | tf_op jit(solution)/shard_map/load_rows/pallas_call | solution.py:324
  34.2 2.4 %collective-permute-done.8.refs_6_ = bf16[64,1920]{1,0:T(8,128)(2,1)S(1)} collective-permute-done((bf16[64,1920]{1,0:T(8,128)(2,1)S(1)}, bf16[64,1920]{1,0:T(8,128)(2,1)S(1)}, u32[]{:S(2)}, u32[]{:S(2)}) %collective-permute-start.8) | collective-permute-done | bytes 245792 | tf_op jit(solution)/shard_map/ppermute | solution.py:43
  37.3 1.6 %collective-permute-start.17 = (bf16[64,1920]{1,0:T(8,128)(2,1)S(1)}, bf16[64,1920]{1,0:T(8,128)(2,1)S(1)}, u32[]{:S(2)}, u32[]{:S(2)}) collective-permute-start(bf16[64,1920]{1,0:T(8,128)(2,1)S(1)} %collective-permute-done.6.refs_2_), channel_id=1, source_target_pairs={{0,24},{4,28},{8,16},{12,20},{16,8},{20,12},{24,0},{28,4},{1,25},{... | collective-permute-start | bytes 737288 | tf_op jit(solution)/shard_map/ppermute | solution.py:43
  38.9 1.3 %collective-permute-start.15 = (bf16[64,1920]{1,0:T(8,128)(2,1)S(1)}, bf16[64,1920]{1,0:T(8,128)(2,1)S(1)}, u32[]{:S(2)}, u32[]{:S(2)}) collective-permute-start(bf16[64,1920]{1,0:T(8,128)(2,1)S(1)} %collective-permute-done.6.refs_2_), channel_id=1, source_target_pairs={{0,16},{4,20},{8,24},{12,28},{16,0},{20,4},{24,8},{28,12},{1,17},{... | collective-permute-start | bytes 737288 | tf_op jit(solution)/shard_map/ppermute | solution.py:43
  40.8 9.9 %gate_up.2 = (f32[4,256,512]{2,1,0:T(8,128)S(1)}, f32[4,256,512]{2,1,0:T(8,128)S(1)}, f32[256,128]{1,0:T(8,128)S(1)}, bf16[4,3584,512]{2,1,0:T(8,128)(2,1)S(1)},...) custom-call(s32[1]{0:T(128)} %bitcast.me, ...), custom_call_target="tpu_custom_call", output_to_operand_aliasing={{3}: (5, {}), {4}: (6, {})} | custom-call | flops 7516192768 | bytes 29360128 | tf_op jit(solution)/shard_map/gate_up/pallas_call | solution.py:395
  50.7 1.1 %collective-permute-done.15.refs_6_ = bf16[64,1920]{1,0:T(8,128)(2,1)S(1)} collective-permute-done((bf16[64,1920]{1,0:T(8,128)(2,1)S(1)}, bf16[64,1920]{1,0:T(8,128)(2,1)S(1)}, u32[]{:S(2)}, u32[]{:S(2)}) %collective-permute-start.15) | collective-permute-done | bytes 245792 | tf_op jit(solution)/shard_map/ppermute | solution.py:43
  54.4 8.9 %gate_up.3 = (bf16[256,2048]{1,0:T(8,128)(2,1)S(1)}, bf16[4,3584,512]{2,1,0:T(8,128)(2,1)S(1)}, bf16[4,3584,512]{2,1,0:T(8,128)(2,1)S(1)}, bf16[4,512,1792]{2,1,0:T(8,128)(2,1)S(1)}) custom-call(s32[1]{0:T(128)} %bitcast.me, s32[1]{0:T(128)} %bitcast.1.first, bf16[4,7168,512]{2,1,0:T(8,128)(2,1)} %gate_hbm.3, ...), custom_call_target="tpu_custom_call", output_to_operand_aliasing={{1}: (5, {}), {2}: (6, {})} | custom-call | flops 7516192768 | bytes 29360128 | tf_op jit(solution)/shard_map/gate_up/pallas_call | solution.py:395
  63.3 4.4 %down.4 = (bf16[128,1792]{1,0:T(8,128)(2,1)S(1)}, bf16[128,1792]{1,0:T(8,128)(2,1)S(1)}, bf16[4,512,1792]{2,1,0:T(8,128)(2,1)S(1)}) custom-call(s32[1]{0:T(128)} %bitcast.me, bf16[256,2048]{1,0:T(8,128)(2,1)S(1)} %get-tuple-element.95.activation, bf16[4,512,1792]{2,1,0:T(8,128)(2,1)S(1)} %get-tuple-element.83.w_down, bf16[4,512,7168]{2,1,0:T(8,128)(2,1)} %refs_0_.3), custom_call_target="tpu_custom_call" | custom-call | flops 1879048192 | bytes 7340032 | tf_op jit(solution)/shard_map/down/pallas_call | solution.py:439
  67.9 4.3 %down.5 = (bf16[128,1792]{1,0:T(8,128)(2,1)S(1)}, bf16[128,1792]{1,0:T(8,128)(2,1)S(1)}, bf16[4,512,1792]{2,1,0:T(8,128)(2,1)S(1)}) custom-call(s32[1]{0:T(128)} %bitcast.me, bf16[256,2048]{1,0:T(8,128)(2,1)S(1)} %get-tuple-element.95.activation, bf16[4,512,1792]{2,1,0:T(8,128)(2,1)S(1)} %get-tuple-element.86.w_down, bf16[4,512,7168]{2,1,0:T(8,128)(2,1)} %refs_0_.3), custom_call_target="tpu_custom_call" | custom-call | flops 1879048192 | bytes 7340032 | tf_op jit(solution)/shard_map/down/pallas_call | solution.py:439
  72.7 1.4 %collective-permute-start.20 = (bf16[64,1792]{1,0:T(8,128)(2,1)S(1)}, bf16[64,1792]{1,0:T(8,128)(2,1)S(1)}, u32[]{:S(2)}, u32[]{:S(2)}) collective-permute-start(bf16[64,1792]{1,0:T(8,128)(2,1)S(1)} %get-tuple-element.112), channel_id=1, source_target_pairs={{0,16},{4,20},{8,24},{12,28},{16,0},{20,4},{24,8},{28,12},{1,17},{... | collective-permute-start | bytes 688136 | tf_op jit(solution)/shard_map/ppermute | solution.py:43
  74.3 1.4 %collective-permute-start.24 = (bf16[64,1792]{1,0:T(8,128)(2,1)S(1)}, bf16[64,1792]{1,0:T(8,128)(2,1)S(1)}, u32[]{:S(2)}, u32[]{:S(2)}) collective-permute-start(bf16[64,1792]{1,0:T(8,128)(2,1)S(1)} %get-tuple-element.114), channel_id=1, source_target_pairs={{0,8},{4,12},{8,0},{12,4},{16,24},{20,28},{24,16},{28,20},{1,9},{5... | collective-permute-start | bytes 688136 | tf_op jit(solution)/shard_map/ppermute | solution.py:43
  75.8 2.6 %down.7 = (bf16[128,1792]{1,0:T(8,128)(2,1)S(1)}, bf16[128,1792]{1,0:T(8,128)(2,1)S(1)}) custom-call(s32[1]{0:T(128)} %bitcast.me, bf16[256,2048]{1,0:T(8,128)(2,1)S(1)} %get-tuple-element.95.activation, bf16[4,512,1792]{2,1,0:T(8,128)(2,1)S(1)} %get-tuple-element.96.w_down), custom_call_target="tpu_custom_call" | custom-call | flops 1879048192 | bytes 7340032 | tf_op jit(solution)/shard_map/down/pallas_call | solution.py:439
  78.5 2.6 %down.6 = (bf16[128,1792]{1,0:T(8,128)(2,1)S(1)}, bf16[128,1792]{1,0:T(8,128)(2,1)S(1)}) custom-call(s32[1]{0:T(128)} %bitcast.me, bf16[256,2048]{1,0:T(8,128)(2,1)S(1)} %get-tuple-element.95.activation, bf16[4,512,1792]{2,1,0:T(8,128)(2,1)S(1)} %get-tuple-element.92.w_down), custom_call_target="tpu_custom_call" | custom-call | flops 1879048192 | bytes 7340032 | tf_op jit(solution)/shard_map/down/pallas_call | solution.py:439
  82.5 1.3 %collective-permute-start.28 = (bf16[64,1792]{1,0:T(8,128)(2,1)S(1)}, bf16[64,1792]{1,0:T(8,128)(2,1)S(1)}, u32[]{:S(2)}, u32[]{:S(2)}) collective-permute-start(bf16[64,1792]{1,0:T(8,128)(2,1)S(1)} %get-tuple-element.108), channel_id=1, source_target_pairs={{0,16},{4,20},{8,24},{12,28},{16,0},{20,4},{24,8},{28,12},{1,17},{... | collective-permute-start | bytes 688136 | tf_op jit(solution)/shard_map/ppermute | solution.py:43
  84.8 1.5 %collective-permute-start.31 = (bf16[64,1792]{1,0:T(8,128)(2,1)S(1)}, bf16[64,1792]{1,0:T(8,128)(2,1)S(1)}, u32[]{:S(2)}, u32[]{:S(2)}) collective-permute-start(bf16[64,1792]{1,0:T(8,128)(2,1)S(1)} %get-tuple-element.109), channel_id=1, source_target_pairs={{0,8},{4,12},{8,0},{12,4},{16,24},{20,28},{24,16},{28,20},{1,9},{5... | collective-permute-start | bytes 688136 | tf_op jit(solution)/shard_map/ppermute | solution.py:43
  87.1 1.0 collective-permute-start.26
  88.0 3.1 %collective-permute-done.28 = bf16[64,1792]{1,0:T(8,128)(2,1)S(1)} collective-permute-done((bf16[64,1792]{1,0:T(8,128)(2,1)S(1)}, bf16[64,1792]{1,0:T(8,128)(2,1)S(1)}, u32[]{:S(2)}, u32[]{:S(2)}) %collective-permute-start.28) | collective-permute-done | bytes 229408 | tf_op jit(solution)/shard_map/ppermute | solution.py:43
  91.1 1.5 %collective-permute-start.30 = (bf16[32,1792]{1,0:T(8,128)(2,1)S(1)}, bf16[32,1792]{1,0:T(8,128)(2,1)S(1)}, u32[]{:S(2)}, u32[]{:S(2)}) collective-permute-start(bf16[32,1792]{1,0:T(8,128)(2,1)S(1)} %add_convert_fusion.14), channel_id=1, source_target_pairs={{0,8},{4,12},{8,0},{12,4},{16,24},{20,28},{24,16},{28,20},{1,9},{5... | collective-permute-start | bytes 344072 | tf_op jit(solution)/shard_map/ppermute | solution.py:43
  93.0 1.2 %collective-permute-start.33 = (bf16[32,1792]{1,0:T(8,128)(2,1)S(1)}, bf16[32,1792]{1,0:T(8,128)(2,1)S(1)}, u32[]{:S(2)}, u32[]{:S(2)}) collective-permute-start(bf16[32,1792]{1,0:T(8,128)(2,1)S(1)} %add_convert_fusion.11), channel_id=1, source_target_pairs={{0,16},{4,20},{8,24},{12,28},{16,0},{20,4},{24,8},{28,12},{1,17},{... | collective-permute-start | bytes 344072 | tf_op jit(solution)/shard_map/ppermute | solution.py:43
  94.2 1.8 %collective-permute-done.30 = bf16[32,1792]{1,0:T(8,128)(2,1)S(1)} collective-permute-done((bf16[32,1792]{1,0:T(8,128)(2,1)S(1)}, bf16[32,1792]{1,0:T(8,128)(2,1)S(1)}, u32[]{:S(2)}, u32[]{:S(2)}) %collective-permute-start.30) | collective-permute-done | bytes 114720 | tf_op jit(solution)/shard_map/ppermute | solution.py:43
  96.4 1.5 %collective-permute-done.33 = bf16[32,1792]{1,0:T(8,128)(2,1)S(1)} collective-permute-done((bf16[32,1792]{1,0:T(8,128)(2,1)S(1)}, bf16[32,1792]{1,0:T(8,128)(2,1)S(1)}, u32[]{:S(2)}, u32[]{:S(2)}) %collective-permute-start.33) | collective-permute-done | bytes 114720 | tf_op jit(solution)/shard_map/ppermute | solution.py:43
  97.9 1.6 %collective-permute-done.29 = bf16[32,1792]{1,0:T(8,128)(2,1)S(1)} collective-permute-done((bf16[32,1792]{1,0:T(8,128)(2,1)S(1)}, bf16[32,1792]{1,0:T(8,128)(2,1)S(1)}, u32[]{:S(2)}, u32[]{:S(2)}) %collective-permute-start.29) | collective-permute-done | bytes 114720 | tf_op jit(solution)/shard_map/ppermute | solution.py:43
  99.4 1.5 %collective-permute-done.32 = bf16[32,1792]{1,0:T(8,128)(2,1)S(1)} collective-permute-done((bf16[32,1792]{1,0:T(8,128)(2,1)S(1)}, bf16[32,1792]{1,0:T(8,128)(2,1)S(1)}, u32[]{:S(2)}, u32[]{:S(2)}) %collective-permute-start.32) | collective-permute-done | bytes 114720 | tf_op jit(solution)/shard_map/ppermute | solution.py:43
  (62 shorter events, 13.3 us)
Async XLA Ops:
  1.5 13.2 %collective-permute-start = (bf16[32,1920]{1,0:T(8,128)(2,1)S(1)}, bf16[32,1920]{1,0:T(8,128)(2,1)S(1)}, u32[]{:S(2)}, u32[]{:S(2)}) collective-permute-start(bf16[32,1920]{1,0:T(8,128)(2,1)S(1)} %get-tuple-element.62), channel_id=1, source_target_pairs={{0,1},{1,0},{2,3},{3,2},{4,5},{5,4},{6,7},{7,6},{8,9},{9,8},{10,11... | collective-permute-start | bytes 368648 | tf_op jit(solution)/shard_map/ppermute | solution.py:43
  4.6 12.3 %collective-permute-start.1 = (bf16[32,1920]{1,0:T(8,128)(2,1)S(1)}, bf16[32,1920]{1,0:T(8,128)(2,1)S(1)}, u32[]{:S(2)}, u32[]{:S(2)}) collective-permute-start(bf16[32,1920]{1,0:T(8,128)(2,1)S(1)} %get-tuple-element.63), channel_id=1, source_target_pairs={{0,2},{1,3},{2,0},{3,1},{4,6},{5,7},{6,4},{7,5},{8,10},{9,11},{10,... | collective-permute-start | bytes 368648 | tf_op jit(solution)/shard_map/ppermute | solution.py:43
  7.2 9.7 %collective-permute-start.2 = (bf16[32,1920]{1,0:T(8,128)(2,1)S(1)}, bf16[32,1920]{1,0:T(8,128)(2,1)S(1)}, u32[]{:S(2)}, u32[]{:S(2)}) collective-permute-start(bf16[32,1920]{1,0:T(8,128)(2,1)S(1)} %get-tuple-element.64), channel_id=1, source_target_pairs={{0,3},{1,2},{2,1},{3,0},{4,7},{5,6},{6,5},{7,4},{8,11},{9,10},{10,... | collective-permute-start | bytes 368648 | tf_op jit(solution)/shard_map/ppermute | solution.py:43
  17.2 4.9 %collective-permute-start.3 = (bf16[32,1920]{1,0:T(8,128)(2,1)S(1)}, bf16[32,1920]{1,0:T(8,128)(2,1)S(1)}, u32[]{:S(2)}, u32[]{:S(2)}) collective-permute-start(bf16[32,1920]{1,0:T(8,128)(2,1)S(1)} %get-tuple-element.67.refs_0_), channel_id=1, source_target_pairs={{0,1},{1,0},{2,3},{3,2},{4,5},{5,4},{6,7},{7,6},{8,9},{9,8},{10,11... | collective-permute-start | bytes 368648 | tf_op jit(solution)/shard_map/ppermute | solution.py:43
  22.2 12.1 %collective-permute-start.6 = (bf16[64,1920]{1,0:T(8,128)(2,1)S(1)}, bf16[64,1920]{1,0:T(8,128)(2,1)S(1)}, u32[]{:S(2)}, u32[]{:S(2)}) collective-permute-start(bf16[64,1920]{1,0:T(8,128)(2,1)S(1)} %join.1.refs_2_), channel_id=1, source_target_pairs={{0,2},{1,3},{2,0},{3,1},{4,6},{5,7},{6,4},{7,5},{8,10},{9,11},{10,... | collective-permute-start | bytes 737288 | tf_op jit(solution)/shard_map/ppermute | solution.py:43
  25.2 9.0 %collective-permute-start.10 = (bf16[64,1920]{1,0:T(8,128)(2,1)S(1)}, bf16[64,1920]{1,0:T(8,128)(2,1)S(1)}, u32[]{:S(2)}, u32[]{:S(2)}) collective-permute-start(bf16[64,1920]{1,0:T(8,128)(2,1)S(1)} %join.1.refs_2_), channel_id=1, source_target_pairs={{0,24},{4,28},{8,16},{12,20},{16,8},{20,12},{24,0},{28,4},{1,25},{... | collective-permute-start | bytes 737288 | tf_op jit(solution)/shard_map/ppermute | solution.py:43
  27.7 8.9 %collective-permute-start.8 = (bf16[64,1920]{1,0:T(8,128)(2,1)S(1)}, bf16[64,1920]{1,0:T(8,128)(2,1)S(1)}, u32[]{:S(2)}, u32[]{:S(2)}) collective-permute-start(bf16[64,1920]{1,0:T(8,128)(2,1)S(1)} %join.1.refs_2_), channel_id=1, source_target_pairs={{0,16},{4,20},{8,24},{12,28},{16,0},{20,4},{24,8},{28,12},{1,17},{... | collective-permute-start | bytes 737288 | tf_op jit(solution)/shard_map/ppermute | solution.py:43
  28.2 8.6 %collective-permute-start.5 = (bf16[64,1920]{1,0:T(8,128)(2,1)S(1)}, bf16[64,1920]{1,0:T(8,128)(2,1)S(1)}, u32[]{:S(2)}, u32[]{:S(2)}) collective-permute-start(bf16[64,1920]{1,0:T(8,128)(2,1)S(1)} %join.1.refs_2_), channel_id=1, source_target_pairs={{0,8},{4,12},{8,0},{12,4},{16,24},{20,28},{24,16},{28,20},{1,9},{5... | collective-permute-start | bytes 737288 | tf_op jit(solution)/shard_map/ppermute | solution.py:43
  28.7 10.1 %collective-permute-start.4 = (bf16[64,1920]{1,0:T(8,128)(2,1)S(1)}, bf16[64,1920]{1,0:T(8,128)(2,1)S(1)}, u32[]{:S(2)}, u32[]{:S(2)}) collective-permute-start(bf16[64,1920]{1,0:T(8,128)(2,1)S(1)} %join.1.refs_2_), channel_id=1, source_target_pairs={{0,4},{4,0},{8,12},{12,8},{16,20},{20,16},{24,28},{28,24},{1,5},{5... | collective-permute-start | bytes 737288 | tf_op jit(solution)/shard_map/ppermute | solution.py:43
  36.7 3.5 %collective-permute-start.7 = (bf16[64,1920]{1,0:T(8,128)(2,1)S(1)}, bf16[64,1920]{1,0:T(8,128)(2,1)S(1)}, u32[]{:S(2)}, u32[]{:S(2)}) collective-permute-start(bf16[64,1920]{1,0:T(8,128)(2,1)S(1)} %collective-permute-done.5.refs_4_), channel_id=1, source_target_pairs={{0,4},{4,0},{8,12},{12,8},{16,20},{20,16},{24,28},{28,24},{1,5},{5... | collective-permute-start | bytes 737288 | tf_op jit(solution)/shard_map/ppermute | solution.py:43
  36.8 4.0 %collective-permute-start.9 = (bf16[64,1920]{1,0:T(8,128)(2,1)S(1)}, bf16[64,1920]{1,0:T(8,128)(2,1)S(1)}, u32[]{:S(2)}, u32[]{:S(2)}) collective-permute-start(bf16[64,1920]{1,0:T(8,128)(2,1)S(1)} %collective-permute-done.8.refs_6_), channel_id=1, source_target_pairs={{0,4},{4,0},{8,12},{12,8},{16,20},{20,16},{24,28},{28,24},{1,5},{5... | collective-permute-start | bytes 737288 | tf_op jit(solution)/shard_map/ppermute | solution.py:43
  37.3 3.5 %collective-permute-start.11 = (bf16[64,1920]{1,0:T(8,128)(2,1)S(1)}, bf16[64,1920]{1,0:T(8,128)(2,1)S(1)}, u32[]{:S(2)}, u32[]{:S(2)}) collective-permute-start(bf16[64,1920]{1,0:T(8,128)(2,1)S(1)} %collective-permute-done.10.refs_8_), channel_id=1, source_target_pairs={{0,4},{4,0},{8,12},{12,8},{16,20},{20,16},{24,28},{28,24},{1,5},{5... | collective-permute-start | bytes 737288 | tf_op jit(solution)/shard_map/ppermute | solution.py:43
  37.3 13.4 %collective-permute-start.17 = (bf16[64,1920]{1,0:T(8,128)(2,1)S(1)}, bf16[64,1920]{1,0:T(8,128)(2,1)S(1)}, u32[]{:S(2)}, u32[]{:S(2)}) collective-permute-start(bf16[64,1920]{1,0:T(8,128)(2,1)S(1)} %collective-permute-done.6.refs_2_), channel_id=1, source_target_pairs={{0,24},{4,28},{8,16},{12,20},{16,8},{20,12},{24,0},{28,4},{1,25},{... | collective-permute-start | bytes 737288 | tf_op jit(solution)/shard_map/ppermute | solution.py:43
  38.9 12.9 %collective-permute-start.15 = (bf16[64,1920]{1,0:T(8,128)(2,1)S(1)}, bf16[64,1920]{1,0:T(8,128)(2,1)S(1)}, u32[]{:S(2)}, u32[]{:S(2)}) collective-permute-start(bf16[64,1920]{1,0:T(8,128)(2,1)S(1)} %collective-permute-done.6.refs_2_), channel_id=1, source_target_pairs={{0,16},{4,20},{8,24},{12,28},{16,0},{20,4},{24,8},{28,12},{1,17},{... | collective-permute-start | bytes 737288 | tf_op jit(solution)/shard_map/ppermute | solution.py:43
  40.2 11.6 %collective-permute-start.13 = (bf16[64,1920]{1,0:T(8,128)(2,1)S(1)}, bf16[64,1920]{1,0:T(8,128)(2,1)S(1)}, u32[]{:S(2)}, u32[]{:S(2)}) collective-permute-start(bf16[64,1920]{1,0:T(8,128)(2,1)S(1)} %collective-permute-done.6.refs_2_), channel_id=1, source_target_pairs={{0,8},{4,12},{8,0},{12,4},{16,24},{20,28},{24,16},{28,20},{1,9},{5... | collective-permute-start | bytes 737288 | tf_op jit(solution)/shard_map/ppermute | solution.py:43
  51.8 1.8 %collective-permute-start.14 = (bf16[64,1920]{1,0:T(8,128)(2,1)S(1)}, bf16[64,1920]{1,0:T(8,128)(2,1)S(1)}, u32[]{:S(2)}, u32[]{:S(2)}) collective-permute-start(bf16[64,1920]{1,0:T(8,128)(2,1)S(1)} %collective-permute-done.13.refs_4_), channel_id=1, source_target_pairs={{0,4},{4,0},{8,12},{12,8},{16,20},{20,16},{24,28},{28,24},{1,5},{5... | collective-permute-start | bytes 737288 | tf_op jit(solution)/shard_map/ppermute | solution.py:43
  52.4 2.0 %collective-permute-start.18 = (bf16[64,1920]{1,0:T(8,128)(2,1)S(1)}, bf16[64,1920]{1,0:T(8,128)(2,1)S(1)}, u32[]{:S(2)}, u32[]{:S(2)}) collective-permute-start(bf16[64,1920]{1,0:T(8,128)(2,1)S(1)} %collective-permute-done.17.refs_8_), channel_id=1, source_target_pairs={{0,4},{4,0},{8,12},{12,8},{16,20},{20,16},{24,28},{28,24},{1,5},{5... | collective-permute-start | bytes 737288 | tf_op jit(solution)/shard_map/ppermute | solution.py:43
  67.7 4.9 %collective-permute-start.19 = (bf16[128,1792]{1,0:T(8,128)(2,1)S(1)}, bf16[128,1792]{1,0:T(8,128)(2,1)S(1)}, u32[]{:S(2)}, u32[]{:S(2)}) collective-permute-start(bf16[128,1792]{1,0:T(8,128)(2,1)S(1)} %get-tuple-element.85), channel_id=1, source_target_pairs={{0,4},{4,0},{8,12},{12,8},{16,20},{20,16},{24,28},{28,24},{1,5},{5... | collective-permute-start | bytes 1376264 | tf_op jit(solution)/shard_map/ppermute | solution.py:43
  72.2 2.0 %collective-permute-start.21 = (bf16[128,1792]{1,0:T(8,128)(2,1)S(1)}, bf16[128,1792]{1,0:T(8,128)(2,1)S(1)}, u32[]{:S(2)}, u32[]{:S(2)}) collective-permute-start(bf16[128,1792]{1,0:T(8,128)(2,1)S(1)} %get-tuple-element.88), channel_id=1, source_target_pairs={{0,4},{4,0},{8,12},{12,8},{16,20},{20,16},{24,28},{28,24},{1,5},{5... | collective-permute-start | bytes 1376264 | tf_op jit(solution)/shard_map/ppermute | solution.py:43
  72.7 8.9 %collective-permute-start.20 = (bf16[64,1792]{1,0:T(8,128)(2,1)S(1)}, bf16[64,1792]{1,0:T(8,128)(2,1)S(1)}, u32[]{:S(2)}, u32[]{:S(2)}) collective-permute-start(bf16[64,1792]{1,0:T(8,128)(2,1)S(1)} %get-tuple-element.112), channel_id=1, source_target_pairs={{0,16},{4,20},{8,24},{12,28},{16,0},{20,4},{24,8},{28,12},{1,17},{... | collective-permute-start | bytes 688136 | tf_op jit(solution)/shard_map/ppermute | solution.py:43
  74.3 9.5 %collective-permute-start.24 = (bf16[64,1792]{1,0:T(8,128)(2,1)S(1)}, bf16[64,1792]{1,0:T(8,128)(2,1)S(1)}, u32[]{:S(2)}, u32[]{:S(2)}) collective-permute-start(bf16[64,1792]{1,0:T(8,128)(2,1)S(1)} %get-tuple-element.114), channel_id=1, source_target_pairs={{0,8},{4,12},{8,0},{12,4},{16,24},{20,28},{24,16},{28,20},{1,9},{5... | collective-permute-start | bytes 688136 | tf_op jit(solution)/shard_map/ppermute | solution.py:43
  78.4 4.0 %collective-permute-start.25 = (bf16[128,1792]{1,0:T(8,128)(2,1)S(1)}, bf16[128,1792]{1,0:T(8,128)(2,1)S(1)}, u32[]{:S(2)}, u32[]{:S(2)}) collective-permute-start(bf16[128,1792]{1,0:T(8,128)(2,1)S(1)} %get-tuple-element.98), channel_id=1, source_target_pairs={{0,4},{4,0},{8,12},{12,8},{16,20},{20,16},{24,28},{28,24},{1,5},{5... | collective-permute-start | bytes 1376264 | tf_op jit(solution)/shard_map/ppermute | solution.py:43
  81.1 3.6 %collective-permute-start.23 = (bf16[128,1792]{1,0:T(8,128)(2,1)S(1)}, bf16[128,1792]{1,0:T(8,128)(2,1)S(1)}, u32[]{:S(2)}, u32[]{:S(2)}) collective-permute-start(bf16[128,1792]{1,0:T(8,128)(2,1)S(1)} %get-tuple-element.94), channel_id=1, source_target_pairs={{0,4},{4,0},{8,12},{12,8},{16,20},{20,16},{24,28},{28,24},{1,5},{5... | collective-permute-start | bytes 1376264 | tf_op jit(solution)/shard_map/ppermute | solution.py:43
  81.7 5.3 %collective-permute-start.22 = (bf16[32,1792]{1,0:T(8,128)(2,1)S(1)}, bf16[32,1792]{1,0:T(8,128)(2,1)S(1)}, u32[]{:S(2)}, u32[]{:S(2)}) collective-permute-start(bf16[32,1792]{1,0:T(8,128)(2,1)S(1)} %add_convert_fusion.18), channel_id=1, source_target_pairs={{0,8},{4,12},{8,0},{12,4},{16,24},{20,28},{24,16},{28,20},{1,9},{5... | collective-permute-start | bytes 344072 | tf_op jit(solution)/shard_map/ppermute | solution.py:43
  82.5 8.6 %collective-permute-start.28 = (bf16[64,1792]{1,0:T(8,128)(2,1)S(1)}, bf16[64,1792]{1,0:T(8,128)(2,1)S(1)}, u32[]{:S(2)}, u32[]{:S(2)}) collective-permute-start(bf16[64,1792]{1,0:T(8,128)(2,1)S(1)} %get-tuple-element.108), channel_id=1, source_target_pairs={{0,16},{4,20},{8,24},{12,28},{16,0},{20,4},{24,8},{28,12},{1,17},{... | collective-permute-start | bytes 688136 | tf_op jit(solution)/shard_map/ppermute | solution.py:43
  83.9 8.7 %collective-permute-start.27 = (bf16[32,1792]{1,0:T(8,128)(2,1)S(1)}, bf16[32,1792]{1,0:T(8,128)(2,1)S(1)}, u32[]{:S(2)}, u32[]{:S(2)}) collective-permute-start(bf16[32,1792]{1,0:T(8,128)(2,1)S(1)} %add_convert_fusion.17), channel_id=1, source_target_pairs={{0,16},{4,20},{8,24},{12,28},{16,0},{20,4},{24,8},{28,12},{1,17},{... | collective-permute-start | bytes 344072 | tf_op jit(solution)/shard_map/ppermute | solution.py:43
  84.8 8.1 %collective-permute-start.31 = (bf16[64,1792]{1,0:T(8,128)(2,1)S(1)}, bf16[64,1792]{1,0:T(8,128)(2,1)S(1)}, u32[]{:S(2)}, u32[]{:S(2)}) collective-permute-start(bf16[64,1792]{1,0:T(8,128)(2,1)S(1)} %get-tuple-element.109), channel_id=1, source_target_pairs={{0,8},{4,12},{8,0},{12,4},{16,24},{20,28},{24,16},{28,20},{1,9},{5... | collective-permute-start | bytes 688136 | tf_op jit(solution)/shard_map/ppermute | solution.py:43
  87.1 9.3 %collective-permute-start.26 = (bf16[32,1792]{1,0:T(8,128)(2,1)S(1)}, bf16[32,1792]{1,0:T(8,128)(2,1)S(1)}, u32[]{:S(2)}, u32[]{:S(2)}) collective-permute-start(bf16[32,1792]{1,0:T(8,128)(2,1)S(1)} %add_convert_fusion.16), channel_id=1, source_target_pairs={{0,3},{1,2},{2,1},{3,0},{4,7},{5,6},{6,5},{7,4},{8,11},{9,10},{10,... | collective-permute-start | bytes 344072 | tf_op jit(solution)/shard_map/ppermute | solution.py:43
  91.1 4.9 %collective-permute-start.30 = (bf16[32,1792]{1,0:T(8,128)(2,1)S(1)}, bf16[32,1792]{1,0:T(8,128)(2,1)S(1)}, u32[]{:S(2)}, u32[]{:S(2)}) collective-permute-start(bf16[32,1792]{1,0:T(8,128)(2,1)S(1)} %add_convert_fusion.14), channel_id=1, source_target_pairs={{0,8},{4,12},{8,0},{12,4},{16,24},{20,28},{24,16},{28,20},{1,9},{5... | collective-permute-start | bytes 344072 | tf_op jit(solution)/shard_map/ppermute | solution.py:43
  92.6 6.8 %collective-permute-start.29 = (bf16[32,1792]{1,0:T(8,128)(2,1)S(1)}, bf16[32,1792]{1,0:T(8,128)(2,1)S(1)}, u32[]{:S(2)}, u32[]{:S(2)}) collective-permute-start(bf16[32,1792]{1,0:T(8,128)(2,1)S(1)} %add_convert_fusion.13), channel_id=1, source_target_pairs={{0,2},{1,3},{2,0},{3,1},{4,6},{5,7},{6,4},{7,5},{8,10},{9,11},{10,... | collective-permute-start | bytes 344072 | tf_op jit(solution)/shard_map/ppermute | solution.py:43
  93.0 4.9 %collective-permute-start.33 = (bf16[32,1792]{1,0:T(8,128)(2,1)S(1)}, bf16[32,1792]{1,0:T(8,128)(2,1)S(1)}, u32[]{:S(2)}, u32[]{:S(2)}) collective-permute-start(bf16[32,1792]{1,0:T(8,128)(2,1)S(1)} %add_convert_fusion.11), channel_id=1, source_target_pairs={{0,16},{4,20},{8,24},{12,28},{16,0},{20,4},{24,8},{28,12},{1,17},{... | collective-permute-start | bytes 344072 | tf_op jit(solution)/shard_map/ppermute | solution.py:43
  96.0 4.9 %collective-permute-start.32 = (bf16[32,1792]{1,0:T(8,128)(2,1)S(1)}, bf16[32,1792]{1,0:T(8,128)(2,1)S(1)}, u32[]{:S(2)}, u32[]{:S(2)}) collective-permute-start(bf16[32,1792]{1,0:T(8,128)(2,1)S(1)} %add_convert_fusion.10), channel_id=1, source_target_pairs={{0,1},{1,0},{2,3},{3,2},{4,5},{5,4},{6,7},{7,6},{8,9},{9,8},{10,11... | collective-permute-start | bytes 344072 | tf_op jit(solution)/shard_map/ppermute | solution.py:43
  (2 other events, 3.2 us)

commit v6 on v5

--- a/solution.py
+++ b/solution.py
@@ -131,7 +131,7 @@
     sems = refs.pop()
     side_scratch = refs.pop() if last else None
     x = refs.pop()
-    held_down = refs.pop()
+    held_down = [refs.pop() for _ in ahead][::-1]
     if held:
         w_up, w_gate = refs.pop(), refs.pop()
     if last:
@@ -148,11 +148,13 @@
     expert = pl.program_id(0)
     count = down_hbm.shape[0]
     width = x.shape[1] // chunks
-    down = copies_of(down_hbm, held_down, sems.at[0], me[0] ^ ahead, 1, range(count))
+    down = []
+    for i, (place, target) in enumerate(zip(ahead, held_down)):
+        down += copies_of(down_hbm, target, sems.at[2 + i], me[0] ^ place, 1, range(count))
 
     def rows_of(flip, some):
         block = (me[0] ^ flip) // chunks
-        return copies_of(gate_hbm, w_gate, sems.at[1], block, 0, some) + copies_of(up_hbm, w_up, sems.at[2], block, 0, some)
+        return copies_of(gate_hbm, w_gate, sems.at[0], block, 0, some) + copies_of(up_hbm, w_up, sems.at[1], block, 0, some)
 
     @pl.when(expert == 0)
     def _():
@@ -365,7 +367,7 @@
             plane = {pattern: after(piece, state[-1]) for pattern, piece in plane.items()}
         pieces = cross_core(plane)
         chunks, flip = sizes[i], starts[i]
-        ahead = places[i]
+        ahead = places[i : i + 1]
         start, last = i == 0, i == len(groups) - 1
         down_shape = pltpu.VMEM((local_experts, hidden, cols), BF16)
         acc = pltpu.VMEM((local_experts, total_rows, hidden), F32)
@@ -394,15 +396,15 @@
             out_specs += [vmem()] * 2
         found = pl.pallas_call(
             functools.partial(up_kernel, start, last, held, late, refill, chunks, ahead, full, experts),
-            out_shape=out_shape + [down_shape],
+            out_shape=out_shape + [down_shape] * len(ahead),
             grid_spec=pltpu.PrefetchScalarGridSpec(
                 num_scalar_prefetch=2,
                 grid=(local_experts,),
                 in_specs=[pl.BlockSpec(memory_space=pltpu.HBM)] * 3 + specs + [vmem()] * (len(pieces) + len(state)),
-                out_specs=out_specs + [vmem()],
+                out_specs=out_specs + [vmem()] * len(ahead),
                 scratch_shapes=[pltpu.VMEM((total_rows, chunks * cols), BF16)]
                 + ([pltpu.VMEM((total_rows, tail), F32)] if last else [])
-                + [pltpu.SemaphoreType.DMA((3, local_experts))],
+                + [pltpu.SemaphoreType.DMA((2 + len(ahead), local_experts))],
             ),
             input_output_aliases=aliases,
             compiler_params=params(6 if held else 22),
@@ -418,23 +420,34 @@
             *pieces,
             *[on_chip(v) for v in state],
         )
-        held_down[ahead] = found[-1]
+        held_down.update(zip(ahead, found[-len(ahead) :]))
         if held:
-            held_gate, held_up = found[-3:-1]
+            held_gate, held_up = found[len(out_shape) - 2 : len(out_shape)]
         state = found[: 1 if last else 3]
     activation = state[0]
 
     steps = 2 if cols % (2 * LANES) == 0 else 1
     width = cols // steps
     stages = len(orders[0]) + 1
-    events = [(float(j), j, None) for j in range(tp_count)]
-    events += [(j + 1.5 + 2 * stage, j, stage) for j in range(tp_count) for stage in range(stages)]
+    pairs = [(low, low + 1) for low in range(0, tp_count, 2)]
+    events, open_stage = [], {}
+    for n, pair in enumerate(pairs):
+        events += [(j, None) for j in pair]
+        for before in pairs[:n]:
+            open_stage[before] += 1
+            events += [(j, open_stage[before]) for j in before if open_stage[before] < stages]
+        events += [(j, 0) for j in pair]
+        open_stage[pair] = 0
+    for _ in range(stages):
+        for pair in pairs:
+            open_stage[pair] += 1
+            events += [(j, open_stage[pair]) for j in pair if open_stage[pair] < stages]
     mine, theirs, opened, done = {}, {}, [], []
-    for _, j, stage in sorted(events, key=lambda event: event[:2]):
+    for j, stage in events:
         k = places[j]
         order = orders[k % 2]
         if stage is None:
-            ahead = places[j + len(groups)] if j + len(groups) < tp_count else None
+            ahead = next((p for p in places[: j + 3 - j % 2] if p not in held_down), None)
             held = [] if ahead is None else [pltpu.VMEM((local_experts, hidden, cols), BF16)]
             keep, send, *found = pl.pallas_call(
                 functools.partial(down_kernel, relative_order([core] + order), ahead),

time: 102 us -> 104 us (1.020)
  waiting for transfers between devices: 20.7 us -> 24.2 us
    ppermute x34, waiting for transfers between devices: 20.7 us -> 24.2 us  [swap(): return lax.ppermute(value, axis, [(i, i ^ bit) for i in range(count)])]
    ppermute x34, starting transfers between devices: 31.9 us -> 30.9 us  [swap(): return lax.ppermute(value, axis, [(i, i ^ bit) for i in range(count)])]
  transfers between devices with their start and end apart: 34 -> 34, of which waited for: 16 -> 17; matrix products, arithmetic and copies ran while one was open for 3% -> 3% of each run, Pallas kernels for 30% -> 29%
where the time goes in v6:
time: 104 us
  Pallas kernels  45.1 us (43%)
  starting transfers between devices  30.9 us (30%)
  waiting for transfers between devices  24.2 us (23%)
  local copies, waits for them, and re-layouts  2.22 us (2%)
  other arithmetic  1.48 us (1%)
    ppermute x34, starting transfers between devices, swap(): return lax.ppermute(value, axis, [(i, i ^ bit) for i in range(count)])  30.9 us
    ppermute x34, waiting for transfers between devices, swap(): return lax.ppermute(value, axis, [(i, i ^ bit) for i in range(count)])  24.2 us
    pallas_call x2, Pallas kernels, local(): pl.pallas_call(functools.partial(up_kernel, start, last, held, late, refi...  18.8 us
    pallas_call x4, Pallas kernels, local(): pl.pallas_call(functools.partial(down_kernel, relative_order([core] + ord...  13.9 us
    pallas_call x2, Pallas kernels, load(): pl.pallas_call(load_kernel, out_shape=pltpu.VMEM((local_experts, 2 * cols...  10.6 us
  transfers between devices with their start and end apart: 34, of which 17 were waited for; matrix products, arithmetic and copies ran while one was open for 3% of the time, Pallas kernels for 29%

profile of v6, /device:TPU:0, one launch (start us, length us, event | category | flops | bytes accessed | tf_op | source)
XLA Modules:
  0.0 104.0 jit_solution(6072601041564364939)
XLA Ops:
  0.0 1.5 %cut_heads.1 = (bf16[32,1920]{1,0:T(8,128)(2,1)S(1)}, bf16[32,1920]{1,0:T(8,128)(2,1)S(1)}, bf16[32,1920]{1,0:T(8,128)(2,1)S(1)}, f32[32,1792]{1,0:T(8,128)S(1)}...) custom-call(s32[1]{0:T(128)} %bitcast.me, bf16[32,7168]{1,0:T(8,128)(2,1)} %bitcast.4, bf16[32,1792]{1,0:T(8,128)(2,1)} %resid_hbm.1, ...), custom_call_target="tpu_custom_call" | custom-call | tf_op jit(solution)/shard_map/cut_heads/pallas_call | solution.py:308
  1.5 3.1 %collective-permute-start = (bf16[32,1920]{1,0:T(8,128)(2,1)S(1)}, bf16[32,1920]{1,0:T(8,128)(2,1)S(1)}, u32[]{:S(2)}, u32[]{:S(2)}) collective-permute-start(bf16[32,1920]{1,0:T(8,128)(2,1)S(1)} %get-tuple-element.61), channel_id=1, source_target_pairs={{0,1},{1,0},{2,3},{3,2},{4,5},{5,4},{6,7},{7,6},{8,9},{9,8},{10,11... | collective-permute-start | bytes 368648 | tf_op jit(solution)/shard_map/ppermute | solution.py:43
  4.6 2.6 %collective-permute-start.1 = (bf16[32,1920]{1,0:T(8,128)(2,1)S(1)}, bf16[32,1920]{1,0:T(8,128)(2,1)S(1)}, u32[]{:S(2)}, u32[]{:S(2)}) collective-permute-start(bf16[32,1920]{1,0:T(8,128)(2,1)S(1)} %get-tuple-element.62), channel_id=1, source_target_pairs={{0,2},{1,3},{2,0},{3,1},{4,6},{5,7},{6,4},{7,5},{8,10},{9,11},{10,... | collective-permute-start | bytes 368648 | tf_op jit(solution)/shard_map/ppermute | solution.py:43
  9.4 5.3 %load_rows.2.refs_0_ = bf16[4,3584,512]{2,1,0:T(8,128)(2,1)S(1)} custom-call(s32[1]{0:T(128)} %bitcast.me, bf16[4,7168,512]{2,1,0:T(8,128)(2,1)} %gate_hbm.3), custom_call_target="tpu_custom_call" | custom-call | bytes 14680064 | tf_op jit(solution)/shard_map/load_rows/pallas_call | solution.py:326
  14.7 2.2 %collective-permute-done.1.refs_1_ = bf16[32,1920]{1,0:T(8,128)(2,1)S(1)} collective-permute-done((bf16[32,1920]{1,0:T(8,128)(2,1)S(1)}, bf16[32,1920]{1,0:T(8,128)(2,1)S(1)}, u32[]{:S(2)}, u32[]{:S(2)}) %collective-permute-start.1) | collective-permute-done | bytes 122912 | tf_op jit(solution)/shard_map/ppermute | solution.py:43
  17.2 1.9 %collective-permute-start.3 = (bf16[32,1920]{1,0:T(8,128)(2,1)S(1)}, bf16[32,1920]{1,0:T(8,128)(2,1)S(1)}, u32[]{:S(2)}, u32[]{:S(2)}) collective-permute-start(bf16[32,1920]{1,0:T(8,128)(2,1)S(1)} %get-tuple-element.66.refs_0_), channel_id=1, source_target_pairs={{0,1},{1,0},{2,3},{3,2},{4,5},{5,4},{6,7},{7,6},{8,9},{9,8},{10,11... | collective-permute-start | bytes 368648 | tf_op jit(solution)/shard_map/ppermute | solution.py:43
  19.1 3.0 %collective-permute-done.3.refs_1_ = bf16[32,1920]{1,0:T(8,128)(2,1)S(1)} collective-permute-done((bf16[32,1920]{1,0:T(8,128)(2,1)S(1)}, bf16[32,1920]{1,0:T(8,128)(2,1)S(1)}, u32[]{:S(2)}, u32[]{:S(2)}) %collective-permute-start.3) | collective-permute-done | bytes 122912 | tf_op jit(solution)/shard_map/ppermute | solution.py:43
  22.2 3.1 %collective-permute-start.6 = (bf16[64,1920]{1,0:T(8,128)(2,1)S(1)}, bf16[64,1920]{1,0:T(8,128)(2,1)S(1)}, u32[]{:S(2)}, u32[]{:S(2)}) collective-permute-start(bf16[64,1920]{1,0:T(8,128)(2,1)S(1)} %join.1.refs_2_), channel_id=1, source_target_pairs={{0,2},{1,3},{2,0},{3,1},{4,6},{5,7},{6,4},{7,5},{8,10},{9,11},{10,... | collective-permute-start | bytes 737288 | tf_op jit(solution)/shard_map/ppermute | solution.py:43
  25.2 2.4 %collective-permute-start.10 = (bf16[64,1920]{1,0:T(8,128)(2,1)S(1)}, bf16[64,1920]{1,0:T(8,128)(2,1)S(1)}, u32[]{:S(2)}, u32[]{:S(2)}) collective-permute-start(bf16[64,1920]{1,0:T(8,128)(2,1)S(1)} %join.1.refs_2_), channel_id=1, source_target_pairs={{0,24},{4,28},{8,16},{12,20},{16,8},{20,12},{24,0},{28,4},{1,25},{... | collective-permute-start | bytes 737288 | tf_op jit(solution)/shard_map/ppermute | solution.py:43
  28.7 5.3 %load_rows.3.refs_1_ = bf16[4,3584,512]{2,1,0:T(8,128)(2,1)S(1)} custom-call(s32[1]{0:T(128)} %bitcast.me, bf16[4,7168,512]{2,1,0:T(8,128)(2,1)} %up_hbm.3), custom_call_target="tpu_custom_call" | custom-call | bytes 14680064 | tf_op jit(solution)/shard_map/load_rows/pallas_call | solution.py:326
  34.2 2.4 %collective-permute-done.8.refs_6_ = bf16[64,1920]{1,0:T(8,128)(2,1)S(1)} collective-permute-done((bf16[64,1920]{1,0:T(8,128)(2,1)S(1)}, bf16[64,1920]{1,0:T(8,128)(2,1)S(1)}, u32[]{:S(2)}, u32[]{:S(2)}) %collective-permute-start.8) | collective-permute-done | bytes 245792 | tf_op jit(solution)/shard_map/ppermute | solution.py:43
  37.3 1.6 %collective-permute-start.17 = (bf16[64,1920]{1,0:T(8,128)(2,1)S(1)}, bf16[64,1920]{1,0:T(8,128)(2,1)S(1)}, u32[]{:S(2)}, u32[]{:S(2)}) collective-permute-start(bf16[64,1920]{1,0:T(8,128)(2,1)S(1)} %collective-permute-done.6.refs_2_), channel_id=1, source_target_pairs={{0,24},{4,28},{8,16},{12,20},{16,8},{20,12},{24,0},{28,4},{1,25},{... | collective-permute-start | bytes 737288 | tf_op jit(solution)/shard_map/ppermute | solution.py:43
  38.9 1.3 %collective-permute-start.15 = (bf16[64,1920]{1,0:T(8,128)(2,1)S(1)}, bf16[64,1920]{1,0:T(8,128)(2,1)S(1)}, u32[]{:S(2)}, u32[]{:S(2)}) collective-permute-start(bf16[64,1920]{1,0:T(8,128)(2,1)S(1)} %collective-permute-done.6.refs_2_), channel_id=1, source_target_pairs={{0,16},{4,20},{8,24},{12,28},{16,0},{20,4},{24,8},{28,12},{1,17},{... | collective-permute-start | bytes 737288 | tf_op jit(solution)/shard_map/ppermute | solution.py:43
  40.8 9.9 %gate_up.2 = (f32[4,256,512]{2,1,0:T(8,128)S(1)}, f32[4,256,512]{2,1,0:T(8,128)S(1)}, f32[256,128]{1,0:T(8,128)S(1)}, bf16[4,3584,512]{2,1,0:T(8,128)(2,1)S(1)},...) custom-call(s32[1]{0:T(128)} %bitcast.me, ...), custom_call_target="tpu_custom_call", output_to_operand_aliasing={{3}: (5, {}), {4}: (6, {})} | custom-call | flops 7516192768 | bytes 29360128 | tf_op jit(solution)/shard_map/gate_up/pallas_call | solution.py:397
  50.7 1.1 %collective-permute-done.15.refs_6_ = bf16[64,1920]{1,0:T(8,128)(2,1)S(1)} collective-permute-done((bf16[64,1920]{1,0:T(8,128)(2,1)S(1)}, bf16[64,1920]{1,0:T(8,128)(2,1)S(1)}, u32[]{:S(2)}, u32[]{:S(2)}) %collective-permute-start.15) | collective-permute-done | bytes 245792 | tf_op jit(solution)/shard_map/ppermute | solution.py:43
  54.4 8.9 %gate_up.3 = (bf16[256,2048]{1,0:T(8,128)(2,1)S(1)}, bf16[4,3584,512]{2,1,0:T(8,128)(2,1)S(1)}, bf16[4,3584,512]{2,1,0:T(8,128)(2,1)S(1)}, bf16[4,512,1792]{2,1,0:T(8,128)(2,1)S(1)}) custom-call(s32[1]{0:T(128)} %bitcast.me, s32[1]{0:T(128)} %bitcast.1.first, bf16[4,7168,512]{2,1,0:T(8,128)(2,1)} %gate_hbm.3, ...), custom_call_target="tpu_custom_call", output_to_operand_aliasing={{1}: (5, {}), {2}: (6, {})} | custom-call | flops 7516192768 | bytes 29360128 | tf_op jit(solution)/shard_map/gate_up/pallas_call | solution.py:397
  63.3 4.4 %down.4 = (bf16[128,1792]{1,0:T(8,128)(2,1)S(1)}, bf16[128,1792]{1,0:T(8,128)(2,1)S(1)}, bf16[4,512,1792]{2,1,0:T(8,128)(2,1)S(1)}) custom-call(s32[1]{0:T(128)} %bitcast.me, bf16[256,2048]{1,0:T(8,128)(2,1)S(1)} %get-tuple-element.90.activation, bf16[4,512,1792]{2,1,0:T(8,128)(2,1)S(1)} %get-tuple-element.82.w_down, bf16[4,512,7168]{2,1,0:T(8,128)(2,1)} %refs_0_.3), custom_call_target="tpu_custom_call" | custom-call | flops 1879048192 | bytes 7340032 | tf_op jit(solution)/shard_map/down/pallas_call | solution.py:452
  67.9 2.6 %down.5 = (bf16[128,1792]{1,0:T(8,128)(2,1)S(1)}, bf16[128,1792]{1,0:T(8,128)(2,1)S(1)}) custom-call(s32[1]{0:T(128)} %bitcast.me, bf16[256,2048]{1,0:T(8,128)(2,1)S(1)} %get-tuple-element.90.activation, bf16[4,512,1792]{2,1,0:T(8,128)(2,1)S(1)} %get-tuple-element.85.w_down), custom_call_target="tpu_custom_call" | custom-call | flops 1879048192 | bytes 7340032 | tf_op jit(solution)/shard_map/down/pallas_call | solution.py:452
  71.1 1.3 %collective-permute-done.21 = bf16[128,1792]{1,0:T(8,128)(2,1)S(1)} collective-permute-done((bf16[128,1792]{1,0:T(8,128)(2,1)S(1)}, bf16[128,1792]{1,0:T(8,128)(2,1)S(1)}, u32[]{:S(2)}, u32[]{:S(2)}) %collective-permute-start.21) | collective-permute-done | bytes 458784 | tf_op jit(solution)/shard_map/ppermute | solution.py:43
  72.5 1.6 %collective-permute-start.25 = (bf16[64,1792]{1,0:T(8,128)(2,1)S(1)}, bf16[64,1792]{1,0:T(8,128)(2,1)S(1)}, u32[]{:S(2)}, u32[]{:S(2)}) collective-permute-start(bf16[64,1792]{1,0:T(8,128)(2,1)S(1)} %get-tuple-element.112), channel_id=1, source_target_pairs={{0,8},{4,12},{8,0},{12,4},{16,24},{20,28},{24,16},{28,20},{1,9},{5... | collective-permute-start | bytes 688136 | tf_op jit(solution)/shard_map/ppermute | solution.py:43
  74.8 4.3 %down.6 = (bf16[128,1792]{1,0:T(8,128)(2,1)S(1)}, bf16[128,1792]{1,0:T(8,128)(2,1)S(1)}, bf16[4,512,1792]{2,1,0:T(8,128)(2,1)S(1)}) custom-call(s32[1]{0:T(128)} %bitcast.me, bf16[256,2048]{1,0:T(8,128)(2,1)S(1)} %get-tuple-element.90.activation, bf16[4,512,1792]{2,1,0:T(8,128)(2,1)S(1)} %get-tuple-element.91.w_down, bf16[4,512,7168]{2,1,0:T(8,128)(2,1)} %refs_0_.3), custom_call_target="tpu_custom_call" | custom-call | flops 1879048192 | bytes 7340032 | tf_op jit(solution)/shard_map/down/pallas_call | solution.py:452
  79.1 2.6 %down.7 = (bf16[128,1792]{1,0:T(8,128)(2,1)S(1)}, bf16[128,1792]{1,0:T(8,128)(2,1)S(1)}) custom-call(s32[1]{0:T(128)} %bitcast.me, bf16[256,2048]{1,0:T(8,128)(2,1)S(1)} %get-tuple-element.90.activation, bf16[4,512,1792]{2,1,0:T(8,128)(2,1)S(1)} %get-tuple-element.92.w_down), custom_call_target="tpu_custom_call" | custom-call | flops 1879048192 | bytes 7340032 | tf_op jit(solution)/shard_map/down/pallas_call | solution.py:452
  82.3 1.3 %collective-permute-start.22 = (bf16[32,1792]{1,0:T(8,128)(2,1)S(1)}, bf16[32,1792]{1,0:T(8,128)(2,1)S(1)}, u32[]{:S(2)}, u32[]{:S(2)}) collective-permute-start(bf16[32,1792]{1,0:T(8,128)(2,1)S(1)} %add_convert_fusion.18), channel_id=1, source_target_pairs={{0,8},{4,12},{8,0},{12,4},{16,24},{20,28},{24,16},{28,20},{1,9},{5... | collective-permute-start | bytes 344072 | tf_op jit(solution)/shard_map/ppermute | solution.py:43
  84.5 1.4 %collective-permute-start.29 = (bf16[64,1792]{1,0:T(8,128)(2,1)S(1)}, bf16[64,1792]{1,0:T(8,128)(2,1)S(1)}, u32[]{:S(2)}, u32[]{:S(2)}) collective-permute-start(bf16[64,1792]{1,0:T(8,128)(2,1)S(1)} %get-tuple-element.106), channel_id=1, source_target_pairs={{0,16},{4,20},{8,24},{12,28},{16,0},{20,4},{24,8},{28,12},{1,17},{... | collective-permute-start | bytes 688136 | tf_op jit(solution)/shard_map/ppermute | solution.py:43
  86.0 0.9 collective-permute-start.31
  87.6 0.9 collective-permute-start.26
  88.5 1.3 %collective-permute-done.27 = bf16[32,1792]{1,0:T(8,128)(2,1)S(1)} collective-permute-done((bf16[32,1792]{1,0:T(8,128)(2,1)S(1)}, bf16[32,1792]{1,0:T(8,128)(2,1)S(1)}, u32[]{:S(2)}, u32[]{:S(2)}) %collective-permute-start.27) | collective-permute-done | bytes 114720 | tf_op jit(solution)/shard_map/ppermute | solution.py:43
  90.2 3.3 %collective-permute-done.29 = bf16[64,1792]{1,0:T(8,128)(2,1)S(1)} collective-permute-done((bf16[64,1792]{1,0:T(8,128)(2,1)S(1)}, bf16[64,1792]{1,0:T(8,128)(2,1)S(1)}, u32[]{:S(2)}, u32[]{:S(2)}) %collective-permute-start.29) | collective-permute-done | bytes 229408 | tf_op jit(solution)/shard_map/ppermute | solution.py:43
  93.5 0.9 collective-permute-start.30
  94.4 1.4 %collective-permute-start.33 = (bf16[32,1792]{1,0:T(8,128)(2,1)S(1)}, bf16[32,1792]{1,0:T(8,128)(2,1)S(1)}, u32[]{:S(2)}, u32[]{:S(2)}) collective-permute-start(bf16[32,1792]{1,0:T(8,128)(2,1)S(1)} %add_convert_fusion.11), channel_id=1, source_target_pairs={{0,16},{4,20},{8,24},{12,28},{16,0},{20,4},{24,8},{28,12},{1,17},{... | collective-permute-start | bytes 344072 | tf_op jit(solution)/shard_map/ppermute | solution.py:43
  95.8 2.5 %collective-permute-done.30 = bf16[32,1792]{1,0:T(8,128)(2,1)S(1)} collective-permute-done((bf16[32,1792]{1,0:T(8,128)(2,1)S(1)}, bf16[32,1792]{1,0:T(8,128)(2,1)S(1)}, u32[]{:S(2)}, u32[]{:S(2)}) %collective-permute-start.30) | collective-permute-done | bytes 114720 | tf_op jit(solution)/shard_map/ppermute | solution.py:43
  99.6 3.7 %collective-permute-done.32 = bf16[32,1792]{1,0:T(8,128)(2,1)S(1)} collective-permute-done((bf16[32,1792]{1,0:T(8,128)(2,1)S(1)}, bf16[32,1792]{1,0:T(8,128)(2,1)S(1)}, u32[]{:S(2)}, u32[]{:S(2)}) %collective-permute-start.32) | collective-permute-done | bytes 114720 | tf_op jit(solution)/shard_map/ppermute | solution.py:43
  (62 shorter events, 13.9 us)
Async XLA Ops:
  1.5 13.2 %collective-permute-start = (bf16[32,1920]{1,0:T(8,128)(2,1)S(1)}, bf16[32,1920]{1,0:T(8,128)(2,1)S(1)}, u32[]{:S(2)}, u32[]{:S(2)}) collective-permute-start(bf16[32,1920]{1,0:T(8,128)(2,1)S(1)} %get-tuple-element.61), channel_id=1, source_target_pairs={{0,1},{1,0},{2,3},{3,2},{4,5},{5,4},{6,7},{7,6},{8,9},{9,8},{10,11... | collective-permute-start | bytes 368648 | tf_op jit(solution)/shard_map/ppermute | solution.py:43
  4.6 12.3 %collective-permute-start.1 = (bf16[32,1920]{1,0:T(8,128)(2,1)S(1)}, bf16[32,1920]{1,0:T(8,128)(2,1)S(1)}, u32[]{:S(2)}, u32[]{:S(2)}) collective-permute-start(bf16[32,1920]{1,0:T(8,128)(2,1)S(1)} %get-tuple-element.62), channel_id=1, source_target_pairs={{0,2},{1,3},{2,0},{3,1},{4,6},{5,7},{6,4},{7,5},{8,10},{9,11},{10,... | collective-permute-start | bytes 368648 | tf_op jit(solution)/shard_map/ppermute | solution.py:43
  7.2 9.7 %collective-permute-start.2 = (bf16[32,1920]{1,0:T(8,128)(2,1)S(1)}, bf16[32,1920]{1,0:T(8,128)(2,1)S(1)}, u32[]{:S(2)}, u32[]{:S(2)}) collective-permute-start(bf16[32,1920]{1,0:T(8,128)(2,1)S(1)} %get-tuple-element.63), channel_id=1, source_target_pairs={{0,3},{1,2},{2,1},{3,0},{4,7},{5,6},{6,5},{7,4},{8,11},{9,10},{10,... | collective-permute-start | bytes 368648 | tf_op jit(solution)/shard_map/ppermute | solution.py:43
  17.2 4.9 %collective-permute-start.3 = (bf16[32,1920]{1,0:T(8,128)(2,1)S(1)}, bf16[32,1920]{1,0:T(8,128)(2,1)S(1)}, u32[]{:S(2)}, u32[]{:S(2)}) collective-permute-start(bf16[32,1920]{1,0:T(8,128)(2,1)S(1)} %get-tuple-element.66.refs_0_), channel_id=1, source_target_pairs={{0,1},{1,0},{2,3},{3,2},{4,5},{5,4},{6,7},{7,6},{8,9},{9,8},{10,11... | collective-permute-start | bytes 368648 | tf_op jit(solution)/shard_map/ppermute | solution.py:43
  22.2 12.1 %collective-permute-start.6 = (bf16[64,1920]{1,0:T(8,128)(2,1)S(1)}, bf16[64,1920]{1,0:T(8,128)(2,1)S(1)}, u32[]{:S(2)}, u32[]{:S(2)}) collective-permute-start(bf16[64,1920]{1,0:T(8,128)(2,1)S(1)} %join.1.refs_2_), channel_id=1, source_target_pairs={{0,2},{1,3},{2,0},{3,1},{4,6},{5,7},{6,4},{7,5},{8,10},{9,11},{10,... | collective-permute-start | bytes 737288 | tf_op jit(solution)/shard_map/ppermute | solution.py:43
  25.2 9.0 %collective-permute-start.10 = (bf16[64,1920]{1,0:T(8,128)(2,1)S(1)}, bf16[64,1920]{1,0:T(8,128)(2,1)S(1)}, u32[]{:S(2)}, u32[]{:S(2)}) collective-permute-start(bf16[64,1920]{1,0:T(8,128)(2,1)S(1)} %join.1.refs_2_), channel_id=1, source_target_pairs={{0,24},{4,28},{8,16},{12,20},{16,8},{20,12},{24,0},{28,4},{1,25},{... | collective-permute-start | bytes 737288 | tf_op jit(solution)/shard_map/ppermute | solution.py:43
  27.7 8.9 %collective-permute-start.8 = (bf16[64,1920]{1,0:T(8,128)(2,1)S(1)}, bf16[64,1920]{1,0:T(8,128)(2,1)S(1)}, u32[]{:S(2)}, u32[]{:S(2)}) collective-permute-start(bf16[64,1920]{1,0:T(8,128)(2,1)S(1)} %join.1.refs_2_), channel_id=1, source_target_pairs={{0,16},{4,20},{8,24},{12,28},{16,0},{20,4},{24,8},{28,12},{1,17},{... | collective-permute-start | bytes 737288 | tf_op jit(solution)/shard_map/ppermute | solution.py:43
  28.2 8.6 %collective-permute-start.5 = (bf16[64,1920]{1,0:T(8,128)(2,1)S(1)}, bf16[64,1920]{1,0:T(8,128)(2,1)S(1)}, u32[]{:S(2)}, u32[]{:S(2)}) collective-permute-start(bf16[64,1920]{1,0:T(8,128)(2,1)S(1)} %join.1.refs_2_), channel_id=1, source_target_pairs={{0,8},{4,12},{8,0},{12,4},{16,24},{20,28},{24,16},{28,20},{1,9},{5... | collective-permute-start | bytes 737288 | tf_op jit(solution)/shard_map/ppermute | solution.py:43
  28.7 10.1 %collective-permute-start.4 = (bf16[64,1920]{1,0:T(8,128)(2,1)S(1)}, bf16[64,1920]{1,0:T(8,128)(2,1)S(1)}, u32[]{:S(2)}, u32[]{:S(2)}) collective-permute-start(bf16[64,1920]{1,0:T(8,128)(2,1)S(1)} %join.1.refs_2_), channel_id=1, source_target_pairs={{0,4},{4,0},{8,12},{12,8},{16,20},{20,16},{24,28},{28,24},{1,5},{5... | collective-permute-start | bytes 737288 | tf_op jit(solution)/shard_map/ppermute | solution.py:43
  36.7 3.5 %collective-permute-start.7 = (bf16[64,1920]{1,0:T(8,128)(2,1)S(1)}, bf16[64,1920]{1,0:T(8,128)(2,1)S(1)}, u32[]{:S(2)}, u32[]{:S(2)}) collective-permute-start(bf16[64,1920]{1,0:T(8,128)(2,1)S(1)} %collective-permute-done.5.refs_4_), channel_id=1, source_target_pairs={{0,4},{4,0},{8,12},{12,8},{16,20},{20,16},{24,28},{28,24},{1,5},{5... | collective-permute-start | bytes 737288 | tf_op jit(solution)/shard_map/ppermute | solution.py:43
  36.8 4.0 %collective-permute-start.9 = (bf16[64,1920]{1,0:T(8,128)(2,1)S(1)}, bf16[64,1920]{1,0:T(8,128)(2,1)S(1)}, u32[]{:S(2)}, u32[]{:S(2)}) collective-permute-start(bf16[64,1920]{1,0:T(8,128)(2,1)S(1)} %collective-permute-done.8.refs_6_), channel_id=1, source_target_pairs={{0,4},{4,0},{8,12},{12,8},{16,20},{20,16},{24,28},{28,24},{1,5},{5... | collective-permute-start | bytes 737288 | tf_op jit(solution)/shard_map/ppermute | solution.py:43
  37.3 3.5 %collective-permute-start.11 = (bf16[64,1920]{1,0:T(8,128)(2,1)S(1)}, bf16[64,1920]{1,0:T(8,128)(2,1)S(1)}, u32[]{:S(2)}, u32[]{:S(2)}) collective-permute-start(bf16[64,1920]{1,0:T(8,128)(2,1)S(1)} %collective-permute-done.10.refs_8_), channel_id=1, source_target_pairs={{0,4},{4,0},{8,12},{12,8},{16,20},{20,16},{24,28},{28,24},{1,5},{5... | collective-permute-start | bytes 737288 | tf_op jit(solution)/shard_map/ppermute | solution.py:43
  37.3 13.4 %collective-permute-start.17 = (bf16[64,1920]{1,0:T(8,128)(2,1)S(1)}, bf16[64,1920]{1,0:T(8,128)(2,1)S(1)}, u32[]{:S(2)}, u32[]{:S(2)}) collective-permute-start(bf16[64,1920]{1,0:T(8,128)(2,1)S(1)} %collective-permute-done.6.refs_2_), channel_id=1, source_target_pairs={{0,24},{4,28},{8,16},{12,20},{16,8},{20,12},{24,0},{28,4},{1,25},{... | collective-permute-start | bytes 737288 | tf_op jit(solution)/shard_map/ppermute | solution.py:43
  38.9 12.9 %collective-permute-start.15 = (bf16[64,1920]{1,0:T(8,128)(2,1)S(1)}, bf16[64,1920]{1,0:T(8,128)(2,1)S(1)}, u32[]{:S(2)}, u32[]{:S(2)}) collective-permute-start(bf16[64,1920]{1,0:T(8,128)(2,1)S(1)} %collective-permute-done.6.refs_2_), channel_id=1, source_target_pairs={{0,16},{4,20},{8,24},{12,28},{16,0},{20,4},{24,8},{28,12},{1,17},{... | collective-permute-start | bytes 737288 | tf_op jit(solution)/shard_map/ppermute | solution.py:43
  40.2 11.6 %collective-permute-start.13 = (bf16[64,1920]{1,0:T(8,128)(2,1)S(1)}, bf16[64,1920]{1,0:T(8,128)(2,1)S(1)}, u32[]{:S(2)}, u32[]{:S(2)}) collective-permute-start(bf16[64,1920]{1,0:T(8,128)(2,1)S(1)} %collective-permute-done.6.refs_2_), channel_id=1, source_target_pairs={{0,8},{4,12},{8,0},{12,4},{16,24},{20,28},{24,16},{28,20},{1,9},{5... | collective-permute-start | bytes 737288 | tf_op jit(solution)/shard_map/ppermute | solution.py:43
  51.8 1.8 %collective-permute-start.14 = (bf16[64,1920]{1,0:T(8,128)(2,1)S(1)}, bf16[64,1920]{1,0:T(8,128)(2,1)S(1)}, u32[]{:S(2)}, u32[]{:S(2)}) collective-permute-start(bf16[64,1920]{1,0:T(8,128)(2,1)S(1)} %collective-permute-done.13.refs_4_), channel_id=1, source_target_pairs={{0,4},{4,0},{8,12},{12,8},{16,20},{20,16},{24,28},{28,24},{1,5},{5... | collective-permute-start | bytes 737288 | tf_op jit(solution)/shard_map/ppermute | solution.py:43
  52.4 2.0 %collective-permute-start.18 = (bf16[64,1920]{1,0:T(8,128)(2,1)S(1)}, bf16[64,1920]{1,0:T(8,128)(2,1)S(1)}, u32[]{:S(2)}, u32[]{:S(2)}) collective-permute-start(bf16[64,1920]{1,0:T(8,128)(2,1)S(1)} %collective-permute-done.17.refs_8_), channel_id=1, source_target_pairs={{0,4},{4,0},{8,12},{12,8},{16,20},{20,16},{24,28},{28,24},{1,5},{5... | collective-permute-start | bytes 737288 | tf_op jit(solution)/shard_map/ppermute | solution.py:43
  67.7 3.3 %collective-permute-start.19 = (bf16[128,1792]{1,0:T(8,128)(2,1)S(1)}, bf16[128,1792]{1,0:T(8,128)(2,1)S(1)}, u32[]{:S(2)}, u32[]{:S(2)}) collective-permute-start(bf16[128,1792]{1,0:T(8,128)(2,1)S(1)} %get-tuple-element.84), channel_id=1, source_target_pairs={{0,4},{4,0},{8,12},{12,8},{16,20},{20,16},{24,28},{28,24},{1,5},{5... | collective-permute-start | bytes 1376264 | tf_op jit(solution)/shard_map/ppermute | solution.py:43
  70.5 1.9 %collective-permute-start.21 = (bf16[128,1792]{1,0:T(8,128)(2,1)S(1)}, bf16[128,1792]{1,0:T(8,128)(2,1)S(1)}, u32[]{:S(2)}, u32[]{:S(2)}) collective-permute-start(bf16[128,1792]{1,0:T(8,128)(2,1)S(1)} %get-tuple-element.87), channel_id=1, source_target_pairs={{0,4},{4,0},{8,12},{12,8},{16,20},{20,16},{24,28},{28,24},{1,5},{5... | collective-permute-start | bytes 1376264 | tf_op jit(solution)/shard_map/ppermute | solution.py:43
  72.5 11.1 %collective-permute-start.25 = (bf16[64,1792]{1,0:T(8,128)(2,1)S(1)}, bf16[64,1792]{1,0:T(8,128)(2,1)S(1)}, u32[]{:S(2)}, u32[]{:S(2)}) collective-permute-start(bf16[64,1792]{1,0:T(8,128)(2,1)S(1)} %get-tuple-element.112), channel_id=1, source_target_pairs={{0,8},{4,12},{8,0},{12,4},{16,24},{20,28},{24,16},{28,20},{1,9},{5... | collective-permute-start | bytes 688136 | tf_op jit(solution)/shard_map/ppermute | solution.py:43
  74.1 8.2 %collective-permute-start.20 = (bf16[64,1792]{1,0:T(8,128)(2,1)S(1)}, bf16[64,1792]{1,0:T(8,128)(2,1)S(1)}, u32[]{:S(2)}, u32[]{:S(2)}) collective-permute-start(bf16[64,1792]{1,0:T(8,128)(2,1)S(1)} %get-tuple-element.110), channel_id=1, source_target_pairs={{0,16},{4,20},{8,24},{12,28},{16,0},{20,4},{24,8},{28,12},{1,17},{... | collective-permute-start | bytes 688136 | tf_op jit(solution)/shard_map/ppermute | solution.py:43
  81.7 4.2 %collective-permute-start.23 = (bf16[128,1792]{1,0:T(8,128)(2,1)S(1)}, bf16[128,1792]{1,0:T(8,128)(2,1)S(1)}, u32[]{:S(2)}, u32[]{:S(2)}) collective-permute-start(bf16[128,1792]{1,0:T(8,128)(2,1)S(1)} %get-tuple-element.94), channel_id=1, source_target_pairs={{0,4},{4,0},{8,12},{12,8},{16,20},{20,16},{24,28},{28,24},{1,5},{5... | collective-permute-start | bytes 1376264 | tf_op jit(solution)/shard_map/ppermute | solution.py:43
  81.8 2.6 %collective-permute-start.24 = (bf16[128,1792]{1,0:T(8,128)(2,1)S(1)}, bf16[128,1792]{1,0:T(8,128)(2,1)S(1)}, u32[]{:S(2)}, u32[]{:S(2)}) collective-permute-start(bf16[128,1792]{1,0:T(8,128)(2,1)S(1)} %get-tuple-element.96), channel_id=1, source_target_pairs={{0,4},{4,0},{8,12},{12,8},{16,20},{20,16},{24,28},{28,24},{1,5},{5... | collective-permute-start | bytes 1376264 | tf_op jit(solution)/shard_map/ppermute | solution.py:43
  82.3 5.2 %collective-permute-start.22 = (bf16[32,1792]{1,0:T(8,128)(2,1)S(1)}, bf16[32,1792]{1,0:T(8,128)(2,1)S(1)}, u32[]{:S(2)}, u32[]{:S(2)}) collective-permute-start(bf16[32,1792]{1,0:T(8,128)(2,1)S(1)} %add_convert_fusion.18), channel_id=1, source_target_pairs={{0,8},{4,12},{8,0},{12,4},{16,24},{20,28},{24,16},{28,20},{1,9},{5... | collective-permute-start | bytes 344072 | tf_op jit(solution)/shard_map/ppermute | solution.py:43
  83.6 6.1 %collective-permute-start.27 = (bf16[32,1792]{1,0:T(8,128)(2,1)S(1)}, bf16[32,1792]{1,0:T(8,128)(2,1)S(1)}, u32[]{:S(2)}, u32[]{:S(2)}) collective-permute-start(bf16[32,1792]{1,0:T(8,128)(2,1)S(1)} %add_convert_fusion.17), channel_id=1, source_target_pairs={{0,16},{4,20},{8,24},{12,28},{16,0},{20,4},{24,8},{28,12},{1,17},{... | collective-permute-start | bytes 344072 | tf_op jit(solution)/shard_map/ppermute | solution.py:43
  84.5 9.0 %collective-permute-start.29 = (bf16[64,1792]{1,0:T(8,128)(2,1)S(1)}, bf16[64,1792]{1,0:T(8,128)(2,1)S(1)}, u32[]{:S(2)}, u32[]{:S(2)}) collective-permute-start(bf16[64,1792]{1,0:T(8,128)(2,1)S(1)} %get-tuple-element.106), channel_id=1, source_target_pairs={{0,16},{4,20},{8,24},{12,28},{16,0},{20,4},{24,8},{28,12},{1,17},{... | collective-permute-start | bytes 688136 | tf_op jit(solution)/shard_map/ppermute | solution.py:43
  86.0 8.3 %collective-permute-start.31 = (bf16[64,1792]{1,0:T(8,128)(2,1)S(1)}, bf16[64,1792]{1,0:T(8,128)(2,1)S(1)}, u32[]{:S(2)}, u32[]{:S(2)}) collective-permute-start(bf16[64,1792]{1,0:T(8,128)(2,1)S(1)} %get-tuple-element.107), channel_id=1, source_target_pairs={{0,8},{4,12},{8,0},{12,4},{16,24},{20,28},{24,16},{28,20},{1,9},{5... | collective-permute-start | bytes 688136 | tf_op jit(solution)/shard_map/ppermute | solution.py:43
  87.6 12.0 %collective-permute-start.26 = (bf16[32,1792]{1,0:T(8,128)(2,1)S(1)}, bf16[32,1792]{1,0:T(8,128)(2,1)S(1)}, u32[]{:S(2)}, u32[]{:S(2)}) collective-permute-start(bf16[32,1792]{1,0:T(8,128)(2,1)S(1)} %add_convert_fusion.16), channel_id=1, source_target_pairs={{0,3},{1,2},{2,1},{3,0},{4,7},{5,6},{6,5},{7,4},{8,11},{9,10},{10,... | collective-permute-start | bytes 344072 | tf_op jit(solution)/shard_map/ppermute | solution.py:43
  89.8 9.8 %collective-permute-start.28 = (bf16[32,1792]{1,0:T(8,128)(2,1)S(1)}, bf16[32,1792]{1,0:T(8,128)(2,1)S(1)}, u32[]{:S(2)}, u32[]{:S(2)}) collective-permute-start(bf16[32,1792]{1,0:T(8,128)(2,1)S(1)} %add_convert_fusion.14), channel_id=1, source_target_pairs={{0,2},{1,3},{2,0},{3,1},{4,6},{5,7},{6,4},{7,5},{8,10},{9,11},{10,... | collective-permute-start | bytes 344072 | tf_op jit(solution)/shard_map/ppermute | solution.py:43
  93.5 4.9 %collective-permute-start.30 = (bf16[32,1792]{1,0:T(8,128)(2,1)S(1)}, bf16[32,1792]{1,0:T(8,128)(2,1)S(1)}, u32[]{:S(2)}, u32[]{:S(2)}) collective-permute-start(bf16[32,1792]{1,0:T(8,128)(2,1)S(1)} %add_convert_fusion.12), channel_id=1, source_target_pairs={{0,8},{4,12},{8,0},{12,4},{16,24},{20,28},{24,16},{28,20},{1,9},{5... | collective-permute-start | bytes 344072 | tf_op jit(solution)/shard_map/ppermute | solution.py:43
  94.4 5.2 %collective-permute-start.33 = (bf16[32,1792]{1,0:T(8,128)(2,1)S(1)}, bf16[32,1792]{1,0:T(8,128)(2,1)S(1)}, u32[]{:S(2)}, u32[]{:S(2)}) collective-permute-start(bf16[32,1792]{1,0:T(8,128)(2,1)S(1)} %add_convert_fusion.11), channel_id=1, source_target_pairs={{0,16},{4,20},{8,24},{12,28},{16,0},{20,4},{24,8},{28,12},{1,17},{... | collective-permute-start | bytes 344072 | tf_op jit(solution)/shard_map/ppermute | solution.py:43
  98.4 4.9 %collective-permute-start.32 = (bf16[32,1792]{1,0:T(8,128)(2,1)S(1)}, bf16[32,1792]{1,0:T(8,128)(2,1)S(1)}, u32[]{:S(2)}, u32[]{:S(2)}) collective-permute-start(bf16[32,1792]{1,0:T(8,128)(2,1)S(1)} %add_convert_fusion.10), channel_id=1, source_target_pairs={{0,1},{1,0},{2,3},{3,2},{4,5},{5,4},{6,7},{7,6},{8,9},{9,8},{10,11... | collective-permute-start | bytes 344072 | tf_op jit(solution)/shard_map/ppermute | solution.py:43
  (2 other events, 3.2 us)

commit v7 on v6

--- a/solution.py
+++ b/solution.py
@@ -111,11 +111,11 @@
     message[:, width:] = tail.astype(BF16)
 
 
-def copies_of(source, target, sems, block, axis, experts):
+def copies_of(source, target, sems, block, axis, experts, low=0):
     size = target.shape[1 + axis]
     there = pl.ds(pl.multiple_of(block * size, LANES), size)
     place = (there, slice(None)) if axis == 0 else (slice(None), there)
-    return [pltpu.make_async_copy(source.at[(e, *place)], target.at[e], sems.at[e]) for e in experts]
+    return [pltpu.make_async_copy(source.at[(e, *place)], target.at[e - low], sems.at[e]) for e in experts]
 
 
 def load_kernel(me, hbm, held, sems):
@@ -149,8 +149,8 @@
     count = down_hbm.shape[0]
     width = x.shape[1] // chunks
     down = []
-    for i, (place, target) in enumerate(zip(ahead, held_down)):
-        down += copies_of(down_hbm, target, sems.at[2 + i], me[0] ^ place, 1, range(count))
+    for i, ((place, low, high), target) in enumerate(zip(ahead, held_down)):
+        down += copies_of(down_hbm, target, sems.at[2 + i], me[0] ^ place, 1, range(low, high), low)
 
     def rows_of(flip, some):
         block = (me[0] ^ flip) // chunks
@@ -217,12 +217,15 @@
             copy.wait()
 
 
-def down_kernel(order, ahead, me, activation, w_down, *refs):
-    if ahead is None:
+def down_kernel(order, ranges, ahead, me, activation, *refs):
+    parts, refs = refs[: len(ranges)], refs[len(ranges) :]
+    if not ahead:
         keep, send = refs
     else:
-        down_hbm, keep, send, held_down, sems = refs
-        copies = copies_of(down_hbm, held_down, sems, me[0] ^ ahead, 1, range(held_down.shape[0]))
+        down_hbm, keep, send, *held_down, sems = refs
+        copies = []
+        for i, ((place, low, high), target) in enumerate(zip(ahead, held_down)):
+            copies += copies_of(down_hbm, target, sems.at[i], me[0] ^ place, 1, range(low, high), low)
 
         @pl.when(pl.program_id(0) == 0)
         def _():
@@ -230,16 +233,20 @@
                 copy.start()
 
     width = keep.shape[1]
+    hidden = parts[0].shape[1]
     here = pl.ds(pl.multiple_of(pl.program_id(0) * width, LANES), width)
-    weights = w_down[:, :, here].reshape(-1, width)
-    total = jnp.dot(activation[...], weights, preferred_element_type=F32).astype(BF16)
+    total = 0.0
+    for (low, high), part in zip(ranges, parts):
+        weights = part[:, :, here].reshape(-1, width)
+        total = total + jnp.dot(activation[:, low * hidden : high * hidden], weights, preferred_element_type=F32)
+    total = total.astype(BF16)
     height = total.shape[0] // len(order)
     middle = len(order) // 2
     for i, pattern in enumerate(order):
         out = keep if i < middle else send
         at = i % middle
         out[at * height : (at + 1) * height, :] = total[pattern * height : (pattern + 1) * height]
-    if ahead is not None:
+    if ahead:
 
         @pl.when(pl.program_id(0) == pl.num_programs(0) - 1)
         def _():
@@ -299,6 +306,7 @@
     experts = local_experts * exp_count
     tail = -(-(experts + PARTS) // LANES) * LANES
     total_rows = rows * exp_count
+    small = 4 * max(1, total_rows // 256)
     me = lax.axis_index("tp").astype(jnp.int32).reshape(1)
     first = (lax.axis_index("exp") * local_experts).astype(jnp.int32).reshape(1)
     me, first = lax.optimization_barrier((me, first))
@@ -361,15 +369,20 @@
 
     state, held_down = [], {}
     places = list(reversed(range(tp_count)))
+    halves = [(0, local_experts)] if local_experts == 1 else [(0, local_experts // 2), (local_experts // 2, local_experts)]
+    units = [(k, low, high) for k in places for low, high in halves]
+
+    def part_of(unit):
+        return pltpu.VMEM((unit[2] - unit[1], hidden, cols), BF16)
+
     for i, group in enumerate(groups):
         if i:
             plane = cross_plane(group, exp_count)
             plane = {pattern: after(piece, state[-1]) for pattern, piece in plane.items()}
         pieces = cross_core(plane)
         chunks, flip = sizes[i], starts[i]
-        ahead = places[i : i + 1]
         start, last = i == 0, i == len(groups) - 1
-        down_shape = pltpu.VMEM((local_experts, hidden, cols), BF16)
+        ahead = units[len(held_down) :][: len(halves)]
         acc = pltpu.VMEM((local_experts, total_rows, hidden), F32)
         held = i == 0 or chunks == sizes[i - 1]
         late = held and i > 0
@@ -396,7 +409,7 @@
             out_specs += [vmem()] * 2
         found = pl.pallas_call(
             functools.partial(up_kernel, start, last, held, late, refill, chunks, ahead, full, experts),
-            out_shape=out_shape + [down_shape] * len(ahead),
+            out_shape=out_shape + [part_of(unit) for unit in ahead],
             grid_spec=pltpu.PrefetchScalarGridSpec(
                 num_scalar_prefetch=2,
                 grid=(local_experts,),
@@ -407,7 +420,7 @@
                 + [pltpu.SemaphoreType.DMA((2 + len(ahead), local_experts))],
             ),
             input_output_aliases=aliases,
-            compiler_params=params(6 if held else 22),
+            compiler_params=params(small * 3 // 2 if held else 22),
             cost_estimate=pl.CostEstimate(
                 flops=4 * total_rows * chunks * cols * hidden * local_experts,
                 bytes_accessed=4 * chunks * cols * hidden * local_experts,
@@ -429,46 +442,41 @@
     steps = 2 if cols % (2 * LANES) == 0 else 1
     width = cols // steps
     stages = len(orders[0]) + 1
-    pairs = [(low, low + 1) for low in range(0, tp_count, 2)]
-    events, open_stage = [], {}
-    for n, pair in enumerate(pairs):
-        events += [(j, None) for j in pair]
-        for before in pairs[:n]:
-            open_stage[before] += 1
-            events += [(j, open_stage[before]) for j in before if open_stage[before] < stages]
-        events += [(j, 0) for j in pair]
-        open_stage[pair] = 0
-    for _ in range(stages):
-        for pair in pairs:
-            open_stage[pair] += 1
-            events += [(j, open_stage[pair]) for j in pair if open_stage[pair] < stages]
+    events = [(0, None)]
+    for j in range(1, tp_count):
+        events += [(j, None)] + ([(j - 1, 0)] if j < tp_count - 1 else [])
+    for turn in range(stages):
+        for j in range(tp_count):
+            stage = turn + (1 if j < tp_count - 2 else 0)
+            events += [(j, stage)] if stage < stages else []
     mine, theirs, opened, done = {}, {}, [], []
     for j, stage in events:
         k = places[j]
         order = orders[k % 2]
         if stage is None:
-            ahead = next((p for p in places[: j + 3 - j % 2] if p not in held_down), None)
-            held = [] if ahead is None else [pltpu.VMEM((local_experts, hidden, cols), BF16)]
+            ahead = units[len(held_down) :]
+            ahead = ahead[: max(1, sum(unit[0] in places[: j + 2] for unit in ahead))]
+            held = [part_of(unit) for unit in ahead]
+            parts = [on_chip(held_down[(k, low, high)]) for low, high in halves]
             keep, send, *found = pl.pallas_call(
-                functools.partial(down_kernel, relative_order([core] + order), ahead),
+                functools.partial(down_kernel, relative_order([core] + order), halves, ahead),
                 out_shape=[shape(total_rows // 2, cols)] * 2 + held,
                 grid_spec=pltpu.PrefetchScalarGridSpec(
                     num_scalar_prefetch=1,
                     grid=(steps,),
-                    in_specs=[vmem()] * 2 + [pl.BlockSpec(memory_space=pltpu.HBM)] * len(held),
+                    in_specs=[vmem()] * (1 + len(parts)) + [pl.BlockSpec(memory_space=pltpu.HBM)] * bool(held),
                     out_specs=[pl.BlockSpec((total_rows // 2, width), lambda i, me: (0, i))] * 2 + [vmem()] * len(held),
-                    scratch_shapes=[pltpu.SemaphoreType.DMA((local_experts,))] * len(held),
+                    scratch_shapes=[pltpu.SemaphoreType.DMA((len(held), local_experts))] * bool(held),
                 ),
-                compiler_params=params(8),
+                compiler_params=params(2 * small),
                 cost_estimate=pl.CostEstimate(
                     flops=2 * total_rows * cols * hidden * local_experts,
                     bytes_accessed=2 * cols * hidden * local_experts,
                     transcendentals=0,
                 ),
                 name="down",
-            )(me, after(activation, *opened[-1:]), on_chip(held_down[k]), *[off_chip(w_down)] * len(held))
-            if found:
-                held_down[ahead] = found[0]
+            )(me, after(activation, *opened[-1:]), *parts, *[off_chip(w_down)] * bool(held))
+            held_down.update(zip(ahead, found))
             mine[k], theirs[k] = keep, swap(send, "exp", core)
         elif stage < stages - 1:
             middle = mine[k].shape[0] // 2

time: 104 us -> 103 us (level)
  waiting for transfers between devices: 24.2 us -> 21.9 us
    ppermute x34, waiting for transfers between devices: 24.2 us -> 21.9 us  [swap(): return lax.ppermute(value, axis, [(i, i ^ bit) for i in range(count)])]
  transfers between devices with their start and end apart: 34 -> 34, of which waited for: 17 -> 16; matrix products, arithmetic and copies ran while one was open for 3% -> 3% of each run, Pallas kernels for 29% -> 30%
where the time goes in v7:
time: 103 us; the launch traced here: 102 us
  Pallas kernels  44.7 us (43%)
  starting transfers between devices  31.9 us (31%)
  waiting for transfers between devices  21.9 us (21%)
  local copies, waits for them, and re-layouts  2.22 us (2%)
  other arithmetic  1.43 us (1%)
    ppermute x34, starting transfers between devices, swap(): return lax.ppermute(value, axis, [(i, i ^ bit) for i in range(count)])  31.9 us
    ppermute x34, waiting for transfers between devices, swap(): return lax.ppermute(value, axis, [(i, i ^ bit) for i in range(count)])  21.9 us
    pallas_call x2, Pallas kernels, local(): pl.pallas_call(functools.partial(up_kernel, start, last, held, late, refi...  18.9 us
    pallas_call x4, Pallas kernels, local(): pl.pallas_call(functools.partial(down_kernel, relative_order([core] + ord...  13.4 us
    pallas_call x2, Pallas kernels, load(): pl.pallas_call(load_kernel, out_shape=pltpu.VMEM((local_experts, 2 * cols...  10.6 us
  transfers between devices with their start and end apart: 34, of which 16 were waited for; matrix products, arithmetic and copies ran while one was open for 3% of the time, Pallas kernels for 30%

profile of v7, /device:TPU:0, one launch (start us, length us, event | category | flops | bytes accessed | tf_op | source)
XLA Modules:
  0.0 102.3 jit_solution(6374397922832992966)
XLA Ops:
  0.0 1.5 %cut_heads.1 = (bf16[32,1920]{1,0:T(8,128)(2,1)S(1)}, bf16[32,1920]{1,0:T(8,128)(2,1)S(1)}, bf16[32,1920]{1,0:T(8,128)(2,1)S(1)}, f32[32,1792]{1,0:T(8,128)S(1)}...) custom-call(s32[1]{0:T(128)} %bitcast.me, bf16[32,7168]{1,0:T(8,128)(2,1)} %bitcast.4, bf16[32,1792]{1,0:T(8,128)(2,1)} %resid_hbm.1, ...), custom_call_target="tpu_custom_call" | custom-call | tf_op jit(solution)/shard_map/cut_heads/pallas_call | solution.py:316
  1.5 3.1 %collective-permute-start = (bf16[32,1920]{1,0:T(8,128)(2,1)S(1)}, bf16[32,1920]{1,0:T(8,128)(2,1)S(1)}, u32[]{:S(2)}, u32[]{:S(2)}) collective-permute-start(bf16[32,1920]{1,0:T(8,128)(2,1)S(1)} %get-tuple-element.66), channel_id=1, source_target_pairs={{0,1},{1,0},{2,3},{3,2},{4,5},{5,4},{6,7},{7,6},{8,9},{9,8},{10,11... | collective-permute-start | bytes 368648 | tf_op jit(solution)/shard_map/ppermute | solution.py:43
  4.6 2.6 %collective-permute-start.1 = (bf16[32,1920]{1,0:T(8,128)(2,1)S(1)}, bf16[32,1920]{1,0:T(8,128)(2,1)S(1)}, u32[]{:S(2)}, u32[]{:S(2)}) collective-permute-start(bf16[32,1920]{1,0:T(8,128)(2,1)S(1)} %get-tuple-element.67), channel_id=1, source_target_pairs={{0,2},{1,3},{2,0},{3,1},{4,6},{5,7},{6,4},{7,5},{8,10},{9,11},{10,... | collective-permute-start | bytes 368648 | tf_op jit(solution)/shard_map/ppermute | solution.py:43
  9.4 5.3 %load_rows.2.refs_0_ = bf16[4,3584,512]{2,1,0:T(8,128)(2,1)S(1)} custom-call(s32[1]{0:T(128)} %bitcast.me, bf16[4,7168,512]{2,1,0:T(8,128)(2,1)} %gate_hbm.3), custom_call_target="tpu_custom_call" | custom-call | bytes 14680064 | tf_op jit(solution)/shard_map/load_rows/pallas_call | solution.py:334
  14.7 2.2 %collective-permute-done.1.refs_1_ = bf16[32,1920]{1,0:T(8,128)(2,1)S(1)} collective-permute-done((bf16[32,1920]{1,0:T(8,128)(2,1)S(1)}, bf16[32,1920]{1,0:T(8,128)(2,1)S(1)}, u32[]{:S(2)}, u32[]{:S(2)}) %collective-permute-start.1) | collective-permute-done | bytes 122912 | tf_op jit(solution)/shard_map/ppermute | solution.py:43
  17.2 1.9 %collective-permute-start.3 = (bf16[32,1920]{1,0:T(8,128)(2,1)S(1)}, bf16[32,1920]{1,0:T(8,128)(2,1)S(1)}, u32[]{:S(2)}, u32[]{:S(2)}) collective-permute-start(bf16[32,1920]{1,0:T(8,128)(2,1)S(1)} %get-tuple-element.71.refs_0_), channel_id=1, source_target_pairs={{0,1},{1,0},{2,3},{3,2},{4,5},{5,4},{6,7},{7,6},{8,9},{9,8},{10,11... | collective-permute-start | bytes 368648 | tf_op jit(solution)/shard_map/ppermute | solution.py:43
  19.1 3.0 %collective-permute-done.3.refs_1_ = bf16[32,1920]{1,0:T(8,128)(2,1)S(1)} collective-permute-done((bf16[32,1920]{1,0:T(8,128)(2,1)S(1)}, bf16[32,1920]{1,0:T(8,128)(2,1)S(1)}, u32[]{:S(2)}, u32[]{:S(2)}) %collective-permute-start.3) | collective-permute-done | bytes 122912 | tf_op jit(solution)/shard_map/ppermute | solution.py:43
  22.2 3.1 %collective-permute-start.6 = (bf16[64,1920]{1,0:T(8,128)(2,1)S(1)}, bf16[64,1920]{1,0:T(8,128)(2,1)S(1)}, u32[]{:S(2)}, u32[]{:S(2)}) collective-permute-start(bf16[64,1920]{1,0:T(8,128)(2,1)S(1)} %join.1.refs_2_), channel_id=1, source_target_pairs={{0,2},{1,3},{2,0},{3,1},{4,6},{5,7},{6,4},{7,5},{8,10},{9,11},{10,... | collective-permute-start | bytes 737288 | tf_op jit(solution)/shard_map/ppermute | solution.py:43
  25.2 2.4 %collective-permute-start.10 = (bf16[64,1920]{1,0:T(8,128)(2,1)S(1)}, bf16[64,1920]{1,0:T(8,128)(2,1)S(1)}, u32[]{:S(2)}, u32[]{:S(2)}) collective-permute-start(bf16[64,1920]{1,0:T(8,128)(2,1)S(1)} %join.1.refs_2_), channel_id=1, source_target_pairs={{0,24},{4,28},{8,16},{12,20},{16,8},{20,12},{24,0},{28,4},{1,25},{... | collective-permute-start | bytes 737288 | tf_op jit(solution)/shard_map/ppermute | solution.py:43
  28.7 5.3 %load_rows.3.refs_1_ = bf16[4,3584,512]{2,1,0:T(8,128)(2,1)S(1)} custom-call(s32[1]{0:T(128)} %bitcast.me, bf16[4,7168,512]{2,1,0:T(8,128)(2,1)} %up_hbm.3), custom_call_target="tpu_custom_call" | custom-call | bytes 14680064 | tf_op jit(solution)/shard_map/load_rows/pallas_call | solution.py:334
  34.2 2.4 %collective-permute-done.8.refs_6_ = bf16[64,1920]{1,0:T(8,128)(2,1)S(1)} collective-permute-done((bf16[64,1920]{1,0:T(8,128)(2,1)S(1)}, bf16[64,1920]{1,0:T(8,128)(2,1)S(1)}, u32[]{:S(2)}, u32[]{:S(2)}) %collective-permute-start.8) | collective-permute-done | bytes 245792 | tf_op jit(solution)/shard_map/ppermute | solution.py:43
  37.3 1.6 %collective-permute-start.17 = (bf16[64,1920]{1,0:T(8,128)(2,1)S(1)}, bf16[64,1920]{1,0:T(8,128)(2,1)S(1)}, u32[]{:S(2)}, u32[]{:S(2)}) collective-permute-start(bf16[64,1920]{1,0:T(8,128)(2,1)S(1)} %collective-permute-done.6.refs_2_), channel_id=1, source_target_pairs={{0,24},{4,28},{8,16},{12,20},{16,8},{20,12},{24,0},{28,4},{1,25},{... | collective-permute-start | bytes 737288 | tf_op jit(solution)/shard_map/ppermute | solution.py:43
  38.9 1.3 %collective-permute-start.15 = (bf16[64,1920]{1,0:T(8,128)(2,1)S(1)}, bf16[64,1920]{1,0:T(8,128)(2,1)S(1)}, u32[]{:S(2)}, u32[]{:S(2)}) collective-permute-start(bf16[64,1920]{1,0:T(8,128)(2,1)S(1)} %collective-permute-done.6.refs_2_), channel_id=1, source_target_pairs={{0,16},{4,20},{8,24},{12,28},{16,0},{20,4},{24,8},{28,12},{1,17},{... | collective-permute-start | bytes 737288 | tf_op jit(solution)/shard_map/ppermute | solution.py:43
  40.8 9.9 %gate_up.2 = (f32[4,256,512]{2,1,0:T(8,128)S(1)}, f32[4,256,512]{2,1,0:T(8,128)S(1)}, f32[256,128]{1,0:T(8,128)S(1)}, bf16[4,3584,512]{2,1,0:T(8,128)(2,1)S(1)},...) custom-call(s32[1]{0:T(128)} %bitcast.me, ...), custom_call_target="tpu_custom_call", output_to_operand_aliasing={{3}: (5, {}), {4}: (6, {})} | custom-call | flops 7516192768 | bytes 29360128 | tf_op jit(solution)/shard_map/gate_up/pallas_call | solution.py:410
  50.7 1.1 %collective-permute-done.15.refs_6_ = bf16[64,1920]{1,0:T(8,128)(2,1)S(1)} collective-permute-done((bf16[64,1920]{1,0:T(8,128)(2,1)S(1)}, bf16[64,1920]{1,0:T(8,128)(2,1)S(1)}, u32[]{:S(2)}, u32[]{:S(2)}) %collective-permute-start.15) | collective-permute-done | bytes 245792 | tf_op jit(solution)/shard_map/ppermute | solution.py:43
  54.4 9.0 %gate_up.3 = (bf16[256,2048]{1,0:T(8,128)(2,1)S(1)}, bf16[4,3584,512]{2,1,0:T(8,128)(2,1)S(1)}, bf16[4,3584,512]{2,1,0:T(8,128)(2,1)S(1)}, bf16[2,512,1792]{2,1,0:T(8,128)(2,1)S(1)}, bf16[2,512,1792]{2,1,0:T(8,128)(2,1)S(1)}) custom-call(s32[1]{0:T(128)} %bitcast.me, s32[1]{0:T(128)} %bitcast.1.first, ...), custom_call_target="tpu_custom_call", output_to_operand_aliasing={{1}: (5, {}), {2}: (6, {})} | custom-call | flops 7516192768 | bytes 29360128 | tf_op jit(solution)/shard_map/gate_up/pallas_call | solution.py:410
  63.3 3.2 %down.4 = (bf16[128,1792]{1,0:T(8,128)(2,1)S(1)}, bf16[128,1792]{1,0:T(8,128)(2,1)S(1)}, bf16[2,512,1792]{2,1,0:T(8,128)(2,1)S(1)}) custom-call(s32[1]{0:T(128)} %bitcast.me, bf16[256,2048]{1,0:T(8,128)(2,1)S(1)} %get-tuple-element.98.activation, bf16[2,512,1792]{2,1,0:T(8,128)(2,1)S(1)} %get-tuple-element.87.refs_0_, ...), custom_call_target="tpu_custom_call" | custom-call | flops 1879048192 | bytes 7340032 | tf_op jit(solution)/shard_map/down/pallas_call | solution.py:461
  66.8 3.2 %down.5 = (bf16[128,1792]{1,0:T(8,128)(2,1)S(1)}, bf16[128,1792]{1,0:T(8,128)(2,1)S(1)}, bf16[2,512,1792]{2,1,0:T(8,128)(2,1)S(1)}) custom-call(s32[1]{0:T(128)} %bitcast.me, bf16[256,2048]{1,0:T(8,128)(2,1)S(1)} %get-tuple-element.98.activation, bf16[2,512,1792]{2,1,0:T(8,128)(2,1)S(1)} %get-tuple-element.91.refs_0_, ...), custom_call_target="tpu_custom_call" | custom-call | flops 1879048192 | bytes 7340032 | tf_op jit(solution)/shard_map/down/pallas_call | solution.py:461
  70.5 1.4 %collective-permute-start.20 = (bf16[64,1792]{1,0:T(8,128)(2,1)S(1)}, bf16[64,1792]{1,0:T(8,128)(2,1)S(1)}, u32[]{:S(2)}, u32[]{:S(2)}) collective-permute-start(bf16[64,1792]{1,0:T(8,128)(2,1)S(1)} %get-tuple-element.120), channel_id=1, source_target_pairs={{0,16},{4,20},{8,24},{12,28},{16,0},{20,4},{24,8},{28,12},{1,17},{... | collective-permute-start | bytes 688136 | tf_op jit(solution)/shard_map/ppermute | solution.py:43
  72.1 1.5 %collective-permute-start.25 = (bf16[64,1792]{1,0:T(8,128)(2,1)S(1)}, bf16[64,1792]{1,0:T(8,128)(2,1)S(1)}, u32[]{:S(2)}, u32[]{:S(2)}) collective-permute-start(bf16[64,1792]{1,0:T(8,128)(2,1)S(1)} %get-tuple-element.122), channel_id=1, source_target_pairs={{0,8},{4,12},{8,0},{12,4},{16,24},{20,28},{24,16},{28,20},{1,9},{5... | collective-permute-start | bytes 688136 | tf_op jit(solution)/shard_map/ppermute | solution.py:43
  73.5 4.3 %down.6 = (bf16[128,1792]{1,0:T(8,128)(2,1)S(1)}, bf16[128,1792]{1,0:T(8,128)(2,1)S(1)}, bf16[2,512,1792]{2,1,0:T(8,128)(2,1)S(1)}, bf16[2,512,1792]{2,1,0:T(8,128)(2,1)S(1)}) custom-call(s32[1]{0:T(128)} %bitcast.me, bf16[256,2048]{1,0:T(8,128)(2,1)S(1)} %get-tuple-element.98.activation, bf16[2,512,1792]{2,1,0:T(8,128)(2,1)S(1)} %get-tuple-element.99.refs_0_, ...), custom_call_target="tpu_custom_call" | custom-call | flops 1879048192 | bytes 7340032 | tf_op jit(solution)/shard_map/down/pallas_call | solution.py:461
  77.9 2.7 %down.7 = (bf16[128,1792]{1,0:T(8,128)(2,1)S(1)}, bf16[128,1792]{1,0:T(8,128)(2,1)S(1)}) custom-call(s32[1]{0:T(128)} %bitcast.me, bf16[256,2048]{1,0:T(8,128)(2,1)S(1)} %get-tuple-element.98.activation, bf16[2,512,1792]{2,1,0:T(8,128)(2,1)S(1)} %get-tuple-element.101.refs_0_, bf16[2,512,1792]{2,1,0:T(8,128)(2,1)S(1)} %get-tuple-element.102.refs_1_), custom_call_target="tpu_custom_call" | custom-call | flops 1879048192 | bytes 7340032 | tf_op jit(solution)/shard_map/down/pallas_call | solution.py:461
  81.9 1.3 %collective-permute-start.27 = (bf16[32,1792]{1,0:T(8,128)(2,1)S(1)}, bf16[32,1792]{1,0:T(8,128)(2,1)S(1)}, u32[]{:S(2)}, u32[]{:S(2)}) collective-permute-start(bf16[32,1792]{1,0:T(8,128)(2,1)S(1)} %add_convert_fusion.17), channel_id=1, source_target_pairs={{0,16},{4,20},{8,24},{12,28},{16,0},{20,4},{24,8},{28,12},{1,17},{... | collective-permute-start | bytes 344072 | tf_op jit(solution)/shard_map/ppermute | solution.py:43
  83.3 0.8 collective-permute-start.29
  84.3 1.5 %collective-permute-start.31 = (bf16[64,1792]{1,0:T(8,128)(2,1)S(1)}, bf16[64,1792]{1,0:T(8,128)(2,1)S(1)}, u32[]{:S(2)}, u32[]{:S(2)}) collective-permute-start(bf16[64,1792]{1,0:T(8,128)(2,1)S(1)} %get-tuple-element.117), channel_id=1, source_target_pairs={{0,8},{4,12},{8,0},{12,4},{16,24},{20,28},{24,16},{28,20},{1,9},{5... | collective-permute-start | bytes 688136 | tf_op jit(solution)/shard_map/ppermute | solution.py:43
  86.4 1.0 collective-permute-start.26
  88.3 3.4 %collective-permute-done.29 = bf16[64,1792]{1,0:T(8,128)(2,1)S(1)} collective-permute-done((bf16[64,1792]{1,0:T(8,128)(2,1)S(1)}, bf16[64,1792]{1,0:T(8,128)(2,1)S(1)}, u32[]{:S(2)}, u32[]{:S(2)}) %collective-permute-start.29) | collective-permute-done | bytes 229408 | tf_op jit(solution)/shard_map/ppermute | solution.py:43
  91.7 1.5 %collective-permute-start.30 = (bf16[32,1792]{1,0:T(8,128)(2,1)S(1)}, bf16[32,1792]{1,0:T(8,128)(2,1)S(1)}, u32[]{:S(2)}, u32[]{:S(2)}) collective-permute-start(bf16[32,1792]{1,0:T(8,128)(2,1)S(1)} %add_convert_fusion.12), channel_id=1, source_target_pairs={{0,8},{4,12},{8,0},{12,4},{16,24},{20,28},{24,16},{28,20},{1,9},{5... | collective-permute-start | bytes 344072 | tf_op jit(solution)/shard_map/ppermute | solution.py:43
  93.2 0.8 collective-permute-start.33
  94.0 2.6 %collective-permute-done.30 = bf16[32,1792]{1,0:T(8,128)(2,1)S(1)} collective-permute-done((bf16[32,1792]{1,0:T(8,128)(2,1)S(1)}, bf16[32,1792]{1,0:T(8,128)(2,1)S(1)}, u32[]{:S(2)}, u32[]{:S(2)}) %collective-permute-start.30) | collective-permute-done | bytes 114720 | tf_op jit(solution)/shard_map/ppermute | solution.py:43
  97.0 1.4 %collective-permute-done.28 = bf16[32,1792]{1,0:T(8,128)(2,1)S(1)} collective-permute-done((bf16[32,1792]{1,0:T(8,128)(2,1)S(1)}, bf16[32,1792]{1,0:T(8,128)(2,1)S(1)}, u32[]{:S(2)}, u32[]{:S(2)}) %collective-permute-start.28) | collective-permute-done | bytes 114720 | tf_op jit(solution)/shard_map/ppermute | solution.py:43
  98.4 3.1 %collective-permute-done.32 = bf16[32,1792]{1,0:T(8,128)(2,1)S(1)} collective-permute-done((bf16[32,1792]{1,0:T(8,128)(2,1)S(1)}, bf16[32,1792]{1,0:T(8,128)(2,1)S(1)}, u32[]{:S(2)}, u32[]{:S(2)}) %collective-permute-start.32) | collective-permute-done | bytes 114720 | tf_op jit(solution)/shard_map/ppermute | solution.py:43
  (62 shorter events, 12.9 us)
Async XLA Ops:
  1.5 13.2 %collective-permute-start = (bf16[32,1920]{1,0:T(8,128)(2,1)S(1)}, bf16[32,1920]{1,0:T(8,128)(2,1)S(1)}, u32[]{:S(2)}, u32[]{:S(2)}) collective-permute-start(bf16[32,1920]{1,0:T(8,128)(2,1)S(1)} %get-tuple-element.66), channel_id=1, source_target_pairs={{0,1},{1,0},{2,3},{3,2},{4,5},{5,4},{6,7},{7,6},{8,9},{9,8},{10,11... | collective-permute-start | bytes 368648 | tf_op jit(solution)/shard_map/ppermute | solution.py:43
  4.6 12.3 %collective-permute-start.1 = (bf16[32,1920]{1,0:T(8,128)(2,1)S(1)}, bf16[32,1920]{1,0:T(8,128)(2,1)S(1)}, u32[]{:S(2)}, u32[]{:S(2)}) collective-permute-start(bf16[32,1920]{1,0:T(8,128)(2,1)S(1)} %get-tuple-element.67), channel_id=1, source_target_pairs={{0,2},{1,3},{2,0},{3,1},{4,6},{5,7},{6,4},{7,5},{8,10},{9,11},{10,... | collective-permute-start | bytes 368648 | tf_op jit(solution)/shard_map/ppermute | solution.py:43
  7.2 9.7 %collective-permute-start.2 = (bf16[32,1920]{1,0:T(8,128)(2,1)S(1)}, bf16[32,1920]{1,0:T(8,128)(2,1)S(1)}, u32[]{:S(2)}, u32[]{:S(2)}) collective-permute-start(bf16[32,1920]{1,0:T(8,128)(2,1)S(1)} %get-tuple-element.68), channel_id=1, source_target_pairs={{0,3},{1,2},{2,1},{3,0},{4,7},{5,6},{6,5},{7,4},{8,11},{9,10},{10,... | collective-permute-start | bytes 368648 | tf_op jit(solution)/shard_map/ppermute | solution.py:43
  17.2 4.9 %collective-permute-start.3 = (bf16[32,1920]{1,0:T(8,128)(2,1)S(1)}, bf16[32,1920]{1,0:T(8,128)(2,1)S(1)}, u32[]{:S(2)}, u32[]{:S(2)}) collective-permute-start(bf16[32,1920]{1,0:T(8,128)(2,1)S(1)} %get-tuple-element.71.refs_0_), channel_id=1, source_target_pairs={{0,1},{1,0},{2,3},{3,2},{4,5},{5,4},{6,7},{7,6},{8,9},{9,8},{10,11... | collective-permute-start | bytes 368648 | tf_op jit(solution)/shard_map/ppermute | solution.py:43
  22.2 12.1 %collective-permute-start.6 = (bf16[64,1920]{1,0:T(8,128)(2,1)S(1)}, bf16[64,1920]{1,0:T(8,128)(2,1)S(1)}, u32[]{:S(2)}, u32[]{:S(2)}) collective-permute-start(bf16[64,1920]{1,0:T(8,128)(2,1)S(1)} %join.1.refs_2_), channel_id=1, source_target_pairs={{0,2},{1,3},{2,0},{3,1},{4,6},{5,7},{6,4},{7,5},{8,10},{9,11},{10,... | collective-permute-start | bytes 737288 | tf_op jit(solution)/shard_map/ppermute | solution.py:43
  25.2 9.0 %collective-permute-start.10 = (bf16[64,1920]{1,0:T(8,128)(2,1)S(1)}, bf16[64,1920]{1,0:T(8,128)(2,1)S(1)}, u32[]{:S(2)}, u32[]{:S(2)}) collective-permute-start(bf16[64,1920]{1,0:T(8,128)(2,1)S(1)} %join.1.refs_2_), channel_id=1, source_target_pairs={{0,24},{4,28},{8,16},{12,20},{16,8},{20,12},{24,0},{28,4},{1,25},{... | collective-permute-start | bytes 737288 | tf_op jit(solution)/shard_map/ppermute | solution.py:43
  27.7 8.9 %collective-permute-start.8 = (bf16[64,1920]{1,0:T(8,128)(2,1)S(1)}, bf16[64,1920]{1,0:T(8,128)(2,1)S(1)}, u32[]{:S(2)}, u32[]{:S(2)}) collective-permute-start(bf16[64,1920]{1,0:T(8,128)(2,1)S(1)} %join.1.refs_2_), channel_id=1, source_target_pairs={{0,16},{4,20},{8,24},{12,28},{16,0},{20,4},{24,8},{28,12},{1,17},{... | collective-permute-start | bytes 737288 | tf_op jit(solution)/shard_map/ppermute | solution.py:43
  28.2 8.6 %collective-permute-start.5 = (bf16[64,1920]{1,0:T(8,128)(2,1)S(1)}, bf16[64,1920]{1,0:T(8,128)(2,1)S(1)}, u32[]{:S(2)}, u32[]{:S(2)}) collective-permute-start(bf16[64,1920]{1,0:T(8,128)(2,1)S(1)} %join.1.refs_2_), channel_id=1, source_target_pairs={{0,8},{4,12},{8,0},{12,4},{16,24},{20,28},{24,16},{28,20},{1,9},{5... | collective-permute-start | bytes 737288 | tf_op jit(solution)/shard_map/ppermute | solution.py:43
  28.7 10.1 %collective-permute-start.4 = (bf16[64,1920]{1,0:T(8,128)(2,1)S(1)}, bf16[64,1920]{1,0:T(8,128)(2,1)S(1)}, u32[]{:S(2)}, u32[]{:S(2)}) collective-permute-start(bf16[64,1920]{1,0:T(8,128)(2,1)S(1)} %join.1.refs_2_), channel_id=1, source_target_pairs={{0,4},{4,0},{8,12},{12,8},{16,20},{20,16},{24,28},{28,24},{1,5},{5... | collective-permute-start | bytes 737288 | tf_op jit(solution)/shard_map/ppermute | solution.py:43
  36.7 3.5 %collective-permute-start.7 = (bf16[64,1920]{1,0:T(8,128)(2,1)S(1)}, bf16[64,1920]{1,0:T(8,128)(2,1)S(1)}, u32[]{:S(2)}, u32[]{:S(2)}) collective-permute-start(bf16[64,1920]{1,0:T(8,128)(2,1)S(1)} %collective-permute-done.5.refs_4_), channel_id=1, source_target_pairs={{0,4},{4,0},{8,12},{12,8},{16,20},{20,16},{24,28},{28,24},{1,5},{5... | collective-permute-start | bytes 737288 | tf_op jit(solution)/shard_map/ppermute | solution.py:43
  36.8 4.0 %collective-permute-start.9 = (bf16[64,1920]{1,0:T(8,128)(2,1)S(1)}, bf16[64,1920]{1,0:T(8,128)(2,1)S(1)}, u32[]{:S(2)}, u32[]{:S(2)}) collective-permute-start(bf16[64,1920]{1,0:T(8,128)(2,1)S(1)} %collective-permute-done.8.refs_6_), channel_id=1, source_target_pairs={{0,4},{4,0},{8,12},{12,8},{16,20},{20,16},{24,28},{28,24},{1,5},{5... | collective-permute-start | bytes 737288 | tf_op jit(solution)/shard_map/ppermute | solution.py:43
  37.3 3.5 %collective-permute-start.11 = (bf16[64,1920]{1,0:T(8,128)(2,1)S(1)}, bf16[64,1920]{1,0:T(8,128)(2,1)S(1)}, u32[]{:S(2)}, u32[]{:S(2)}) collective-permute-start(bf16[64,1920]{1,0:T(8,128)(2,1)S(1)} %collective-permute-done.10.refs_8_), channel_id=1, source_target_pairs={{0,4},{4,0},{8,12},{12,8},{16,20},{20,16},{24,28},{28,24},{1,5},{5... | collective-permute-start | bytes 737288 | tf_op jit(solution)/shard_map/ppermute | solution.py:43
  37.3 13.5 %collective-permute-start.17 = (bf16[64,1920]{1,0:T(8,128)(2,1)S(1)}, bf16[64,1920]{1,0:T(8,128)(2,1)S(1)}, u32[]{:S(2)}, u32[]{:S(2)}) collective-permute-start(bf16[64,1920]{1,0:T(8,128)(2,1)S(1)} %collective-permute-done.6.refs_2_), channel_id=1, source_target_pairs={{0,24},{4,28},{8,16},{12,20},{16,8},{20,12},{24,0},{28,4},{1,25},{... | collective-permute-start | bytes 737288 | tf_op jit(solution)/shard_map/ppermute | solution.py:43
  38.9 12.9 %collective-permute-start.15 = (bf16[64,1920]{1,0:T(8,128)(2,1)S(1)}, bf16[64,1920]{1,0:T(8,128)(2,1)S(1)}, u32[]{:S(2)}, u32[]{:S(2)}) collective-permute-start(bf16[64,1920]{1,0:T(8,128)(2,1)S(1)} %collective-permute-done.6.refs_2_), channel_id=1, source_target_pairs={{0,16},{4,20},{8,24},{12,28},{16,0},{20,4},{24,8},{28,12},{1,17},{... | collective-permute-start | bytes 737288 | tf_op jit(solution)/shard_map/ppermute | solution.py:43
  40.2 11.6 %collective-permute-start.13 = (bf16[64,1920]{1,0:T(8,128)(2,1)S(1)}, bf16[64,1920]{1,0:T(8,128)(2,1)S(1)}, u32[]{:S(2)}, u32[]{:S(2)}) collective-permute-start(bf16[64,1920]{1,0:T(8,128)(2,1)S(1)} %collective-permute-done.6.refs_2_), channel_id=1, source_target_pairs={{0,8},{4,12},{8,0},{12,4},{16,24},{20,28},{24,16},{28,20},{1,9},{5... | collective-permute-start | bytes 737288 | tf_op jit(solution)/shard_map/ppermute | solution.py:43
  51.8 1.8 %collective-permute-start.14 = (bf16[64,1920]{1,0:T(8,128)(2,1)S(1)}, bf16[64,1920]{1,0:T(8,128)(2,1)S(1)}, u32[]{:S(2)}, u32[]{:S(2)}) collective-permute-start(bf16[64,1920]{1,0:T(8,128)(2,1)S(1)} %collective-permute-done.13.refs_4_), channel_id=1, source_target_pairs={{0,4},{4,0},{8,12},{12,8},{16,20},{20,16},{24,28},{28,24},{1,5},{5... | collective-permute-start | bytes 737288 | tf_op jit(solution)/shard_map/ppermute | solution.py:43
  52.4 2.0 %collective-permute-start.18 = (bf16[64,1920]{1,0:T(8,128)(2,1)S(1)}, bf16[64,1920]{1,0:T(8,128)(2,1)S(1)}, u32[]{:S(2)}, u32[]{:S(2)}) collective-permute-start(bf16[64,1920]{1,0:T(8,128)(2,1)S(1)} %collective-permute-done.17.refs_8_), channel_id=1, source_target_pairs={{0,4},{4,0},{8,12},{12,8},{16,20},{20,16},{24,28},{28,24},{1,5},{5... | collective-permute-start | bytes 737288 | tf_op jit(solution)/shard_map/ppermute | solution.py:43
  66.6 3.8 %collective-permute-start.19 = (bf16[128,1792]{1,0:T(8,128)(2,1)S(1)}, bf16[128,1792]{1,0:T(8,128)(2,1)S(1)}, u32[]{:S(2)}, u32[]{:S(2)}) collective-permute-start(bf16[128,1792]{1,0:T(8,128)(2,1)S(1)} %get-tuple-element.90), channel_id=1, source_target_pairs={{0,4},{4,0},{8,12},{12,8},{16,20},{20,16},{24,28},{28,24},{1,5},{5... | collective-permute-start | bytes 1376264 | tf_op jit(solution)/shard_map/ppermute | solution.py:43
  70.0 2.0 %collective-permute-start.21 = (bf16[128,1792]{1,0:T(8,128)(2,1)S(1)}, bf16[128,1792]{1,0:T(8,128)(2,1)S(1)}, u32[]{:S(2)}, u32[]{:S(2)}) collective-permute-start(bf16[128,1792]{1,0:T(8,128)(2,1)S(1)} %get-tuple-element.94), channel_id=1, source_target_pairs={{0,4},{4,0},{8,12},{12,8},{16,20},{20,16},{24,28},{28,24},{1,5},{5... | collective-permute-start | bytes 1376264 | tf_op jit(solution)/shard_map/ppermute | solution.py:43
  70.5 10.6 %collective-permute-start.20 = (bf16[64,1792]{1,0:T(8,128)(2,1)S(1)}, bf16[64,1792]{1,0:T(8,128)(2,1)S(1)}, u32[]{:S(2)}, u32[]{:S(2)}) collective-permute-start(bf16[64,1792]{1,0:T(8,128)(2,1)S(1)} %get-tuple-element.120), channel_id=1, source_target_pairs={{0,16},{4,20},{8,24},{12,28},{16,0},{20,4},{24,8},{28,12},{1,17},{... | collective-permute-start | bytes 688136 | tf_op jit(solution)/shard_map/ppermute | solution.py:43
  72.1 9.8 %collective-permute-start.25 = (bf16[64,1792]{1,0:T(8,128)(2,1)S(1)}, bf16[64,1792]{1,0:T(8,128)(2,1)S(1)}, u32[]{:S(2)}, u32[]{:S(2)}) collective-permute-start(bf16[64,1792]{1,0:T(8,128)(2,1)S(1)} %get-tuple-element.122), channel_id=1, source_target_pairs={{0,8},{4,12},{8,0},{12,4},{16,24},{20,28},{24,16},{28,20},{1,9},{5... | collective-permute-start | bytes 688136 | tf_op jit(solution)/shard_map/ppermute | solution.py:43
  80.5 3.6 %collective-permute-start.23 = (bf16[128,1792]{1,0:T(8,128)(2,1)S(1)}, bf16[128,1792]{1,0:T(8,128)(2,1)S(1)}, u32[]{:S(2)}, u32[]{:S(2)}) collective-permute-start(bf16[128,1792]{1,0:T(8,128)(2,1)S(1)} %get-tuple-element.104), channel_id=1, source_target_pairs={{0,4},{4,0},{8,12},{12,8},{16,20},{20,16},{24,28},{28,24},{1,5},{5... | collective-permute-start | bytes 1376264 | tf_op jit(solution)/shard_map/ppermute | solution.py:43
  80.7 2.6 %collective-permute-start.24 = (bf16[128,1792]{1,0:T(8,128)(2,1)S(1)}, bf16[128,1792]{1,0:T(8,128)(2,1)S(1)}, u32[]{:S(2)}, u32[]{:S(2)}) collective-permute-start(bf16[128,1792]{1,0:T(8,128)(2,1)S(1)} %get-tuple-element.106), channel_id=1, source_target_pairs={{0,4},{4,0},{8,12},{12,8},{16,20},{20,16},{24,28},{28,24},{1,5},{5... | collective-permute-start | bytes 1376264 | tf_op jit(solution)/shard_map/ppermute | solution.py:43
  81.1 5.2 %collective-permute-start.22 = (bf16[32,1792]{1,0:T(8,128)(2,1)S(1)}, bf16[32,1792]{1,0:T(8,128)(2,1)S(1)}, u32[]{:S(2)}, u32[]{:S(2)}) collective-permute-start(bf16[32,1792]{1,0:T(8,128)(2,1)S(1)} %add_convert_fusion.18), channel_id=1, source_target_pairs={{0,8},{4,12},{8,0},{12,4},{16,24},{20,28},{24,16},{28,20},{1,9},{5... | collective-permute-start | bytes 344072 | tf_op jit(solution)/shard_map/ppermute | solution.py:43
  81.9 5.8 %collective-permute-start.27 = (bf16[32,1792]{1,0:T(8,128)(2,1)S(1)}, bf16[32,1792]{1,0:T(8,128)(2,1)S(1)}, u32[]{:S(2)}, u32[]{:S(2)}) collective-permute-start(bf16[32,1792]{1,0:T(8,128)(2,1)S(1)} %add_convert_fusion.17), channel_id=1, source_target_pairs={{0,16},{4,20},{8,24},{12,28},{16,0},{20,4},{24,8},{28,12},{1,17},{... | collective-permute-start | bytes 344072 | tf_op jit(solution)/shard_map/ppermute | solution.py:43
  83.3 8.4 %collective-permute-start.29 = (bf16[64,1792]{1,0:T(8,128)(2,1)S(1)}, bf16[64,1792]{1,0:T(8,128)(2,1)S(1)}, u32[]{:S(2)}, u32[]{:S(2)}) collective-permute-start(bf16[64,1792]{1,0:T(8,128)(2,1)S(1)} %get-tuple-element.116), channel_id=1, source_target_pairs={{0,16},{4,20},{8,24},{12,28},{16,0},{20,4},{24,8},{28,12},{1,17},{... | collective-permute-start | bytes 688136 | tf_op jit(solution)/shard_map/ppermute | solution.py:43
  84.3 8.9 %collective-permute-start.31 = (bf16[64,1792]{1,0:T(8,128)(2,1)S(1)}, bf16[64,1792]{1,0:T(8,128)(2,1)S(1)}, u32[]{:S(2)}, u32[]{:S(2)}) collective-permute-start(bf16[64,1792]{1,0:T(8,128)(2,1)S(1)} %get-tuple-element.117), channel_id=1, source_target_pairs={{0,8},{4,12},{8,0},{12,4},{16,24},{20,28},{24,16},{28,20},{1,9},{5... | collective-permute-start | bytes 688136 | tf_op jit(solution)/shard_map/ppermute | solution.py:43
  86.4 12.1 %collective-permute-start.26 = (bf16[32,1792]{1,0:T(8,128)(2,1)S(1)}, bf16[32,1792]{1,0:T(8,128)(2,1)S(1)}, u32[]{:S(2)}, u32[]{:S(2)}) collective-permute-start(bf16[32,1792]{1,0:T(8,128)(2,1)S(1)} %add_convert_fusion.16), channel_id=1, source_target_pairs={{0,3},{1,2},{2,1},{3,0},{4,7},{5,6},{6,5},{7,4},{8,11},{9,10},{10,... | collective-permute-start | bytes 344072 | tf_op jit(solution)/shard_map/ppermute | solution.py:43
  87.7 10.7 %collective-permute-start.28 = (bf16[32,1792]{1,0:T(8,128)(2,1)S(1)}, bf16[32,1792]{1,0:T(8,128)(2,1)S(1)}, u32[]{:S(2)}, u32[]{:S(2)}) collective-permute-start(bf16[32,1792]{1,0:T(8,128)(2,1)S(1)} %add_convert_fusion.14), channel_id=1, source_target_pairs={{0,2},{1,3},{2,0},{3,1},{4,6},{5,7},{6,4},{7,5},{8,10},{9,11},{10,... | collective-permute-start | bytes 344072 | tf_op jit(solution)/shard_map/ppermute | solution.py:43
  91.7 4.9 %collective-permute-start.30 = (bf16[32,1792]{1,0:T(8,128)(2,1)S(1)}, bf16[32,1792]{1,0:T(8,128)(2,1)S(1)}, u32[]{:S(2)}, u32[]{:S(2)}) collective-permute-start(bf16[32,1792]{1,0:T(8,128)(2,1)S(1)} %add_convert_fusion.12), channel_id=1, source_target_pairs={{0,8},{4,12},{8,0},{12,4},{16,24},{20,28},{24,16},{28,20},{1,9},{5... | collective-permute-start | bytes 344072 | tf_op jit(solution)/shard_map/ppermute | solution.py:43
  93.2 5.2 %collective-permute-start.33 = (bf16[32,1792]{1,0:T(8,128)(2,1)S(1)}, bf16[32,1792]{1,0:T(8,128)(2,1)S(1)}, u32[]{:S(2)}, u32[]{:S(2)}) collective-permute-start(bf16[32,1792]{1,0:T(8,128)(2,1)S(1)} %add_convert_fusion.11), channel_id=1, source_target_pairs={{0,16},{4,20},{8,24},{12,28},{16,0},{20,4},{24,8},{28,12},{1,17},{... | collective-permute-start | bytes 344072 | tf_op jit(solution)/shard_map/ppermute | solution.py:43
  96.6 4.9 %collective-permute-start.32 = (bf16[32,1792]{1,0:T(8,128)(2,1)S(1)}, bf16[32,1792]{1,0:T(8,128)(2,1)S(1)}, u32[]{:S(2)}, u32[]{:S(2)}) collective-permute-start(bf16[32,1792]{1,0:T(8,128)(2,1)S(1)} %add_convert_fusion.10), channel_id=1, source_target_pairs={{0,1},{1,0},{2,3},{3,2},{4,5},{5,4},{6,7},{7,6},{8,9},{9,8},{10,11... | collective-permute-start | bytes 344072 | tf_op jit(solution)/shard_map/ppermute | solution.py:43
  (2 other events, 3.2 us)

commit v8 on v7

--- a/solution.py
+++ b/solution.py
@@ -445,10 +445,11 @@
     events = [(0, None)]
     for j in range(1, tp_count):
         events += [(j, None)] + ([(j - 1, 0)] if j < tp_count - 1 else [])
-    for turn in range(stages):
-        for j in range(tp_count):
-            stage = turn + (1 if j < tp_count - 2 else 0)
-            events += [(j, stage)] if stage < stages else []
+    near = tp_count - 2
+    for stage in range(1, stages):
+        events += [(j, stage) for j in range(near)]
+        events += [(near, 0)] if stage == 1 else []
+    events += [(near + 1, 0), (near, stages - 1), (near + 1, stages - 1)]
     mine, theirs, opened, done = {}, {}, [], []
     for j, stage in events:
         k = places[j]
@@ -479,17 +480,25 @@
             held_down.update(zip(ahead, found))
             mine[k], theirs[k] = keep, swap(send, "exp", core)
         elif stage < stages - 1:
-            middle = mine[k].shape[0] // 2
             got = after(theirs[k], *opened[-1:])
-            away = add(mine[k][middle:], got[middle:])
-            opened.append(away)
-            mine[k], theirs[k] = add(mine[k][:middle], got[:middle]), swap(away, "exp", order[stage])
-        elif k:
-            away = add(mine[k], after(theirs[k], *opened[-1:]))
-            opened.append(away)
-            done.append(swap(away, "tp", k))
+            if j < near:
+                middle = mine[k].shape[0] // 2
+                away = [add(mine[k][middle:], got[middle:])]
+                mine[k], theirs[k] = add(mine[k][:middle], got[:middle]), swap(away[0], "exp", order[stage])
+            else:
+                sums = [add(mine[k][i : i + rows], got[i : i + rows]) for i in range(0, got.shape[0], rows)]
+                mine[k], away = sums[0], sums[1:]
+                theirs[k] = [swap(part, "exp", pattern) for part, pattern in zip(away, relative_order(order)[1:])]
+            opened.append(away[-1])
         else:
-            done += [mine[k], theirs[k]]
+            last, *others = theirs[k] if j >= near else [theirs[k]]
+            parts = [mine[k], after(last, *opened[-1:]), *others]
+            if k:
+                away = functools.reduce(sum_of, parts).astype(BF16)
+                opened.append(away)
+                done.append(swap(away, "tp", k))
+            else:
+                done += parts
     return functools.reduce(sum_of, [projected] + done).astype(BF16)
 
 

time: 103 us -> 109 us (1.058)
  starting transfers between devices: 31.9 us -> 37 us
    ppermute x34 -> x36, starting transfers between devices: 31.9 us -> 37 us  [swap(): return lax.ppermute(value, axis, [(i, i ^ bit) for i in range(count)])]
    ppermute x34 -> x36, waiting for transfers between devices: 21.9 us -> 22.8 us  [swap(): return lax.ppermute(value, axis, [(i, i ^ bit) for i in range(count)])]
  transfers between devices with their start and end apart: 34 -> 36, of which waited for: 16 -> 16; matrix products, arithmetic and copies ran while one was open for 3% -> 3% of each run, Pallas kernels for 30% -> 28%
where the time goes in v8:
time: 109 us; the launch traced here: 108 us
  Pallas kernels  44.7 us (41%)
  starting transfers between devices  37 us (34%)
  waiting for transfers between devices  22.8 us (21%)
  local copies, waits for them, and re-layouts  2.22 us (2%)
  other arithmetic  1.38 us (1%)
    ppermute x36, starting transfers between devices, swap(): return lax.ppermute(value, axis, [(i, i ^ bit) for i in range(count)])  37 us
    ppermute x36, waiting for transfers between devices, swap(): return lax.ppermute(value, axis, [(i, i ^ bit) for i in range(count)])  22.8 us
    pallas_call x2, Pallas kernels, local(): pl.pallas_call(functools.partial(up_kernel, start, last, held, late, refi...  18.9 us
    pallas_call x4, Pallas kernels, local(): pl.pallas_call(functools.partial(down_kernel, relative_order([core] + ord...  13.4 us
    pallas_call x2, Pallas kernels, load(): pl.pallas_call(load_kernel, out_shape=pltpu.VMEM((local_experts, 2 * cols...  10.6 us
  transfers between devices with their start and end apart: 36, of which 16 were waited for; matrix products, arithmetic and copies ran while one was open for 3% of the time, Pallas kernels for 28%

profile of v8, /device:TPU:0, one launch (start us, length us, event | category | flops | bytes accessed | tf_op | source)
XLA Modules:
  0.0 108.3 jit_solution(4703297926480710409)
XLA Ops:
  0.0 1.5 %cut_heads.1 = (bf16[32,1920]{1,0:T(8,128)(2,1)S(1)}, bf16[32,1920]{1,0:T(8,128)(2,1)S(1)}, bf16[32,1920]{1,0:T(8,128)(2,1)S(1)}, f32[32,1792]{1,0:T(8,128)S(1)}...) custom-call(s32[1]{0:T(128)} %bitcast.me, bf16[32,7168]{1,0:T(8,128)(2,1)} %bitcast.4, bf16[32,1792]{1,0:T(8,128)(2,1)} %resid_hbm.1, ...), custom_call_target="tpu_custom_call" | custom-call | tf_op jit(solution)/shard_map/cut_heads/pallas_call | solution.py:316
  1.5 3.1 %collective-permute-start = (bf16[32,1920]{1,0:T(8,128)(2,1)S(1)}, bf16[32,1920]{1,0:T(8,128)(2,1)S(1)}, u32[]{:S(2)}, u32[]{:S(2)}) collective-permute-start(bf16[32,1920]{1,0:T(8,128)(2,1)S(1)} %get-tuple-element.65), channel_id=1, source_target_pairs={{0,1},{1,0},{2,3},{3,2},{4,5},{5,4},{6,7},{7,6},{8,9},{9,8},{10,11... | collective-permute-start | bytes 368648 | tf_op jit(solution)/shard_map/ppermute | solution.py:43
  4.6 2.6 %collective-permute-start.1 = (bf16[32,1920]{1,0:T(8,128)(2,1)S(1)}, bf16[32,1920]{1,0:T(8,128)(2,1)S(1)}, u32[]{:S(2)}, u32[]{:S(2)}) collective-permute-start(bf16[32,1920]{1,0:T(8,128)(2,1)S(1)} %get-tuple-element.66), channel_id=1, source_target_pairs={{0,2},{1,3},{2,0},{3,1},{4,6},{5,7},{6,4},{7,5},{8,10},{9,11},{10,... | collective-permute-start | bytes 368648 | tf_op jit(solution)/shard_map/ppermute | solution.py:43
  9.4 5.3 %load_rows.2.refs_0_ = bf16[4,3584,512]{2,1,0:T(8,128)(2,1)S(1)} custom-call(s32[1]{0:T(128)} %bitcast.me, bf16[4,7168,512]{2,1,0:T(8,128)(2,1)} %gate_hbm.3), custom_call_target="tpu_custom_call" | custom-call | bytes 14680064 | tf_op jit(solution)/shard_map/load_rows/pallas_call | solution.py:334
  14.7 2.2 %collective-permute-done.1.refs_1_ = bf16[32,1920]{1,0:T(8,128)(2,1)S(1)} collective-permute-done((bf16[32,1920]{1,0:T(8,128)(2,1)S(1)}, bf16[32,1920]{1,0:T(8,128)(2,1)S(1)}, u32[]{:S(2)}, u32[]{:S(2)}) %collective-permute-start.1) | collective-permute-done | bytes 122912 | tf_op jit(solution)/shard_map/ppermute | solution.py:43
  17.2 1.9 %collective-permute-start.3 = (bf16[32,1920]{1,0:T(8,128)(2,1)S(1)}, bf16[32,1920]{1,0:T(8,128)(2,1)S(1)}, u32[]{:S(2)}, u32[]{:S(2)}) collective-permute-start(bf16[32,1920]{1,0:T(8,128)(2,1)S(1)} %get-tuple-element.70.refs_0_), channel_id=1, source_target_pairs={{0,1},{1,0},{2,3},{3,2},{4,5},{5,4},{6,7},{7,6},{8,9},{9,8},{10,11... | collective-permute-start | bytes 368648 | tf_op jit(solution)/shard_map/ppermute | solution.py:43
  19.1 3.0 %collective-permute-done.3.refs_1_ = bf16[32,1920]{1,0:T(8,128)(2,1)S(1)} collective-permute-done((bf16[32,1920]{1,0:T(8,128)(2,1)S(1)}, bf16[32,1920]{1,0:T(8,128)(2,1)S(1)}, u32[]{:S(2)}, u32[]{:S(2)}) %collective-permute-start.3) | collective-permute-done | bytes 122912 | tf_op jit(solution)/shard_map/ppermute | solution.py:43
  22.2 3.1 %collective-permute-start.6 = (bf16[64,1920]{1,0:T(8,128)(2,1)S(1)}, bf16[64,1920]{1,0:T(8,128)(2,1)S(1)}, u32[]{:S(2)}, u32[]{:S(2)}) collective-permute-start(bf16[64,1920]{1,0:T(8,128)(2,1)S(1)} %join.1.refs_2_), channel_id=1, source_target_pairs={{0,2},{1,3},{2,0},{3,1},{4,6},{5,7},{6,4},{7,5},{8,10},{9,11},{10,... | collective-permute-start | bytes 737288 | tf_op jit(solution)/shard_map/ppermute | solution.py:43
  25.2 2.4 %collective-permute-start.10 = (bf16[64,1920]{1,0:T(8,128)(2,1)S(1)}, bf16[64,1920]{1,0:T(8,128)(2,1)S(1)}, u32[]{:S(2)}, u32[]{:S(2)}) collective-permute-start(bf16[64,1920]{1,0:T(8,128)(2,1)S(1)} %join.1.refs_2_), channel_id=1, source_target_pairs={{0,24},{4,28},{8,16},{12,20},{16,8},{20,12},{24,0},{28,4},{1,25},{... | collective-permute-start | bytes 737288 | tf_op jit(solution)/shard_map/ppermute | solution.py:43
  28.7 5.3 %load_rows.3.refs_1_ = bf16[4,3584,512]{2,1,0:T(8,128)(2,1)S(1)} custom-call(s32[1]{0:T(128)} %bitcast.me, bf16[4,7168,512]{2,1,0:T(8,128)(2,1)} %up_hbm.3), custom_call_target="tpu_custom_call" | custom-call | bytes 14680064 | tf_op jit(solution)/shard_map/load_rows/pallas_call | solution.py:334
  34.2 2.4 %collective-permute-done.8.refs_6_ = bf16[64,1920]{1,0:T(8,128)(2,1)S(1)} collective-permute-done((bf16[64,1920]{1,0:T(8,128)(2,1)S(1)}, bf16[64,1920]{1,0:T(8,128)(2,1)S(1)}, u32[]{:S(2)}, u32[]{:S(2)}) %collective-permute-start.8) | collective-permute-done | bytes 245792 | tf_op jit(solution)/shard_map/ppermute | solution.py:43
  37.3 1.6 %collective-permute-start.17 = (bf16[64,1920]{1,0:T(8,128)(2,1)S(1)}, bf16[64,1920]{1,0:T(8,128)(2,1)S(1)}, u32[]{:S(2)}, u32[]{:S(2)}) collective-permute-start(bf16[64,1920]{1,0:T(8,128)(2,1)S(1)} %collective-permute-done.6.refs_2_), channel_id=1, source_target_pairs={{0,24},{4,28},{8,16},{12,20},{16,8},{20,12},{24,0},{28,4},{1,25},{... | collective-permute-start | bytes 737288 | tf_op jit(solution)/shard_map/ppermute | solution.py:43
  38.9 1.3 %collective-permute-start.15 = (bf16[64,1920]{1,0:T(8,128)(2,1)S(1)}, bf16[64,1920]{1,0:T(8,128)(2,1)S(1)}, u32[]{:S(2)}, u32[]{:S(2)}) collective-permute-start(bf16[64,1920]{1,0:T(8,128)(2,1)S(1)} %collective-permute-done.6.refs_2_), channel_id=1, source_target_pairs={{0,16},{4,20},{8,24},{12,28},{16,0},{20,4},{24,8},{28,12},{1,17},{... | collective-permute-start | bytes 737288 | tf_op jit(solution)/shard_map/ppermute | solution.py:43
  40.8 9.9 %gate_up.2 = (f32[4,256,512]{2,1,0:T(8,128)S(1)}, f32[4,256,512]{2,1,0:T(8,128)S(1)}, f32[256,128]{1,0:T(8,128)S(1)}, bf16[4,3584,512]{2,1,0:T(8,128)(2,1)S(1)},...) custom-call(s32[1]{0:T(128)} %bitcast.me, ...), custom_call_target="tpu_custom_call", output_to_operand_aliasing={{3}: (5, {}), {4}: (6, {})} | custom-call | flops 7516192768 | bytes 29360128 | tf_op jit(solution)/shard_map/gate_up/pallas_call | solution.py:410
  50.7 1.1 collective-permute-done.15.refs_6_
  54.4 9.0 %gate_up.3 = (bf16[256,2048]{1,0:T(8,128)(2,1)S(1)}, bf16[4,3584,512]{2,1,0:T(8,128)(2,1)S(1)}, bf16[4,3584,512]{2,1,0:T(8,128)(2,1)S(1)}, bf16[2,512,1792]{2,1,0:T(8,128)(2,1)S(1)}, bf16[2,512,1792]{2,1,0:T(8,128)(2,1)S(1)}) custom-call(s32[1]{0:T(128)} %bitcast.me, s32[1]{0:T(128)} %bitcast.1.first, ...), custom_call_target="tpu_custom_call", output_to_operand_aliasing={{1}: (5, {}), {2}: (6, {})} | custom-call | flops 7516192768 | bytes 29360128 | tf_op jit(solution)/shard_map/gate_up/pallas_call | solution.py:410
  63.3 3.2 %down.4 = (bf16[128,1792]{1,0:T(8,128)(2,1)S(1)}, bf16[128,1792]{1,0:T(8,128)(2,1)S(1)}, bf16[2,512,1792]{2,1,0:T(8,128)(2,1)S(1)}) custom-call(s32[1]{0:T(128)} %bitcast.me, bf16[256,2048]{1,0:T(8,128)(2,1)S(1)} %get-tuple-element.96.activation, bf16[2,512,1792]{2,1,0:T(8,128)(2,1)S(1)} %get-tuple-element.86.refs_0_, ...), custom_call_target="tpu_custom_call" | custom-call | flops 1879048192 | bytes 7340032 | tf_op jit(solution)/shard_map/down/pallas_call | solution.py:462
  66.8 3.2 %down.5 = (bf16[128,1792]{1,0:T(8,128)(2,1)S(1)}, bf16[128,1792]{1,0:T(8,128)(2,1)S(1)}, bf16[2,512,1792]{2,1,0:T(8,128)(2,1)S(1)}) custom-call(s32[1]{0:T(128)} %bitcast.me, bf16[256,2048]{1,0:T(8,128)(2,1)S(1)} %get-tuple-element.96.activation, bf16[2,512,1792]{2,1,0:T(8,128)(2,1)S(1)} %get-tuple-element.90.refs_0_, ...), custom_call_target="tpu_custom_call" | custom-call | flops 1879048192 | bytes 7340032 | tf_op jit(solution)/shard_map/down/pallas_call | solution.py:462
  70.5 1.4 %collective-permute-start.20 = (bf16[64,1792]{1,0:T(8,128)(2,1)S(1)}, bf16[64,1792]{1,0:T(8,128)(2,1)S(1)}, u32[]{:S(2)}, u32[]{:S(2)}) collective-permute-start(bf16[64,1792]{1,0:T(8,128)(2,1)S(1)} %get-tuple-element.120), channel_id=1, source_target_pairs={{0,16},{4,20},{8,24},{12,28},{16,0},{20,4},{24,8},{28,12},{1,17},{... | collective-permute-start | bytes 688136 | tf_op jit(solution)/shard_map/ppermute | solution.py:43
  72.1 1.5 %collective-permute-start.24 = (bf16[64,1792]{1,0:T(8,128)(2,1)S(1)}, bf16[64,1792]{1,0:T(8,128)(2,1)S(1)}, u32[]{:S(2)}, u32[]{:S(2)}) collective-permute-start(bf16[64,1792]{1,0:T(8,128)(2,1)S(1)} %get-tuple-element.122), channel_id=1, source_target_pairs={{0,8},{4,12},{8,0},{12,4},{16,24},{20,28},{24,16},{28,20},{1,9},{5... | collective-permute-start | bytes 688136 | tf_op jit(solution)/shard_map/ppermute | solution.py:43
  73.5 4.3 %down.6 = (bf16[128,1792]{1,0:T(8,128)(2,1)S(1)}, bf16[128,1792]{1,0:T(8,128)(2,1)S(1)}, bf16[2,512,1792]{2,1,0:T(8,128)(2,1)S(1)}, bf16[2,512,1792]{2,1,0:T(8,128)(2,1)S(1)}) custom-call(s32[1]{0:T(128)} %bitcast.me, bf16[256,2048]{1,0:T(8,128)(2,1)S(1)} %get-tuple-element.96.activation, bf16[2,512,1792]{2,1,0:T(8,128)(2,1)S(1)} %get-tuple-element.97.refs_0_, ...), custom_call_target="tpu_custom_call" | custom-call | flops 1879048192 | bytes 7340032 | tf_op jit(solution)/shard_map/down/pallas_call | solution.py:462
  77.9 2.7 %down.7 = (bf16[128,1792]{1,0:T(8,128)(2,1)S(1)}, bf16[128,1792]{1,0:T(8,128)(2,1)S(1)}) custom-call(s32[1]{0:T(128)} %bitcast.me, bf16[256,2048]{1,0:T(8,128)(2,1)S(1)} %get-tuple-element.96.activation, bf16[2,512,1792]{2,1,0:T(8,128)(2,1)S(1)} %get-tuple-element.106.refs_0_, bf16[2,512,1792]{2,1,0:T(8,128)(2,1)S(1)} %get-tuple-element.107.refs_1_), custom_call_target="tpu_custom_call" | custom-call | flops 1879048192 | bytes 7340032 | tf_op jit(solution)/shard_map/down/pallas_call | solution.py:462
  81.9 1.3 %collective-permute-start.26 = (bf16[32,1792]{1,0:T(8,128)(2,1)S(1)}, bf16[32,1792]{1,0:T(8,128)(2,1)S(1)}, u32[]{:S(2)}, u32[]{:S(2)}) collective-permute-start(bf16[32,1792]{1,0:T(8,128)(2,1)S(1)} %add_convert_fusion.17), channel_id=1, source_target_pairs={{0,16},{4,20},{8,24},{12,28},{16,0},{20,4},{24,8},{28,12},{1,17},{... | collective-permute-start | bytes 344072 | tf_op jit(solution)/shard_map/ppermute | solution.py:43
  83.3 1.6 %collective-permute-start.31 = (bf16[32,1792]{1,0:T(8,128)(2,1)S(1)}, bf16[32,1792]{1,0:T(8,128)(2,1)S(1)}, u32[]{:S(2)}, u32[]{:S(2)}) collective-permute-start(bf16[32,1792]{1,0:T(8,128)(2,1)S(1)} %get-tuple-element.115), channel_id=1, source_target_pairs={{0,24},{4,28},{8,16},{12,20},{16,8},{20,12},{24,0},{28,4},{1,25},{... | collective-permute-start | bytes 344072 | tf_op jit(solution)/shard_map/ppermute | solution.py:43
  84.9 1.5 %collective-permute-done.22 = bf16[32,1792]{1,0:T(8,128)(2,1)S(1)} collective-permute-done((bf16[32,1792]{1,0:T(8,128)(2,1)S(1)}, bf16[32,1792]{1,0:T(8,128)(2,1)S(1)}, u32[]{:S(2)}, u32[]{:S(2)}) %collective-permute-start.22) | collective-permute-done | bytes 114720 | tf_op jit(solution)/shard_map/ppermute | solution.py:43
  86.5 1.0 collective-permute-start.25
  88.5 2.5 %collective-permute-start.28 = (bf16[32,1792]{1,0:T(8,128)(2,1)S(1)}, bf16[32,1792]{1,0:T(8,128)(2,1)S(1)}, u32[]{:S(2)}, u32[]{:S(2)}) collective-permute-start(bf16[32,1792]{1,0:T(8,128)(2,1)S(1)} %get-tuple-element.113), channel_id=1, source_target_pairs={{0,8},{4,12},{8,0},{12,4},{16,24},{20,28},{24,16},{28,20},{1,9},{5... | collective-permute-start | bytes 344072 | tf_op jit(solution)/shard_map/ppermute | solution.py:43
  91.9 2.7 %collective-permute-done.28 = bf16[32,1792]{1,0:T(8,128)(2,1)S(1)} collective-permute-done((bf16[32,1792]{1,0:T(8,128)(2,1)S(1)}, bf16[32,1792]{1,0:T(8,128)(2,1)S(1)}, u32[]{:S(2)}, u32[]{:S(2)}) %collective-permute-start.28) | collective-permute-done | bytes 114720 | tf_op jit(solution)/shard_map/ppermute | solution.py:43
  94.6 2.7 %collective-permute-start.35 = (bf16[32,1792]{1,0:T(8,128)(2,1)S(1)}, bf16[32,1792]{1,0:T(8,128)(2,1)S(1)}, u32[]{:S(2)}, u32[]{:S(2)}) collective-permute-start(bf16[32,1792]{1,0:T(8,128)(2,1)S(1)} %get-tuple-element.118), channel_id=1, source_target_pairs={{0,24},{4,28},{8,16},{12,20},{16,8},{20,12},{24,0},{28,4},{1,25},{... | collective-permute-start | bytes 344072 | tf_op jit(solution)/shard_map/ppermute | solution.py:43
  98.7 1.3 %collective-permute-start.34 = (bf16[32,1792]{1,0:T(8,128)(2,1)S(1)}, bf16[32,1792]{1,0:T(8,128)(2,1)S(1)}, u32[]{:S(2)}, u32[]{:S(2)}) collective-permute-start(bf16[32,1792]{1,0:T(8,128)(2,1)S(1)} %get-tuple-element.117), channel_id=1, source_target_pairs={{0,8},{4,12},{8,0},{12,4},{16,24},{20,28},{24,16},{28,20},{1,9},{5... | collective-permute-start | bytes 344072 | tf_op jit(solution)/shard_map/ppermute | solution.py:43
  100.0 2.7 %collective-permute-done.33 = bf16[32,1792]{1,0:T(8,128)(2,1)S(1)} collective-permute-done((bf16[32,1792]{1,0:T(8,128)(2,1)S(1)}, bf16[32,1792]{1,0:T(8,128)(2,1)S(1)}, u32[]{:S(2)}, u32[]{:S(2)}) %collective-permute-start.33) | collective-permute-done | bytes 114720 | tf_op jit(solution)/shard_map/ppermute | solution.py:43
  103.5 4.0 %collective-permute-done.32 = bf16[32,1792]{1,0:T(8,128)(2,1)S(1)} collective-permute-done((bf16[32,1792]{1,0:T(8,128)(2,1)S(1)}, bf16[32,1792]{1,0:T(8,128)(2,1)S(1)}, u32[]{:S(2)}, u32[]{:S(2)}) %collective-permute-start.32) | collective-permute-done | bytes 114720 | tf_op jit(solution)/shard_map/ppermute | solution.py:43
  (64 shorter events, 14.8 us)
Async XLA Ops:
  1.5 13.2 %collective-permute-start = (bf16[32,1920]{1,0:T(8,128)(2,1)S(1)}, bf16[32,1920]{1,0:T(8,128)(2,1)S(1)}, u32[]{:S(2)}, u32[]{:S(2)}) collective-permute-start(bf16[32,1920]{1,0:T(8,128)(2,1)S(1)} %get-tuple-element.65), channel_id=1, source_target_pairs={{0,1},{1,0},{2,3},{3,2},{4,5},{5,4},{6,7},{7,6},{8,9},{9,8},{10,11... | collective-permute-start | bytes 368648 | tf_op jit(solution)/shard_map/ppermute | solution.py:43
  4.6 12.3 %collective-permute-start.1 = (bf16[32,1920]{1,0:T(8,128)(2,1)S(1)}, bf16[32,1920]{1,0:T(8,128)(2,1)S(1)}, u32[]{:S(2)}, u32[]{:S(2)}) collective-permute-start(bf16[32,1920]{1,0:T(8,128)(2,1)S(1)} %get-tuple-element.66), channel_id=1, source_target_pairs={{0,2},{1,3},{2,0},{3,1},{4,6},{5,7},{6,4},{7,5},{8,10},{9,11},{10,... | collective-permute-start | bytes 368648 | tf_op jit(solution)/shard_map/ppermute | solution.py:43
  7.2 9.7 %collective-permute-start.2 = (bf16[32,1920]{1,0:T(8,128)(2,1)S(1)}, bf16[32,1920]{1,0:T(8,128)(2,1)S(1)}, u32[]{:S(2)}, u32[]{:S(2)}) collective-permute-start(bf16[32,1920]{1,0:T(8,128)(2,1)S(1)} %get-tuple-element.67), channel_id=1, source_target_pairs={{0,3},{1,2},{2,1},{3,0},{4,7},{5,6},{6,5},{7,4},{8,11},{9,10},{10,... | collective-permute-start | bytes 368648 | tf_op jit(solution)/shard_map/ppermute | solution.py:43
  17.2 4.9 %collective-permute-start.3 = (bf16[32,1920]{1,0:T(8,128)(2,1)S(1)}, bf16[32,1920]{1,0:T(8,128)(2,1)S(1)}, u32[]{:S(2)}, u32[]{:S(2)}) collective-permute-start(bf16[32,1920]{1,0:T(8,128)(2,1)S(1)} %get-tuple-element.70.refs_0_), channel_id=1, source_target_pairs={{0,1},{1,0},{2,3},{3,2},{4,5},{5,4},{6,7},{7,6},{8,9},{9,8},{10,11... | collective-permute-start | bytes 368648 | tf_op jit(solution)/shard_map/ppermute | solution.py:43
  22.2 12.1 %collective-permute-start.6 = (bf16[64,1920]{1,0:T(8,128)(2,1)S(1)}, bf16[64,1920]{1,0:T(8,128)(2,1)S(1)}, u32[]{:S(2)}, u32[]{:S(2)}) collective-permute-start(bf16[64,1920]{1,0:T(8,128)(2,1)S(1)} %join.1.refs_2_), channel_id=1, source_target_pairs={{0,2},{1,3},{2,0},{3,1},{4,6},{5,7},{6,4},{7,5},{8,10},{9,11},{10,... | collective-permute-start | bytes 737288 | tf_op jit(solution)/shard_map/ppermute | solution.py:43
  25.2 9.0 %collective-permute-start.10 = (bf16[64,1920]{1,0:T(8,128)(2,1)S(1)}, bf16[64,1920]{1,0:T(8,128)(2,1)S(1)}, u32[]{:S(2)}, u32[]{:S(2)}) collective-permute-start(bf16[64,1920]{1,0:T(8,128)(2,1)S(1)} %join.1.refs_2_), channel_id=1, source_target_pairs={{0,24},{4,28},{8,16},{12,20},{16,8},{20,12},{24,0},{28,4},{1,25},{... | collective-permute-start | bytes 737288 | tf_op jit(solution)/shard_map/ppermute | solution.py:43
  27.7 8.9 %collective-permute-start.8 = (bf16[64,1920]{1,0:T(8,128)(2,1)S(1)}, bf16[64,1920]{1,0:T(8,128)(2,1)S(1)}, u32[]{:S(2)}, u32[]{:S(2)}) collective-permute-start(bf16[64,1920]{1,0:T(8,128)(2,1)S(1)} %join.1.refs_2_), channel_id=1, source_target_pairs={{0,16},{4,20},{8,24},{12,28},{16,0},{20,4},{24,8},{28,12},{1,17},{... | collective-permute-start | bytes 737288 | tf_op jit(solution)/shard_map/ppermute | solution.py:43
  28.2 8.6 %collective-permute-start.5 = (bf16[64,1920]{1,0:T(8,128)(2,1)S(1)}, bf16[64,1920]{1,0:T(8,128)(2,1)S(1)}, u32[]{:S(2)}, u32[]{:S(2)}) collective-permute-start(bf16[64,1920]{1,0:T(8,128)(2,1)S(1)} %join.1.refs_2_), channel_id=1, source_target_pairs={{0,8},{4,12},{8,0},{12,4},{16,24},{20,28},{24,16},{28,20},{1,9},{5... | collective-permute-start | bytes 737288 | tf_op jit(solution)/shard_map/ppermute | solution.py:43
  28.7 10.1 %collective-permute-start.4 = (bf16[64,1920]{1,0:T(8,128)(2,1)S(1)}, bf16[64,1920]{1,0:T(8,128)(2,1)S(1)}, u32[]{:S(2)}, u32[]{:S(2)}) collective-permute-start(bf16[64,1920]{1,0:T(8,128)(2,1)S(1)} %join.1.refs_2_), channel_id=1, source_target_pairs={{0,4},{4,0},{8,12},{12,8},{16,20},{20,16},{24,28},{28,24},{1,5},{5... | collective-permute-start | bytes 737288 | tf_op jit(solution)/shard_map/ppermute | solution.py:43
  36.7 3.5 %collective-permute-start.7 = (bf16[64,1920]{1,0:T(8,128)(2,1)S(1)}, bf16[64,1920]{1,0:T(8,128)(2,1)S(1)}, u32[]{:S(2)}, u32[]{:S(2)}) collective-permute-start(bf16[64,1920]{1,0:T(8,128)(2,1)S(1)} %collective-permute-done.5.refs_4_), channel_id=1, source_target_pairs={{0,4},{4,0},{8,12},{12,8},{16,20},{20,16},{24,28},{28,24},{1,5},{5... | collective-permute-start | bytes 737288 | tf_op jit(solution)/shard_map/ppermute | solution.py:43
  36.8 4.0 %collective-permute-start.9 = (bf16[64,1920]{1,0:T(8,128)(2,1)S(1)}, bf16[64,1920]{1,0:T(8,128)(2,1)S(1)}, u32[]{:S(2)}, u32[]{:S(2)}) collective-permute-start(bf16[64,1920]{1,0:T(8,128)(2,1)S(1)} %collective-permute-done.8.refs_6_), channel_id=1, source_target_pairs={{0,4},{4,0},{8,12},{12,8},{16,20},{20,16},{24,28},{28,24},{1,5},{5... | collective-permute-start | bytes 737288 | tf_op jit(solution)/shard_map/ppermute | solution.py:43
  37.3 3.5 %collective-permute-start.11 = (bf16[64,1920]{1,0:T(8,128)(2,1)S(1)}, bf16[64,1920]{1,0:T(8,128)(2,1)S(1)}, u32[]{:S(2)}, u32[]{:S(2)}) collective-permute-start(bf16[64,1920]{1,0:T(8,128)(2,1)S(1)} %collective-permute-done.10.refs_8_), channel_id=1, source_target_pairs={{0,4},{4,0},{8,12},{12,8},{16,20},{20,16},{24,28},{28,24},{1,5},{5... | collective-permute-start | bytes 737288 | tf_op jit(solution)/shard_map/ppermute | solution.py:43
  37.3 13.5 %collective-permute-start.17 = (bf16[64,1920]{1,0:T(8,128)(2,1)S(1)}, bf16[64,1920]{1,0:T(8,128)(2,1)S(1)}, u32[]{:S(2)}, u32[]{:S(2)}) collective-permute-start(bf16[64,1920]{1,0:T(8,128)(2,1)S(1)} %collective-permute-done.6.refs_2_), channel_id=1, source_target_pairs={{0,24},{4,28},{8,16},{12,20},{16,8},{20,12},{24,0},{28,4},{1,25},{... | collective-permute-start | bytes 737288 | tf_op jit(solution)/shard_map/ppermute | solution.py:43
  38.9 12.9 %collective-permute-start.15 = (bf16[64,1920]{1,0:T(8,128)(2,1)S(1)}, bf16[64,1920]{1,0:T(8,128)(2,1)S(1)}, u32[]{:S(2)}, u32[]{:S(2)}) collective-permute-start(bf16[64,1920]{1,0:T(8,128)(2,1)S(1)} %collective-permute-done.6.refs_2_), channel_id=1, source_target_pairs={{0,16},{4,20},{8,24},{12,28},{16,0},{20,4},{24,8},{28,12},{1,17},{... | collective-permute-start | bytes 737288 | tf_op jit(solution)/shard_map/ppermute | solution.py:43
  40.2 11.6 %collective-permute-start.13 = (bf16[64,1920]{1,0:T(8,128)(2,1)S(1)}, bf16[64,1920]{1,0:T(8,128)(2,1)S(1)}, u32[]{:S(2)}, u32[]{:S(2)}) collective-permute-start(bf16[64,1920]{1,0:T(8,128)(2,1)S(1)} %collective-permute-done.6.refs_2_), channel_id=1, source_target_pairs={{0,8},{4,12},{8,0},{12,4},{16,24},{20,28},{24,16},{28,20},{1,9},{5... | collective-permute-start | bytes 737288 | tf_op jit(solution)/shard_map/ppermute | solution.py:43
  52.4 2.0 %collective-permute-start.18 = (bf16[64,1920]{1,0:T(8,128)(2,1)S(1)}, bf16[64,1920]{1,0:T(8,128)(2,1)S(1)}, u32[]{:S(2)}, u32[]{:S(2)}) collective-permute-start(bf16[64,1920]{1,0:T(8,128)(2,1)S(1)} %collective-permute-done.17.refs_8_), channel_id=1, source_target_pairs={{0,4},{4,0},{8,12},{12,8},{16,20},{20,16},{24,28},{28,24},{1,5},{5... | collective-permute-start | bytes 737288 | tf_op jit(solution)/shard_map/ppermute | solution.py:43
  66.6 3.8 %collective-permute-start.19 = (bf16[128,1792]{1,0:T(8,128)(2,1)S(1)}, bf16[128,1792]{1,0:T(8,128)(2,1)S(1)}, u32[]{:S(2)}, u32[]{:S(2)}) collective-permute-start(bf16[128,1792]{1,0:T(8,128)(2,1)S(1)} %get-tuple-element.89), channel_id=1, source_target_pairs={{0,4},{4,0},{8,12},{12,8},{16,20},{20,16},{24,28},{28,24},{1,5},{5... | collective-permute-start | bytes 1376264 | tf_op jit(solution)/shard_map/ppermute | solution.py:43
  70.5 10.6 %collective-permute-start.20 = (bf16[64,1792]{1,0:T(8,128)(2,1)S(1)}, bf16[64,1792]{1,0:T(8,128)(2,1)S(1)}, u32[]{:S(2)}, u32[]{:S(2)}) collective-permute-start(bf16[64,1792]{1,0:T(8,128)(2,1)S(1)} %get-tuple-element.120), channel_id=1, source_target_pairs={{0,16},{4,20},{8,24},{12,28},{16,0},{20,4},{24,8},{28,12},{1,17},{... | collective-permute-start | bytes 688136 | tf_op jit(solution)/shard_map/ppermute | solution.py:43
  72.1 9.8 %collective-permute-start.24 = (bf16[64,1792]{1,0:T(8,128)(2,1)S(1)}, bf16[64,1792]{1,0:T(8,128)(2,1)S(1)}, u32[]{:S(2)}, u32[]{:S(2)}) collective-permute-start(bf16[64,1792]{1,0:T(8,128)(2,1)S(1)} %get-tuple-element.122), channel_id=1, source_target_pairs={{0,8},{4,12},{8,0},{12,4},{16,24},{20,28},{24,16},{28,20},{1,9},{5... | collective-permute-start | bytes 688136 | tf_op jit(solution)/shard_map/ppermute | solution.py:43
  80.5 8.0 %collective-permute-start.29 = (bf16[128,1792]{1,0:T(8,128)(2,1)S(1)}, bf16[128,1792]{1,0:T(8,128)(2,1)S(1)}, u32[]{:S(2)}, u32[]{:S(2)}) collective-permute-start(bf16[128,1792]{1,0:T(8,128)(2,1)S(1)} %get-tuple-element.109), channel_id=1, source_target_pairs={{0,4},{4,0},{8,12},{12,8},{16,20},{20,16},{24,28},{28,24},{1,5},{5... | collective-permute-start | bytes 1376264 | tf_op jit(solution)/shard_map/ppermute | solution.py:43
  80.7 2.6 %collective-permute-start.23 = (bf16[128,1792]{1,0:T(8,128)(2,1)S(1)}, bf16[128,1792]{1,0:T(8,128)(2,1)S(1)}, u32[]{:S(2)}, u32[]{:S(2)}) collective-permute-start(bf16[128,1792]{1,0:T(8,128)(2,1)S(1)} %get-tuple-element.100), channel_id=1, source_target_pairs={{0,4},{4,0},{8,12},{12,8},{16,20},{20,16},{24,28},{28,24},{1,5},{5... | collective-permute-start | bytes 1376264 | tf_op jit(solution)/shard_map/ppermute | solution.py:43
  81.1 5.3 %collective-permute-start.22 = (bf16[32,1792]{1,0:T(8,128)(2,1)S(1)}, bf16[32,1792]{1,0:T(8,128)(2,1)S(1)}, u32[]{:S(2)}, u32[]{:S(2)}) collective-permute-start(bf16[32,1792]{1,0:T(8,128)(2,1)S(1)} %add_convert_fusion.18), channel_id=1, source_target_pairs={{0,8},{4,12},{8,0},{12,4},{16,24},{20,28},{24,16},{28,20},{1,9},{5... | collective-permute-start | bytes 344072 | tf_op jit(solution)/shard_map/ppermute | solution.py:43
  81.9 5.6 %collective-permute-start.26 = (bf16[32,1792]{1,0:T(8,128)(2,1)S(1)}, bf16[32,1792]{1,0:T(8,128)(2,1)S(1)}, u32[]{:S(2)}, u32[]{:S(2)}) collective-permute-start(bf16[32,1792]{1,0:T(8,128)(2,1)S(1)} %add_convert_fusion.17), channel_id=1, source_target_pairs={{0,16},{4,20},{8,24},{12,28},{16,0},{20,4},{24,8},{28,12},{1,17},{... | collective-permute-start | bytes 344072 | tf_op jit(solution)/shard_map/ppermute | solution.py:43
  83.3 15.4 %collective-permute-start.31 = (bf16[32,1792]{1,0:T(8,128)(2,1)S(1)}, bf16[32,1792]{1,0:T(8,128)(2,1)S(1)}, u32[]{:S(2)}, u32[]{:S(2)}) collective-permute-start(bf16[32,1792]{1,0:T(8,128)(2,1)S(1)} %get-tuple-element.115), channel_id=1, source_target_pairs={{0,24},{4,28},{8,16},{12,20},{16,8},{20,12},{24,0},{28,4},{1,25},{... | collective-permute-start | bytes 344072 | tf_op jit(solution)/shard_map/ppermute | solution.py:43
  86.5 16.3 %collective-permute-start.25 = (bf16[32,1792]{1,0:T(8,128)(2,1)S(1)}, bf16[32,1792]{1,0:T(8,128)(2,1)S(1)}, u32[]{:S(2)}, u32[]{:S(2)}) collective-permute-start(bf16[32,1792]{1,0:T(8,128)(2,1)S(1)} %add_convert_fusion.15), channel_id=1, source_target_pairs={{0,3},{1,2},{2,1},{3,0},{4,7},{5,6},{6,5},{7,4},{8,11},{9,10},{10,... | collective-permute-start | bytes 344072 | tf_op jit(solution)/shard_map/ppermute | solution.py:43
  87.6 15.3 %collective-permute-start.27 = (bf16[32,1792]{1,0:T(8,128)(2,1)S(1)}, bf16[32,1792]{1,0:T(8,128)(2,1)S(1)}, u32[]{:S(2)}, u32[]{:S(2)}) collective-permute-start(bf16[32,1792]{1,0:T(8,128)(2,1)S(1)} %add_convert_fusion.13), channel_id=1, source_target_pairs={{0,2},{1,3},{2,0},{3,1},{4,6},{5,7},{6,4},{7,5},{8,10},{9,11},{10,... | collective-permute-start | bytes 344072 | tf_op jit(solution)/shard_map/ppermute | solution.py:43
  88.5 6.1 %collective-permute-start.28 = (bf16[32,1792]{1,0:T(8,128)(2,1)S(1)}, bf16[32,1792]{1,0:T(8,128)(2,1)S(1)}, u32[]{:S(2)}, u32[]{:S(2)}) collective-permute-start(bf16[32,1792]{1,0:T(8,128)(2,1)S(1)} %get-tuple-element.113), channel_id=1, source_target_pairs={{0,8},{4,12},{8,0},{12,4},{16,24},{20,28},{24,16},{28,20},{1,9},{5... | collective-permute-start | bytes 344072 | tf_op jit(solution)/shard_map/ppermute | solution.py:43
  91.1 6.9 %collective-permute-start.30 = (bf16[32,1792]{1,0:T(8,128)(2,1)S(1)}, bf16[32,1792]{1,0:T(8,128)(2,1)S(1)}, u32[]{:S(2)}, u32[]{:S(2)}) collective-permute-start(bf16[32,1792]{1,0:T(8,128)(2,1)S(1)} %get-tuple-element.114), channel_id=1, source_target_pairs={{0,16},{4,20},{8,24},{12,28},{16,0},{20,4},{24,8},{28,12},{1,17},{... | collective-permute-start | bytes 344072 | tf_op jit(solution)/shard_map/ppermute | solution.py:43
  94.6 8.9 %collective-permute-start.35 = (bf16[32,1792]{1,0:T(8,128)(2,1)S(1)}, bf16[32,1792]{1,0:T(8,128)(2,1)S(1)}, u32[]{:S(2)}, u32[]{:S(2)}) collective-permute-start(bf16[32,1792]{1,0:T(8,128)(2,1)S(1)} %get-tuple-element.118), channel_id=1, source_target_pairs={{0,24},{4,28},{8,16},{12,20},{16,8},{20,12},{24,0},{28,4},{1,25},{... | collective-permute-start | bytes 344072 | tf_op jit(solution)/shard_map/ppermute | solution.py:43
  97.9 4.8 %collective-permute-start.33 = (bf16[32,1792]{1,0:T(8,128)(2,1)S(1)}, bf16[32,1792]{1,0:T(8,128)(2,1)S(1)}, u32[]{:S(2)}, u32[]{:S(2)}) collective-permute-start(bf16[32,1792]{1,0:T(8,128)(2,1)S(1)} %get-tuple-element.116), channel_id=1, source_target_pairs={{0,16},{4,20},{8,24},{12,28},{16,0},{20,4},{24,8},{28,12},{1,17},{... | collective-permute-start | bytes 344072 | tf_op jit(solution)/shard_map/ppermute | solution.py:43
  98.7 4.8 %collective-permute-start.34 = (bf16[32,1792]{1,0:T(8,128)(2,1)S(1)}, bf16[32,1792]{1,0:T(8,128)(2,1)S(1)}, u32[]{:S(2)}, u32[]{:S(2)}) collective-permute-start(bf16[32,1792]{1,0:T(8,128)(2,1)S(1)} %get-tuple-element.117), channel_id=1, source_target_pairs={{0,8},{4,12},{8,0},{12,4},{16,24},{20,28},{24,16},{28,20},{1,9},{5... | collective-permute-start | bytes 344072 | tf_op jit(solution)/shard_map/ppermute | solution.py:43
  102.7 4.8 %collective-permute-start.32 = (bf16[32,1792]{1,0:T(8,128)(2,1)S(1)}, bf16[32,1792]{1,0:T(8,128)(2,1)S(1)}, u32[]{:S(2)}, u32[]{:S(2)}) collective-permute-start(bf16[32,1792]{1,0:T(8,128)(2,1)S(1)} %add_convert_fusion.8), channel_id=1, source_target_pairs={{0,1},{1,0},{2,3},{3,2},{4,5},{5,4},{6,7},{7,6},{8,9},{9,8},{10,11... | collective-permute-start | bytes 344072 | tf_op jit(solution)/shard_map/ppermute | solution.py:43
  (4 other events, 7.0 us)
